TPU v7x, 32 devices: a whole 2x2x4 slice. The times are simulated.
32 devices in a mesh: rep: 2 (over x), shard: 16 (over z, y, core).
Axes of the slice: x: 2, y: 2, z: 4, core: 2. Of those that a mesh axis runs over, the one named last changes fastest.
Arguments:
- tokens: bfloat16 [2, 32, 64, 1024], P(None, ('rep', 'shard')), may hold values from -6 to 6
- prefix: int32 [2, 32], P(None, ('rep', 'shard')), may hold values from 6 to 32
- qkv_weight: bfloat16 [1024, 3072], P('shard'), may hold values from -0.1875 to 0.1875
- out_weight: bfloat16 [1024, 1024], P('shard'), may hold values from -1 to 1
- in_weight: bfloat16 [1024, 5632], P('shard'), may hold values from -0.1875 to 0.1875
- down_weight: bfloat16 [2816, 1024], P('shard'), may hold values from -0.109375 to 0.109375
- cotangent: bfloat16 [2, 32, 64, 1024], P(None, ('rep', 'shard')), may hold values from -6 to 6
Outputs:
- result: bfloat16 [2, 32, 64, 1024], P(None, ('rep', 'shard'))
- grad_tokens: float32 [2, 32, 64, 1024], P(None, ('rep', 'shard'))
- grad_qkv: float32 [1024, 3072], P('shard')
- grad_out: float32 [1024, 1024], P('shard')
- grad_in: float32 [1024, 5632], P('shard')
- grad_down: float32 [2816, 1024], P('shard')
Inputs may be any that keep to these rules, and one draw needn't show every extreme that they name: Each sequence's prefix length, a tenth to a half of 64.
All inputs are finite; a program needn't handle non-finite values.
Results may differ from a plain program's by a relative error of at most 0.014.
Values may be sent and summed in bfloat16 or wider, within the bound.
No kernel may reach another device: no remote copies, remote signals or barrier semaphores. Data moves between devices by JAX's collectives and lax.ppermute only.
A program may use at most 256 MiB of HBM per device.

v0:
```python
import functools

import jax
import jax.numpy as jnp
import numpy as np
from jax import lax
from jax.experimental import pallas as pl
from jax.experimental.pallas import tpu as pltpu
from jax.sharding import Mesh, PartitionSpec as P

H = 16
HD = 64
HALF = HD // 2
LANES = 128
PACK = 16
BF = jnp.bfloat16
F32 = jnp.float32
SWAP = ((0, 1), (1, 0))
MIB = 1 << 20
BLOCKS = ((0, 1, 2, 3), (1, 0, 3, 2), (2, 3, 0, 1), (3, 2, 1, 0))


def dot(left, right):
    return jnp.dot(left, right, preferred_element_type=F32)


def dot_rt(left, right):
    return lax.dot_general(left, right, (((1,), (1,)), ((), ())), preferred_element_type=F32)


def dot_lt(left, right):
    return lax.dot_general(left, right, (((0,), (0,)), ((), ())), preferred_element_type=F32)


def norm_rows(values):
    centre = values - jnp.mean(values, axis=-1, keepdims=True)
    inverse = lax.rsqrt(jnp.mean(centre * centre, axis=-1, keepdims=True) + 1e-05)
    return (centre * inverse, inverse)


def norm_back(normed, inverse, upstream):
    return inverse * (
        upstream
        - jnp.mean(upstream, axis=-1, keepdims=True)
        - normed * jnp.mean(upstream * normed, axis=-1, keepdims=True)
    )


def across(value):
    return lax.ppermute(value, "rep", SWAP)


def sibling(value):
    return lax.ppermute(value, "core", SWAP)


def order_of(size):
    return list(range(0, size, 2)) + list(range(size - 1, 0, -2))


def scalar_table(size):
    order = order_of(size)
    place = np.argsort(order)
    table = np.zeros((2, size, 2, 2 * size + 5), np.int32)
    for rep in range(2):
        for g in range(size):
            for core in range(2):
                at = [order[(place[g] + k) % size] for k in range(size)]
                of = [(place[o] - place[g]) % size for o in range(size)]
                members = [2 * core + rep, 2 * (1 - core) + rep, 2 * core + 1 - rep, 2 * (1 - core) + 1 - rep]
                table[rep, g, core] = at + of + [core] + members
    return table


def upper_half(rows):
    return -(-(rows // 2) // PACK) * PACK


class Ring:
    def __init__(self, size):
        self.size = size
        self.half = size // 2
        order = order_of(size)
        self.right = [(order[i], order[(i + 1) % size]) for i in range(size)]
        self.left = [(b, a) for a, b in self.right]

    def go_right(self, value):
        return lax.ppermute(value, "ring", self.right)

    def go_left(self, value):
        return lax.ppermute(value, "ring", self.left)

    def gather(self, chunk):
        got = {0: chunk}
        right = left = chunk
        for step in range(1, self.half):
            right = self.go_right(right)
            left = self.go_left(left)
            got[self.size - step] = right
            got[step] = left
        cut = upper_half(chunk.shape[0])
        far = [self.go_right(right[:cut]), self.go_left(left[cut:])]
        return [got[k] for k in range(self.size) if k != self.half] + far

    def scatter(self, parts):
        cut = upper_half(parts.shape[1])
        rest = parts.shape[1] - cut
        far = parts[self.half]
        right = self.go_right(far[:cut].astype(BF)).astype(F32)
        left = self.go_left(far[cut:].astype(BF)).astype(F32)
        right = jnp.pad(right, ((0, rest), (0, 0)))
        left = jnp.pad(left, ((cut, 0), (0, 0)))
        for step in range(self.half - 1, 0, -1):
            right = self.go_right((parts[step] + right).astype(BF)).astype(F32)
            left = self.go_left((parts[self.size - step] + left).astype(BF)).astype(F32)
        return parts[0] + right + left


def call(body, outs, scratch, limit, flops, *args):
    nbytes = sum(a.size * a.dtype.itemsize for a in args) + sum(o.size * o.dtype.itemsize for o in outs)
    return pl.pallas_call(
        body,
        out_shape=outs,
        in_specs=[pl.BlockSpec(memory_space=pltpu.SMEM)] + [pl.BlockSpec(memory_space=pltpu.VMEM)] * (len(args) - 1),
        out_specs=[pl.BlockSpec(memory_space=pltpu.VMEM)] * len(outs),
        scratch_shapes=scratch,
        compiler_params=pltpu.CompilerParams(vmem_limit_bytes=limit * MIB),
        cost_estimate=pl.CostEstimate(flops=flops, bytes_accessed=nbytes, transcendentals=0),
    )(*args)


def shape(dims, dtype):
    return jax.ShapeDtypeStruct(dims, dtype)


def lanes(start, size):
    return pl.ds(pl.multiple_of(start, LANES), size)


def pack_first(size, width, scal, qkv_ref, out_ref, own_ref, sib_ref):
    quarter = width // 4
    for ref, member in ((own_ref, scal[2 * size + 1]), (sib_ref, scal[2 * size + 2])):
        for j in range(3):
            ref[:, j * quarter : (j + 1) * quarter] = qkv_ref[:, lanes(j * width + member * quarter, quarter)]
        ref[:, 3 * quarter :] = out_ref[:, lanes(member * quarter, quarter)]


def pack_in(size, units, piece, padded, scal, in_ref, own_ref, sib_ref):
    for ref, member in ((own_ref, scal[2 * size + 1]), (sib_ref, scal[2 * size + 2])):
        ref[...] = jnp.zeros_like(ref)
        for q in range(4):

            @pl.when(member == q)
            def _(ref=ref, q=q):
                for part in range(2):
                    for g in range(size):
                        start = part * units + (g * 4 + q) * piece
                        to = (part * size + g) * padded
                        ref[:, to : to + piece] = in_ref[:, start : start + piece]


def place_chunks(size, scal, chunk_refs, store):
    half = size // 2
    places = [k for k in range(size) if k != half]
    for k, ref in zip(places, chunk_refs, strict=False):
        store(scal[k], 0, ref[...])
    top, bottom = chunk_refs[-2:]
    store(scal[half], 0, top[...])
    store(scal[half], top.shape[0], bottom[...])


def place_rows(size, shard_rows, scal, chunk_refs, put):
    core = scal[2 * size]

    def store(chip, first, value):
        for lower in range(2):
            begin = lower * shard_rows - first
            if begin < 0 or begin >= value.shape[0]:
                continue
            row = chip * (2 * shard_rows) + (core if lower == 0 else 1 - core) * shard_rows
            put(pl.multiple_of(row, PACK), value[begin : begin + shard_rows])

    place_chunks(size, scal, chunk_refs, store)


def turned(values):
    lane = lax.broadcasted_iota(jnp.int32, values.shape, 1) % HD
    wide = values.shape[1]
    return jnp.where(lane < HALF, pltpu.roll(values, wide - HALF, 1), pltpu.roll(values, HALF, 1))


def visible(rows, length, limits):
    query = lax.broadcasted_iota(jnp.int32, (rows, rows), 0)
    key = lax.broadcasted_iota(jnp.int32, (rows, rows), 1)
    inside = (key % length).astype(F32)
    limit = jnp.zeros((rows, rows), F32)
    for s in range(rows // length):
        limit = jnp.where(key // length == s, limits[s : s + 1, :rows].astype(F32), limit)
    return (query // length == key // length) & ((key <= query) | (inside < limit))


def attention(size, shard_rows, rows, length, width, n_chunks, scal, *refs):
    blocks = refs[:4]
    chunks = refs[4 : 4 + n_chunks]
    cos_ref, sin_ref, o_ref, h1_ref, qkv_ref, p_ref, w_ref, out_ref = refs[4 + n_chunks :]
    quarter = width // 4

    def put(row, value):
        w_ref[pl.ds(row, shard_rows), :] = value[:, : 3 * quarter]
        out_ref[pl.ds(row, shard_rows), :] = value[:, 3 * quarter :]

    place_rows(size, shard_rows, scal, chunks, put)
    for b in range(4):
        normed, _ = norm_rows(blocks[b][:rows, :].astype(F32))
        h1_ref[b * rows : (b + 1) * rows, :] = normed.astype(BF)
    for j in range(3):
        mixed = dot(h1_ref[...], w_ref[:, j * quarter : (j + 1) * quarter])
        for b in range(4):
            piece = mixed[b * rows : (b + 1) * rows, :]
            if j < 2:
                piece = piece * cos_ref[...] + turned(piece) * sin_ref[...]
            qkv_ref[b * rows : (b + 1) * rows, j * quarter : (j + 1) * quarter] = piece.astype(BF)
    for b in range(4):
        allowed = visible(rows, length, blocks[b][rows:, :])
        block = slice(b * rows, (b + 1) * rows)
        for h in range(quarter // HD):
            query = qkv_ref[block, h * HD : (h + 1) * HD]
            keys = qkv_ref[block, quarter + h * HD : quarter + (h + 1) * HD]
            values = qkv_ref[block, 2 * quarter + h * HD : 2 * quarter + (h + 1) * HD]
            scores = jnp.where(allowed, dot_rt(query, keys) * HD ** (-0.5), -1e30)
            expo = jnp.exp(scores - jnp.max(scores, axis=-1, keepdims=True))
            probs = expo / jnp.sum(expo, axis=-1, keepdims=True)
            p_ref[b * (quarter // HD) + h] = probs
            o_ref[b, :, h * HD : (h + 1) * HD] = dot(probs.astype(BF), values).astype(BF)


def middle(size, rows, width, scal, *refs):
    blocks = refs[:4]
    o_own, o_far, o_near, w_own, w_near, w_far, x2_ref, h2_ref, o_ref, rows_ref, w_full = refs[4:]
    quarter = width // 4
    members = [scal[2 * size + 1 + m] for m in range(4)]
    weights = (w_own[...], w_near[...], w_far[0], w_far[1])
    for m in range(4):
        w_full[:, lanes(members[m] * quarter, quarter)] = weights[m]
        for b in range(4):
            kept = BLOCKS[m][b]
            value = (o_own, o_near.at[0], o_far, o_near.at[1])[m][kept]
            o_ref[b * rows : (b + 1) * rows, lanes(members[m] * quarter, quarter)] = value
    rows_ref[...] = w_full[pl.ds(pl.multiple_of(members[0] * quarter, quarter), quarter), :]
    for j in range(4):
        columns = slice(j * quarter, (j + 1) * quarter)
        added = dot(o_ref[...], w_full[:, columns])
        for b in range(4):
            x2_ref[b * rows : (b + 1) * rows, columns] = blocks[b][:rows, columns].astype(F32) + added[b * rows : (b + 1) * rows, :]
    for b in range(4):
        block = slice(b * rows, (b + 1) * rows)
        normed, _ = norm_rows(x2_ref[block, :])
        h2_ref[block, :] = normed.astype(BF)


def hidden_units(size, shard_rows, members_units, n_chunks, scal, h2_ref, *refs):
    chunks = refs[:n_chunks]
    up_ref, gate_ref, hid_ref, w_ref = refs[n_chunks:]

    def put(row, value):
        w_ref[pl.ds(row, shard_rows), :] = value

    place_rows(size, shard_rows, scal, chunks, put)
    tile = 256

    @pl.loop(0, members_units // tile)
    def _(i):
        at = pl.multiple_of(i * tile, tile)
        up = dot(h2_ref[...], w_ref[:, pl.ds(at, tile)])
        gate = dot(h2_ref[...], w_ref[:, pl.ds(members_units + at, tile)])
        up_ref[:, pl.ds(at, tile)] = up
        gate_ref[:, pl.ds(at, tile)] = gate
        hid_ref[:, pl.ds(at, tile)] = (gate * jax.nn.sigmoid(gate) * up).astype(BF)


def hidden_back(size, rows, padded, piece, n_chunks, scal, *refs):
    cots = refs[:4]
    chunks = refs[4 : 4 + n_chunks]
    up_ref, gate_ref, w_in, ggu_ref, keep_ref, give_ref, down_ref, gm_ref = refs[4 + n_chunks :]
    units = up_ref.shape[1]
    width = gm_ref.shape[1]
    down_ref[...] = jnp.zeros_like(down_ref)

    def store(chip, first, value):
        down_ref[pl.ds(pl.multiple_of(chip * padded + first, PACK), value.shape[0]), :] = value

    place_chunks(size, scal, chunks, store)
    for b in range(4):
        gm_ref[b * rows : (b + 1) * rows, :] = cots[b][...]
    tile = 256

    @pl.loop(0, units // tile)
    def _(i):
        at = pl.multiple_of(i * tile, tile)
        grad = dot_rt(gm_ref[...], down_ref[pl.ds(at, tile), :])
        up = up_ref[:, pl.ds(at, tile)]
        gate = gate_ref[:, pl.ds(at, tile)]
        sig = jax.nn.sigmoid(gate)
        ggu_ref[:, pl.ds(at, tile)] = (grad * (gate * sig)).astype(BF)
        ggu_ref[:, pl.ds(units + at, tile)] = (grad * up * (sig * (1.0 + gate * (1.0 - sig)))).astype(BF)

    @pl.loop(0, width // tile)
    def _(i):
        at = pl.multiple_of(i * tile, tile)
        back = dot_rt(ggu_ref[...], w_in[pl.ds(at, tile), :])
        share(back, rows, keep_ref, give_ref, pl.ds(at, tile))


def share(partial, rows, keep_ref, give_ref, columns):
    keep_ref[0, :, columns] = partial[:rows]
    give_ref[0, :, columns] = partial[rows : 2 * rows].astype(BF)
    keep_ref[1, :, columns] = partial[2 * rows : 3 * rows]
    give_ref[1, :, columns] = partial[3 * rows :].astype(BF)


def last_projection(rows, scal, hid_ref, down_ref, keep_ref, give_ref):
    tile = 256

    @pl.loop(0, down_ref.shape[1] // tile)
    def _(i):
        columns = pl.ds(pl.multiple_of(i * tile, tile), tile)
        share(dot(hid_ref[...], down_ref[:, columns]), rows, keep_ref, give_ref, columns)


def grad_down_parts(size, padded, piece, scal, hid_ref, gm_ref, part_ref):
    tile = 256

    @pl.loop(0, gm_ref.shape[1] // tile)
    def _(i):
        columns = pl.ds(pl.multiple_of(i * tile, tile), tile)
        grads = dot_lt(hid_ref[...], gm_ref[:, columns])
        for g in range(size):
            part_ref[scal[size + g], :, columns] = grads[g * padded : g * padded + piece]


def grad_in_parts(size, double, scal, h2_ref, ggu_ref, part_ref):
    tile = 256

    @pl.loop(0, ggu_ref.shape[1] // tile)
    def _(i):
        columns = pl.ds(pl.multiple_of(i * tile, tile), tile)
        grads = dot_lt(h2_ref[...], ggu_ref[:, columns])
        for g in range(size):
            part_ref[scal[size + g], :, columns] = grads[g * double : (g + 1) * double]


def middle_back(rows, scal, keep_ref, got_ref, far_ref, x2_ref, cot_own, cot_far, gx2_ref, ga_ref):
    for i, cot in ((0, cot_own), (1, cot_far)):
        upstream = keep_ref[i] + got_ref[i].astype(F32) + far_ref[1 - i].astype(F32)
        normed, inverse = norm_rows(x2_ref[2 * i * rows : (2 * i + 1) * rows, :])
        total = cot[...].astype(F32) + norm_back(normed, inverse, upstream)
        if i == 0:
            gx2_ref[...] = total
        ga_ref[i] = total.astype(BF)


def attention_back(rows, width, scal, ga_own, ga_near, out_rows, qkv_ref, p_ref, w_ref, cos_ref, sin_ref, gqkv_ref, ga_ref, keep_ref, give_ref, go_ref, grad_ref):
    quarter = width // 4
    for b, value in enumerate((ga_own[0], ga_near[0], ga_own[1], ga_near[1])):
        ga_ref[b * rows : (b + 1) * rows, :] = value
    go_ref[...] = dot_rt(ga_ref[...], out_rows[...]).astype(BF)
    for b in range(4):
        block = slice(b * rows, (b + 1) * rows)
        for h in range(quarter // HD):
            head = slice(h * HD, (h + 1) * HD)
            query = qkv_ref[block, h * HD : (h + 1) * HD]
            keys = qkv_ref[block, quarter + h * HD : quarter + (h + 1) * HD]
            values = qkv_ref[block, 2 * quarter + h * HD : 2 * quarter + (h + 1) * HD]
            probs = p_ref[b * (quarter // HD) + h]
            go = go_ref[block, head]
            dprob = dot_rt(go, values)
            centre = jnp.sum(probs * dprob, axis=-1, keepdims=True)
            dscore = (probs * (dprob - centre)).astype(BF)
            grad_ref[0, :, head] = dot(dscore, keys) * HD ** (-0.5)
            grad_ref[1, :, head] = dot_lt(dscore, query) * HD ** (-0.5)
            grad_ref[2, :, head] = dot_lt(probs.astype(BF), go)
        for j in range(3):
            grad = grad_ref[j]
            if j < 2:
                grad = grad * cos_ref[...] - turned(grad) * sin_ref[...]
            gqkv_ref[block, j * quarter : (j + 1) * quarter] = grad.astype(BF)
    for j in range(4):
        columns = slice(j * quarter, (j + 1) * quarter)
        share(dot_rt(gqkv_ref[...], w_ref[columns, :]), rows, keep_ref, give_ref, columns)


def grad_first_parts(size, double, width, scal, h1_ref, gqkv_ref, o_ref, ga_ref, part_ref):
    quarter = width // 4
    for j in range(4):
        if j < 3:
            grads = dot_lt(h1_ref[...], gqkv_ref[:, j * quarter : (j + 1) * quarter])
        else:
            grads = dot_lt(o_ref[...], ga_ref[:, lanes(scal[2 * size + 1] * quarter, quarter)])
        for g in range(size):
            part_ref[scal[size + g], :, j * quarter : (j + 1) * quarter] = grads[g * double : (g + 1) * double]


def finish_tokens(rows, scal, keep_ref, got_ref, far_ref, block_ref, gx2_ref, out_ref):
    upstream = keep_ref[0] + got_ref[0].astype(F32) + far_ref[...].astype(F32)
    normed, inverse = norm_rows(block_ref[:rows, :].astype(F32))
    out_ref[...] = gx2_ref[...] + norm_back(normed, inverse, upstream)


def unpack_first(size, width, scal, pair_ref, other_ref, qkv_ref, out_ref):
    quarter = width // 4
    for m, value in enumerate((pair_ref[0], pair_ref[1], other_ref[0], other_ref[1])):
        value = value.astype(F32)
        at = scal[2 * size + 1 + m] * quarter
        for j in range(3):
            qkv_ref[:, lanes(j * width + at, quarter)] = value[:, j * quarter : (j + 1) * quarter]
        out_ref[:, lanes(at, quarter)] = value[:, 3 * quarter :]


def unpack_in(size, units, piece, padded, scal, pair_ref, other_ref, in_ref, held):
    for m, value in enumerate((pair_ref[0], pair_ref[1], other_ref[0], other_ref[1])):
        held[scal[2 * size + 1 + m]] = value.astype(F32)
    for q in range(4):
        for part in range(2):
            for g in range(size):
                start = part * units + (g * 4 + q) * piece
                frm = (part * size + g) * padded
                in_ref[:, start : start + piece] = held[q, :, frm : frm + piece]


def local(tokens, prefix, qkv_weight, out_weight, in_weight, down_weight, cotangent):
    micro, _, length, width = tokens.shape
    rows = micro * length
    size = lax.axis_size("ring")
    ring = Ring(size)
    rep = lax.axis_index("rep")
    core = lax.axis_index("core")
    shard_rows = qkv_weight.shape[0]
    double = 2 * shard_rows
    units = in_weight.shape[1] // 2
    quarter = width // 4
    heads = quarter // HD
    piece = units // (4 * size)
    padded = -(-piece // PACK) * PACK
    while size * padded % 256:
        padded += PACK
    member_units = size * padded
    chunks = size + 1
    table = scalar_table(size)
    scal = lax.dynamic_slice(
        jnp.asarray(table.reshape(-1, table.shape[-1])), ((rep * size + lax.axis_index("ring")) * 2 + core, 0), (1, table.shape[-1])
    )[0]

    position = np.arange(length, dtype=np.float32)[:, None]
    frequency = np.float32(10000.0) ** (-np.arange(0, HD, 2, dtype=np.float32) / np.float32(HD))
    angles = (position * frequency[None, :]).astype(np.float32)
    angles = np.concatenate([angles, angles], axis=-1)
    sign = np.where(np.arange(HD) < HALF, -1.0, 1.0).astype(np.float32)
    cosine = jnp.asarray(np.tile(np.cos(angles), (micro, heads)).astype(np.float32))
    sine = jnp.asarray(np.tile(np.sin(angles) * sign, (micro, heads)).astype(np.float32))

    own = jnp.concatenate([tokens.reshape(rows, width), jnp.broadcast_to(prefix.astype(BF), (micro, width))], axis=0)
    cot_own = cotangent.reshape(rows, width)
    far = across(own)
    near = sibling(own)
    blocks = [own, near, far, sibling(far)]
    cot_far = across(cot_own)
    cots = [cot_own, sibling(cot_own), cot_far, sibling(cot_far)]

    a_own, a_sib = call(
        functools.partial(pack_first, size, width), [shape((shard_rows, width), BF)] * 2, [], 8, 0, scal, qkv_weight, out_weight
    )
    a_chunks = ring.gather(jnp.concatenate([a_own, sibling(a_sib)], axis=0))
    b_own, b_sib = call(
        functools.partial(pack_in, size, units, piece, padded), [shape((shard_rows, 2 * member_units), BF)] * 2, [], 8, 0, scal, in_weight
    )
    b_chunks = ring.gather(jnp.concatenate([b_own, sibling(b_sib)], axis=0))
    c_chunks = ring.gather(lax.dynamic_slice(down_weight, (rep * piece, 0), (piece, width)))

    o_own, h1, qkv, probs, qkv_mine, out_mine = call(
        functools.partial(attention, size, shard_rows, rows, length, width, chunks),
        [
            shape((4, rows, quarter), BF),
            shape((4 * rows, width), BF),
            shape((4 * rows, 3 * quarter), BF),
            shape((4 * heads, rows, rows), F32),
            shape((width, 3 * quarter), BF),
            shape((width, quarter), BF),
        ],
        [],
        24,
        2 * 4 * rows * width * 3 * quarter,
        scal,
        *blocks,
        *a_chunks,
        cosine,
        sine,
    )
    out_near = sibling(out_mine)
    out_far = across(jnp.stack([out_mine, out_near]))
    o_far = across(o_own)
    o_near = sibling(jnp.stack([o_own, o_far]))
    x2, h2, o_all, out_rows = call(
        functools.partial(middle, size, rows, width),
        [
            shape((4 * rows, width), F32),
            shape((4 * rows, width), BF),
            shape((4 * rows, width), BF),
            shape((quarter, width), BF),
        ],
        [pltpu.VMEM((width, width), BF)],
        24,
        2 * 4 * rows * width * width,
        scal,
        *blocks,
        o_own,
        o_far,
        o_near,
        out_mine,
        out_near,
        out_far,
    )
    up, gate, hid, in_mine = call(
        functools.partial(hidden_units, size, shard_rows, member_units, chunks),
        [
            shape((4 * rows, member_units), F32),
            shape((4 * rows, member_units), F32),
            shape((4 * rows, member_units), BF),
            shape((width, 2 * member_units), BF),
        ],
        [],
        28,
        4 * 4 * rows * width * member_units,
        scal,
        h2,
        *b_chunks,
    )
    pair_low = shape((2, rows, width), BF)
    pair_full = shape((2, rows, width), F32)
    ggu, u2_keep, u2_give, down_mine, gm = call(
        functools.partial(hidden_back, size, rows, padded, piece, chunks),
        [shape((4 * rows, 2 * member_units), BF), pair_full, pair_low, shape((member_units, width), BF), shape((4 * rows, width), BF)],
        [],
        32,
        6 * 4 * rows * width * member_units,
        scal,
        *cots,
        *c_chunks,
        up,
        gate,
        in_mine,
    )
    u2_got = sibling(u2_give)
    u2_far = across((u2_keep + u2_got.astype(F32)).astype(BF))

    y_keep, y_give = call(
        functools.partial(last_projection, rows), [pair_full, pair_low], [], 16, 2 * 4 * rows * width * member_units, scal, hid, down_mine
    )
    y_got = sibling(y_give)
    y_far = across((y_keep[1] + y_got[1].astype(F32)).astype(BF))
    result = (x2[:rows] + (y_keep[0] + y_got[0].astype(F32) + y_far.astype(F32))).astype(BF)

    (down_parts,) = call(
        functools.partial(grad_down_parts, size, padded, piece),
        [shape((size, piece, width), F32)],
        [],
        16,
        2 * 4 * rows * width * member_units,
        scal,
        hid,
        gm,
    )
    down_low = ring.scatter(down_parts).astype(BF)
    down_other = across(down_low)
    grad_down = jnp.where(rep == 0, jnp.concatenate([down_low, down_other]), jnp.concatenate([down_other, down_low])).astype(F32)
    (in_parts,) = call(
        functools.partial(grad_in_parts, size, double),
        [shape((size, double, 2 * member_units), F32)],
        [],
        24,
        4 * 4 * rows * width * member_units,
        scal,
        h2,
        ggu,
    )

    def all_members(summed):
        low = summed.astype(BF)
        keep = lax.dynamic_slice(low, (core * shard_rows, 0), (shard_rows, low.shape[1]))
        give = lax.dynamic_slice(low, ((1 - core) * shard_rows, 0), (shard_rows, low.shape[1]))
        pair = jnp.stack([keep, sibling(give)])
        return pair, across(pair)

    gx2, ga = call(
        functools.partial(middle_back, rows), [shape((rows, width), F32), pair_low], [], 16, 0, scal, u2_keep, u2_got, u2_far, x2, cots[0], cots[2]
    )
    ga_near = sibling(ga)
    gqkv, ga_all, u1_keep, u1_give = call(
        functools.partial(attention_back, rows, width),
        [shape((4 * rows, 3 * quarter), BF), shape((4 * rows, width), BF), pair_full, pair_low],
        [pltpu.VMEM((4 * rows, quarter), BF), pltpu.VMEM((3, rows, quarter), F32)],
        24,
        4 * 4 * rows * width * 3 * quarter,
        scal,
        ga,
        ga_near,
        out_rows,
        qkv,
        probs,
        qkv_mine,
        cosine,
        sine,
    )
    in_pair, in_other = all_members(ring.scatter(in_parts))
    (grad_in,) = call(
        functools.partial(unpack_in, size, units, piece, padded),
        [shape((shard_rows, 2 * units), F32)],
        [pltpu.VMEM((4, shard_rows, 2 * member_units), F32)],
        16,
        0,
        scal,
        in_pair,
        in_other,
    )
    u1_got = sibling(u1_give)
    u1_far = across((u1_keep[1] + u1_got[1].astype(F32)).astype(BF))
    (first_parts,) = call(
        functools.partial(grad_first_parts, size, double, width),
        [shape((size, double, width), F32)],
        [],
        24,
        2 * 4 * rows * width * width,
        scal,
        h1,
        gqkv,
        o_all,
        ga_all,
    )
    (grad_tokens,) = call(
        functools.partial(finish_tokens, rows), [shape((rows, width), F32)], [], 16, 0, scal, u1_keep, u1_got, u1_far, own, gx2
    )
    first_pair, first_other = all_members(ring.scatter(first_parts))
    grad_qkv, grad_out = call(
        functools.partial(unpack_first, size, width),
        [shape((shard_rows, 3 * width), F32), shape((shard_rows, width), F32)],
        [],
        16,
        0,
        scal,
        first_pair,
        first_other,
    )
    return (
        result.reshape(micro, 1, length, width),
        grad_tokens.reshape(micro, 1, length, width),
        grad_qkv,
        grad_out,
        grad_in,
        grad_down,
    )


def solution(mesh):
    inner = Mesh(mesh.devices.reshape(mesh.shape["rep"], mesh.shape["shard"] // 2, 2), ("rep", "ring", "core"))
    everyone = ("rep", "ring", "core")
    group = ("ring", "core")
    sequences = P(None, everyone, None, None)
    weights = P(group, None)
    return jax.shard_map(
        local,
        mesh=inner,
        in_specs=(sequences, P(None, everyone), weights, weights, weights, weights, sequences),
        out_specs=(sequences, sequences, weights, weights, weights, weights),
        check_vma=False,
    )
```

profile of v0, /device:TPU:0, one launch (start us, length us, event | category | flops | bytes accessed | tf_op | source)
XLA Modules:
  0.0 262.2 jit_solution(11911564070260943209)
XLA Ops:
  5.4 2.9 %collective-permute-start.4 = (bf16[128,1024]{1,0:T(8,128)(2,1)S(1)}, bf16[128,1024]{1,0:T(8,128)(2,1)S(1)}, u32[]{:S(2)}, u32[]{:S(2)}) collective-permute-start(bf16[128,1024]{1,0:T(8,128)(2,1)S(1)} %constant_dynamic-update-slice_fusion.refs_4_), channel_id=1, source_target_pairs={{4,0},{8,4},{12,8},{14,12},{10,14},{6,10},{2,6},{0,2},{5,1},{9,5},... | collective-permute-start | bytes 786440 | tf_op jit(solution)/shard_map/ppermute | solution.py:91
  9.1 5.9 %collective-permute-done.4.refs_5_ = bf16[128,1024]{1,0:T(8,128)(2,1)S(1)} collective-permute-done((bf16[128,1024]{1,0:T(8,128)(2,1)S(1)}, bf16[128,1024]{1,0:T(8,128)(2,1)S(1)}, u32[]{:S(2)}, u32[]{:S(2)}) %collective-permute-start.4) | collective-permute-done | bytes 262176 | tf_op jit(solution)/shard_map/ppermute | solution.py:91
  19.8 4.1 %collective-permute-done.8.refs_9_ = bf16[128,1024]{1,0:T(8,128)(2,1)S(1)} collective-permute-done((bf16[128,1024]{1,0:T(8,128)(2,1)S(1)}, bf16[128,1024]{1,0:T(8,128)(2,1)S(1)}, u32[]{:S(2)}, u32[]{:S(2)}) %collective-permute-start.8) | collective-permute-done | bytes 262176 | tf_op jit(solution)/shard_map/ppermute | solution.py:88
  32.5 2.8 %collective-permute-done.10.refs_11_ = bf16[64,1024]{1,0:T(8,128)(2,1)S(1)} collective-permute-done((bf16[64,1024]{1,0:T(8,128)(2,1)S(1)}, bf16[64,1024]{1,0:T(8,128)(2,1)S(1)}, u32[]{:S(2)}, u32[]{:S(2)}) %collective-permute-start.10) | collective-permute-done | bytes 131104 | tf_op jit(solution)/shard_map/ppermute | solution.py:88
  36.4 7.0 %shard_map.146 = (bf16[4,128,256]{2,1,0:T(8,128)(2,1)S(1)}, bf16[512,1024]{1,0:T(8,128)(2,1)S(1)}, bf16[512,768]{1,0:T(8,128)(2,1)S(1)}, f32[16,128,128]{2,1,0:T...) custom-call(s32[21]{0:T(128)S(1)} %fusion.50.scal, ...), custom_call_target="tpu_custom_call" | custom-call | flops 805306368 | bytes 8667220 | tf_op jit(solution)/shard_map/pallas_call | solution.py:121
  50.7 8.8 %collective-permute-done.17.refs_1_ = bf16[128,1536]{1,0:T(8,128)(2,1)} collective-permute-done((bf16[128,1536]{1,0:T(8,128)(2,1)S(1)}, bf16[128,1536]{1,0:T(8,128)(2,1)}, u32[]{:S(2)}, u32[]{:S(2)}) %collective-permute-start.17) | collective-permute-done | bytes 393248 | tf_op jit(solution)/shard_map/ppermute | solution.py:91
  65.8 9.0 %collective-permute-done.31.refs_10_ = bf16[88,1024]{1,0:T(8,128)(2,1)S(1)} collective-permute-done((bf16[88,1024]{1,0:T(8,128)(2,1)S(1)}, bf16[88,1024]{1,0:T(8,128)(2,1)S(1)}, u32[]{:S(2)}, u32[]{:S(2)}) %collective-permute-start.31) | collective-permute-done | bytes 180256 | tf_op jit(solution)/shard_map/ppermute | solution.py:88
  79.1 13.2 %collective-permute-done.12.refs_5_ = bf16[4,128,256]{2,1,0:T(8,128)(2,1)S(1)} collective-permute-done((bf16[4,128,256]{2,1,0:T(8,128)(2,1)S(1)}, bf16[4,128,256]{2,1,0:T(8,128)(2,1)S(1)}, u32[]{:S(2)}, u32[]{:S(2)}) %collective-permute-start.12) | collective-permute-done | bytes 262176 | tf_op jit(solution)/shard_map/ppermute | solution.py:50
  96.3 5.2 %collective-permute-done.22.refs_4_ = bf16[128,1536]{1,0:T(8,128)(2,1)S(1)} collective-permute-done((bf16[128,1536]{1,0:T(8,128)(2,1)S(1)}, bf16[128,1536]{1,0:T(8,128)(2,1)S(1)}, u32[]{:S(2)}, u32[]{:S(2)}) %collective-permute-start.22) | collective-permute-done | bytes 393248 | tf_op jit(solution)/shard_map/ppermute | solution.py:88
  106.7 2.1 collective-permute-done.33.refs_8_
  112.3 3.4 %shard_map.147 = (f32[512,1024]{1,0:T(8,128)S(1)}, bf16[512,1024]{1,0:T(8,128)(2,1)S(1)}, bf16[512,1024]{1,0:T(8,128)(2,1)S(1)}, bf16[256,1024]{1,0:T(8,128)(2,1)S(1)}) custom-call(s32[21]{0:T(128)S(1)} %fusion.50.scal, bf16[130,1024]{1,0:T(8,128)(2,1)S(1)} %pad_maximum_fusion.3.refs_0_.block_ref, bf16[130,1024]{1,0:T(8,128)(2,1)S(1)} %collective-permute-done.refs_1_, ...), custom_call_target="tpu_custom_call" | custom-call | flops 1073741824 | bytes 8929364 | tf_op jit(solution)/shard_map/pallas_call | solution.py:121
  117.3 3.7 %shard_map.149 = (f32[512,768]{1,0:T(8,128)S(1)}, f32[512,768]{1,0:T(8,128)S(1)}, bf16[512,768]{1,0:T(8,128)(2,1)S(1)}, bf16[1024,1536]{1,0:T(8,128)(2,1)S(1)}) custom-call(s32[21]{0:T(128)S(1)} %fusion.50.scal, bf16[512,1024]{1,0:T(8,128)(2,1)S(1)} %get-tuple-element.44.h2_ref, bf16[128,1536]{1,0:T(8,128)(2,1)S(1)} %copy-done.17, ...), custom_call_target="tpu_custom_call" | custom-call | flops 1610612736 | bytes 11272276 | tf_op jit(solution)/shard_map/pallas_call | solution.py:121
  121.2 5.5 %shard_map.150 = (bf16[512,1536]{1,0:T(8,128)(2,1)S(1)}, f32[2,128,1024]{2,1,0:T(8,128)S(1)}, bf16[2,128,1024]{2,1,0:T(8,128)(2,1)S(1)}, bf16[768,1024]{1,0:T(8,128)(2,1)S(1)}, bf16[512,1024]{1,0:T(8,128)(2,1)S(1)}) custom-call(s32[21]{0:T(128)S(1)} %fusion.50.scal, bf16[128,1024]{1,0:T(8,128)(2,1)S(1)} %bitcast.182, ...), custom_call_target="tpu_custom_call" | custom-call | flops 2415919104 | bytes 14549076 | tf_op jit(solution)/shard_map/pallas_call | solution.py:121
  126.7 2.1 shard_map.151
  129.3 3.7 %shard_map.157 = f32[8,128,1536]{2,1,0:T(8,128)S(1)} custom-call(s32[21]{0:T(128)S(1)} %fusion.50.scal, bf16[512,1024]{1,0:T(8,128)(2,1)S(1)} %get-tuple-element.44.h2_ref, bf16[512,1536]{1,0:T(8,128)(2,1)S(1)} %get-tuple-element.70.ggu_ref), custom_call_target="tpu_custom_call" | custom-call | flops 1610612736 | bytes 8912980 | tf_op jit(solution)/shard_map/pallas_call | solution.py:121
  135.6 2.2 shard_map.159
  143.8 4.4 %collective-permute-done.64 = bf16[88,1024]{1,0:T(8,128)(2,1)S(1)} collective-permute-done((bf16[88,1024]{1,0:T(8,128)(2,1)S(1)}, bf16[88,1024]{1,0:T(8,128)(2,1)S(1)}, u32[]{:S(2)}, u32[]{:S(2)}) %collective-permute-start.64) | collective-permute-done | bytes 180256 | tf_op jit(solution)/shard_map/ppermute | solution.py:88
  149.5 2.9 %collective-permute-done.39.far_ref = bf16[2,128,1024]{2,1,0:T(8,128)(2,1)S(1)} collective-permute-done((bf16[2,128,1024]{2,1,0:T(8,128)(2,1)S(1)}, bf16[2,128,1024]{2,1,0:T(8,128)(2,1)S(1)}, u32[]{:S(2)}, u32[]{:S(2)}) %collective-permute-start.39) | collective-permute-done | bytes 524320 | tf_op jit(solution)/shard_map/ppermute | solution.py:50
  160.1 7.0 %shard_map.153 = (bf16[512,768]{1,0:T(8,128)(2,1)S(1)}, bf16[512,1024]{1,0:T(8,128)(2,1)S(1)}, f32[2,128,1024]{2,1,0:T(8,128)S(1)}, bf16[2,128,1024]{2,1,0:T(8,128)(2,1)S(1)}) custom-call(s32[21]{0:T(128)S(1)} %fusion.50.scal, bf16[2,128,1024]{2,1,0:T(8,128)(2,1)S(1)} %get-tuple-element.56.ga_own, bf16[2,128,1024]{2,1,0:T(8,128)(2,1)S(1)} %collective-permute-done.40.ga_near, ...), custom_call_target="tpu_custom_call" | custom-call | flops 1610612736 | bytes 8650836 | tf_op jit(solution)/shard_map/pallas_call | solution.py:121
  171.2 3.3 %collective-permute-done.43 = bf16[64,1024]{1,0:T(8,128)(2,1)S(1)} collective-permute-done((bf16[64,1024]{1,0:T(8,128)(2,1)S(1)}, bf16[64,1024]{1,0:T(8,128)(2,1)S(1)}, u32[]{:S(2)}, u32[]{:S(2)}) %collective-permute-start.43) | collective-permute-done | bytes 131104 | tf_op jit(solution)/shard_map/ppermute | solution.py:88
  179.6 6.0 %collective-permute-done.44 = bf16[128,1024]{1,0:T(8,128)(2,1)S(1)} collective-permute-done((bf16[128,1024]{1,0:T(8,128)(2,1)S(1)}, bf16[128,1024]{1,0:T(8,128)(2,1)S(1)}, u32[]{:S(2)}, u32[]{:S(2)}) %collective-permute-start.44) | collective-permute-done | bytes 262176 | tf_op jit(solution)/shard_map/ppermute | solution.py:88
  187.7 6.0 %collective-permute-done.55 = bf16[128,1536]{1,0:T(8,128)(2,1)S(1)} collective-permute-done((bf16[128,1536]{1,0:T(8,128)(2,1)S(1)}, bf16[128,1536]{1,0:T(8,128)(2,1)S(1)}, u32[]{:S(2)}, u32[]{:S(2)}) %collective-permute-start.55) | collective-permute-done | bytes 393248 | tf_op jit(solution)/shard_map/ppermute | solution.py:88
  194.9 12.0 %collective-permute-done.47 = bf16[64,1024]{1,0:T(8,128)(2,1)S(1)} collective-permute-done((bf16[64,1024]{1,0:T(8,128)(2,1)S(1)}, bf16[64,1024]{1,0:T(8,128)(2,1)S(1)}, u32[]{:S(2)}, u32[]{:S(2)}) %collective-permute-start.47) | collective-permute-done | bytes 131104 | tf_op jit(solution)/shard_map/ppermute | solution.py:91
  209.8 4.2 %collective-permute-done.70 = bf16[88,1024]{1,0:T(8,128)(2,1)S(1)} collective-permute-done((bf16[88,1024]{1,0:T(8,128)(2,1)S(1)}, bf16[88,1024]{1,0:T(8,128)(2,1)S(1)}, u32[]{:S(2)}, u32[]{:S(2)}) %collective-permute-start.70) | collective-permute-done | bytes 180256 | tf_op jit(solution)/shard_map/ppermute | solution.py:91
  214.7 2.1 collective-permute-done.48
  216.9 5.1 %collective-permute-done.59 = bf16[128,1536]{1,0:T(8,128)(2,1)S(1)} collective-permute-done((bf16[128,1536]{1,0:T(8,128)(2,1)S(1)}, bf16[128,1536]{1,0:T(8,128)(2,1)S(1)}, u32[]{:S(2)}, u32[]{:S(2)}) %collective-permute-start.59) | collective-permute-done | bytes 393248 | tf_op jit(solution)/shard_map/ppermute | solution.py:91
  223.1 7.8 %collective-permute-done.49 = bf16[128,1024]{1,0:T(8,128)(2,1)S(1)} collective-permute-done((bf16[128,1024]{1,0:T(8,128)(2,1)S(1)}, bf16[128,1024]{1,0:T(8,128)(2,1)S(1)}, u32[]{:S(2)}, u32[]{:S(2)}) %collective-permute-start.49) | collective-permute-done | bytes 262176 | tf_op jit(solution)/shard_map/ppermute | solution.py:91
  232.9 3.9 %collective-permute-done.60 = bf16[128,1536]{1,0:T(8,128)(2,1)S(1)} collective-permute-done((bf16[128,1536]{1,0:T(8,128)(2,1)S(1)}, bf16[128,1536]{1,0:T(8,128)(2,1)S(1)}, u32[]{:S(2)}, u32[]{:S(2)}) %collective-permute-start.60) | collective-permute-done | bytes 393248 | tf_op jit(solution)/shard_map/ppermute | solution.py:91
  237.9 5.3 %collective-permute-done.50 = bf16[128,1024]{1,0:T(8,128)(2,1)S(1)} collective-permute-done((bf16[128,1024]{1,0:T(8,128)(2,1)S(1)}, bf16[128,1024]{1,0:T(8,128)(2,1)S(1)}, u32[]{:S(2)}, u32[]{:S(2)}) %collective-permute-start.50) | collective-permute-done | bytes 262176 | tf_op jit(solution)/shard_map/ppermute | solution.py:91
  249.2 6.2 %collective-permute-done.62.other_ref = bf16[2,64,1536]{2,1,0:T(8,128)(2,1)S(1)} collective-permute-done((bf16[2,64,1536]{2,1,0:T(8,128)(2,1)S(1)}, bf16[2,64,1536]{2,1,0:T(8,128)(2,1)S(1)}, u32[]{:S(2)}, u32[]{:S(2)}) %collective-permute-start.62) | collective-permute-done | bytes 393248 | tf_op jit(solution)/shard_map/ppermute | solution.py:50
  255.5 2.4 shard_map.158
  257.9 2.8 %collective-permute-done.52.other_ref = bf16[2,64,1024]{2,1,0:T(8,128)(2,1)S(1)} collective-permute-done((bf16[2,64,1024]{2,1,0:T(8,128)(2,1)S(1)}, bf16[2,64,1024]{2,1,0:T(8,128)(2,1)S(1)}, u32[]{:S(2)}, u32[]{:S(2)}) %collective-permute-start.52) | collective-permute-done | bytes 262176 | tf_op jit(solution)/shard_map/ppermute | solution.py:50
  (258 shorter events, 97.6 us)
Async XLA Ops:
  28.4 19.0 %collective-permute-start.16 = (bf16[64,1536]{1,0:T(8,128)(2,1)S(1)}, bf16[64,1536]{1,0:T(8,128)(2,1)S(1)}, u32[]{:S(2)}, u32[]{:S(2)}) collective-permute-start(bf16[64,1536]{1,0:T(8,128)(2,1)S(1)} %get-tuple-element.46), channel_id=1, source_target_pairs={{0,1},{1,0},{2,3},{3,2},{4,5},{5,4},{6,7},{7,6},{8,9},{9,8},{10,11... | collective-permute-start | bytes 589832 | tf_op jit(solution)/shard_map/ppermute | solution.py:54
  47.4 14.1 %collective-permute-start.14 = (bf16[1024,256]{1,0:T(8,128)(2,1)S(1)}, bf16[1024,256]{1,0:T(8,128)(2,1)S(1)}, u32[]{:S(2)}, u32[]{:S(2)}) collective-permute-start(bf16[1024,256]{1,0:T(8,128)(2,1)S(1)} %get-tuple-element.42.refs_7_), channel_id=1, source_target_pairs={{0,1},{1,0},{2,3},{3,2},{4,5},{5,4},{6,7},{7,6},{8,9},{9,8},{10,11... | collective-permute-start | bytes 1572872 | tf_op jit(solution)/shard_map/ppermute | solution.py:54
  47.5 12.1 %collective-permute-start.17 = (bf16[128,1536]{1,0:T(8,128)(2,1)S(1)}, bf16[128,1536]{1,0:T(8,128)(2,1)}, u32[]{:S(2)}, u32[]{:S(2)}) collective-permute-start(bf16[128,1536]{1,0:T(8,128)(2,1)S(1)} %constant_dynamic-update-slice_fusion.2.refs_0_), channel_id=1, source_target_pairs={{4,0},{8,4},{12,8},{14,12},{10,14},{6,10},{2,6},{0,2},{5,1},{9,5},... | collective-permute-start | bytes 1179656 | tf_op jit(solution)/shard_map/ppermute | solution.py:91
  48.6 12.0 %collective-permute-start.20 = (bf16[128,1536]{1,0:T(8,128)(2,1)S(1)}, bf16[128,1536]{1,0:T(8,128)(2,1)}, u32[]{:S(2)}, u32[]{:S(2)}) collective-permute-start(bf16[128,1536]{1,0:T(8,128)(2,1)S(1)} %constant_dynamic-update-slice_fusion.2.refs_0_), channel_id=1, source_target_pairs={{0,4},{4,8},{8,12},{12,14},{14,10},{10,6},{6,2},{2,0},{1,5},{5,9},... | collective-permute-start | bytes 1179656 | tf_op jit(solution)/shard_map/ppermute | solution.py:88
  49.6 15.1 %collective-permute-start.28 = (bf16[88,1024]{1,0:T(8,128)(2,1)S(1)}, bf16[88,1024]{1,0:T(8,128)(2,1)S(1)}, u32[]{:S(2)}, u32[]{:S(2)}) collective-permute-start(bf16[88,1024]{1,0:T(8,128)(2,1)S(1)} %constant_dynamic-slice_fusion.2.refs_4_), channel_id=1, source_target_pairs={{4,0},{8,4},{12,8},{14,12},{10,14},{6,10},{2,6},{0,2},{5,1},{9,5},... | collective-permute-start | bytes 540680 | tf_op jit(solution)/shard_map/ppermute | solution.py:91
  59.5 16.8 %collective-permute-start.18 = (bf16[128,1536]{1,0:T(8,128)(2,1)}, bf16[128,1536]{1,0:T(8,128)(2,1)S(1)}, u32[]{:S(2)}, u32[]{:S(2)}) collective-permute-start(bf16[128,1536]{1,0:T(8,128)(2,1)} %collective-permute-done.17.refs_1_), channel_id=1, source_target_pairs={{4,0},{8,4},{12,8},{14,12},{10,14},{6,10},{2,6},{0,2},{5,1},{9,5},... | collective-permute-start | bytes 1179656 | tf_op jit(solution)/shard_map/ppermute | solution.py:91
  60.6 17.3 %collective-permute-start.21 = (bf16[128,1536]{1,0:T(8,128)(2,1)}, bf16[128,1536]{1,0:T(8,128)(2,1)S(1)}, u32[]{:S(2)}, u32[]{:S(2)}) collective-permute-start(bf16[128,1536]{1,0:T(8,128)(2,1)} %collective-permute-done.20.refs_6_), channel_id=1, source_target_pairs={{0,4},{4,8},{8,12},{12,14},{14,10},{10,6},{6,2},{2,0},{1,5},{5,9},... | collective-permute-start | bytes 1179656 | tf_op jit(solution)/shard_map/ppermute | solution.py:88
  62.6 48.9 %collective-permute-start.15 = (bf16[2,1024,256]{2,1,0:T(8,128)(2,1)}, bf16[2,1024,256]{2,1,0:T(8,128)(2,1)}, u32[]{:S(2)}, u32[]{:S(2)}) collective-permute-start(bf16[2,1024,256]{2,1,0:T(8,128)(2,1)} %pad_maximum_fusion), channel_id=1, source_target_pairs={{0,16},{16,0},{1,17},{17,1},{2,18},{18,2},{3,19},{19,3},{4,20},{20... | collective-permute-start | bytes 3145736 | tf_op jit(solution)/shard_map/ppermute | solution.py:50
  63.7 28.6 %collective-permute-start.12 = (bf16[4,128,256]{2,1,0:T(8,128)(2,1)S(1)}, bf16[4,128,256]{2,1,0:T(8,128)(2,1)S(1)}, u32[]{:S(2)}, u32[]{:S(2)}) collective-permute-start(bf16[4,128,256]{2,1,0:T(8,128)(2,1)S(1)} %get-tuple-element.41.refs_4_), channel_id=1, source_target_pairs={{0,16},{16,0},{1,17},{17,1},{2,18},{18,2},{3,19},{19,3},{4,20},{20... | collective-permute-start | bytes 786440 | tf_op jit(solution)/shard_map/ppermute | solution.py:50
  74.8 18.7 %collective-permute-start.29 = (bf16[88,1024]{1,0:T(8,128)(2,1)S(1)}, bf16[88,1024]{1,0:T(8,128)(2,1)S(1)}, u32[]{:S(2)}, u32[]{:S(2)}) collective-permute-start(bf16[88,1024]{1,0:T(8,128)(2,1)S(1)} %collective-permute-done.28.refs_5_), channel_id=1, source_target_pairs={{4,0},{8,4},{12,8},{14,12},{10,14},{6,10},{2,6},{0,2},{5,1},{9,5},... | collective-permute-start | bytes 540680 | tf_op jit(solution)/shard_map/ppermute | solution.py:91
  76.4 18.8 %collective-permute-start.19 = (bf16[128,1536]{1,0:T(8,128)(2,1)S(1)}, bf16[128,1536]{1,0:T(8,128)(2,1)S(1)}, u32[]{:S(2)}, u32[]{:S(2)}) collective-permute-start(bf16[128,1536]{1,0:T(8,128)(2,1)S(1)} %collective-permute-done.18.refs_2_), channel_id=1, source_target_pairs={{4,0},{8,4},{12,8},{14,12},{10,14},{6,10},{2,6},{0,2},{5,1},{9,5},... | collective-permute-start | bytes 1179656 | tf_op jit(solution)/shard_map/ppermute | solution.py:91
  78.0 15.7 %collective-permute-start.32 = (bf16[88,1024]{1,0:T(8,128)(2,1)S(1)}, bf16[88,1024]{1,0:T(8,128)(2,1)S(1)}, u32[]{:S(2)}, u32[]{:S(2)}) collective-permute-start(bf16[88,1024]{1,0:T(8,128)(2,1)S(1)} %collective-permute-done.31.refs_10_), channel_id=1, source_target_pairs={{0,4},{4,8},{8,12},{12,14},{14,10},{10,6},{6,2},{2,0},{1,5},{5,9},... | collective-permute-start | bytes 540680 | tf_op jit(solution)/shard_map/ppermute | solution.py:88
  93.5 15.3 %collective-permute-start.13 = (bf16[2,4,128,256]{3,2,1,0:T(8,128)(2,1)S(1)}, bf16[2,4,128,256]{3,2,1,0:T(8,128)(2,1)S(1)}, u32[]{:S(2)}, u32[]{:S(2)}) collective-permute-start(bf16[2,4,128,256]{3,2,1,0:T(8,128)(2,1)S(1)} %pad_maximum_fusion.1), channel_id=1, source_target_pairs={{0,1},{1,0},{2,3},{3,2},{4,5},{5,4},{6,7},{7,6},{8,9},{9,8},{10,11... | collective-permute-start | bytes 1572872 | tf_op jit(solution)/shard_map/ppermute | solution.py:54
  108.8 12.2 %collective-permute-start.25 = (bf16[128,1024]{1,0:T(8,128)(2,1)}, bf16[128,1024]{1,0:T(8,128)(2,1)}, u32[]{:S(2)}, u32[]{:S(2)}) collective-permute-start(bf16[128,1024]{1,0:T(8,128)(2,1)} %bitcast.181), channel_id=1, source_target_pairs={{0,1},{1,0},{2,3},{3,2},{4,5},{5,4},{6,7},{7,6},{8,9},{9,8},{10,11... | collective-permute-start | bytes 786440 | tf_op jit(solution)/shard_map/ppermute | solution.py:54
  128.8 40.8 %collective-permute-start.36 = (bf16[2,128,1024]{2,1,0:T(8,128)(2,1)S(1)}, bf16[2,128,1024]{2,1,0:T(8,128)(2,1)S(1)}, u32[]{:S(2)}, u32[]{:S(2)}) collective-permute-start(bf16[2,128,1024]{2,1,0:T(8,128)(2,1)S(1)} %get-tuple-element.53), channel_id=1, source_target_pairs={{0,1},{1,0},{2,3},{3,2},{4,5},{5,4},{6,7},{7,6},{8,9},{9,8},{10,11... | collective-permute-start | bytes 1572872 | tf_op jit(solution)/shard_map/ppermute | solution.py:54
  133.5 22.4 %collective-permute-start.53 = (bf16[64,1536]{1,0:T(8,128)(2,1)S(1)}, bf16[64,1536]{1,0:T(8,128)(2,1)S(1)}, u32[]{:S(2)}, u32[]{:S(2)}) collective-permute-start(bf16[64,1536]{1,0:T(8,128)(2,1)S(1)} %get-tuple-element.82), channel_id=1, source_target_pairs={{0,4},{4,8},{8,12},{12,14},{14,10},{10,6},{6,2},{2,0},{1,5},{5,9},... | collective-permute-start | bytes 589832 | tf_op jit(solution)/shard_map/ppermute | solution.py:88
  134.6 51.5 %collective-permute-start.57 = (bf16[64,1536]{1,0:T(8,128)(2,1)S(1)}, bf16[64,1536]{1,0:T(8,128)(2,1)S(1)}, u32[]{:S(2)}, u32[]{:S(2)}) collective-permute-start(bf16[64,1536]{1,0:T(8,128)(2,1)S(1)} %get-tuple-element.83), channel_id=1, source_target_pairs={{4,0},{8,4},{12,8},{14,12},{10,14},{6,10},{2,6},{0,2},{5,1},{9,5},... | collective-permute-start | bytes 589832 | tf_op jit(solution)/shard_map/ppermute | solution.py:91
  139.3 13.1 %collective-permute-start.39 = (bf16[2,128,1024]{2,1,0:T(8,128)(2,1)S(1)}, bf16[2,128,1024]{2,1,0:T(8,128)(2,1)S(1)}, u32[]{:S(2)}, u32[]{:S(2)}) collective-permute-start(bf16[2,128,1024]{2,1,0:T(8,128)(2,1)S(1)} %add_convert_fusion), channel_id=1, source_target_pairs={{0,16},{16,0},{1,17},{17,1},{2,18},{18,2},{3,19},{19,3},{4,20},{20... | collective-permute-start | bytes 1572872 | tf_op jit(solution)/shard_map/ppermute | solution.py:50
  156.1 20.0 %collective-permute-start.54 = (bf16[128,1536]{1,0:T(8,128)(2,1)S(1)}, bf16[128,1536]{1,0:T(8,128)(2,1)S(1)}, u32[]{:S(2)}, u32[]{:S(2)}) collective-permute-start(bf16[128,1536]{1,0:T(8,128)(2,1)S(1)} %fusion.7), channel_id=1, source_target_pairs={{0,4},{4,8},{8,12},{12,14},{14,10},{10,6},{6,2},{2,0},{1,5},{5,9},... | collective-permute-start | bytes 1179656 | tf_op jit(solution)/shard_map/ppermute | solution.py:88
  158.0 20.1 %collective-permute-start.68 = (bf16[88,1024]{1,0:T(8,128)(2,1)S(1)}, bf16[88,1024]{1,0:T(8,128)(2,1)S(1)}, u32[]{:S(2)}, u32[]{:S(2)}) collective-permute-start(bf16[88,1024]{1,0:T(8,128)(2,1)S(1)} %get-tuple-element.85), channel_id=1, source_target_pairs={{4,0},{8,4},{12,8},{14,12},{10,14},{6,10},{2,6},{0,2},{5,1},{9,5},... | collective-permute-start | bytes 540680 | tf_op jit(solution)/shard_map/ppermute | solution.py:91
  159.0 50.7 %collective-permute-start.66 = (bf16[88,1024]{1,0:T(8,128)(2,1)S(1)}, bf16[88,1024]{1,0:T(8,128)(2,1)S(1)}, u32[]{:S(2)}, u32[]{:S(2)}) collective-permute-start(bf16[88,1024]{1,0:T(8,128)(2,1)S(1)} %get-tuple-element.84), channel_id=1, source_target_pairs={{0,4},{4,8},{8,12},{12,14},{14,10},{10,6},{6,2},{2,0},{1,5},{5,9},... | collective-permute-start | bytes 540680 | tf_op jit(solution)/shard_map/ppermute | solution.py:88
  174.5 71.1 %collective-permute-start.37 = (bf16[128,1024]{1,0:T(8,128)(2,1)S(1)}, bf16[128,1024]{1,0:T(8,128)(2,1)S(1)}, u32[]{:S(2)}, u32[]{:S(2)}) collective-permute-start(bf16[128,1024]{1,0:T(8,128)(2,1)S(1)} %fusion.48), channel_id=1, source_target_pairs={{0,16},{16,0},{1,17},{17,1},{2,18},{18,2},{3,19},{19,3},{4,20},{20... | collective-permute-start | bytes 786440 | tf_op jit(solution)/shard_map/ppermute | solution.py:50
  178.1 15.7 %collective-permute-start.55 = (bf16[128,1536]{1,0:T(8,128)(2,1)S(1)}, bf16[128,1536]{1,0:T(8,128)(2,1)S(1)}, u32[]{:S(2)}, u32[]{:S(2)}) collective-permute-start(bf16[128,1536]{1,0:T(8,128)(2,1)S(1)} %fusion.9), channel_id=1, source_target_pairs={{0,4},{4,8},{8,12},{12,14},{14,10},{10,6},{6,2},{2,0},{1,5},{5,9},... | collective-permute-start | bytes 1179656 | tf_op jit(solution)/shard_map/ppermute | solution.py:88
  186.1 21.3 %collective-permute-start.45 = (bf16[128,1024]{1,0:T(8,128)(2,1)S(1)}, bf16[128,1024]{1,0:T(8,128)(2,1)S(1)}, u32[]{:S(2)}, u32[]{:S(2)}) collective-permute-start(bf16[128,1024]{1,0:T(8,128)(2,1)S(1)} %fusion.24), channel_id=1, source_target_pairs={{0,4},{4,8},{8,12},{12,14},{14,10},{10,6},{6,2},{2,0},{1,5},{5,9},... | collective-permute-start | bytes 786440 | tf_op jit(solution)/shard_map/ppermute | solution.py:88
  193.9 15.2 %collective-permute-start.58 = (bf16[128,1536]{1,0:T(8,128)(2,1)S(1)}, bf16[128,1536]{1,0:T(8,128)(2,1)S(1)}, u32[]{:S(2)}, u32[]{:S(2)}) collective-permute-start(bf16[128,1536]{1,0:T(8,128)(2,1)S(1)} %get-tuple-element.79), channel_id=1, source_target_pairs={{4,0},{8,4},{12,8},{14,12},{10,14},{6,10},{2,6},{0,2},{5,1},{9,5},... | collective-permute-start | bytes 1179656 | tf_op jit(solution)/shard_map/ppermute | solution.py:91
  194.5 12.4 %collective-permute-start.47 = (bf16[64,1024]{1,0:T(8,128)(2,1)S(1)}, bf16[64,1024]{1,0:T(8,128)(2,1)S(1)}, u32[]{:S(2)}, u32[]{:S(2)}) collective-permute-start(bf16[64,1024]{1,0:T(8,128)(2,1)S(1)} %get-tuple-element.87), channel_id=1, source_target_pairs={{4,0},{8,4},{12,8},{14,12},{10,14},{6,10},{2,6},{0,2},{5,1},{9,5},... | collective-permute-start | bytes 393224 | tf_op jit(solution)/shard_map/ppermute | solution.py:91
  207.5 24.0 %collective-permute-start.56 = (bf16[128,1536]{1,0:T(8,128)(2,1)S(1)}, bf16[128,1536]{1,0:T(8,128)(2,1)S(1)}, u32[]{:S(2)}, u32[]{:S(2)}) collective-permute-start(bf16[128,1536]{1,0:T(8,128)(2,1)S(1)} %get-tuple-element.78), channel_id=1, source_target_pairs={{0,4},{4,8},{8,12},{12,14},{14,10},{10,6},{6,2},{2,0},{1,5},{5,9},... | collective-permute-start | bytes 1179656 | tf_op jit(solution)/shard_map/ppermute | solution.py:88
  209.7 12.2 %collective-permute-start.59 = (bf16[128,1536]{1,0:T(8,128)(2,1)S(1)}, bf16[128,1536]{1,0:T(8,128)(2,1)S(1)}, u32[]{:S(2)}, u32[]{:S(2)}) collective-permute-start(bf16[128,1536]{1,0:T(8,128)(2,1)S(1)} %fusion.3), channel_id=1, source_target_pairs={{4,0},{8,4},{12,8},{14,12},{10,14},{6,10},{2,6},{0,2},{5,1},{9,5},... | collective-permute-start | bytes 1179656 | tf_op jit(solution)/shard_map/ppermute | solution.py:91
  214.1 32.4 %collective-permute-start.71 = (bf16[88,1024]{1,0:T(8,128)(2,1)S(1)}, bf16[88,1024]{1,0:T(8,128)(2,1)S(1)}, u32[]{:S(2)}, u32[]{:S(2)}) collective-permute-start(bf16[88,1024]{1,0:T(8,128)(2,1)S(1)} %fusion.46), channel_id=1, source_target_pairs={{0,16},{16,0},{1,17},{17,1},{2,18},{18,2},{3,19},{19,3},{4,20},{20... | collective-permute-start | bytes 540680 | tf_op jit(solution)/shard_map/ppermute | solution.py:50
  222.6 14.3 %collective-permute-start.60 = (bf16[128,1536]{1,0:T(8,128)(2,1)S(1)}, bf16[128,1536]{1,0:T(8,128)(2,1)S(1)}, u32[]{:S(2)}, u32[]{:S(2)}) collective-permute-start(bf16[128,1536]{1,0:T(8,128)(2,1)S(1)} %fusion.5), channel_id=1, source_target_pairs={{4,0},{8,4},{12,8},{14,12},{10,14},{6,10},{2,6},{0,2},{5,1},{9,5},... | collective-permute-start | bytes 1179656 | tf_op jit(solution)/shard_map/ppermute | solution.py:91
  230.8 16.6 %collective-permute-start.42 = (bf16[128,1024]{1,0:T(8,128)(2,1)S(1)}, bf16[128,1024]{1,0:T(8,128)(2,1)S(1)}, u32[]{:S(2)}, u32[]{:S(2)}) collective-permute-start(bf16[128,1024]{1,0:T(8,128)(2,1)S(1)} %fusion.49), channel_id=1, source_target_pairs={{0,16},{16,0},{1,17},{17,1},{2,18},{18,2},{3,19},{19,3},{4,20},{20... | collective-permute-start | bytes 786440 | tf_op jit(solution)/shard_map/ppermute | solution.py:50
  244.8 15.9 %collective-permute-start.52 = (bf16[2,64,1024]{2,1,0:T(8,128)(2,1)S(1)}, bf16[2,64,1024]{2,1,0:T(8,128)(2,1)S(1)}, u32[]{:S(2)}, u32[]{:S(2)}) collective-permute-start(bf16[2,64,1024]{2,1,0:T(8,128)(2,1)S(1)} %pad_maximum_fusion.4.pair_ref), channel_id=1, source_target_pairs={{0,16},{16,0},{1,17},{17,1},{2,18},{18,2},{3,19},{19,3},{4,20},{20... | collective-permute-start | bytes 786440 | tf_op jit(solution)/shard_map/ppermute | solution.py:50
  (80 other events, 718.9 us)
where the time goes:
time: 263 us; the launch traced here: 262 us
  waiting for transfers between devices  130 us (49%)
  starting transfers between devices  63.6 us (24%)
  Pallas kernels  45.7 us (17%)
  local copies, waits for them, and re-layouts  14 us (5%)
  other arithmetic  7.15 us (3%)
    ppermute x24, waiting for transfers between devices, go_left(): return lax.ppermute(value, 'ring', self.left)  56.1 us
    ppermute x24, waiting for transfers between devices, go_right(): return lax.ppermute(value, 'ring', self.right)  47.3 us
    pallas_call x15, Pallas kernels, call(): pl.pallas_call(body, out_shape=outs, in_specs=[pl.BlockSpec(memory_space=...  45.7 us
    ppermute x24, starting transfers between devices, go_right(): return lax.ppermute(value, 'ring', self.right)  27.3 us
    ppermute x10, waiting for transfers between devices, across(): return lax.ppermute(value, 'rep', SWAP)  25.2 us
    ppermute x24, starting transfers between devices, go_left(): return lax.ppermute(value, 'ring', self.left)  23.5 us
    ppermute x10, starting transfers between devices, across(): return lax.ppermute(value, 'rep', SWAP)  10.9 us
    unnamed x82, local copies, waits for them, and re-layouts  9.77 us
  transfers between devices with their start and end apart: 72, of which 29 were waited for; matrix products, arithmetic and copies ran while one was open for 4% of the time, Pallas kernels for 14%

commit v1 on v0

--- a/solution.py
+++ b/solution.py
@@ -84,42 +84,75 @@
         self.right = [(order[i], order[(i + 1) % size]) for i in range(size)]
         self.left = [(b, a) for a, b in self.right]
 
-    def go_right(self, value):
-        return lax.ppermute(value, "ring", self.right)
-
-    def go_left(self, value):
-        return lax.ppermute(value, "ring", self.left)
-
-    def gather(self, chunk):
-        got = {0: chunk}
-        right = left = chunk
-        for step in range(1, self.half):
-            right = self.go_right(right)
-            left = self.go_left(left)
-            got[self.size - step] = right
-            got[step] = left
-        cut = upper_half(chunk.shape[0])
-        far = [self.go_right(right[:cut]), self.go_left(left[cut:])]
-        return [got[k] for k in range(self.size) if k != self.half] + far
-
-    def scatter(self, parts):
-        cut = upper_half(parts.shape[1])
-        rest = parts.shape[1] - cut
-        far = parts[self.half]
-        right = self.go_right(far[:cut].astype(BF)).astype(F32)
-        left = self.go_left(far[cut:].astype(BF)).astype(F32)
-        right = jnp.pad(right, ((0, rest), (0, 0)))
-        left = jnp.pad(left, ((cut, 0), (0, 0)))
-        for step in range(self.half - 1, 0, -1):
-            right = self.go_right((parts[step] + right).astype(BF)).astype(F32)
-            left = self.go_left((parts[self.size - step] + left).astype(BF)).astype(F32)
-        return parts[0] + right + left
+    def exchange(self, pair):
+        return lax.ppermute(pair[0], "ring", self.right), lax.ppermute(pair[1], "ring", self.left)
+
+
+class Gather:
+    def __init__(self, ring, chunk):
+        self.ring = ring
+        self.step = 0
+        self.got = {0: chunk}
+        self.cut = upper_half(chunk.shape[0])
+        self.state = (chunk, chunk)
+
+    def advance(self):
+        if self.step == self.ring.half:
+            return
+        self.step += 1
+        if self.step == self.ring.half:
+            self.far = self.ring.exchange((self.state[0][: self.cut], self.state[1][self.cut :]))
+            self.state = ()
+            return
+        self.state = self.ring.exchange(self.state)
+        self.got[self.ring.size - self.step], self.got[self.step] = self.state
+
+    def finish(self):
+        while self.step < self.ring.half:
+            self.advance()
+        return [self.got[k] for k in range(self.ring.size) if k != self.ring.half] + list(self.far)
+
+
+class Scatter:
+    def __init__(self, ring, parts):
+        self.ring = ring
+        self.step = 0
+        self.parts = parts
+        self.cut = upper_half(parts.shape[1])
+        far = parts[ring.half]
+        self.state = (far[: self.cut].astype(BF), far[self.cut :].astype(BF))
+
+    def advance(self):
+        ring = self.ring
+        if self.step == ring.half:
+            return
+        right, left = (v.astype(F32) for v in ring.exchange(self.state))
+        if self.step == 0:
+            right = jnp.pad(right, ((0, self.parts.shape[1] - self.cut), (0, 0)))
+            left = jnp.pad(left, ((self.cut, 0), (0, 0)))
+        self.step += 1
+        if self.step == ring.half:
+            self.total = self.parts[0] + right + left
+            self.state = ()
+            return
+        place = ring.half - self.step
+        self.state = ((self.parts[place] + right).astype(BF), (self.parts[ring.size - place] + left).astype(BF))
+
+    def finish(self):
+        while self.step < self.ring.half:
+            self.advance()
+        return self.total
+
+
+def sync(*values):
+    return lax.optimization_barrier(values)
 
 
 def call(body, outs, scratch, limit, flops, *args):
     nbytes = sum(a.size * a.dtype.itemsize for a in args) + sum(o.size * o.dtype.itemsize for o in outs)
     return pl.pallas_call(
         body,
+        name=body.func.__name__,
         out_shape=outs,
         in_specs=[pl.BlockSpec(memory_space=pltpu.SMEM)] + [pl.BlockSpec(memory_space=pltpu.VMEM)] * (len(args) - 1),
         out_specs=[pl.BlockSpec(memory_space=pltpu.VMEM)] * len(outs),
@@ -199,15 +232,23 @@
     return (query // length == key // length) & ((key <= query) | (inside < limit))
 
 
+def gather_out(size, shard_rows, quarter, scal, *refs):
+    out_ref = refs[-1]
+
+    def put(row, value):
+        out_ref[pl.ds(row, shard_rows), :] = value[:, 3 * quarter :]
+
+    place_rows(size, shard_rows, scal, refs[:-1], put)
+
+
 def attention(size, shard_rows, rows, length, width, n_chunks, scal, *refs):
     blocks = refs[:4]
     chunks = refs[4 : 4 + n_chunks]
-    cos_ref, sin_ref, o_ref, h1_ref, qkv_ref, p_ref, w_ref, out_ref = refs[4 + n_chunks :]
+    cos_ref, sin_ref, o_ref, h1_ref, qkv_ref, p_ref, w_ref = refs[4 + n_chunks :]
     quarter = width // 4
 
     def put(row, value):
         w_ref[pl.ds(row, shard_rows), :] = value[:, : 3 * quarter]
-        out_ref[pl.ds(row, shard_rows), :] = value[:, 3 * quarter :]
 
     place_rows(size, shard_rows, scal, chunks, put)
     for b in range(4):
@@ -235,17 +276,15 @@
 
 
 def middle(size, rows, width, scal, *refs):
-    blocks = refs[:4]
-    o_own, o_far, o_near, w_own, w_near, w_far, x2_ref, h2_ref, o_ref, rows_ref, w_full = refs[4:]
+    blocks, cots, outputs, weights = refs[:4], refs[4:8], refs[8:12], refs[12:16]
+    x2_ref, h2_ref, o_ref, rows_ref, gm_ref, w_full = refs[16:]
     quarter = width // 4
     members = [scal[2 * size + 1 + m] for m in range(4)]
-    weights = (w_own[...], w_near[...], w_far[0], w_far[1])
     for m in range(4):
-        w_full[:, lanes(members[m] * quarter, quarter)] = weights[m]
+        w_full[:, lanes(members[m] * quarter, quarter)] = weights[m][...]
+        gm_ref[m * rows : (m + 1) * rows, :] = cots[m][...]
         for b in range(4):
-            kept = BLOCKS[m][b]
-            value = (o_own, o_near.at[0], o_far, o_near.at[1])[m][kept]
-            o_ref[b * rows : (b + 1) * rows, lanes(members[m] * quarter, quarter)] = value
+            o_ref[b * rows : (b + 1) * rows, lanes(members[m] * quarter, quarter)] = outputs[m][BLOCKS[m][b]]
     rows_ref[...] = w_full[pl.ds(pl.multiple_of(members[0] * quarter, quarter), quarter), :]
     for j in range(4):
         columns = slice(j * quarter, (j + 1) * quarter)
@@ -279,9 +318,9 @@
 
 
 def hidden_back(size, rows, padded, piece, n_chunks, scal, *refs):
-    cots = refs[:4]
-    chunks = refs[4 : 4 + n_chunks]
-    up_ref, gate_ref, w_in, ggu_ref, keep_ref, give_ref, down_ref, gm_ref = refs[4 + n_chunks :]
+    gm_ref = refs[0]
+    chunks = refs[1 : 1 + n_chunks]
+    up_ref, gate_ref, w_in, ggu_ref, keep_ref, give_ref, down_ref = refs[1 + n_chunks :]
     units = up_ref.shape[1]
     width = gm_ref.shape[1]
     down_ref[...] = jnp.zeros_like(down_ref)
@@ -290,8 +329,6 @@
         down_ref[pl.ds(pl.multiple_of(chip * padded + first, PACK), value.shape[0]), :] = value
 
     place_chunks(size, scal, chunks, store)
-    for b in range(4):
-        gm_ref[b * rows : (b + 1) * rows, :] = cots[b][...]
     tile = 256
 
     @pl.loop(0, units // tile)
@@ -458,148 +495,174 @@
     cosine = jnp.asarray(np.tile(np.cos(angles), (micro, heads)).astype(np.float32))
     sine = jnp.asarray(np.tile(np.sin(angles) * sign, (micro, heads)).astype(np.float32))
 
+    full_rows = 4 * rows
+    pair_low = shape((2, rows, width), BF)
+    pair_full = shape((2, rows, width), F32)
+    project = 2 * full_rows * width * quarter
+
     own = jnp.concatenate([tokens.reshape(rows, width), jnp.broadcast_to(prefix.astype(BF), (micro, width))], axis=0)
     cot_own = cotangent.reshape(rows, width)
-    far = across(own)
-    near = sibling(own)
-    blocks = [own, near, far, sibling(far)]
-    cot_far = across(cot_own)
-    cots = [cot_own, sibling(cot_own), cot_far, sibling(cot_far)]
-
     a_own, a_sib = call(
         functools.partial(pack_first, size, width), [shape((shard_rows, width), BF)] * 2, [], 8, 0, scal, qkv_weight, out_weight
     )
-    a_chunks = ring.gather(jnp.concatenate([a_own, sibling(a_sib)], axis=0))
+    a_got = sibling(a_sib)
+    near = sibling(own)
+    a = Gather(ring, jnp.concatenate([a_own, a_got], axis=0))
+
+    a.state, own, cot_own, in_weight, near = sync(a.state, own, cot_own, in_weight, near)
+    a.advance()
+    far = across(own)
+    cot_near = sibling(cot_own)
     b_own, b_sib = call(
         functools.partial(pack_in, size, units, piece, padded), [shape((shard_rows, 2 * member_units), BF)] * 2, [], 8, 0, scal, in_weight
     )
-    b_chunks = ring.gather(jnp.concatenate([b_own, sibling(b_sib)], axis=0))
-    c_chunks = ring.gather(lax.dynamic_slice(down_weight, (rep * piece, 0), (piece, width)))
-
-    o_own, h1, qkv, probs, qkv_mine, out_mine = call(
+
+    a.state, far, cot_own, b_own, b_sib, cot_near = sync(a.state, far, cot_own, b_own, b_sib, cot_near)
+    a.advance()
+    diagonal = sibling(far)
+    cot_far = across(cot_own)
+    b_got = sibling(b_sib)
+
+    a.state, cot_far, b_own, b_got, diagonal, down_weight = sync(a.state, cot_far, b_own, b_got, diagonal, down_weight)
+    a.advance()
+    cot_diagonal = sibling(cot_far)
+    b = Gather(ring, jnp.concatenate([b_own, b_got], axis=0))
+    c = Gather(ring, lax.dynamic_slice(down_weight, (rep * piece, 0), (piece, width)))
+    blocks = [own, near, far, diagonal]
+
+    a.state, b.state, c.state, cot_diagonal, blocks = sync(a.state, b.state, c.state, cot_diagonal, blocks)
+    c.advance()
+    a_chunks = a.finish()
+    cots = [cot_own, cot_near, cot_far, cot_diagonal]
+
+    a_chunks, b.state, c.state = sync(a_chunks, b.state, c.state)
+    b.advance()
+    c.advance()
+    (out_mine,) = call(functools.partial(gather_out, size, shard_rows, quarter), [shape((width, quarter), BF)], [], 8, 0, scal, *a_chunks)
+    out_far = across(out_mine)
+    o_own, h1, qkv, probs, qkv_mine = call(
         functools.partial(attention, size, shard_rows, rows, length, width, chunks),
         [
             shape((4, rows, quarter), BF),
-            shape((4 * rows, width), BF),
-            shape((4 * rows, 3 * quarter), BF),
+            shape((full_rows, width), BF),
+            shape((full_rows, 3 * quarter), BF),
             shape((4 * heads, rows, rows), F32),
             shape((width, 3 * quarter), BF),
-            shape((width, quarter), BF),
         ],
         [],
         24,
-        2 * 4 * rows * width * 3 * quarter,
+        3 * project,
         scal,
         *blocks,
         *a_chunks,
         cosine,
         sine,
     )
+
+    o_own, out_mine, out_far, b.state, c.state = sync(o_own, out_mine, out_far, b.state, c.state)
+    o_far = across(o_own)
+    b.advance()
+    c.advance()
+    o_near = sibling(o_own)
     out_near = sibling(out_mine)
-    out_far = across(jnp.stack([out_mine, out_near]))
-    o_far = across(o_own)
-    o_near = sibling(jnp.stack([o_own, o_far]))
-    x2, h2, o_all, out_rows = call(
+    out_diagonal = sibling(out_far)
+
+    o_far, o_near, out_near, out_diagonal, b.state, c.state = sync(o_far, o_near, out_near, out_diagonal, b.state, c.state)
+    o_diagonal = sibling(o_far)
+    b.advance()
+    c_chunks = c.finish()
+    x2, h2, o_all, out_rows, gm = call(
         functools.partial(middle, size, rows, width),
         [
-            shape((4 * rows, width), F32),
-            shape((4 * rows, width), BF),
-            shape((4 * rows, width), BF),
+            shape((full_rows, width), F32),
+            shape((full_rows, width), BF),
+            shape((full_rows, width), BF),
             shape((quarter, width), BF),
+            shape((full_rows, width), BF),
         ],
         [pltpu.VMEM((width, width), BF)],
         24,
-        2 * 4 * rows * width * width,
+        4 * project,
         scal,
         *blocks,
+        *cots,
         o_own,
+        o_near,
         o_far,
-        o_near,
+        o_diagonal,
         out_mine,
         out_near,
         out_far,
-    )
+        out_diagonal,
+    )
+
+    h2, b.state, c_chunks = sync(h2, b.state, c_chunks)
+    b_chunks = b.finish()
     up, gate, hid, in_mine = call(
         functools.partial(hidden_units, size, shard_rows, member_units, chunks),
         [
-            shape((4 * rows, member_units), F32),
-            shape((4 * rows, member_units), F32),
-            shape((4 * rows, member_units), BF),
+            shape((full_rows, member_units), F32),
+            shape((full_rows, member_units), F32),
+            shape((full_rows, member_units), BF),
             shape((width, 2 * member_units), BF),
         ],
         [],
         28,
-        4 * 4 * rows * width * member_units,
+        6 * project,
         scal,
         h2,
         *b_chunks,
     )
-    pair_low = shape((2, rows, width), BF)
-    pair_full = shape((2, rows, width), F32)
-    ggu, u2_keep, u2_give, down_mine, gm = call(
+    (down_parts,) = call(
+        functools.partial(grad_down_parts, size, padded, piece), [shape((size, piece, width), F32)], [], 16, 3 * project, scal, hid, gm
+    )
+
+    c = Scatter(ring, down_parts)
+    c.state, gm, up = sync(c.state, gm, up)
+    c.advance()
+    ggu, u2_keep, u2_give, down_mine = call(
         functools.partial(hidden_back, size, rows, padded, piece, chunks),
-        [shape((4 * rows, 2 * member_units), BF), pair_full, pair_low, shape((member_units, width), BF), shape((4 * rows, width), BF)],
+        [shape((full_rows, 2 * member_units), BF), pair_full, pair_low, shape((member_units, width), BF)],
         [],
         32,
-        6 * 4 * rows * width * member_units,
+        9 * project,
         scal,
-        *cots,
+        gm,
         *c_chunks,
         up,
         gate,
         in_mine,
     )
+
+    u2_give, c.state, ggu = sync(u2_give, c.state, ggu)
     u2_got = sibling(u2_give)
-    u2_far = across((u2_keep + u2_got.astype(F32)).astype(BF))
-
-    y_keep, y_give = call(
-        functools.partial(last_projection, rows), [pair_full, pair_low], [], 16, 2 * 4 * rows * width * member_units, scal, hid, down_mine
-    )
+    c.advance()
+    (in_parts,) = call(
+        functools.partial(grad_in_parts, size, double), [shape((size, double, 2 * member_units), F32)], [], 24, 6 * project, scal, h2, ggu
+    )
+    b = Scatter(ring, in_parts)
+    u2_low = (u2_keep + u2_got.astype(F32)).astype(BF)
+
+    u2_low, b.state, c.state, hid = sync(u2_low, b.state, c.state, hid)
+    u2_far = across(u2_low)
+    b.advance()
+    c.advance()
+    y_keep, y_give = call(functools.partial(last_projection, rows), [pair_full, pair_low], [], 16, 3 * project, scal, hid, down_mine)
+
+    u2_far, b.state, c.state, y_give = sync(u2_far, b.state, c.state, y_give)
+    b.advance()
+    c.advance()
     y_got = sibling(y_give)
-    y_far = across((y_keep[1] + y_got[1].astype(F32)).astype(BF))
-    result = (x2[:rows] + (y_keep[0] + y_got[0].astype(F32) + y_far.astype(F32))).astype(BF)
-
-    (down_parts,) = call(
-        functools.partial(grad_down_parts, size, padded, piece),
-        [shape((size, piece, width), F32)],
-        [],
-        16,
-        2 * 4 * rows * width * member_units,
-        scal,
-        hid,
-        gm,
-    )
-    down_low = ring.scatter(down_parts).astype(BF)
-    down_other = across(down_low)
-    grad_down = jnp.where(rep == 0, jnp.concatenate([down_low, down_other]), jnp.concatenate([down_other, down_low])).astype(F32)
-    (in_parts,) = call(
-        functools.partial(grad_in_parts, size, double),
-        [shape((size, double, 2 * member_units), F32)],
-        [],
-        24,
-        4 * 4 * rows * width * member_units,
-        scal,
-        h2,
-        ggu,
-    )
-
-    def all_members(summed):
-        low = summed.astype(BF)
-        keep = lax.dynamic_slice(low, (core * shard_rows, 0), (shard_rows, low.shape[1]))
-        give = lax.dynamic_slice(low, ((1 - core) * shard_rows, 0), (shard_rows, low.shape[1]))
-        pair = jnp.stack([keep, sibling(give)])
-        return pair, across(pair)
-
     gx2, ga = call(
         functools.partial(middle_back, rows), [shape((rows, width), F32), pair_low], [], 16, 0, scal, u2_keep, u2_got, u2_far, x2, cots[0], cots[2]
     )
     ga_near = sibling(ga)
     gqkv, ga_all, u1_keep, u1_give = call(
         functools.partial(attention_back, rows, width),
-        [shape((4 * rows, 3 * quarter), BF), shape((4 * rows, width), BF), pair_full, pair_low],
-        [pltpu.VMEM((4 * rows, quarter), BF), pltpu.VMEM((3, rows, quarter), F32)],
+        [shape((full_rows, 3 * quarter), BF), shape((full_rows, width), BF), pair_full, pair_low],
+        [pltpu.VMEM((full_rows, quarter), BF), pltpu.VMEM((3, rows, quarter), F32)],
         24,
-        4 * 4 * rows * width * 3 * quarter,
+        7 * project,
         scal,
         ga,
         ga_near,
@@ -610,7 +673,58 @@
         cosine,
         sine,
     )
-    in_pair, in_other = all_members(ring.scatter(in_parts))
+    (first_parts,) = call(
+        functools.partial(grad_first_parts, size, double, width),
+        [shape((size, double, width), F32)],
+        [],
+        24,
+        4 * project,
+        scal,
+        h1,
+        gqkv,
+        o_all,
+        ga_all,
+    )
+    a = Scatter(ring, first_parts)
+    down_low = c.finish().astype(BF)
+    y_low = (y_keep[1] + y_got[1].astype(F32)).astype(BF)
+
+    a.state, b.state, u1_give, y_low = sync(a.state, b.state, u1_give, y_low)
+    a.advance()
+    b.advance()
+    u1_got = sibling(u1_give)
+    y_far = across(y_low)
+    u1_low = (u1_keep[1] + u1_got[1].astype(F32)).astype(BF)
+
+    def halves(low):
+        keep = lax.dynamic_slice(low, (core * shard_rows, 0), (shard_rows, low.shape[1]))
+        give = lax.dynamic_slice(low, ((1 - core) * shard_rows, 0), (shard_rows, low.shape[1]))
+        return keep, give
+
+    a.state, b.state, u1_low, y_far = sync(a.state, b.state, u1_low, y_far)
+    a.advance()
+    in_low = b.finish().astype(BF)
+    u1_far = across(u1_low)
+    result = (x2[:rows] + (y_keep[0] + y_got[0].astype(F32) + y_far.astype(F32))).astype(BF)
+
+    in_keep, in_give = halves(in_low)
+    a.state, in_give, u1_far, down_low = sync(a.state, in_give, u1_far, down_low)
+    a.advance()
+    in_got = sibling(in_give)
+    down_other = across(down_low)
+    (grad_tokens,) = call(
+        functools.partial(finish_tokens, rows), [shape((rows, width), F32)], [], 16, 0, scal, u1_keep, u1_got, u1_far, own, gx2
+    )
+
+    in_pair = jnp.stack([in_keep, in_got])
+    a.state, in_pair, down_other = sync(a.state, in_pair, down_other)
+    in_other = across(in_pair)
+    first_keep, first_give = halves(a.finish().astype(BF))
+    grad_down = jnp.where(rep == 0, jnp.concatenate([down_low, down_other]), jnp.concatenate([down_other, down_low])).astype(F32)
+
+    first_pair = jnp.stack([first_keep, sibling(first_give)])
+    first_pair, in_other = sync(first_pair, in_other)
+    first_other = across(first_pair)
     (grad_in,) = call(
         functools.partial(unpack_in, size, units, piece, padded),
         [shape((shard_rows, 2 * units), F32)],
@@ -621,24 +735,6 @@
         in_pair,
         in_other,
     )
-    u1_got = sibling(u1_give)
-    u1_far = across((u1_keep[1] + u1_got[1].astype(F32)).astype(BF))
-    (first_parts,) = call(
-        functools.partial(grad_first_parts, size, double, width),
-        [shape((size, double, width), F32)],
-        [],
-        24,
-        2 * 4 * rows * width * width,
-        scal,
-        h1,
-        gqkv,
-        o_all,
-        ga_all,
-    )
-    (grad_tokens,) = call(
-        functools.partial(finish_tokens, rows), [shape((rows, width), F32)], [], 16, 0, scal, u1_keep, u1_got, u1_far, own, gx2
-    )
-    first_pair, first_other = all_members(ring.scatter(first_parts))
     grad_qkv, grad_out = call(
         functools.partial(unpack_first, size, width),
         [shape((shard_rows, 3 * width), F32), shape((shard_rows, width), F32)],

time: 263 us -> 233 us (0.89)
  waiting for transfers between devices: 130 us -> 99.7 us
  other arithmetic: 7.15 us -> 17.6 us
  local copies, waits for them, and re-layouts: 14 us -> 6.71 us
    ppermute x48, waiting for transfers between devices: 103 us -> 83 us  [the longest x24 48.4 us: exchange(): lax.ppermute(pair[1], 'ring', self.left)]
    ppermute x10, waiting for transfers between devices: 25.2 us -> 10.5 us  [across(): return lax.ppermute(value, 'rep', SWAP)]
    convert_element_type x21 -> x15, other arithmetic: 1.56 us -> 10.8 us  [the longest x9 6.22 us: advance(): (self.parts[ring.size - place] + left).astype(BF)]
    unnamed x82 -> x58, local copies, waits for them, and re-layouts: 9.77 us -> 4.15 us
    ppermute x14 -> x16, waiting for transfers between devices: 1.68 us -> 6.29 us  [sibling(): return lax.ppermute(value, 'core', SWAP)]
    slice x6, local copies, waits for them, and re-layouts: 3.33 us -> 0.06 us  [the longest x3 0.03 us: advance(): self.state[0][:self.cut]]
    pallas_call x15 -> x16, Pallas kernels: 45.7 us -> 44.3 us  [call(): pl.pallas_call(body, name=body.func.__name__, out_shape=outs, in_specs=[p...]
  transfers between devices with their start and end apart: 72 -> 74, of which waited for: 29 -> 43; matrix products, arithmetic and copies ran while one was open for 4% -> 8% of each run, Pallas kernels for 14% -> 16%
where the time goes in v1:
time: 233 us
  waiting for transfers between devices  99.7 us (43%)
  starting transfers between devices  62.9 us (27%)
  Pallas kernels  44.3 us (19%)
  other arithmetic  17.6 us (8%)
  local copies, waits for them, and re-layouts  6.71 us (3%)
    ppermute x24, waiting for transfers between devices, exchange(): lax.ppermute(pair[1], 'ring', self.left)  48.4 us
    pallas_call x16, Pallas kernels, call(): pl.pallas_call(body, name=body.func.__name__, out_shape=outs, in_specs=[p...  44.3 us
    ppermute x24, waiting for transfers between devices, exchange(): lax.ppermute(pair[0], 'ring', self.right)  34.6 us
    ppermute x24, starting transfers between devices, exchange(): lax.ppermute(pair[1], 'ring', self.left)  26.3 us
    ppermute x24, starting transfers between devices, exchange(): lax.ppermute(pair[0], 'ring', self.right)  23.2 us
    ppermute x10, starting transfers between devices, across(): return lax.ppermute(value, 'rep', SWAP)  11.5 us
    ppermute x10, waiting for transfers between devices, across(): return lax.ppermute(value, 'rep', SWAP)  10.5 us
    ppermute x16, waiting for transfers between devices, sibling(): return lax.ppermute(value, 'core', SWAP)  6.29 us
  transfers between devices with their start and end apart: 74, of which 43 were waited for; matrix products, arithmetic and copies ran while one was open for 8% of the time, Pallas kernels for 16%

profile of v1, /device:TPU:0, one launch (start us, length us, event | category | flops | bytes accessed | tf_op | source)
XLA Modules:
  0.0 232.6 jit_solution(16062864262673279431)
XLA Ops:
  7.6 2.7 %collective-permute-start.4 = (bf16[130,1024]{1,0:T(8,128)(2,1)S(1)}, bf16[130,1024]{1,0:T(8,128)(2,1)S(1)}, u32[]{:S(2)}, u32[]{:S(2)}) collective-permute-start(bf16[130,1024]{1,0:T(8,128)(2,1)S(1)} %pad_maximum_fusion.1.refs_0_.block_ref), channel_id=1, source_target_pairs={{0,16},{16,0},{1,17},{17,1},{2,18},{18,2},{3,19},{19,3},{4,20},{20... | collective-permute-start | bytes 798728 | tf_op jit(solution)/shard_map/ppermute | solution.py:50
  14.9 3.6 %collective-permute-done.2.refs_10_.refs_6_ = bf16[128,1024]{1,0:T(8,128)(2,1)S(1)} collective-permute-done((bf16[128,1024]{1,0:T(8,128)(2,1)S(1)}, bf16[128,1024]{1,0:T(8,128)(2,1)S(1)}, u32[]{:S(2)}, u32[]{:S(2)}) %collective-permute-start.2) | collective-permute-done | bytes 262176 | tf_op jit(solution)/shard_map/ppermute | solution.py:88
  22.5 1.8 collective-permute-done.9
  24.3 4.3 %collective-permute-done.6.refs_9_.refs_5_ = bf16[128,1024]{1,0:T(8,128)(2,1)S(1)} collective-permute-done((bf16[128,1024]{1,0:T(8,128)(2,1)S(1)}, bf16[128,1024]{1,0:T(8,128)(2,1)S(1)}, u32[]{:S(2)}, u32[]{:S(2)}) %collective-permute-start.6) | collective-permute-done | bytes 262176 | tf_op jit(solution)/shard_map/ppermute | solution.py:88
  33.4 4.1 %collective-permute-done.11.refs_8_.refs_4_ = bf16[128,1024]{1,0:T(8,128)(2,1)S(1)} collective-permute-done((bf16[128,1024]{1,0:T(8,128)(2,1)S(1)}, bf16[128,1024]{1,0:T(8,128)(2,1)S(1)}, u32[]{:S(2)}, u32[]{:S(2)}) %collective-permute-start.11) | collective-permute-done | bytes 262176 | tf_op jit(solution)/shard_map/ppermute | solution.py:88
  43.0 2.9 %collective-permute-done.14.refs_11_.refs_7_ = bf16[64,1024]{1,0:T(8,128)(2,1)S(1)} collective-permute-done((bf16[64,1024]{1,0:T(8,128)(2,1)S(1)}, bf16[64,1024]{1,0:T(8,128)(2,1)S(1)}, u32[]{:S(2)}, u32[]{:S(2)}) %collective-permute-start.14) | collective-permute-done | bytes 131104 | tf_op jit(solution)/shard_map/ppermute | solution.py:88
  52.8 7.0 %attention.1 = (bf16[4,128,256]{2,1,0:T(8,128)(2,1)S(1)}, bf16[512,1024]{1,0:T(8,128)(2,1)S(1)}, bf16[512,768]{1,0:T(8,128)(2,1)S(1)}, f32[16,128,128]{2,1,0:T(8,128)S(1)}, bf16[1024,768]{1,0:T(8,128)(2,1)S(1)}) custom-call(s32[21]{0:T(128)S(1)} %fusion.50.scal, bf16[130,1024]{1,0:T(8,128)(2,1)S(1)} %pad_maximum_fusion.1.refs_0_.block_ref, ...), custom_call_target="tpu_custom_call" | custom-call | flops 805306368 | bytes 8142932 | tf_op jit(solution)/shard_map/attention/pallas_call | solution.py:153
  60.9 2.1 collective-permute-done.22.refs_3_
  72.9 5.1 %collective-permute-done.27.refs_5_ = bf16[128,1536]{1,0:T(8,128)(2,1)S(1)} collective-permute-done((bf16[128,1536]{1,0:T(8,128)(2,1)S(1)}, bf16[128,1536]{1,0:T(8,128)(2,1)S(1)}, u32[]{:S(2)}, u32[]{:S(2)}) %collective-permute-start.27) | collective-permute-done | bytes 393248 | tf_op jit(solution)/shard_map/ppermute | solution.py:88
  82.5 2.8 %middle.1 = (f32[512,1024]{1,0:T(8,128)S(1)}, bf16[512,1024]{1,0:T(8,128)(2,1)S(1)}, bf16[512,1024]{1,0:T(8,128)(2,1)S(1)}, bf16[256,1024]{1,0:T(8,128)(2,1)S(1)}, bf16[512,1024]{1,0:T(8,128)(2,1)S(1)}) custom-call(s32[21]{0:T(128)S(1)} %fusion.50.scal, bf16[130,1024]{1,0:T(8,128)(2,1)S(1)} %pad_maximum_fusion.1.refs_0_.block_ref, ...), custom_call_target="tpu_custom_call" | custom-call | flops 1073741824 | bytes 11026516 | tf_op jit(solution)/shard_map/middle/pallas_call | solution.py:153
  85.2 3.5 %collective-permute-done.35.refs_9_ = bf16[40,1024]{1,0:T(8,128)(2,1)S(1)} collective-permute-done((bf16[40,1024]{1,0:T(8,128)(2,1)S(1)}, bf16[40,1024]{1,0:T(8,128)(2,1)S(1)}, u32[]{:S(2)}, u32[]{:S(2)}) %collective-permute-start.35) | collective-permute-done | bytes 81952 | tf_op jit(solution)/shard_map/ppermute | solution.py:88
  89.9 1.7 collective-permute-start.37
  91.6 3.4 %collective-permute-done.36.refs_7_ = bf16[64,1536]{1,0:T(8,128)(2,1)S(1)} collective-permute-done((bf16[64,1536]{1,0:T(8,128)(2,1)S(1)}, bf16[64,1536]{1,0:T(8,128)(2,1)S(1)}, u32[]{:S(2)}, u32[]{:S(2)}) %collective-permute-start.36) | collective-permute-done | bytes 196640 | tf_op jit(solution)/shard_map/ppermute | solution.py:88
  95.8 2.9 %hidden_units.1 = (f32[512,768]{1,0:T(8,128)S(1)}, f32[512,768]{1,0:T(8,128)S(1)}, bf16[512,768]{1,0:T(8,128)(2,1)S(1)}, bf16[1024,1536]{1,0:T(8,128)(2,1)S(1)}) custom-call(s32[21]{0:T(128)S(1)} %fusion.50.scal, bf16[512,1024]{1,0:T(8,128)(2,1)S(1)} %get-tuple-element.218.h2_ref, bf16[128,1536]{1,0:T(8,128)(2,1)S(1)} %constant_dynamic-update-slice_fusion.2.refs_0_, ...), custom_call_target="tpu_custom_call" | custom-call | flops 1610612736 | bytes 11272276 | tf_op jit(solution)/shard_map/hidden_units/pallas_call | solution.py:153
  98.7 2.2 grad_down_parts.1
  103.3 4.8 %hidden_back.1 = (bf16[512,1536]{1,0:T(8,128)(2,1)S(1)}, f32[2,128,1024]{2,1,0:T(8,128)S(1)}, bf16[2,128,1024]{2,1,0:T(8,128)(2,1)S(1)}, bf16[768,1024]{1,0:T(8,128)(2,1)S(1)}) custom-call(s32[21]{0:T(128)S(1)} %fusion.50.scal, bf16[512,1024]{1,0:T(8,128)(2,1)S(1)} %get-tuple-element.224.gm_ref.refs_0_, ...), custom_call_target="tpu_custom_call" | custom-call | flops 2415919104 | bytes 13500500 | tf_op jit(solution)/shard_map/hidden_back/pallas_call | solution.py:153
  108.3 3.7 %grad_in_parts.1 = f32[8,128,1536]{2,1,0:T(8,128)S(1)} custom-call(s32[21]{0:T(128)S(1)} %fusion.50.scal, bf16[512,1024]{1,0:T(8,128)(2,1)S(1)} %get-tuple-element.218.h2_ref, bf16[512,1536]{1,0:T(8,128)(2,1)S(1)} %get-tuple-element.243.ggu_ref), custom_call_target="tpu_custom_call" | custom-call | flops 1610612736 | bytes 8912980 | tf_op jit(solution)/shard_map/grad_in_parts/pallas_call | solution.py:153
  114.5 4.9 %collective-permute-done.42 = bf16[88,1024]{1,0:T(8,128)(2,1)S(1)} collective-permute-done((bf16[88,1024]{1,0:T(8,128)(2,1)S(1)}, bf16[88,1024]{1,0:T(8,128)(2,1)S(1)}, u32[]{:S(2)}, u32[]{:S(2)}) %collective-permute-start.42) | collective-permute-done | bytes 180256 | tf_op jit(solution)/shard_map/ppermute | solution.py:88
  125.4 2.1 last_projection.1
  132.2 3.5 %collective-permute-done.43.far_ref = bf16[2,128,1024]{2,1,0:T(8,128)(2,1)S(1)} collective-permute-done((bf16[2,128,1024]{2,1,0:T(8,128)(2,1)S(1)}, bf16[2,128,1024]{2,1,0:T(8,128)(2,1)S(1)}, u32[]{:S(2)}, u32[]{:S(2)}) %collective-permute-start.43) | collective-permute-done | bytes 524320 | tf_op jit(solution)/shard_map/ppermute | solution.py:50
  139.5 5.0 %collective-permute-done.51 = bf16[128,1536]{1,0:T(8,128)(2,1)S(1)} collective-permute-done((bf16[128,1536]{1,0:T(8,128)(2,1)S(1)}, bf16[128,1536]{1,0:T(8,128)(2,1)S(1)}, u32[]{:S(2)}, u32[]{:S(2)}) %collective-permute-start.51) | collective-permute-done | bytes 393248 | tf_op jit(solution)/shard_map/ppermute | solution.py:88
  145.9 7.0 %attention_back.1 = (bf16[512,768]{1,0:T(8,128)(2,1)S(1)}, bf16[512,1024]{1,0:T(8,128)(2,1)S(1)}, f32[2,128,1024]{2,1,0:T(8,128)S(1)}, bf16[2,128,1024]{2,1,0:T(8,128)(2,1)S(1)}) custom-call(s32[21]{0:T(128)S(1)} %fusion.50.scal, bf16[2,128,1024]{2,1,0:T(8,128)(2,1)S(1)} %get-tuple-element.258.ga_own, ...), custom_call_target="tpu_custom_call" | custom-call | flops 1879048192 | bytes 8650836 | tf_op jit(solution)/shard_map/attention_back/pallas_call | solution.py:153
  152.9 2.0 grad_first_parts.1
  160.9 7.3 %collective-permute-done.53 = bf16[64,1024]{1,0:T(8,128)(2,1)S(1)} collective-permute-done((bf16[64,1024]{1,0:T(8,128)(2,1)S(1)}, bf16[64,1024]{1,0:T(8,128)(2,1)S(1)}, u32[]{:S(2)}, u32[]{:S(2)}) %collective-permute-start.53) | collective-permute-done | bytes 131104 | tf_op jit(solution)/shard_map/ppermute | solution.py:88
  172.9 5.7 %collective-permute-done.57 = bf16[128,1024]{1,0:T(8,128)(2,1)S(1)} collective-permute-done((bf16[128,1024]{1,0:T(8,128)(2,1)S(1)}, bf16[128,1024]{1,0:T(8,128)(2,1)S(1)}, u32[]{:S(2)}, u32[]{:S(2)}) %collective-permute-start.57) | collective-permute-done | bytes 262176 | tf_op jit(solution)/shard_map/ppermute | solution.py:50
  184.8 3.3 %collective-permute-done.59 = bf16[128,1024]{1,0:T(8,128)(2,1)} collective-permute-done((bf16[128,1024]{1,0:T(8,128)(2,1)}, bf16[128,1024]{1,0:T(8,128)(2,1)}, u32[]{:S(2)}, u32[]{:S(2)}) %collective-permute-start.59) | collective-permute-done | bytes 262176 | tf_op jit(solution)/shard_map/ppermute | solution.py:88
  190.9 4.3 %collective-permute-done.61 = bf16[128,1536]{1,0:T(8,128)(2,1)S(1)} collective-permute-done((bf16[128,1536]{1,0:T(8,128)(2,1)}, bf16[128,1536]{1,0:T(8,128)(2,1)S(1)}, u32[]{:S(2)}, u32[]{:S(2)}) %collective-permute-start.61) | collective-permute-done | bytes 393248 | tf_op jit(solution)/shard_map/ppermute | solution.py:88
  200.8 5.5 %collective-permute-done.66 = bf16[128,1024]{1,0:T(8,128)(2,1)S(1)} collective-permute-done((bf16[128,1024]{1,0:T(8,128)(2,1)S(1)}, bf16[128,1024]{1,0:T(8,128)(2,1)S(1)}, u32[]{:S(2)}, u32[]{:S(2)}) %collective-permute-start.66) | collective-permute-done | bytes 262176 | tf_op jit(solution)/shard_map/ppermute | solution.py:88
  211.5 4.6 %collective-permute-done.70 = bf16[128,1024]{1,0:T(8,128)(2,1)S(1)} collective-permute-done((bf16[128,1024]{1,0:T(8,128)(2,1)S(1)}, bf16[128,1024]{1,0:T(8,128)(2,1)S(1)}, u32[]{:S(2)}, u32[]{:S(2)}) %collective-permute-start.70) | collective-permute-done | bytes 262176 | tf_op jit(solution)/shard_map/ppermute | solution.py:88
  222.7 2.2 fusion.31
  225.9 1.8 finish_tokens.1
  228.6 2.4 %unpack_in.1 = f32[64,5632]{1,0:T(8,128)} custom-call(s32[21]{0:T(128)S(1)} %fusion.50.scal, bf16[2,64,1536]{2,1,0:T(8,128)(2,1)S(1)} %pad_maximum_fusion.pair_ref, bf16[2,64,1536]{2,1,0:T(8,128)(2,1)S(1)} %collective-permute-done.72.other_ref), custom_call_target="tpu_custom_call" | custom-call | bytes 2228308 | tf_op jit(solution)/shard_map/unpack_in/pallas_call | solution.py:153
  (231 shorter events, 111.0 us)
Async XLA Ops:
  7.6 12.3 %collective-permute-start.4 = (bf16[130,1024]{1,0:T(8,128)(2,1)S(1)}, bf16[130,1024]{1,0:T(8,128)(2,1)S(1)}, u32[]{:S(2)}, u32[]{:S(2)}) collective-permute-start(bf16[130,1024]{1,0:T(8,128)(2,1)S(1)} %pad_maximum_fusion.1.refs_0_.block_ref), channel_id=1, source_target_pairs={{0,16},{16,0},{1,17},{17,1},{2,18},{18,2},{3,19},{19,3},{4,20},{20... | collective-permute-start | bytes 798728 | tf_op jit(solution)/shard_map/ppermute | solution.py:50
  19.9 10.4 %collective-permute-start.10 = (bf16[130,1024]{1,0:T(8,128)(2,1)S(1)}, bf16[130,1024]{1,0:T(8,128)(2,1)S(1)}, u32[]{:S(2)}, u32[]{:S(2)}) collective-permute-start(bf16[130,1024]{1,0:T(8,128)(2,1)S(1)} %collective-permute-done.4.refs_2_), channel_id=1, source_target_pairs={{0,1},{1,0},{2,3},{3,2},{4,5},{5,4},{6,7},{7,6},{8,9},{9,8},{10,11... | collective-permute-start | bytes 798728 | tf_op jit(solution)/shard_map/ppermute | solution.py:54
  48.1 14.8 %collective-permute-start.18 = (bf16[1024,256]{1,0:T(8,128)(2,1)S(1)}, bf16[1024,256]{1,0:T(8,128)(2,1)S(1)}, u32[]{:S(2)}, u32[]{:S(2)}) collective-permute-start(bf16[1024,256]{1,0:T(8,128)(2,1)S(1)} %gather_out.1.refs_12_), channel_id=1, source_target_pairs={{0,16},{16,0},{1,17},{17,1},{2,18},{18,2},{3,19},{19,3},{4,20},{20... | collective-permute-start | bytes 1572872 | tf_op jit(solution)/shard_map/ppermute | solution.py:50
  48.7 14.2 %collective-permute-start.19 = (bf16[128,1536]{1,0:T(8,128)(2,1)S(1)}, bf16[128,1536]{1,0:T(8,128)(2,1)S(1)}, u32[]{:S(2)}, u32[]{:S(2)}) collective-permute-start(bf16[128,1536]{1,0:T(8,128)(2,1)S(1)} %constant_dynamic-update-slice_fusion.2.refs_0_), channel_id=1, source_target_pairs={{0,4},{4,8},{8,12},{12,14},{14,10},{10,6},{6,2},{2,0},{1,5},{5,9},... | collective-permute-start | bytes 1179656 | tf_op jit(solution)/shard_map/ppermute | solution.py:88
  50.3 12.7 %collective-permute-start.20 = (bf16[128,1536]{1,0:T(8,128)(2,1)S(1)}, bf16[128,1536]{1,0:T(8,128)(2,1)S(1)}, u32[]{:S(2)}, u32[]{:S(2)}) collective-permute-start(bf16[128,1536]{1,0:T(8,128)(2,1)S(1)} %constant_dynamic-update-slice_fusion.2.refs_0_), channel_id=1, source_target_pairs={{4,0},{8,4},{12,8},{14,12},{10,14},{6,10},{2,6},{0,2},{5,1},{9,5},... | collective-permute-start | bytes 1179656 | tf_op jit(solution)/shard_map/ppermute | solution.py:88
  50.8 10.1 %collective-permute-start.21 = (bf16[88,1024]{1,0:T(8,128)(2,1)S(1)}, bf16[88,1024]{1,0:T(8,128)(2,1)S(1)}, u32[]{:S(2)}, u32[]{:S(2)}) collective-permute-start(bf16[88,1024]{1,0:T(8,128)(2,1)S(1)} %collective-permute-done.16.refs_7_), channel_id=1, source_target_pairs={{0,4},{4,8},{8,12},{12,14},{14,10},{10,6},{6,2},{2,0},{1,5},{5,9},... | collective-permute-start | bytes 540680 | tf_op jit(solution)/shard_map/ppermute | solution.py:88
  52.3 10.7 %collective-permute-start.22 = (bf16[88,1024]{1,0:T(8,128)(2,1)S(1)}, bf16[88,1024]{1,0:T(8,128)(2,1)S(1)}, u32[]{:S(2)}, u32[]{:S(2)}) collective-permute-start(bf16[88,1024]{1,0:T(8,128)(2,1)S(1)} %collective-permute-done.17.refs_2_), channel_id=1, source_target_pairs={{4,0},{8,4},{12,8},{14,12},{10,14},{6,10},{2,6},{0,2},{5,1},{9,5},... | collective-permute-start | bytes 540680 | tf_op jit(solution)/shard_map/ppermute | solution.py:88
  66.5 11.8 %collective-permute-start.25 = (bf16[1024,256]{1,0:T(8,128)(2,1)S(1)}, bf16[1024,256]{1,0:T(8,128)(2,1)S(1)}, u32[]{:S(2)}, u32[]{:S(2)}) collective-permute-start(bf16[1024,256]{1,0:T(8,128)(2,1)S(1)} %gather_out.1.refs_12_), channel_id=1, source_target_pairs={{0,1},{1,0},{2,3},{3,2},{4,5},{5,4},{6,7},{7,6},{8,9},{9,8},{10,11... | collective-permute-start | bytes 1572872 | tf_op jit(solution)/shard_map/ppermute | solution.py:54
  66.5 11.8 %collective-permute-start.26 = (bf16[1024,256]{1,0:T(8,128)(2,1)S(1)}, bf16[1024,256]{1,0:T(8,128)(2,1)S(1)}, u32[]{:S(2)}, u32[]{:S(2)}) collective-permute-start(bf16[1024,256]{1,0:T(8,128)(2,1)S(1)} %collective-permute-done.18.refs_14_), channel_id=1, source_target_pairs={{0,1},{1,0},{2,3},{3,2},{4,5},{5,4},{6,7},{7,6},{8,9},{9,8},{10,11... | collective-permute-start | bytes 1572872 | tf_op jit(solution)/shard_map/ppermute | solution.py:54
  68.5 9.6 %collective-permute-start.27 = (bf16[128,1536]{1,0:T(8,128)(2,1)S(1)}, bf16[128,1536]{1,0:T(8,128)(2,1)S(1)}, u32[]{:S(2)}, u32[]{:S(2)}) collective-permute-start(bf16[128,1536]{1,0:T(8,128)(2,1)S(1)} %collective-permute-done.19.refs_6_), channel_id=1, source_target_pairs={{0,4},{4,8},{8,12},{12,14},{14,10},{10,6},{6,2},{2,0},{1,5},{5,9},... | collective-permute-start | bytes 1179656 | tf_op jit(solution)/shard_map/ppermute | solution.py:88
  69.0 9.3 %collective-permute-start.28 = (bf16[128,1536]{1,0:T(8,128)(2,1)S(1)}, bf16[128,1536]{1,0:T(8,128)(2,1)S(1)}, u32[]{:S(2)}, u32[]{:S(2)}) collective-permute-start(bf16[128,1536]{1,0:T(8,128)(2,1)S(1)} %collective-permute-done.20.refs_1_), channel_id=1, source_target_pairs={{4,0},{8,4},{12,8},{14,12},{10,14},{6,10},{2,6},{0,2},{5,1},{9,5},... | collective-permute-start | bytes 1179656 | tf_op jit(solution)/shard_map/ppermute | solution.py:88
  78.3 10.9 %collective-permute-start.32 = (bf16[128,1536]{1,0:T(8,128)(2,1)S(1)}, bf16[128,1536]{1,0:T(8,128)(2,1)S(1)}, u32[]{:S(2)}, u32[]{:S(2)}) collective-permute-start(bf16[128,1536]{1,0:T(8,128)(2,1)S(1)} %collective-permute-done.27.refs_5_), channel_id=1, source_target_pairs={{0,4},{4,8},{8,12},{12,14},{14,10},{10,6},{6,2},{2,0},{1,5},{5,9},... | collective-permute-start | bytes 1179656 | tf_op jit(solution)/shard_map/ppermute | solution.py:88
  78.8 10.4 %collective-permute-start.33 = (bf16[128,1536]{1,0:T(8,128)(2,1)S(1)}, bf16[128,1536]{1,0:T(8,128)(2,1)S(1)}, u32[]{:S(2)}, u32[]{:S(2)}) collective-permute-start(bf16[128,1536]{1,0:T(8,128)(2,1)S(1)} %collective-permute-done.28.refs_2_), channel_id=1, source_target_pairs={{4,0},{8,4},{12,8},{14,12},{10,14},{6,10},{2,6},{0,2},{5,1},{9,5},... | collective-permute-start | bytes 1179656 | tf_op jit(solution)/shard_map/ppermute | solution.py:88
  80.4 8.9 %collective-permute-start.34 = (bf16[48,1024]{1,0:T(8,128)(2,1)S(1)}, bf16[48,1024]{1,0:T(8,128)(2,1)S(1)}, u32[]{:S(2)}, u32[]{:S(2)}) collective-permute-start(bf16[48,1024]{1,0:T(8,128)(2,1)S(1)} %slice.144), channel_id=1, source_target_pairs={{0,4},{4,8},{8,12},{12,14},{14,10},{10,6},{6,2},{2,0},{1,5},{5,9},... | collective-permute-start | bytes 294920 | tf_op jit(solution)/shard_map/ppermute | solution.py:88
  108.2 12.5 %collective-permute-start.40 = (bf16[2,128,1024]{2,1,0:T(8,128)(2,1)S(1)}, bf16[2,128,1024]{2,1,0:T(8,128)(2,1)S(1)}, u32[]{:S(2)}, u32[]{:S(2)}) collective-permute-start(bf16[2,128,1024]{2,1,0:T(8,128)(2,1)S(1)} %get-tuple-element.242), channel_id=1, source_target_pairs={{0,1},{1,0},{2,3},{3,2},{4,5},{5,4},{6,7},{7,6},{8,9},{9,8},{10,11... | collective-permute-start | bytes 1572872 | tf_op jit(solution)/shard_map/ppermute | solution.py:54
  123.0 12.7 %collective-permute-start.43 = (bf16[2,128,1024]{2,1,0:T(8,128)(2,1)S(1)}, bf16[2,128,1024]{2,1,0:T(8,128)(2,1)S(1)}, u32[]{:S(2)}, u32[]{:S(2)}) collective-permute-start(bf16[2,128,1024]{2,1,0:T(8,128)(2,1)S(1)} %add_convert_fusion), channel_id=1, source_target_pairs={{0,16},{16,0},{1,17},{17,1},{2,18},{18,2},{3,19},{19,3},{4,20},{20... | collective-permute-start | bytes 1572872 | tf_op jit(solution)/shard_map/ppermute | solution.py:50
  135.6 8.9 %collective-permute-start.51 = (bf16[128,1536]{1,0:T(8,128)(2,1)S(1)}, bf16[128,1536]{1,0:T(8,128)(2,1)S(1)}, u32[]{:S(2)}, u32[]{:S(2)}) collective-permute-start(bf16[128,1536]{1,0:T(8,128)(2,1)S(1)} %get-tuple-element.267), channel_id=1, source_target_pairs={{4,0},{8,4},{12,8},{14,12},{10,14},{6,10},{2,6},{0,2},{5,1},{9,5},... | collective-permute-start | bytes 1179656 | tf_op jit(solution)/shard_map/ppermute | solution.py:88
  139.0 16.2 %collective-permute-start.48 = (bf16[2,128,1024]{2,1,0:T(8,128)(2,1)S(1)}, bf16[2,128,1024]{2,1,0:T(8,128)(2,1)S(1)}, u32[]{:S(2)}, u32[]{:S(2)}) collective-permute-start(bf16[2,128,1024]{2,1,0:T(8,128)(2,1)S(1)} %get-tuple-element.255), channel_id=1, source_target_pairs={{0,1},{1,0},{2,3},{3,2},{4,5},{5,4},{6,7},{7,6},{8,9},{9,8},{10,11... | collective-permute-start | bytes 1572872 | tf_op jit(solution)/shard_map/ppermute | solution.py:54
  155.4 14.5 %collective-permute-start.55 = (bf16[128,1536]{1,0:T(8,128)(2,1)S(1)}, bf16[128,1536]{1,0:T(8,128)(2,1)S(1)}, u32[]{:S(2)}, u32[]{:S(2)}) collective-permute-start(bf16[128,1536]{1,0:T(8,128)(2,1)S(1)} %get-tuple-element.272), channel_id=1, source_target_pairs={{4,0},{8,4},{12,8},{14,12},{10,14},{6,10},{2,6},{0,2},{5,1},{9,5},... | collective-permute-start | bytes 1179656 | tf_op jit(solution)/shard_map/ppermute | solution.py:88
  156.8 14.1 %collective-permute-start.54 = (bf16[128,1536]{1,0:T(8,128)(2,1)S(1)}, bf16[128,1536]{1,0:T(8,128)(2,1)S(1)}, u32[]{:S(2)}, u32[]{:S(2)}) collective-permute-start(bf16[128,1536]{1,0:T(8,128)(2,1)S(1)} %get-tuple-element.271), channel_id=1, source_target_pairs={{0,4},{4,8},{8,12},{12,14},{14,10},{10,6},{6,2},{2,0},{1,5},{5,9},... | collective-permute-start | bytes 1179656 | tf_op jit(solution)/shard_map/ppermute | solution.py:88
  157.7 10.4 %collective-permute-start.53 = (bf16[64,1024]{1,0:T(8,128)(2,1)S(1)}, bf16[64,1024]{1,0:T(8,128)(2,1)S(1)}, u32[]{:S(2)}, u32[]{:S(2)}) collective-permute-start(bf16[64,1024]{1,0:T(8,128)(2,1)S(1)} %get-tuple-element.270), channel_id=1, source_target_pairs={{4,0},{8,4},{12,8},{14,12},{10,14},{6,10},{2,6},{0,2},{5,1},{9,5},... | collective-permute-start | bytes 393224 | tf_op jit(solution)/shard_map/ppermute | solution.py:88
  158.8 10.2 %collective-permute-start.52 = (bf16[64,1024]{1,0:T(8,128)(2,1)S(1)}, bf16[64,1024]{1,0:T(8,128)(2,1)S(1)}, u32[]{:S(2)}, u32[]{:S(2)}) collective-permute-start(bf16[64,1024]{1,0:T(8,128)(2,1)S(1)} %get-tuple-element.269), channel_id=1, source_target_pairs={{0,4},{4,8},{8,12},{12,14},{14,10},{10,6},{6,2},{2,0},{1,5},{5,9},... | collective-permute-start | bytes 393224 | tf_op jit(solution)/shard_map/ppermute | solution.py:88
  159.7 22.1 %collective-permute-start.64 = (bf16[88,1024]{1,0:T(8,128)(2,1)}, bf16[88,1024]{1,0:T(8,128)(2,1)}, u32[]{:S(2)}, u32[]{:S(2)}) collective-permute-start(bf16[88,1024]{1,0:T(8,128)(2,1)} %get-tuple-element.283), channel_id=1, source_target_pairs={{4,0},{8,4},{12,8},{14,12},{10,14},{6,10},{2,6},{0,2},{5,1},{9,5},... | collective-permute-start | bytes 540680 | tf_op jit(solution)/shard_map/ppermute | solution.py:88
  168.1 14.6 %collective-permute-start.63 = (bf16[88,1024]{1,0:T(8,128)(2,1)}, bf16[88,1024]{1,0:T(8,128)(2,1)}, u32[]{:S(2)}, u32[]{:S(2)}) collective-permute-start(bf16[88,1024]{1,0:T(8,128)(2,1)} %get-tuple-element.282), channel_id=1, source_target_pairs={{0,4},{4,8},{8,12},{12,14},{14,10},{10,6},{6,2},{2,0},{1,5},{5,9},... | collective-permute-start | bytes 540680 | tf_op jit(solution)/shard_map/ppermute | solution.py:88
  178.6 9.5 %collective-permute-start.59 = (bf16[128,1024]{1,0:T(8,128)(2,1)}, bf16[128,1024]{1,0:T(8,128)(2,1)}, u32[]{:S(2)}, u32[]{:S(2)}) collective-permute-start(bf16[128,1024]{1,0:T(8,128)(2,1)} %get-tuple-element.278), channel_id=1, source_target_pairs={{4,0},{8,4},{12,8},{14,12},{10,14},{6,10},{2,6},{0,2},{5,1},{9,5},... | collective-permute-start | bytes 786440 | tf_op jit(solution)/shard_map/ppermute | solution.py:88
  179.8 9.6 %collective-permute-start.58 = (bf16[128,1024]{1,0:T(8,128)(2,1)}, bf16[128,1024]{1,0:T(8,128)(2,1)}, u32[]{:S(2)}, u32[]{:S(2)}) collective-permute-start(bf16[128,1024]{1,0:T(8,128)(2,1)} %get-tuple-element.277), channel_id=1, source_target_pairs={{0,4},{4,8},{8,12},{12,14},{14,10},{10,6},{6,2},{2,0},{1,5},{5,9},... | collective-permute-start | bytes 786440 | tf_op jit(solution)/shard_map/ppermute | solution.py:88
  180.7 14.5 %collective-permute-start.61 = (bf16[128,1536]{1,0:T(8,128)(2,1)}, bf16[128,1536]{1,0:T(8,128)(2,1)S(1)}, u32[]{:S(2)}, u32[]{:S(2)}) collective-permute-start(bf16[128,1536]{1,0:T(8,128)(2,1)} %get-tuple-element.280), channel_id=1, source_target_pairs={{4,0},{8,4},{12,8},{14,12},{10,14},{6,10},{2,6},{0,2},{5,1},{9,5},... | collective-permute-start | bytes 1179656 | tf_op jit(solution)/shard_map/ppermute | solution.py:88
  181.8 14.3 %collective-permute-start.60 = (bf16[128,1536]{1,0:T(8,128)(2,1)}, bf16[128,1536]{1,0:T(8,128)(2,1)S(1)}, u32[]{:S(2)}, u32[]{:S(2)}) collective-permute-start(bf16[128,1536]{1,0:T(8,128)(2,1)} %get-tuple-element.279), channel_id=1, source_target_pairs={{0,4},{4,8},{8,12},{12,14},{14,10},{10,6},{6,2},{2,0},{1,5},{5,9},... | collective-permute-start | bytes 1179656 | tf_op jit(solution)/shard_map/ppermute | solution.py:88
  183.8 13.6 %collective-permute-start.62 = (bf16[128,1024]{1,0:T(8,128)(2,1)}, bf16[128,1024]{1,0:T(8,128)(2,1)S(1)}, u32[]{:S(2)}, u32[]{:S(2)}) collective-permute-start(bf16[128,1024]{1,0:T(8,128)(2,1)} %fusion.49), channel_id=1, source_target_pairs={{0,16},{16,0},{1,17},{17,1},{2,18},{18,2},{3,19},{19,3},{4,20},{20... | collective-permute-start | bytes 786440 | tf_op jit(solution)/shard_map/ppermute | solution.py:50
  199.6 8.9 %collective-permute-start.68 = (bf16[88,1024]{1,0:T(8,128)(2,1)S(1)}, bf16[88,1024]{1,0:T(8,128)(2,1)S(1)}, u32[]{:S(2)}, u32[]{:S(2)}) collective-permute-start(bf16[88,1024]{1,0:T(8,128)(2,1)S(1)} %fusion.34), channel_id=1, source_target_pairs={{0,16},{16,0},{1,17},{17,1},{2,18},{18,2},{3,19},{19,3},{4,20},{20... | collective-permute-start | bytes 540680 | tf_op jit(solution)/shard_map/ppermute | solution.py:50
  210.6 10.5 %collective-permute-start.72 = (bf16[2,64,1536]{2,1,0:T(8,128)(2,1)S(1)}, bf16[2,64,1536]{2,1,0:T(8,128)(2,1)S(1)}, u32[]{:S(2)}, u32[]{:S(2)}) collective-permute-start(bf16[2,64,1536]{2,1,0:T(8,128)(2,1)S(1)} %pad_maximum_fusion.pair_ref), channel_id=1, source_target_pairs={{0,16},{16,0},{1,17},{17,1},{2,18},{18,2},{3,19},{19,3},{4,20},{20... | collective-permute-start | bytes 1179656 | tf_op jit(solution)/shard_map/ppermute | solution.py:50
  221.1 10.0 %collective-permute-start.73 = (bf16[2,64,1024]{2,1,0:T(8,128)(2,1)S(1)}, bf16[2,64,1024]{2,1,0:T(8,128)(2,1)S(1)}, u32[]{:S(2)}, u32[]{:S(2)}) collective-permute-start(bf16[2,64,1024]{2,1,0:T(8,128)(2,1)S(1)} %pad_maximum_fusion.2.pair_ref), channel_id=1, source_target_pairs={{0,16},{16,0},{1,17},{17,1},{2,18},{18,2},{3,19},{19,3},{4,20},{20... | collective-permute-start | bytes 786440 | tf_op jit(solution)/shard_map/ppermute | solution.py:50
  (70 other events, 823.4 us)

commit v2 on v1

--- a/solution.py
+++ b/solution.py
@@ -118,37 +118,36 @@
         self.ring = ring
         self.step = 0
         self.parts = parts
-        self.cut = upper_half(parts.shape[1])
+        self.cut = upper_half(parts[0].shape[0])
         far = parts[ring.half]
-        self.state = (far[: self.cut].astype(BF), far[self.cut :].astype(BF))
-
-    def advance(self):
+        self.state = (far[: self.cut], far[self.cut :])
+
+    def send(self):
+        self.got = self.ring.exchange(self.state)
+
+    def add(self):
         ring = self.ring
-        if self.step == ring.half:
-            return
-        right, left = (v.astype(F32) for v in ring.exchange(self.state))
-        if self.step == 0:
-            right = jnp.pad(right, ((0, self.parts.shape[1] - self.cut), (0, 0)))
+        self.step += 1
+        place = ring.half - self.step
+        right, left = self.got
+        if self.step == 1:
+            right = jnp.pad(right, ((0, self.parts[0].shape[0] - self.cut), (0, 0)))
             left = jnp.pad(left, ((self.cut, 0), (0, 0)))
-        self.step += 1
-        if self.step == ring.half:
-            self.total = self.parts[0] + right + left
-            self.state = ()
-            return
-        place = ring.half - self.step
-        self.state = ((self.parts[place] + right).astype(BF), (self.parts[ring.size - place] + left).astype(BF))
-
-    def finish(self):
-        while self.step < self.ring.half:
-            self.advance()
-        return self.total
+        terms = (self.parts[place], self.parts[ring.size - place])
+        self.state = tuple((t.astype(F32) + v.astype(F32)).astype(BF) for t, v in zip(terms, (right, left), strict=True))
+
+    def run(self):
+        while self.step < self.ring.half - 1:
+            self.add()
+            self.send()
+        return self.parts[0], *self.got
 
 
 def sync(*values):
     return lax.optimization_barrier(values)
 
 
-def call(body, outs, scratch, limit, flops, *args):
+def call(body, outs, scratch, flops, *args):
     nbytes = sum(a.size * a.dtype.itemsize for a in args) + sum(o.size * o.dtype.itemsize for o in outs)
     return pl.pallas_call(
         body,
@@ -157,7 +156,7 @@
         in_specs=[pl.BlockSpec(memory_space=pltpu.SMEM)] + [pl.BlockSpec(memory_space=pltpu.VMEM)] * (len(args) - 1),
         out_specs=[pl.BlockSpec(memory_space=pltpu.VMEM)] * len(outs),
         scratch_shapes=scratch,
-        compiler_params=pltpu.CompilerParams(vmem_limit_bytes=limit * MIB),
+        compiler_params=pltpu.CompilerParams(vmem_limit_bytes=32 * MIB),
         cost_estimate=pl.CostEstimate(flops=flops, bytes_accessed=nbytes, transcendentals=0),
     )(*args)
 
@@ -168,6 +167,12 @@
 
 def lanes(start, size):
     return pl.ds(pl.multiple_of(start, LANES), size)
+
+
+def pack_tokens(rows, prefix_ref, tokens_ref, own_ref):
+    own_ref[:rows, :] = tokens_ref[...]
+    for m in range(own_ref.shape[0] - rows):
+        own_ref[rows + m : rows + m + 1, :] = jnp.full((1, own_ref.shape[1]), prefix_ref[m, 0].astype(F32)).astype(BF)
 
 
 def pack_first(size, width, scal, qkv_ref, out_ref, own_ref, sib_ref):
@@ -276,15 +281,24 @@
 
 
 def middle(size, rows, width, scal, *refs):
-    blocks, cots, outputs, weights = refs[:4], refs[4:8], refs[8:12], refs[12:16]
-    x2_ref, h2_ref, o_ref, rows_ref, gm_ref, w_full = refs[16:]
+    blocks, cots = refs[:4], refs[4:8]
+    o_own, o_far, w_own, w_far, near_ref = refs[8:13]
+    full = 4 * rows
+    outputs = (
+        lambda b: o_own[b],
+        lambda b: near_ref[b * rows : (b + 1) * rows],
+        lambda b: o_far[b],
+        lambda b: near_ref[full + b * rows : full + (b + 1) * rows],
+    )
+    weights = (w_own, near_ref.at[2 * full : 2 * full + width], w_far, near_ref.at[2 * full + width :])
+    x2_ref, h2_ref, o_ref, rows_ref, gm_ref, w_full = refs[13:]
     quarter = width // 4
     members = [scal[2 * size + 1 + m] for m in range(4)]
     for m in range(4):
         w_full[:, lanes(members[m] * quarter, quarter)] = weights[m][...]
         gm_ref[m * rows : (m + 1) * rows, :] = cots[m][...]
         for b in range(4):
-            o_ref[b * rows : (b + 1) * rows, lanes(members[m] * quarter, quarter)] = outputs[m][BLOCKS[m][b]]
+            o_ref[b * rows : (b + 1) * rows, lanes(members[m] * quarter, quarter)] = outputs[m](BLOCKS[m][b])
     rows_ref[...] = w_full[pl.ds(pl.multiple_of(members[0] * quarter, quarter), quarter), :]
     for j in range(4):
         columns = slice(j * quarter, (j + 1) * quarter)
@@ -364,26 +378,33 @@
         share(dot(hid_ref[...], down_ref[:, columns]), rows, keep_ref, give_ref, columns)
 
 
-def grad_down_parts(size, padded, piece, scal, hid_ref, gm_ref, part_ref):
+def write_parts(size, stride, scal, total, refs):
+    for k, ref in enumerate(refs):
+        ref[...] = total[pl.ds(pl.multiple_of(scal[k] * stride, PACK), ref.shape[0]), :].astype(BF)
+
+
+def grad_down_parts(size, padded, scal, hid_ref, gm_ref, *refs):
+    total = refs[-1]
     tile = 256
 
     @pl.loop(0, gm_ref.shape[1] // tile)
     def _(i):
         columns = pl.ds(pl.multiple_of(i * tile, tile), tile)
-        grads = dot_lt(hid_ref[...], gm_ref[:, columns])
-        for g in range(size):
-            part_ref[scal[size + g], :, columns] = grads[g * padded : g * padded + piece]
-
-
-def grad_in_parts(size, double, scal, h2_ref, ggu_ref, part_ref):
+        total[:, columns] = dot_lt(hid_ref[...], gm_ref[:, columns])
+
+    write_parts(size, padded, scal, total, refs[:-1])
+
+
+def grad_in_parts(size, double, scal, h2_ref, ggu_ref, *refs):
+    total = refs[-1]
     tile = 256
 
     @pl.loop(0, ggu_ref.shape[1] // tile)
     def _(i):
         columns = pl.ds(pl.multiple_of(i * tile, tile), tile)
-        grads = dot_lt(h2_ref[...], ggu_ref[:, columns])
-        for g in range(size):
-            part_ref[scal[size + g], :, columns] = grads[g * double : (g + 1) * double]
+        total[:, columns] = dot_lt(h2_ref[...], ggu_ref[:, columns])
+
+    write_parts(size, double, scal, total, refs[:-1])
 
 
 def middle_back(rows, scal, keep_ref, got_ref, far_ref, x2_ref, cot_own, cot_far, gx2_ref, ga_ref):
@@ -426,15 +447,22 @@
         share(dot_rt(gqkv_ref[...], w_ref[columns, :]), rows, keep_ref, give_ref, columns)
 
 
-def grad_first_parts(size, double, width, scal, h1_ref, gqkv_ref, o_ref, ga_ref, part_ref):
+def grad_first_parts(size, double, width, scal, h1_ref, gqkv_ref, o_ref, ga_ref, *refs):
+    total = refs[-1]
     quarter = width // 4
-    for j in range(4):
-        if j < 3:
-            grads = dot_lt(h1_ref[...], gqkv_ref[:, j * quarter : (j + 1) * quarter])
-        else:
-            grads = dot_lt(o_ref[...], ga_ref[:, lanes(scal[2 * size + 1] * quarter, quarter)])
-        for g in range(size):
-            part_ref[scal[size + g], :, j * quarter : (j + 1) * quarter] = grads[g * double : (g + 1) * double]
+    for j in range(3):
+        columns = slice(j * quarter, (j + 1) * quarter)
+        total[:, columns] = dot_lt(h1_ref[...], gqkv_ref[:, columns])
+    total[:, 3 * quarter :] = dot_lt(o_ref[...], ga_ref[:, lanes(scal[2 * size + 1] * quarter, quarter)])
+    write_parts(size, double, scal, total, refs[:-1])
+
+
+def split_rows(size, scal, own_ref, right_ref, left_ref, keep_ref, give_ref):
+    core = scal[2 * size]
+    rows = keep_ref.shape[0]
+    for ref, first in ((keep_ref, core), (give_ref, 1 - core)):
+        here = pl.ds(pl.multiple_of(first * rows, PACK), rows)
+        ref[...] = (own_ref[here, :].astype(F32) + right_ref[here, :].astype(F32) + left_ref[here, :].astype(F32)).astype(BF)
 
 
 def finish_tokens(rows, scal, keep_ref, got_ref, far_ref, block_ref, gx2_ref, out_ref):
@@ -443,19 +471,19 @@
     out_ref[...] = gx2_ref[...] + norm_back(normed, inverse, upstream)
 
 
-def unpack_first(size, width, scal, pair_ref, other_ref, qkv_ref, out_ref):
+def unpack_first(size, width, scal, own_ref, near_ref, far_ref, diagonal_ref, qkv_ref, out_ref):
     quarter = width // 4
-    for m, value in enumerate((pair_ref[0], pair_ref[1], other_ref[0], other_ref[1])):
-        value = value.astype(F32)
+    for m, ref in enumerate((own_ref, near_ref, far_ref, diagonal_ref)):
+        value = ref[...].astype(F32)
         at = scal[2 * size + 1 + m] * quarter
         for j in range(3):
             qkv_ref[:, lanes(j * width + at, quarter)] = value[:, j * quarter : (j + 1) * quarter]
         out_ref[:, lanes(at, quarter)] = value[:, 3 * quarter :]
 
 
-def unpack_in(size, units, piece, padded, scal, pair_ref, other_ref, in_ref, held):
-    for m, value in enumerate((pair_ref[0], pair_ref[1], other_ref[0], other_ref[1])):
-        held[scal[2 * size + 1 + m]] = value.astype(F32)
+def unpack_in(size, units, piece, padded, scal, own_ref, near_ref, far_ref, diagonal_ref, in_ref, held):
+    for m, ref in enumerate((own_ref, near_ref, far_ref, diagonal_ref)):
+        held[scal[2 * size + 1 + m]] = ref[...].astype(F32)
     for q in range(4):
         for part in range(2):
             for g in range(size):
@@ -500,45 +528,44 @@
     pair_full = shape((2, rows, width), F32)
     project = 2 * full_rows * width * quarter
 
-    own = jnp.concatenate([tokens.reshape(rows, width), jnp.broadcast_to(prefix.astype(BF), (micro, width))], axis=0)
+    tokens = tokens.reshape(rows, width)
     cot_own = cotangent.reshape(rows, width)
-    a_own, a_sib = call(
-        functools.partial(pack_first, size, width), [shape((shard_rows, width), BF)] * 2, [], 8, 0, scal, qkv_weight, out_weight
-    )
-    a_got = sibling(a_sib)
-    near = sibling(own)
-    a = Gather(ring, jnp.concatenate([a_own, a_got], axis=0))
-
-    a.state, own, cot_own, in_weight, near = sync(a.state, own, cot_own, in_weight, near)
+    a_own, a_sib = call(functools.partial(pack_first, size, width), [shape((shard_rows, width), BF)] * 2, [], 0, scal, qkv_weight, out_weight)
+    a = Gather(ring, jnp.concatenate([a_own, sibling(a_sib)], axis=0))
+
+    a.state, in_weight = sync(a.state, in_weight)
+    a.advance()
+    b_own, b_sib = call(
+        functools.partial(pack_in, size, units, piece, padded), [shape((shard_rows, 2 * member_units), BF)] * 2, [], 0, scal, in_weight
+    )
+    b_own, b_sib, tokens = sync(b_own, b_sib, tokens)
+    (own,) = call(functools.partial(pack_tokens, rows), [shape((rows + micro, width), BF)], [], 0, prefix, tokens)
+
+    a.state, own, b_own, b_sib = sync(a.state, own, b_own, b_sib)
     a.advance()
     far = across(own)
+    near = sibling(own)
+    b_got = sibling(b_sib)
+
+    a.state, cot_own, far, near, b_own, b_got, down_weight = sync(a.state, cot_own, far, near, b_own, b_got, down_weight)
+    a.advance()
+    cot_far = across(cot_own)
+    diagonal = sibling(far)
     cot_near = sibling(cot_own)
-    b_own, b_sib = call(
-        functools.partial(pack_in, size, units, piece, padded), [shape((shard_rows, 2 * member_units), BF)] * 2, [], 8, 0, scal, in_weight
-    )
-
-    a.state, far, cot_own, b_own, b_sib, cot_near = sync(a.state, far, cot_own, b_own, b_sib, cot_near)
-    a.advance()
-    diagonal = sibling(far)
-    cot_far = across(cot_own)
-    b_got = sibling(b_sib)
-
-    a.state, cot_far, b_own, b_got, diagonal, down_weight = sync(a.state, cot_far, b_own, b_got, diagonal, down_weight)
-    a.advance()
-    cot_diagonal = sibling(cot_far)
     b = Gather(ring, jnp.concatenate([b_own, b_got], axis=0))
     c = Gather(ring, lax.dynamic_slice(down_weight, (rep * piece, 0), (piece, width)))
-    blocks = [own, near, far, diagonal]
-
-    a.state, b.state, c.state, cot_diagonal, blocks = sync(a.state, b.state, c.state, cot_diagonal, blocks)
+
+    a.state, b.state, c.state, cot_near, cot_far, diagonal = sync(a.state, b.state, c.state, cot_near, cot_far, diagonal)
     c.advance()
     a_chunks = a.finish()
+    cot_diagonal = sibling(cot_far)
+    blocks = [own, near, far, diagonal]
     cots = [cot_own, cot_near, cot_far, cot_diagonal]
 
     a_chunks, b.state, c.state = sync(a_chunks, b.state, c.state)
     b.advance()
     c.advance()
-    (out_mine,) = call(functools.partial(gather_out, size, shard_rows, quarter), [shape((width, quarter), BF)], [], 8, 0, scal, *a_chunks)
+    (out_mine,) = call(functools.partial(gather_out, size, shard_rows, quarter), [shape((width, quarter), BF)], [], 0, scal, *a_chunks)
     out_far = across(out_mine)
     o_own, h1, qkv, probs, qkv_mine = call(
         functools.partial(attention, size, shard_rows, rows, length, width, chunks),
@@ -550,7 +577,6 @@
             shape((width, 3 * quarter), BF),
         ],
         [],
-        24,
         3 * project,
         scal,
         *blocks,
@@ -563,12 +589,10 @@
     o_far = across(o_own)
     b.advance()
     c.advance()
-    o_near = sibling(o_own)
-    out_near = sibling(out_mine)
-    out_diagonal = sibling(out_far)
-
-    o_far, o_near, out_near, out_diagonal, b.state, c.state = sync(o_far, o_near, out_near, out_diagonal, b.state, c.state)
-    o_diagonal = sibling(o_far)
+
+    o_far, b.state, c.state = sync(o_far, b.state, c.state)
+    kept = [o_own.reshape(full_rows, quarter), o_far.reshape(full_rows, quarter), out_mine, out_far]
+    near_all = sibling(jnp.concatenate(kept, axis=0))
     b.advance()
     c_chunks = c.finish()
     x2, h2, o_all, out_rows, gm = call(
@@ -581,19 +605,15 @@
             shape((full_rows, width), BF),
         ],
         [pltpu.VMEM((width, width), BF)],
-        24,
         4 * project,
         scal,
         *blocks,
         *cots,
         o_own,
-        o_near,
         o_far,
-        o_diagonal,
         out_mine,
-        out_near,
         out_far,
-        out_diagonal,
+        near_all,
     )
 
     h2, b.state, c_chunks = sync(h2, b.state, c_chunks)
@@ -607,24 +627,22 @@
             shape((width, 2 * member_units), BF),
         ],
         [],
-        28,
         6 * project,
         scal,
         h2,
         *b_chunks,
     )
-    (down_parts,) = call(
-        functools.partial(grad_down_parts, size, padded, piece), [shape((size, piece, width), F32)], [], 16, 3 * project, scal, hid, gm
+    down_parts = call(
+        functools.partial(grad_down_parts, size, padded), [shape((piece, width), BF)] * size, [pltpu.VMEM((member_units, width), F32)], 3 * project, scal, hid, gm
     )
 
     c = Scatter(ring, down_parts)
     c.state, gm, up = sync(c.state, gm, up)
-    c.advance()
+    c.send()
     ggu, u2_keep, u2_give, down_mine = call(
         functools.partial(hidden_back, size, rows, padded, piece, chunks),
         [shape((full_rows, 2 * member_units), BF), pair_full, pair_low, shape((member_units, width), BF)],
         [],
-        32,
         9 * project,
         scal,
         gm,
@@ -634,34 +652,49 @@
         in_mine,
     )
 
-    u2_give, c.state, ggu = sync(u2_give, c.state, ggu)
+    u2_give, c.got = sync(u2_give, c.got)
     u2_got = sibling(u2_give)
-    c.advance()
-    (in_parts,) = call(
-        functools.partial(grad_in_parts, size, double), [shape((size, double, 2 * member_units), F32)], [], 24, 6 * project, scal, h2, ggu
-    )
+    c.add()
+    c.send()
+    u2_low = (u2_keep + u2_got.astype(F32)).astype(BF)
+
+    u2_low, ggu = sync(u2_low, ggu)
+    u2_far = across(u2_low)
+    in_parts = call(
+        functools.partial(grad_in_parts, size, double),
+        [shape((double, 2 * member_units), BF)] * size,
+        [pltpu.VMEM((width, 2 * member_units), F32)],
+        6 * project,
+        scal,
+        h2,
+        ggu,
+    )
+
     b = Scatter(ring, in_parts)
-    u2_low = (u2_keep + u2_got.astype(F32)).astype(BF)
-
-    u2_low, b.state, c.state, hid = sync(u2_low, b.state, c.state, hid)
-    u2_far = across(u2_low)
-    b.advance()
-    c.advance()
-    y_keep, y_give = call(functools.partial(last_projection, rows), [pair_full, pair_low], [], 16, 3 * project, scal, hid, down_mine)
-
-    u2_far, b.state, c.state, y_give = sync(u2_far, b.state, c.state, y_give)
-    b.advance()
-    c.advance()
+    b.state, c.got, hid = sync(b.state, c.got, hid)
+    b.send()
+    c.add()
+    c.send()
+    y_keep, y_give = call(functools.partial(last_projection, rows), [pair_full, pair_low], [], 3 * project, scal, hid, down_mine)
+
+    y_give, c.got, b.got = sync(y_give, c.got, b.got)
+    b.add()
+    b.send()
+    c.add()
+    c.send()
+    gx2, ga = call(
+        functools.partial(middle_back, rows), [shape((rows, width), F32), pair_low], [], 0, scal, u2_keep, u2_got, u2_far, x2, cots[0], cots[2]
+    )
+    ga_near = sibling(ga)
     y_got = sibling(y_give)
-    gx2, ga = call(
-        functools.partial(middle_back, rows), [shape((rows, width), F32), pair_low], [], 16, 0, scal, u2_keep, u2_got, u2_far, x2, cots[0], cots[2]
-    )
-    ga_near = sibling(ga)
+    y_low = (y_keep[1] + y_got[1].astype(F32)).astype(BF)
+
+    y_low, ga_near = sync(y_low, ga_near)
+    y_far = across(y_low)
     gqkv, ga_all, u1_keep, u1_give = call(
         functools.partial(attention_back, rows, width),
         [shape((full_rows, 3 * quarter), BF), shape((full_rows, width), BF), pair_full, pair_low],
         [pltpu.VMEM((full_rows, quarter), BF), pltpu.VMEM((3, rows, quarter), F32)],
-        24,
         7 * project,
         scal,
         ga,
@@ -673,11 +706,15 @@
         cosine,
         sine,
     )
-    (first_parts,) = call(
+
+    gqkv, u1_give, c.got, b.got, y_far = sync(gqkv, u1_give, c.got, b.got, y_far)
+    b.add()
+    b.send()
+    u1_got = sibling(u1_give)
+    first_parts = call(
         functools.partial(grad_first_parts, size, double, width),
-        [shape((size, double, width), F32)],
-        [],
-        24,
+        [shape((double, width), BF)] * size,
+        [pltpu.VMEM((width, width), F32)],
         4 * project,
         scal,
         h1,
@@ -685,65 +722,71 @@
         o_all,
         ga_all,
     )
+    down_low = sum(v.astype(F32) for v in c.run()).astype(BF)
+
     a = Scatter(ring, first_parts)
-    down_low = c.finish().astype(BF)
-    y_low = (y_keep[1] + y_got[1].astype(F32)).astype(BF)
-
-    a.state, b.state, u1_give, y_low = sync(a.state, b.state, u1_give, y_low)
-    a.advance()
-    b.advance()
-    u1_got = sibling(u1_give)
-    y_far = across(y_low)
+    a.state, u1_got, down_low = sync(a.state, u1_got, down_low)
+    a.send()
     u1_low = (u1_keep[1] + u1_got[1].astype(F32)).astype(BF)
-
-    def halves(low):
-        keep = lax.dynamic_slice(low, (core * shard_rows, 0), (shard_rows, low.shape[1]))
-        give = lax.dynamic_slice(low, ((1 - core) * shard_rows, 0), (shard_rows, low.shape[1]))
-        return keep, give
-
-    a.state, b.state, u1_low, y_far = sync(a.state, b.state, u1_low, y_far)
-    a.advance()
-    in_low = b.finish().astype(BF)
     u1_far = across(u1_low)
+
+    a.got, b.got, u1_far = sync(a.got, b.got, u1_far)
+    a.add()
+    a.send()
+    b.add()
+    b.send()
+    down_other = across(down_low)
+
+    while a.step < ring.half - 2:
+        (a.got,) = sync(a.got)
+        a.add()
+        a.send()
+
+    def halves(summed):
+        columns = summed[0].shape[1]
+        return call(functools.partial(split_rows, size), [shape((shard_rows, columns), BF)] * 2, [], 0, scal, *summed)
+
+    b_sum = b.run()
+    a.got, b_sum, down_other = sync(a.got, b_sum, down_other)
+    a.add()
+    a.send()
+    in_keep, in_give = halves(b_sum)
+    in_near = sibling(in_give)
+    in_pair = jnp.stack([in_keep, in_near])
+    in_other = across(in_pair)
+    a_sum = a.run()
+    first_keep, first_give = halves(a_sum)
+    first_keep, first_give, in_other = sync(first_keep, first_give, in_other)
+    first_far = across(first_keep)
+    first_near = sibling(first_give)
+    first_diagonal = across(first_near)
+    u1_far, y_far, down_other, in_near, first_near = sync(u1_far, y_far, down_other, in_near, first_near)
+    (grad_tokens,) = call(
+        functools.partial(finish_tokens, rows), [shape((rows, width), F32)], [], 0, scal, u1_keep, u1_got, u1_far, own, gx2
+    )
     result = (x2[:rows] + (y_keep[0] + y_got[0].astype(F32) + y_far.astype(F32))).astype(BF)
-
-    in_keep, in_give = halves(in_low)
-    a.state, in_give, u1_far, down_low = sync(a.state, in_give, u1_far, down_low)
-    a.advance()
-    in_got = sibling(in_give)
-    down_other = across(down_low)
-    (grad_tokens,) = call(
-        functools.partial(finish_tokens, rows), [shape((rows, width), F32)], [], 16, 0, scal, u1_keep, u1_got, u1_far, own, gx2
-    )
-
-    in_pair = jnp.stack([in_keep, in_got])
-    a.state, in_pair, down_other = sync(a.state, in_pair, down_other)
-    in_other = across(in_pair)
-    first_keep, first_give = halves(a.finish().astype(BF))
     grad_down = jnp.where(rep == 0, jnp.concatenate([down_low, down_other]), jnp.concatenate([down_other, down_low])).astype(F32)
-
-    first_pair = jnp.stack([first_keep, sibling(first_give)])
-    first_pair, in_other = sync(first_pair, in_other)
-    first_other = across(first_pair)
     (grad_in,) = call(
         functools.partial(unpack_in, size, units, piece, padded),
         [shape((shard_rows, 2 * units), F32)],
         [pltpu.VMEM((4, shard_rows, 2 * member_units), F32)],
-        16,
         0,
         scal,
-        in_pair,
-        in_other,
+        in_keep,
+        in_near,
+        in_other[0],
+        in_other[1],
     )
     grad_qkv, grad_out = call(
         functools.partial(unpack_first, size, width),
         [shape((shard_rows, 3 * width), F32), shape((shard_rows, width), F32)],
         [],
-        16,
         0,
         scal,
-        first_pair,
-        first_other,
+        first_keep,
+        first_near,
+        first_far,
+        first_diagonal,
     )
     return (
         result.reshape(micro, 1, length, width),

time: 233 us -> 214 us (0.918)
  other arithmetic: 17.6 us -> 6.37 us
  waiting for transfers between devices: 99.7 us -> 92.4 us
  Pallas kernels: 44.3 us -> 47.4 us
    ppermute x24, waiting for transfers between devices: 48.4 us -> 39.5 us  [exchange(): lax.ppermute(pair[1], 'ring', self.left)]
    convert_element_type x12 -> x19, other arithmetic: 9.74 us -> 2.49 us  [the longest x18 2.42 us: add(): (t.astype(F32) + v.astype(F32)).astype(BF)]
    ppermute x24, waiting for transfers between devices: 34.6 us -> 40.6 us  [exchange(): lax.ppermute(pair[0], 'ring', self.right)]
    pallas_call x16 -> x19, Pallas kernels: 44.3 us -> 47.4 us  [call(): pl.pallas_call(body, name=body.func.__name__, out_shape=outs, in_specs=[p...]
    ppermute x10 -> x11, starting transfers between devices: 11.5 us -> 8.99 us  [across(): return lax.ppermute(value, 'rep', SWAP)]
    ppermute x16 -> x13, waiting for transfers between devices: 6.29 us -> 3.95 us  [sibling(): return lax.ppermute(value, 'core', SWAP)]
    ppermute x10 -> x11, waiting for transfers between devices: 10.5 us -> 8.3 us  [across(): return lax.ppermute(value, 'rep', SWAP)]
  transfers between devices with their start and end apart: 74 -> 72, of which waited for: 43 -> 38; matrix products, arithmetic and copies ran while one was open for 8% -> 4% of each run, Pallas kernels for 16% -> 18%
where the time goes in v2:
time: 214 us
  waiting for transfers between devices  92.4 us (43%)
  starting transfers between devices  61.1 us (29%)
  Pallas kernels  47.4 us (22%)
  other arithmetic  6.37 us (3%)
  local copies, waits for them, and re-layouts  5.47 us (3%)
    pallas_call x19, Pallas kernels, call(): pl.pallas_call(body, name=body.func.__name__, out_shape=outs, in_specs=[p...  47.4 us
    ppermute x24, waiting for transfers between devices, exchange(): lax.ppermute(pair[0], 'ring', self.right)  40.6 us
    ppermute x24, waiting for transfers between devices, exchange(): lax.ppermute(pair[1], 'ring', self.left)  39.5 us
    ppermute x24, starting transfers between devices, exchange(): lax.ppermute(pair[1], 'ring', self.left)  28.2 us
    ppermute x24, starting transfers between devices, exchange(): lax.ppermute(pair[0], 'ring', self.right)  23.1 us
    ppermute x11, starting transfers between devices, across(): return lax.ppermute(value, 'rep', SWAP)  8.99 us
    ppermute x11, waiting for transfers between devices, across(): return lax.ppermute(value, 'rep', SWAP)  8.3 us
  transfers between devices with their start and end apart: 72, of which 38 were waited for; matrix products, arithmetic and copies ran while one was open for 4% of the time, Pallas kernels for 18%

profile of v2, /device:TPU:0, one launch (start us, length us, event | category | flops | bytes accessed | tf_op | source)
XLA Modules:
  0.0 214.0 jit_solution(1596720683989007254)
XLA Ops:
  5.5 3.0 %collective-permute-start.1 = (bf16[128,1024]{1,0:T(8,128)(2,1)S(1)}, bf16[128,1024]{1,0:T(8,128)(2,1)S(1)}, u32[]{:S(2)}, u32[]{:S(2)}) collective-permute-start(bf16[128,1024]{1,0:T(8,128)(2,1)S(1)} %constant_dynamic-update-slice_fusion.refs_4_.refs_0_), channel_id=1, source_target_pairs={{0,4},{4,8},{8,12},{12,14},{14,10},{10,6},{6,2},{2,0},{1,5},{5,9},... | collective-permute-start | bytes 786440 | tf_op jit(solution)/shard_map/ppermute | solution.py:88
  11.3 3.7 %collective-permute-done.1.refs_10_.refs_6_ = bf16[128,1024]{1,0:T(8,128)(2,1)S(1)} collective-permute-done((bf16[128,1024]{1,0:T(8,128)(2,1)S(1)}, bf16[128,1024]{1,0:T(8,128)(2,1)S(1)}, u32[]{:S(2)}, u32[]{:S(2)}) %collective-permute-start.1) | collective-permute-done | bytes 262176 | tf_op jit(solution)/shard_map/ppermute | solution.py:88
  20.1 1.6 collective-permute-done.7
  21.7 4.8 %collective-permute-done.3.refs_9_.refs_5_ = bf16[128,1024]{1,0:T(8,128)(2,1)S(1)} collective-permute-done((bf16[128,1024]{1,0:T(8,128)(2,1)S(1)}, bf16[128,1024]{1,0:T(8,128)(2,1)S(1)}, u32[]{:S(2)}, u32[]{:S(2)}) %collective-permute-start.3) | collective-permute-done | bytes 262176 | tf_op jit(solution)/shard_map/ppermute | solution.py:88
  30.5 6.6 %collective-permute-done.8.refs_8_.refs_4_ = bf16[128,1024]{1,0:T(8,128)(2,1)S(1)} collective-permute-done((bf16[128,1024]{1,0:T(8,128)(2,1)S(1)}, bf16[128,1024]{1,0:T(8,128)(2,1)S(1)}, u32[]{:S(2)}, u32[]{:S(2)}) %collective-permute-start.8) | collective-permute-done | bytes 262176 | tf_op jit(solution)/shard_map/ppermute | solution.py:88
  42.6 5.8 %collective-permute-done.15.refs_12_.refs_8_ = bf16[64,1024]{1,0:T(8,128)(2,1)S(1)} collective-permute-done((bf16[64,1024]{1,0:T(8,128)(2,1)S(1)}, bf16[64,1024]{1,0:T(8,128)(2,1)S(1)}, u32[]{:S(2)}, u32[]{:S(2)}) %collective-permute-start.15) | collective-permute-done | bytes 131104 | tf_op jit(solution)/shard_map/ppermute | solution.py:88
  54.6 7.0 %attention.1 = (bf16[4,128,256]{2,1,0:T(8,128)(2,1)S(1)}, bf16[512,1024]{1,0:T(8,128)(2,1)S(1)}, bf16[512,768]{1,0:T(8,128)(2,1)S(1)}, f32[16,128,128]{2,1,0:T(8,128)S(1)}, bf16[1024,768]{1,0:T(8,128)(2,1)S(1)}) custom-call(s32[21]{0:T(128)S(1)} %dynamic-slice_bitcast_fusion.scal, bf16[130,1024]{1,0:T(8,128)(2,1)S(1)} %pack_tokens.1.refs_0_.block_ref, ...), custom_call_target="tpu_custom_call" | custom-call | flops 805306368 | bytes 8142932 | tf_op jit(solution)/shard_map/attention/pallas_call | solution.py:152
  61.6 1.7 collective-permute-done.21.refs_6_
  68.5 7.2 %collective-permute-done.26.refs_5_ = bf16[88,1024]{1,0:T(8,128)(2,1)S(1)} collective-permute-done((bf16[88,1024]{1,0:T(8,128)(2,1)S(1)}, bf16[88,1024]{1,0:T(8,128)(2,1)S(1)}, u32[]{:S(2)}, u32[]{:S(2)}) %collective-permute-start.26) | collective-permute-done | bytes 180256 | tf_op jit(solution)/shard_map/ppermute | solution.py:88
  81.0 2.8 %middle.1 = (f32[512,1024]{1,0:T(8,128)S(1)}, bf16[512,1024]{1,0:T(8,128)(2,1)S(1)}, bf16[512,1024]{1,0:T(8,128)(2,1)S(1)}, bf16[256,1024]{1,0:T(8,128)(2,1)S(1)}, bf16[512,1024]{1,0:T(8,128)(2,1)S(1)}) custom-call(s32[21]{0:T(128)S(1)} %copy-done.20, bf16[130,1024]{1,0:T(8,128)(2,1)S(1)} %pack_tokens.1.refs_0_.block_ref, ...), custom_call_target="tpu_custom_call" | custom-call | flops 1073741824 | bytes 11026516 | tf_op jit(solution)/shard_map/middle/pallas_call | solution.py:152
  83.8 6.5 %collective-permute-done.32.refs_9_ = bf16[40,1024]{1,0:T(8,128)(2,1)S(1)} collective-permute-done((bf16[40,1024]{1,0:T(8,128)(2,1)S(1)}, bf16[40,1024]{1,0:T(8,128)(2,1)S(1)}, u32[]{:S(2)}, u32[]{:S(2)}) %collective-permute-start.32) | collective-permute-done | bytes 81952 | tf_op jit(solution)/shard_map/ppermute | solution.py:88
  92.4 4.4 %collective-permute-done.34.refs_8_ = bf16[64,1536]{1,0:T(8,128)(2,1)S(1)} collective-permute-done((bf16[64,1536]{1,0:T(8,128)(2,1)S(1)}, bf16[64,1536]{1,0:T(8,128)(2,1)S(1)}, u32[]{:S(2)}, u32[]{:S(2)}) %collective-permute-start.34) | collective-permute-done | bytes 196640 | tf_op jit(solution)/shard_map/ppermute | solution.py:88
  97.6 2.9 %hidden_units.1 = (f32[512,768]{1,0:T(8,128)S(1)}, f32[512,768]{1,0:T(8,128)S(1)}, bf16[512,768]{1,0:T(8,128)(2,1)S(1)}, bf16[1024,1536]{1,0:T(8,128)(2,1)S(1)}) custom-call(s32[21]{0:T(128)S(1)} %copy-done.20, bf16[512,1024]{1,0:T(8,128)(2,1)S(1)} %get-tuple-element.244.h2_ref, bf16[128,1536]{1,0:T(8,128)(2,1)S(1)} %constant_dynamic-update-slice_fusion.2.refs_0_, ...), custom_call_target="tpu_custom_call" | custom-call | flops 1610612736 | bytes 11272276 | tf_op jit(solution)/shard_map/hidden_units/pallas_call | solution.py:152
  100.6 2.4 %grad_down_parts.1 = (bf16[88,1024]{1,0:T(8,128)(2,1)S(1)}, bf16[88,1024]{1,0:T(8,128)(2,1)S(1)}, bf16[88,1024]{1,0:T(8,128)(2,1)S(1)}, bf16[88,1024]{1,0:T(8,12...) custom-call(s32[21]{0:T(128)S(1)} %copy-done.20, ...), custom_call_target="tpu_custom_call" | custom-call | flops 805306368 | bytes 3276884 | tf_op jit(solution)/shard_map/grad_down_parts/pallas_call | solution.py:152
  105.1 4.8 %hidden_back.1 = (bf16[512,1536]{1,0:T(8,128)(2,1)S(1)}, f32[2,128,1024]{2,1,0:T(8,128)S(1)}, bf16[2,128,1024]{2,1,0:T(8,128)(2,1)S(1)}, bf16[768,1024]{1,0:T(8,128)(2,1)S(1)}) custom-call(s32[21]{0:T(128)S(1)} %copy-done.20, bf16[512,1024]{1,0:T(8,128)(2,1)S(1)} %get-tuple-element.251.gm_ref.refs_0_, ...), custom_call_target="tpu_custom_call" | custom-call | flops 2415919104 | bytes 13500500 | tf_op jit(solution)/shard_map/hidden_back/pallas_call | solution.py:152
  112.4 4.0 %grad_in_parts.1 = (bf16[128,1536]{1,0:T(8,128)(2,1)S(1)}, bf16[128,1536]{1,0:T(8,128)(2,1)S(1)}, bf16[128,1536]{1,0:T(8,128)(2,1)S(1)}, bf16[128,1536]{1,0:T(8,...) custom-call(s32[21]{0:T(128)S(1)} %copy-done.20, ...), custom_call_target="tpu_custom_call" | custom-call | flops 1610612736 | bytes 5767252 | tf_op jit(solution)/shard_map/grad_in_parts/pallas_call | solution.py:152
  122.6 2.1 last_projection.1
  125.4 3.1 %collective-permute-done.41 = bf16[88,1024]{1,0:T(8,128)(2,1)S(1)} collective-permute-done((bf16[88,1024]{1,0:T(8,128)(2,1)S(1)}, bf16[88,1024]{1,0:T(8,128)(2,1)S(1)}, u32[]{:S(2)}, u32[]{:S(2)}) %collective-permute-start.41) | collective-permute-done | bytes 180256 | tf_op jit(solution)/shard_map/ppermute | solution.py:88
  131.3 2.8 %collective-permute-done.45.far_ref = bf16[2,128,1024]{2,1,0:T(8,128)(2,1)S(1)} collective-permute-done((bf16[2,128,1024]{2,1,0:T(8,128)(2,1)S(1)}, bf16[2,128,1024]{2,1,0:T(8,128)(2,1)S(1)}, u32[]{:S(2)}, u32[]{:S(2)}) %collective-permute-start.45) | collective-permute-done | bytes 524320 | tf_op jit(solution)/shard_map/ppermute | solution.py:50
  139.1 7.0 %attention_back.1 = (bf16[512,768]{1,0:T(8,128)(2,1)S(1)}, bf16[512,1024]{1,0:T(8,128)(2,1)S(1)}, f32[2,128,1024]{2,1,0:T(8,128)S(1)}, bf16[2,128,1024]{2,1,0:T(8,128)(2,1)S(1)}) custom-call(s32[21]{0:T(128)S(1)} %copy-done.20, bf16[2,128,1024]{2,1,0:T(8,128)(2,1)S(1)} %get-tuple-element.289.ga_own, ...), custom_call_target="tpu_custom_call" | custom-call | flops 1879048192 | bytes 8650836 | tf_op jit(solution)/shard_map/attention_back/pallas_call | solution.py:152
  146.2 4.8 %collective-permute-done.48 = bf16[88,1024]{1,0:T(8,128)(2,1)S(1)} collective-permute-done((bf16[88,1024]{1,0:T(8,128)(2,1)S(1)}, bf16[88,1024]{1,0:T(8,128)(2,1)S(1)}, u32[]{:S(2)}, u32[]{:S(2)}) %collective-permute-start.48) | collective-permute-done | bytes 180256 | tf_op jit(solution)/shard_map/ppermute | solution.py:88
  151.8 1.7 collective-permute-start.56
  153.6 2.1 grad_first_parts.1
  158.5 4.7 %collective-permute-done.55 = bf16[128,1536]{1,0:T(8,128)(2,1)S(1)} collective-permute-done((bf16[128,1536]{1,0:T(8,128)(2,1)S(1)}, bf16[128,1536]{1,0:T(8,128)(2,1)S(1)}, u32[]{:S(2)}, u32[]{:S(2)}) %collective-permute-start.55) | collective-permute-done | bytes 393248 | tf_op jit(solution)/shard_map/ppermute | solution.py:88
  169.9 4.8 %collective-permute-done.58 = bf16[128,1024]{1,0:T(8,128)(2,1)S(1)} collective-permute-done((bf16[128,1024]{1,0:T(8,128)(2,1)S(1)}, bf16[128,1024]{1,0:T(8,128)(2,1)S(1)}, u32[]{:S(2)}, u32[]{:S(2)}) %collective-permute-start.58) | collective-permute-done | bytes 262176 | tf_op jit(solution)/shard_map/ppermute | solution.py:88
  178.1 5.0 %collective-permute-done.64 = bf16[88,1024]{1,0:T(8,128)(2,1)S(1)} collective-permute-done((bf16[88,1024]{1,0:T(8,128)(2,1)S(1)}, bf16[88,1024]{1,0:T(8,128)(2,1)S(1)}, u32[]{:S(2)}, u32[]{:S(2)}) %collective-permute-start.64) | collective-permute-done | bytes 180256 | tf_op jit(solution)/shard_map/ppermute | solution.py:50
  183.8 3.4 %collective-permute-done.61 = bf16[128,1024]{1,0:T(8,128)(2,1)S(1)} collective-permute-done((bf16[128,1024]{1,0:T(8,128)(2,1)S(1)}, bf16[128,1024]{1,0:T(8,128)(2,1)S(1)}, u32[]{:S(2)}, u32[]{:S(2)}) %collective-permute-start.61) | collective-permute-done | bytes 262176 | tf_op jit(solution)/shard_map/ppermute | solution.py:88
  193.5 4.2 %collective-permute-done.66.right_ref = bf16[128,1024]{1,0:T(8,128)(2,1)} collective-permute-done((bf16[128,1024]{1,0:T(8,128)(2,1)}, bf16[128,1024]{1,0:T(8,128)(2,1)}, u32[]{:S(2)}, u32[]{:S(2)}) %collective-permute-start.66) | collective-permute-done | bytes 262176 | tf_op jit(solution)/shard_map/ppermute | solution.py:88
  197.7 2.8 %collective-permute-done.67.left_ref = bf16[128,1024]{1,0:T(8,128)(2,1)} collective-permute-done((bf16[128,1024]{1,0:T(8,128)(2,1)}, bf16[128,1024]{1,0:T(8,128)(2,1)}, u32[]{:S(2)}, u32[]{:S(2)}) %collective-permute-start.67) | collective-permute-done | bytes 262176 | tf_op jit(solution)/shard_map/ppermute | solution.py:88
  205.4 1.8 fusion.1
  207.2 1.8 finish_tokens.1
  209.0 2.4 %unpack_in.1 = f32[64,5632]{1,0:T(8,128)} custom-call(s32[21]{0:T(128)S(1)} %copy-done.21, bf16[64,1536]{1,0:T(8,128)(2,1)S(1)} %get-tuple-element.350.own_ref, bf16[64,1536]{1,0:T(8,128)(2,1)S(1)} %copy-done.8, bf16[64,1536]{1,0:T(8,128)(2,1)S(1)} %get-tuple-element.369.far_ref, bf16[64,1536]{1,0:T(8,128)(2,1)S(1)} %get-tuple-element.368.diagonal_ref), custom_call_target="tpu_custom_call" | custom-call | bytes 2228308 | tf_op jit(solution)/shard_map/unpack_in/pallas_call | solution.py:152
  (231 shorter events, 89.2 us)
Async XLA Ops:
  16.6 11.2 %collective-permute-start.6 = (bf16[130,1024]{1,0:T(8,128)(2,1)S(1)}, bf16[130,1024]{1,0:T(8,128)(2,1)S(1)}, u32[]{:S(2)}, u32[]{:S(2)}) collective-permute-start(bf16[130,1024]{1,0:T(8,128)(2,1)S(1)} %pack_tokens.1.refs_0_.block_ref), channel_id=1, source_target_pairs={{0,1},{1,0},{2,3},{3,2},{4,5},{5,4},{6,7},{7,6},{8,9},{9,8},{10,11... | collective-permute-start | bytes 798728 | tf_op jit(solution)/shard_map/ppermute | solution.py:54
  16.6 11.2 %collective-permute-start.5 = (bf16[130,1024]{1,0:T(8,128)(2,1)S(1)}, bf16[130,1024]{1,0:T(8,128)(2,1)S(1)}, u32[]{:S(2)}, u32[]{:S(2)}) collective-permute-start(bf16[130,1024]{1,0:T(8,128)(2,1)S(1)} %pack_tokens.1.refs_0_.block_ref), channel_id=1, source_target_pairs={{0,16},{16,0},{1,17},{17,1},{2,18},{18,2},{3,19},{19,3},{4,20},{20... | collective-permute-start | bytes 798728 | tf_op jit(solution)/shard_map/ppermute | solution.py:50
  27.8 10.6 %collective-permute-start.11 = (bf16[128,1024]{1,0:T(8,128)(2,1)S(1)}, bf16[128,1024]{1,0:T(8,128)(2,1)S(1)}, u32[]{:S(2)}, u32[]{:S(2)}) collective-permute-start(bf16[128,1024]{1,0:T(8,128)(2,1)S(1)} %bitcast.28), channel_id=1, source_target_pairs={{0,16},{16,0},{1,17},{17,1},{2,18},{18,2},{3,19},{19,3},{4,20},{20... | collective-permute-start | bytes 786440 | tf_op jit(solution)/shard_map/ppermute | solution.py:50
  28.4 10.0 %collective-permute-start.10 = (bf16[128,1024]{1,0:T(8,128)(2,1)S(1)}, bf16[128,1024]{1,0:T(8,128)(2,1)S(1)}, u32[]{:S(2)}, u32[]{:S(2)}) collective-permute-start(bf16[128,1024]{1,0:T(8,128)(2,1)S(1)} %bitcast.29), channel_id=1, source_target_pairs={{0,1},{1,0},{2,3},{3,2},{4,5},{5,4},{6,7},{7,6},{8,9},{9,8},{10,11... | collective-permute-start | bytes 786440 | tf_op jit(solution)/shard_map/ppermute | solution.py:54
  38.4 10.0 %collective-permute-start.16 = (bf16[88,1024]{1,0:T(8,128)(2,1)S(1)}, bf16[88,1024]{1,0:T(8,128)(2,1)S(1)}, u32[]{:S(2)}, u32[]{:S(2)}) collective-permute-start(bf16[88,1024]{1,0:T(8,128)(2,1)S(1)} %constant_dynamic-slice_fusion.refs_1_), channel_id=1, source_target_pairs={{0,4},{4,8},{8,12},{12,14},{14,10},{10,6},{6,2},{2,0},{1,5},{5,9},... | collective-permute-start | bytes 540680 | tf_op jit(solution)/shard_map/ppermute | solution.py:88
  49.0 14.9 %collective-permute-start.18 = (bf16[1024,256]{1,0:T(8,128)(2,1)S(1)}, bf16[1024,256]{1,0:T(8,128)(2,1)S(1)}, u32[]{:S(2)}, u32[]{:S(2)}) collective-permute-start(bf16[1024,256]{1,0:T(8,128)(2,1)S(1)} %gather_out.1.refs_10_), channel_id=1, source_target_pairs={{0,16},{16,0},{1,17},{17,1},{2,18},{18,2},{3,19},{19,3},{4,20},{20... | collective-permute-start | bytes 1572872 | tf_op jit(solution)/shard_map/ppermute | solution.py:50
  50.6 13.3 %collective-permute-start.19 = (bf16[128,1536]{1,0:T(8,128)(2,1)S(1)}, bf16[128,1536]{1,0:T(8,128)(2,1)S(1)}, u32[]{:S(2)}, u32[]{:S(2)}) collective-permute-start(bf16[128,1536]{1,0:T(8,128)(2,1)S(1)} %constant_dynamic-update-slice_fusion.2.refs_0_), channel_id=1, source_target_pairs={{0,4},{4,8},{8,12},{12,14},{14,10},{10,6},{6,2},{2,0},{1,5},{5,9},... | collective-permute-start | bytes 1179656 | tf_op jit(solution)/shard_map/ppermute | solution.py:88
  51.2 12.7 %collective-permute-start.20 = (bf16[128,1536]{1,0:T(8,128)(2,1)S(1)}, bf16[128,1536]{1,0:T(8,128)(2,1)S(1)}, u32[]{:S(2)}, u32[]{:S(2)}) collective-permute-start(bf16[128,1536]{1,0:T(8,128)(2,1)S(1)} %constant_dynamic-update-slice_fusion.2.refs_0_), channel_id=1, source_target_pairs={{4,0},{8,4},{12,8},{14,12},{10,14},{6,10},{2,6},{0,2},{5,1},{9,5},... | collective-permute-start | bytes 1179656 | tf_op jit(solution)/shard_map/ppermute | solution.py:88
  52.6 10.8 %collective-permute-start.21 = (bf16[88,1024]{1,0:T(8,128)(2,1)S(1)}, bf16[88,1024]{1,0:T(8,128)(2,1)S(1)}, u32[]{:S(2)}, u32[]{:S(2)}) collective-permute-start(bf16[88,1024]{1,0:T(8,128)(2,1)S(1)} %collective-permute-done.16.refs_7_), channel_id=1, source_target_pairs={{0,4},{4,8},{8,12},{12,14},{14,10},{10,6},{6,2},{2,0},{1,5},{5,9},... | collective-permute-start | bytes 540680 | tf_op jit(solution)/shard_map/ppermute | solution.py:88
  53.2 10.7 %collective-permute-start.22 = (bf16[88,1024]{1,0:T(8,128)(2,1)S(1)}, bf16[88,1024]{1,0:T(8,128)(2,1)S(1)}, u32[]{:S(2)}, u32[]{:S(2)}) collective-permute-start(bf16[88,1024]{1,0:T(8,128)(2,1)S(1)} %collective-permute-done.17.refs_2_), channel_id=1, source_target_pairs={{4,0},{8,4},{12,8},{14,12},{10,14},{6,10},{2,6},{0,2},{5,1},{9,5},... | collective-permute-start | bytes 540680 | tf_op jit(solution)/shard_map/ppermute | solution.py:88
  63.9 12.5 %collective-permute-start.24 = (bf16[128,1536]{1,0:T(8,128)(2,1)S(1)}, bf16[128,1536]{1,0:T(8,128)(2,1)S(1)}, u32[]{:S(2)}, u32[]{:S(2)}) collective-permute-start(bf16[128,1536]{1,0:T(8,128)(2,1)S(1)} %collective-permute-done.19.refs_6_), channel_id=1, source_target_pairs={{0,4},{4,8},{8,12},{12,14},{14,10},{10,6},{6,2},{2,0},{1,5},{5,9},... | collective-permute-start | bytes 1179656 | tf_op jit(solution)/shard_map/ppermute | solution.py:88
  64.7 11.8 %collective-permute-start.25 = (bf16[128,1536]{1,0:T(8,128)(2,1)S(1)}, bf16[128,1536]{1,0:T(8,128)(2,1)S(1)}, u32[]{:S(2)}, u32[]{:S(2)}) collective-permute-start(bf16[128,1536]{1,0:T(8,128)(2,1)S(1)} %collective-permute-done.20.refs_1_), channel_id=1, source_target_pairs={{4,0},{8,4},{12,8},{14,12},{10,14},{6,10},{2,6},{0,2},{5,1},{9,5},... | collective-permute-start | bytes 1179656 | tf_op jit(solution)/shard_map/ppermute | solution.py:88
  66.0 10.5 %collective-permute-start.23 = (bf16[4,128,256]{2,1,0:T(8,128)(2,1)S(1)}, bf16[4,128,256]{2,1,0:T(8,128)(2,1)S(1)}, u32[]{:S(2)}, u32[]{:S(2)}) collective-permute-start(bf16[4,128,256]{2,1,0:T(8,128)(2,1)S(1)} %get-tuple-element.230.refs_8_), channel_id=1, source_target_pairs={{0,16},{16,0},{1,17},{17,1},{2,18},{18,2},{3,19},{19,3},{4,20},{20... | collective-permute-start | bytes 786440 | tf_op jit(solution)/shard_map/ppermute | solution.py:50
  76.6 13.6 %collective-permute-start.29 = (bf16[128,1536]{1,0:T(8,128)(2,1)S(1)}, bf16[128,1536]{1,0:T(8,128)(2,1)S(1)}, u32[]{:S(2)}, u32[]{:S(2)}) collective-permute-start(bf16[128,1536]{1,0:T(8,128)(2,1)S(1)} %collective-permute-done.24.refs_5_), channel_id=1, source_target_pairs={{0,4},{4,8},{8,12},{12,14},{14,10},{10,6},{6,2},{2,0},{1,5},{5,9},... | collective-permute-start | bytes 1179656 | tf_op jit(solution)/shard_map/ppermute | solution.py:88
  77.3 13.0 %collective-permute-start.30 = (bf16[128,1536]{1,0:T(8,128)(2,1)S(1)}, bf16[128,1536]{1,0:T(8,128)(2,1)S(1)}, u32[]{:S(2)}, u32[]{:S(2)}) collective-permute-start(bf16[128,1536]{1,0:T(8,128)(2,1)S(1)} %collective-permute-done.25.refs_2_), channel_id=1, source_target_pairs={{4,0},{8,4},{12,8},{14,12},{10,14},{6,10},{2,6},{0,2},{5,1},{9,5},... | collective-permute-start | bytes 1179656 | tf_op jit(solution)/shard_map/ppermute | solution.py:88
  78.7 11.5 %collective-permute-start.32 = (bf16[40,1024]{1,0:T(8,128)(2,1)S(1)}, bf16[40,1024]{1,0:T(8,128)(2,1)S(1)}, u32[]{:S(2)}, u32[]{:S(2)}) collective-permute-start(bf16[40,1024]{1,0:T(8,128)(2,1)S(1)} %slice.67), channel_id=1, source_target_pairs={{4,0},{8,4},{12,8},{14,12},{10,14},{6,10},{2,6},{0,2},{5,1},{9,5},... | collective-permute-start | bytes 245768 | tf_op jit(solution)/shard_map/ppermute | solution.py:88
  80.4 9.9 %collective-permute-start.31 = (bf16[48,1024]{1,0:T(8,128)(2,1)S(1)}, bf16[48,1024]{1,0:T(8,128)(2,1)S(1)}, u32[]{:S(2)}, u32[]{:S(2)}) collective-permute-start(bf16[48,1024]{1,0:T(8,128)(2,1)S(1)} %slice.66), channel_id=1, source_target_pairs={{0,4},{4,8},{8,12},{12,14},{14,10},{10,6},{6,2},{2,0},{1,5},{5,9},... | collective-permute-start | bytes 294920 | tf_op jit(solution)/shard_map/ppermute | solution.py:88
  118.5 10.0 %collective-permute-start.42 = (bf16[64,1536]{1,0:T(8,128)(2,1)S(1)}, bf16[64,1536]{1,0:T(8,128)(2,1)S(1)}, u32[]{:S(2)}, u32[]{:S(2)}) collective-permute-start(bf16[64,1536]{1,0:T(8,128)(2,1)S(1)} %get-tuple-element.284), channel_id=1, source_target_pairs={{0,4},{4,8},{8,12},{12,14},{14,10},{10,6},{6,2},{2,0},{1,5},{5,9},... | collective-permute-start | bytes 589832 | tf_op jit(solution)/shard_map/ppermute | solution.py:88
  122.0 12.1 %collective-permute-start.45 = (bf16[2,128,1024]{2,1,0:T(8,128)(2,1)S(1)}, bf16[2,128,1024]{2,1,0:T(8,128)(2,1)S(1)}, u32[]{:S(2)}, u32[]{:S(2)}) collective-permute-start(bf16[2,128,1024]{2,1,0:T(8,128)(2,1)S(1)} %add_convert_fusion), channel_id=1, source_target_pairs={{0,16},{16,0},{1,17},{17,1},{2,18},{18,2},{3,19},{19,3},{4,20},{20... | collective-permute-start | bytes 1572872 | tf_op jit(solution)/shard_map/ppermute | solution.py:50
  128.5 17.6 %collective-permute-start.47 = (bf16[88,1024]{1,0:T(8,128)(2,1)S(1)}, bf16[88,1024]{1,0:T(8,128)(2,1)S(1)}, u32[]{:S(2)}, u32[]{:S(2)}) collective-permute-start(bf16[88,1024]{1,0:T(8,128)(2,1)S(1)} %add_convert_fusion.17), channel_id=1, source_target_pairs={{0,4},{4,8},{8,12},{12,14},{14,10},{10,6},{6,2},{2,0},{1,5},{5,9},... | collective-permute-start | bytes 540680 | tf_op jit(solution)/shard_map/ppermute | solution.py:88
  129.8 21.2 %collective-permute-start.49 = (bf16[128,1536]{1,0:T(8,128)(2,1)S(1)}, bf16[128,1536]{1,0:T(8,128)(2,1)S(1)}, u32[]{:S(2)}, u32[]{:S(2)}) collective-permute-start(bf16[128,1536]{1,0:T(8,128)(2,1)S(1)} %add_convert_fusion.6), channel_id=1, source_target_pairs={{0,4},{4,8},{8,12},{12,14},{14,10},{10,6},{6,2},{2,0},{1,5},{5,9},... | collective-permute-start | bytes 1179656 | tf_op jit(solution)/shard_map/ppermute | solution.py:88
  135.6 15.4 %collective-permute-start.50 = (bf16[128,1536]{1,0:T(8,128)(2,1)S(1)}, bf16[128,1536]{1,0:T(8,128)(2,1)S(1)}, u32[]{:S(2)}, u32[]{:S(2)}) collective-permute-start(bf16[128,1536]{1,0:T(8,128)(2,1)S(1)} %add_convert_fusion.5), channel_id=1, source_target_pairs={{4,0},{8,4},{12,8},{14,12},{10,14},{6,10},{2,6},{0,2},{5,1},{9,5},... | collective-permute-start | bytes 1179656 | tf_op jit(solution)/shard_map/ppermute | solution.py:88
  137.4 13.6 %collective-permute-start.51 = (bf16[128,1024]{1,0:T(8,128)(2,1)S(1)}, bf16[128,1024]{1,0:T(8,128)(2,1)}, u32[]{:S(2)}, u32[]{:S(2)}) collective-permute-start(bf16[128,1024]{1,0:T(8,128)(2,1)S(1)} %fusion.3), channel_id=1, source_target_pairs={{0,16},{16,0},{1,17},{17,1},{2,18},{18,2},{3,19},{19,3},{4,20},{20... | collective-permute-start | bytes 786440 | tf_op jit(solution)/shard_map/ppermute | solution.py:50
  138.0 13.0 %collective-permute-start.48 = (bf16[88,1024]{1,0:T(8,128)(2,1)S(1)}, bf16[88,1024]{1,0:T(8,128)(2,1)S(1)}, u32[]{:S(2)}, u32[]{:S(2)}) collective-permute-start(bf16[88,1024]{1,0:T(8,128)(2,1)S(1)} %add_convert_fusion.16), channel_id=1, source_target_pairs={{4,0},{8,4},{12,8},{14,12},{10,14},{6,10},{2,6},{0,2},{5,1},{9,5},... | collective-permute-start | bytes 540680 | tf_op jit(solution)/shard_map/ppermute | solution.py:88
  151.1 12.1 %collective-permute-start.55 = (bf16[128,1536]{1,0:T(8,128)(2,1)S(1)}, bf16[128,1536]{1,0:T(8,128)(2,1)S(1)}, u32[]{:S(2)}, u32[]{:S(2)}) collective-permute-start(bf16[128,1536]{1,0:T(8,128)(2,1)S(1)} %add_convert_fusion.4), channel_id=1, source_target_pairs={{0,4},{4,8},{8,12},{12,14},{14,10},{10,6},{6,2},{2,0},{1,5},{5,9},... | collective-permute-start | bytes 1179656 | tf_op jit(solution)/shard_map/ppermute | solution.py:88
  151.8 12.1 %collective-permute-start.56 = (bf16[128,1536]{1,0:T(8,128)(2,1)S(1)}, bf16[128,1536]{1,0:T(8,128)(2,1)S(1)}, u32[]{:S(2)}, u32[]{:S(2)}) collective-permute-start(bf16[128,1536]{1,0:T(8,128)(2,1)S(1)} %add_convert_fusion.3), channel_id=1, source_target_pairs={{4,0},{8,4},{12,8},{14,12},{10,14},{6,10},{2,6},{0,2},{5,1},{9,5},... | collective-permute-start | bytes 1179656 | tf_op jit(solution)/shard_map/ppermute | solution.py:88
  167.7 15.5 %collective-permute-start.62 = (bf16[128,1536]{1,0:T(8,128)(2,1)S(1)}, bf16[128,1536]{1,0:T(8,128)(2,1)S(1)}, u32[]{:S(2)}, u32[]{:S(2)}) collective-permute-start(bf16[128,1536]{1,0:T(8,128)(2,1)S(1)} %add_convert_fusion.2), channel_id=1, source_target_pairs={{0,4},{4,8},{8,12},{12,14},{14,10},{10,6},{6,2},{2,0},{1,5},{5,9},... | collective-permute-start | bytes 1179656 | tf_op jit(solution)/shard_map/ppermute | solution.py:88
  168.4 15.4 %collective-permute-start.63 = (bf16[128,1536]{1,0:T(8,128)(2,1)S(1)}, bf16[128,1536]{1,0:T(8,128)(2,1)S(1)}, u32[]{:S(2)}, u32[]{:S(2)}) collective-permute-start(bf16[128,1536]{1,0:T(8,128)(2,1)S(1)} %add_convert_fusion.1), channel_id=1, source_target_pairs={{4,0},{8,4},{12,8},{14,12},{10,14},{6,10},{2,6},{0,2},{5,1},{9,5},... | collective-permute-start | bytes 1179656 | tf_op jit(solution)/shard_map/ppermute | solution.py:88
  175.4 11.7 %collective-permute-start.61 = (bf16[128,1024]{1,0:T(8,128)(2,1)S(1)}, bf16[128,1024]{1,0:T(8,128)(2,1)S(1)}, u32[]{:S(2)}, u32[]{:S(2)}) collective-permute-start(bf16[128,1024]{1,0:T(8,128)(2,1)S(1)} %add_convert_fusion.9), channel_id=1, source_target_pairs={{4,0},{8,4},{12,8},{14,12},{10,14},{6,10},{2,6},{0,2},{5,1},{9,5},... | collective-permute-start | bytes 786440 | tf_op jit(solution)/shard_map/ppermute | solution.py:88
  177.0 10.1 %collective-permute-start.60 = (bf16[128,1024]{1,0:T(8,128)(2,1)S(1)}, bf16[128,1024]{1,0:T(8,128)(2,1)S(1)}, u32[]{:S(2)}, u32[]{:S(2)}) collective-permute-start(bf16[128,1024]{1,0:T(8,128)(2,1)S(1)} %add_convert_fusion.10), channel_id=1, source_target_pairs={{0,4},{4,8},{8,12},{12,14},{14,10},{10,6},{6,2},{2,0},{1,5},{5,9},... | collective-permute-start | bytes 786440 | tf_op jit(solution)/shard_map/ppermute | solution.py:88
  190.8 11.5 %collective-permute-start.68 = (bf16[2,64,1536]{2,1,0:T(8,128)(2,1)}, bf16[2,64,1536]{2,1,0:T(8,128)(2,1)}, u32[]{:S(2)}, u32[]{:S(2)}) collective-permute-start(bf16[2,64,1536]{2,1,0:T(8,128)(2,1)} %pad_maximum_fusion.1), channel_id=1, source_target_pairs={{0,16},{16,0},{1,17},{17,1},{2,18},{18,2},{3,19},{19,3},{4,20},{20... | collective-permute-start | bytes 1179656 | tf_op jit(solution)/shard_map/ppermute | solution.py:50
  202.3 10.2 %collective-permute-start.70 = (bf16[64,1024]{1,0:T(8,128)(2,1)S(1)}, bf16[64,1024]{1,0:T(8,128)(2,1)S(1)}, u32[]{:S(2)}, u32[]{:S(2)}) collective-permute-start(bf16[64,1024]{1,0:T(8,128)(2,1)S(1)} %get-tuple-element.355.own_ref), channel_id=1, source_target_pairs={{0,16},{16,0},{1,17},{17,1},{2,18},{18,2},{3,19},{19,3},{4,20},{20... | collective-permute-start | bytes 393224 | tf_op jit(solution)/shard_map/ppermute | solution.py:50
  (68 other events, 573.1 us)

commit v3 on v2

--- a/solution.py
+++ b/solution.py
@@ -113,6 +113,17 @@
         return [self.got[k] for k in range(self.ring.size) if k != self.ring.half] + list(self.far)
 
 
+def ring_add(cut, right_term, left_term, right_got, left_got, right_ref, left_ref):
+    if cut is None:
+        right_ref[...] = (right_term[...].astype(F32) + right_got[...].astype(F32)).astype(BF)
+        left_ref[...] = (left_term[...].astype(F32) + left_got[...].astype(F32)).astype(BF)
+    else:
+        right_ref[:cut] = (right_term[:cut].astype(F32) + right_got[...].astype(F32)).astype(BF)
+        right_ref[cut:] = right_term[cut:]
+        left_ref[:cut] = left_term[:cut]
+        left_ref[cut:] = (left_term[cut:].astype(F32) + left_got[...].astype(F32)).astype(BF)
+
+
 class Scatter:
     def __init__(self, ring, parts):
         self.ring = ring
@@ -129,12 +140,9 @@
         ring = self.ring
         self.step += 1
         place = ring.half - self.step
-        right, left = self.got
-        if self.step == 1:
-            right = jnp.pad(right, ((0, self.parts[0].shape[0] - self.cut), (0, 0)))
-            left = jnp.pad(left, ((self.cut, 0), (0, 0)))
         terms = (self.parts[place], self.parts[ring.size - place])
-        self.state = tuple((t.astype(F32) + v.astype(F32)).astype(BF) for t, v in zip(terms, (right, left), strict=True))
+        body = functools.partial(ring_add, self.cut if self.step == 1 else None)
+        self.state = tuple(call(body, [shape(t.shape, BF) for t in terms], [], 0, *terms, *self.got, smem=0))
 
     def run(self):
         while self.step < self.ring.half - 1:
@@ -147,16 +155,16 @@
     return lax.optimization_barrier(values)
 
 
-def call(body, outs, scratch, flops, *args):
+def call(body, outs, scratch, flops, *args, smem=1):
     nbytes = sum(a.size * a.dtype.itemsize for a in args) + sum(o.size * o.dtype.itemsize for o in outs)
     return pl.pallas_call(
         body,
         name=body.func.__name__,
         out_shape=outs,
-        in_specs=[pl.BlockSpec(memory_space=pltpu.SMEM)] + [pl.BlockSpec(memory_space=pltpu.VMEM)] * (len(args) - 1),
+        in_specs=[pl.BlockSpec(memory_space=pltpu.SMEM)] * smem + [pl.BlockSpec(memory_space=pltpu.VMEM)] * (len(args) - smem),
         out_specs=[pl.BlockSpec(memory_space=pltpu.VMEM)] * len(outs),
         scratch_shapes=scratch,
-        compiler_params=pltpu.CompilerParams(vmem_limit_bytes=32 * MIB),
+        compiler_params=pltpu.CompilerParams(vmem_limit_bytes=12 * MIB),
         cost_estimate=pl.CostEstimate(flops=flops, bytes_accessed=nbytes, transcendentals=0),
     )(*args)
 
@@ -172,7 +180,7 @@
 def pack_tokens(rows, prefix_ref, tokens_ref, own_ref):
     own_ref[:rows, :] = tokens_ref[...]
     for m in range(own_ref.shape[0] - rows):
-        own_ref[rows + m : rows + m + 1, :] = jnp.full((1, own_ref.shape[1]), prefix_ref[m, 0].astype(F32)).astype(BF)
+        own_ref[rows + m : rows + m + 1, :] = jnp.broadcast_to(prefix_ref[m : m + 1, :].astype(F32), (1, own_ref.shape[1])).astype(BF)
 
 
 def pack_first(size, width, scal, qkv_ref, out_ref, own_ref, sib_ref):
@@ -183,7 +191,14 @@
         ref[:, 3 * quarter :] = out_ref[:, lanes(member * quarter, quarter)]
 
 
-def pack_in(size, units, piece, padded, scal, in_ref, own_ref, sib_ref):
+def pack_in(size, units, piece, padded, scal, in_ref, down_ref, own_ref, sib_ref, rows_ref):
+    rep = scal[2 * size + 1] - 2 * scal[2 * size]
+    for r in range(2):
+
+        @pl.when(rep == r)
+        def _(r=r):
+            rows_ref[...] = down_ref[r * piece : (r + 1) * piece, :]
+
     for ref, member in ((own_ref, scal[2 * size + 1]), (sib_ref, scal[2 * size + 2])):
         ref[...] = jnp.zeros_like(ref)
         for q in range(4):
@@ -281,8 +296,8 @@
 
 
 def middle(size, rows, width, scal, *refs):
-    blocks, cots = refs[:4], refs[4:8]
-    o_own, o_far, w_own, w_far, near_ref = refs[8:13]
+    blocks = refs[:4]
+    o_own, o_far, w_own, w_far, near_ref = refs[4:9]
     full = 4 * rows
     outputs = (
         lambda b: o_own[b],
@@ -291,12 +306,11 @@
         lambda b: near_ref[full + b * rows : full + (b + 1) * rows],
     )
     weights = (w_own, near_ref.at[2 * full : 2 * full + width], w_far, near_ref.at[2 * full + width :])
-    x2_ref, h2_ref, o_ref, rows_ref, gm_ref, w_full = refs[13:]
+    x2_ref, h2_ref, o_ref, rows_ref, w_full = refs[9:]
     quarter = width // 4
     members = [scal[2 * size + 1 + m] for m in range(4)]
     for m in range(4):
         w_full[:, lanes(members[m] * quarter, quarter)] = weights[m][...]
-        gm_ref[m * rows : (m + 1) * rows, :] = cots[m][...]
         for b in range(4):
             o_ref[b * rows : (b + 1) * rows, lanes(members[m] * quarter, quarter)] = outputs[m](BLOCKS[m][b])
     rows_ref[...] = w_full[pl.ds(pl.multiple_of(members[0] * quarter, quarter), quarter), :]
@@ -383,8 +397,10 @@
         ref[...] = total[pl.ds(pl.multiple_of(scal[k] * stride, PACK), ref.shape[0]), :].astype(BF)
 
 
-def grad_down_parts(size, padded, scal, hid_ref, gm_ref, *refs):
-    total = refs[-1]
+def grad_down_parts(size, rows, padded, scal, hid_ref, *refs):
+    gm_ref, total = refs[-2:]
+    for b in range(4):
+        gm_ref[b * rows : (b + 1) * rows, :] = refs[b][...]
     tile = 256
 
     @pl.loop(0, gm_ref.shape[1] // tile)
@@ -392,7 +408,7 @@
         columns = pl.ds(pl.multiple_of(i * tile, tile), tile)
         total[:, columns] = dot_lt(hid_ref[...], gm_ref[:, columns])
 
-    write_parts(size, padded, scal, total, refs[:-1])
+    write_parts(size, padded, scal, total, refs[4:-2])
 
 
 def grad_in_parts(size, double, scal, h2_ref, ggu_ref, *refs):
@@ -407,9 +423,9 @@
     write_parts(size, double, scal, total, refs[:-1])
 
 
-def middle_back(rows, scal, keep_ref, got_ref, far_ref, x2_ref, cot_own, cot_far, gx2_ref, ga_ref):
+def middle_back(rows, scal, keep_ref, got_ref, far_first, far_second, x2_ref, cot_own, cot_far, gx2_ref, ga_ref):
     for i, cot in ((0, cot_own), (1, cot_far)):
-        upstream = keep_ref[i] + got_ref[i].astype(F32) + far_ref[1 - i].astype(F32)
+        upstream = keep_ref[i] + got_ref[i].astype(F32) + (far_second, far_first)[i][...].astype(F32)
         normed, inverse = norm_rows(x2_ref[2 * i * rows : (2 * i + 1) * rows, :])
         total = cot[...].astype(F32) + norm_back(normed, inverse, upstream)
         if i == 0:
@@ -471,6 +487,16 @@
     out_ref[...] = gx2_ref[...] + norm_back(normed, inverse, upstream)
 
 
+def unpack_down(size, piece, scal, low_ref, other_ref, out_ref):
+    rep = scal[2 * size + 1] - 2 * scal[2 * size]
+    for r in range(2):
+
+        @pl.when(rep == r)
+        def _(r=r):
+            out_ref[r * piece : (r + 1) * piece, :] = low_ref[...].astype(F32)
+            out_ref[(1 - r) * piece : (2 - r) * piece, :] = other_ref[...].astype(F32)
+
+
 def unpack_first(size, width, scal, own_ref, near_ref, far_ref, diagonal_ref, qkv_ref, out_ref):
     quarter = width // 4
     for m, ref in enumerate((own_ref, near_ref, far_ref, diagonal_ref)):
@@ -535,34 +561,41 @@
 
     a.state, in_weight = sync(a.state, in_weight)
     a.advance()
-    b_own, b_sib = call(
-        functools.partial(pack_in, size, units, piece, padded), [shape((shard_rows, 2 * member_units), BF)] * 2, [], 0, scal, in_weight
+    b_own, b_sib, down_rows = call(
+        functools.partial(pack_in, size, units, piece, padded),
+        [shape((shard_rows, 2 * member_units), BF)] * 2 + [shape((piece, width), BF)],
+        [],
+        0,
+        scal,
+        in_weight,
+        down_weight,
     )
     b_own, b_sib, tokens = sync(b_own, b_sib, tokens)
-    (own,) = call(functools.partial(pack_tokens, rows), [shape((rows + micro, width), BF)], [], 0, prefix, tokens)
+    (own,) = call(functools.partial(pack_tokens, rows), [shape((rows + micro, width), BF)], [], 0, prefix, tokens, smem=0)
 
     a.state, own, b_own, b_sib = sync(a.state, own, b_own, b_sib)
     a.advance()
     far = across(own)
     near = sibling(own)
     b_got = sibling(b_sib)
-
-    a.state, cot_own, far, near, b_own, b_got, down_weight = sync(a.state, cot_own, far, near, b_own, b_got, down_weight)
+    b = Gather(ring, jnp.concatenate([b_own, b_got], axis=0))
+
+    a.state, cot_own, far, near, b.state = sync(a.state, cot_own, far, near, b.state)
     a.advance()
+    b.advance()
     cot_far = across(cot_own)
+
+    while a.step < ring.half - 1:
+        (a.state,) = sync(a.state)
+        a.advance()
+    a.state, far, cot_own, cot_far, down_rows = sync(a.state, far, cot_own, cot_far, down_rows)
+    a_chunks = a.finish()
     diagonal = sibling(far)
     cot_near = sibling(cot_own)
-    b = Gather(ring, jnp.concatenate([b_own, b_got], axis=0))
-    c = Gather(ring, lax.dynamic_slice(down_weight, (rep * piece, 0), (piece, width)))
-
-    a.state, b.state, c.state, cot_near, cot_far, diagonal = sync(a.state, b.state, c.state, cot_near, cot_far, diagonal)
-    c.advance()
-    a_chunks = a.finish()
-    cot_diagonal = sibling(cot_far)
+    c = Gather(ring, down_rows)
+
+    a_chunks, b.state, c.state, diagonal, cot_near = sync(a_chunks, b.state, c.state, diagonal, cot_near)
     blocks = [own, near, far, diagonal]
-    cots = [cot_own, cot_near, cot_far, cot_diagonal]
-
-    a_chunks, b.state, c.state = sync(a_chunks, b.state, c.state)
     b.advance()
     c.advance()
     (out_mine,) = call(functools.partial(gather_out, size, shard_rows, quarter), [shape((width, quarter), BF)], [], 0, scal, *a_chunks)
@@ -585,30 +618,28 @@
         sine,
     )
 
-    o_own, out_mine, out_far, b.state, c.state = sync(o_own, out_mine, out_far, b.state, c.state)
+    o_own, out_mine, b.state, c.state = sync(o_own, out_mine, b.state, c.state)
     o_far = across(o_own)
     b.advance()
     c.advance()
 
-    o_far, b.state, c.state = sync(o_far, b.state, c.state)
+    o_far, out_far, b.state, c.state = sync(o_far, out_far, b.state, c.state)
     kept = [o_own.reshape(full_rows, quarter), o_far.reshape(full_rows, quarter), out_mine, out_far]
     near_all = sibling(jnp.concatenate(kept, axis=0))
-    b.advance()
-    c_chunks = c.finish()
-    x2, h2, o_all, out_rows, gm = call(
+    b_chunks = b.finish()
+    c.advance()
+    x2, h2, o_all, out_rows = call(
         functools.partial(middle, size, rows, width),
         [
             shape((full_rows, width), F32),
             shape((full_rows, width), BF),
             shape((full_rows, width), BF),
             shape((quarter, width), BF),
-            shape((full_rows, width), BF),
         ],
         [pltpu.VMEM((width, width), BF)],
         4 * project,
         scal,
         *blocks,
-        *cots,
         o_own,
         o_far,
         out_mine,
@@ -616,8 +647,8 @@
         near_all,
     )
 
-    h2, b.state, c_chunks = sync(h2, b.state, c_chunks)
-    b_chunks = b.finish()
+    h2, b_chunks, cot_far = sync(h2, b_chunks, cot_far)
+    cot_diagonal = sibling(cot_far)
     up, gate, hid, in_mine = call(
         functools.partial(hidden_units, size, shard_rows, member_units, chunks),
         [
@@ -632,12 +663,23 @@
         h2,
         *b_chunks,
     )
-    down_parts = call(
-        functools.partial(grad_down_parts, size, padded), [shape((piece, width), BF)] * size, [pltpu.VMEM((member_units, width), F32)], 3 * project, scal, hid, gm
+    hid, c.state, cot_diagonal = sync(hid, c.state, cot_diagonal)
+    c_chunks = c.finish()
+    *down_parts, gm = call(
+        functools.partial(grad_down_parts, size, rows, padded),
+        [shape((piece, width), BF)] * size + [shape((full_rows, width), BF)],
+        [pltpu.VMEM((member_units, width), F32)],
+        3 * project,
+        scal,
+        hid,
+        cot_own,
+        cot_near,
+        cot_far,
+        cot_diagonal,
     )
 
     c = Scatter(ring, down_parts)
-    c.state, gm, up = sync(c.state, gm, up)
+    c.state, gm, up, c_chunks = sync(c.state, gm, up, c_chunks)
     c.send()
     ggu, u2_keep, u2_give, down_mine = call(
         functools.partial(hidden_back, size, rows, padded, piece, chunks),
@@ -659,7 +701,7 @@
     u2_low = (u2_keep + u2_got.astype(F32)).astype(BF)
 
     u2_low, ggu = sync(u2_low, ggu)
-    u2_far = across(u2_low)
+    u2_first = across(u2_low[0])
     in_parts = call(
         functools.partial(grad_in_parts, size, double),
         [shape((double, 2 * member_units), BF)] * size,
@@ -671,26 +713,33 @@
     )
 
     b = Scatter(ring, in_parts)
-    b.state, c.got, hid = sync(b.state, c.got, hid)
+    b.state, c.got, u2_first, u2_low, hid = sync(b.state, c.got, u2_first, u2_low, hid)
     b.send()
     c.add()
     c.send()
+    u2_second = across(u2_low[1])
     y_keep, y_give = call(functools.partial(last_projection, rows), [pair_full, pair_low], [], 3 * project, scal, hid, down_mine)
 
-    y_give, c.got, b.got = sync(y_give, c.got, b.got)
+    y_give, c.got, b.got, u2_second = sync(y_give, c.got, b.got, u2_second)
     b.add()
     b.send()
     c.add()
     c.send()
     gx2, ga = call(
-        functools.partial(middle_back, rows), [shape((rows, width), F32), pair_low], [], 0, scal, u2_keep, u2_got, u2_far, x2, cots[0], cots[2]
+        functools.partial(middle_back, rows),
+        [shape((rows, width), F32), pair_low],
+        [],
+        0,
+        scal,
+        u2_keep,
+        u2_got,
+        u2_first,
+        u2_second,
+        x2,
+        cot_own,
+        cot_far,
     )
     ga_near = sibling(ga)
-    y_got = sibling(y_give)
-    y_low = (y_keep[1] + y_got[1].astype(F32)).astype(BF)
-
-    y_low, ga_near = sync(y_low, ga_near)
-    y_far = across(y_low)
     gqkv, ga_all, u1_keep, u1_give = call(
         functools.partial(attention_back, rows, width),
         [shape((full_rows, 3 * quarter), BF), shape((full_rows, width), BF), pair_full, pair_low],
@@ -707,7 +756,7 @@
         sine,
     )
 
-    gqkv, u1_give, c.got, b.got, y_far = sync(gqkv, u1_give, c.got, b.got, y_far)
+    gqkv, u1_give, b.got, c.got = sync(gqkv, u1_give, b.got, c.got)
     b.add()
     b.send()
     u1_got = sibling(u1_give)
@@ -730,33 +779,34 @@
     u1_low = (u1_keep[1] + u1_got[1].astype(F32)).astype(BF)
     u1_far = across(u1_low)
 
-    a.got, b.got, u1_far = sync(a.got, b.got, u1_far)
+    a.got, b.got, u1_far, y_give = sync(a.got, b.got, u1_far, y_give)
     a.add()
     a.send()
     b.add()
     b.send()
     down_other = across(down_low)
+    y_got = sibling(y_give)
 
     while a.step < ring.half - 2:
-        (a.got,) = sync(a.got)
+        a.got, down_other = sync(a.got, down_other)
         a.add()
         a.send()
+    y_low = (y_keep[1] + y_got[1].astype(F32)).astype(BF)
+    y_far = across(y_low)
 
     def halves(summed):
         columns = summed[0].shape[1]
         return call(functools.partial(split_rows, size), [shape((shard_rows, columns), BF)] * 2, [], 0, scal, *summed)
 
-    b_sum = b.run()
-    a.got, b_sum, down_other = sync(a.got, b_sum, down_other)
+    in_keep, in_give = halves(b.run())
+    a.got, in_keep, in_give = sync(a.got, in_keep, in_give)
     a.add()
     a.send()
-    in_keep, in_give = halves(b_sum)
+    in_far = across(in_keep)
     in_near = sibling(in_give)
-    in_pair = jnp.stack([in_keep, in_near])
-    in_other = across(in_pair)
-    a_sum = a.run()
-    first_keep, first_give = halves(a_sum)
-    first_keep, first_give, in_other = sync(first_keep, first_give, in_other)
+    in_diagonal = across(in_near)
+    first_keep, first_give = halves(a.run())
+    first_keep, first_give, in_far = sync(first_keep, first_give, in_far)
     first_far = across(first_keep)
     first_near = sibling(first_give)
     first_diagonal = across(first_near)
@@ -765,7 +815,7 @@
         functools.partial(finish_tokens, rows), [shape((rows, width), F32)], [], 0, scal, u1_keep, u1_got, u1_far, own, gx2
     )
     result = (x2[:rows] + (y_keep[0] + y_got[0].astype(F32) + y_far.astype(F32))).astype(BF)
-    grad_down = jnp.where(rep == 0, jnp.concatenate([down_low, down_other]), jnp.concatenate([down_other, down_low])).astype(F32)
+    (grad_down,) = call(functools.partial(unpack_down, size, piece), [shape((2 * piece, width), F32)], [], 0, scal, down_low, down_other)
     (grad_in,) = call(
         functools.partial(unpack_in, size, units, piece, padded),
         [shape((shard_rows, 2 * units), F32)],
@@ -774,8 +824,8 @@
         scal,
         in_keep,
         in_near,
-        in_other[0],
-        in_other[1],
+        in_far,
+        in_diagonal,
     )
     grad_qkv, grad_out = call(
         functools.partial(unpack_first, size, width),

time: 214 us -> 205 us (0.958)
  waiting for transfers between devices: 92.4 us -> 84.9 us
  other arithmetic: 6.37 us -> 1.28 us
  starting transfers between devices: 61.1 us -> 64 us
    ppermute x24, waiting for transfers between devices: 39.5 us -> 19.3 us  [exchange(): lax.ppermute(pair[1], 'ring', self.left)]
    ppermute x24, waiting for transfers between devices: 40.6 us -> 55.7 us  [exchange(): lax.ppermute(pair[0], 'ring', self.right)]
    ppermute x24, starting transfers between devices: 28.2 us -> 22.6 us  [exchange(): lax.ppermute(pair[1], 'ring', self.left)]
    ppermute x24, starting transfers between devices: 23.1 us -> 27.9 us  [exchange(): lax.ppermute(pair[0], 'ring', self.right)]
    convert_element_type x19 -> x0, other arithmetic: 3.36 us -> none  [the longest x18 2.42 us: add(): (t.astype(F32) + v.astype(F32)).astype(BF)]
    ppermute x11 -> x13, starting transfers between devices: 8.99 us -> 12.2 us  [across(): return lax.ppermute(value, 'rep', SWAP)]
    unnamed x59 -> x19, local copies, waits for them, and re-layouts: 3.45 us -> 4.61 us
    ppermute x11 -> x13, waiting for transfers between devices: 8.3 us -> 7.62 us  [across(): return lax.ppermute(value, 'rep', SWAP)]
  transfers between devices with their start and end apart: 72 -> 74, of which waited for: 38 -> 38; matrix products, arithmetic and copies ran while one was open for 4% -> 1% of each run, Pallas kernels for 18% -> 22%
where the time goes in v3:
time: 205 us
  waiting for transfers between devices  84.9 us (41%)
  starting transfers between devices  64 us (31%)
  Pallas kernels  48 us (23%)
  local copies, waits for them, and re-layouts  5.56 us (3%)
    ppermute x24, waiting for transfers between devices, exchange(): lax.ppermute(pair[0], 'ring', self.right)  55.7 us
    pallas_call x29, Pallas kernels, call(): pl.pallas_call(body, name=body.func.__name__, out_shape=outs, in_specs=[p...  48 us
    ppermute x24, starting transfers between devices, exchange(): lax.ppermute(pair[0], 'ring', self.right)  27.9 us
    ppermute x24, starting transfers between devices, exchange(): lax.ppermute(pair[1], 'ring', self.left)  22.6 us
    ppermute x24, waiting for transfers between devices, exchange(): lax.ppermute(pair[1], 'ring', self.left)  19.3 us
    ppermute x13, starting transfers between devices, across(): return lax.ppermute(value, 'rep', SWAP)  12.2 us
    ppermute x13, waiting for transfers between devices, across(): return lax.ppermute(value, 'rep', SWAP)  7.62 us
    unnamed x19, local copies, waits for them, and re-layouts  4.61 us
  transfers between devices with their start and end apart: 74, of which 38 were waited for; matrix products, arithmetic and copies ran while one was open for 1% of the time, Pallas kernels for 22%

profile of v3, /device:TPU:0, one launch (start us, length us, event | category | flops | bytes accessed | tf_op | source)
XLA Modules:
  0.0 204.9 jit_solution(7736816275067671898)
XLA Ops:
  5.4 3.0 %collective-permute-start.1 = (bf16[128,1024]{1,0:T(8,128)(2,1)S(1)}, bf16[128,1024]{1,0:T(8,128)(2,1)S(1)}, u32[]{:S(2)}, u32[]{:S(2)}) collective-permute-start(bf16[128,1024]{1,0:T(8,128)(2,1)S(1)} %constant_dynamic-update-slice_fusion.refs_4_.refs_0_), channel_id=1, source_target_pairs={{0,4},{4,8},{8,12},{12,14},{14,10},{10,6},{6,2},{2,0},{1,5},{5,9},... | collective-permute-start | bytes 786440 | tf_op jit(solution)/shard_map/ppermute | solution.py:88
  12.0 2.9 %collective-permute-done.1.refs_10_.refs_6_ = bf16[128,1024]{1,0:T(8,128)(2,1)S(1)} collective-permute-done((bf16[128,1024]{1,0:T(8,128)(2,1)S(1)}, bf16[128,1024]{1,0:T(8,128)(2,1)S(1)}, u32[]{:S(2)}, u32[]{:S(2)}) %collective-permute-start.1) | collective-permute-done | bytes 262176 | tf_op jit(solution)/shard_map/ppermute | solution.py:88
  18.2 1.6 collective-permute-start.3
  20.3 6.4 %collective-permute-done.3.refs_9_.refs_5_ = bf16[128,1024]{1,0:T(8,128)(2,1)S(1)} collective-permute-done((bf16[128,1024]{1,0:T(8,128)(2,1)S(1)}, bf16[128,1024]{1,0:T(8,128)(2,1)S(1)}, u32[]{:S(2)}, u32[]{:S(2)}) %collective-permute-start.3) | collective-permute-done | bytes 262176 | tf_op jit(solution)/shard_map/ppermute | solution.py:88
  28.0 1.6 collective-permute-start.8
  30.6 1.6 collective-permute-start.13
  32.6 4.7 %collective-permute-done.8.refs_8_.refs_4_ = bf16[128,1024]{1,0:T(8,128)(2,1)S(1)} collective-permute-done((bf16[128,1024]{1,0:T(8,128)(2,1)S(1)}, bf16[128,1024]{1,0:T(8,128)(2,1)S(1)}, u32[]{:S(2)}, u32[]{:S(2)}) %collective-permute-start.8) | collective-permute-done | bytes 262176 | tf_op jit(solution)/shard_map/ppermute | solution.py:88
  39.7 8.2 %collective-permute-done.12.refs_12_.refs_8_ = bf16[64,1024]{1,0:T(8,128)(2,1)S(1)} collective-permute-done((bf16[64,1024]{1,0:T(8,128)(2,1)S(1)}, bf16[64,1024]{1,0:T(8,128)(2,1)S(1)}, u32[]{:S(2)}, u32[]{:S(2)}) %collective-permute-start.12) | collective-permute-done | bytes 131104 | tf_op jit(solution)/shard_map/ppermute | solution.py:88
  49.4 4.0 %collective-permute-done.11.refs_11_.refs_7_ = bf16[64,1024]{1,0:T(8,128)(2,1)S(1)} collective-permute-done((bf16[64,1024]{1,0:T(8,128)(2,1)S(1)}, bf16[64,1024]{1,0:T(8,128)(2,1)S(1)}, u32[]{:S(2)}, u32[]{:S(2)}) %collective-permute-start.11) | collective-permute-done | bytes 131104 | tf_op jit(solution)/shard_map/ppermute | solution.py:88
  58.8 7.0 %attention.1 = (bf16[4,128,256]{2,1,0:T(8,128)(2,1)S(1)}, bf16[512,1024]{1,0:T(8,128)(2,1)S(1)}, bf16[512,768]{1,0:T(8,128)(2,1)S(1)}, f32[16,128,128]{2,1,0:T(8,128)S(1)}, bf16[1024,768]{1,0:T(8,128)(2,1)S(1)}) custom-call(s32[21]{0:T(128)S(1)} %dynamic-slice_bitcast_fusion.scal, bf16[130,1024]{1,0:T(8,128)(2,1)S(1)} %pack_tokens.1.refs_0_.block_ref, ...), custom_call_target="tpu_custom_call" | custom-call | flops 805306368 | bytes 8142932 | tf_op jit(solution)/shard_map/attention/pallas_call | solution.py:160
  71.4 6.0 %collective-permute-done.25.refs_6_ = bf16[88,1024]{1,0:T(8,128)(2,1)S(1)} collective-permute-done((bf16[88,1024]{1,0:T(8,128)(2,1)S(1)}, bf16[88,1024]{1,0:T(8,128)(2,1)S(1)}, u32[]{:S(2)}, u32[]{:S(2)}) %collective-permute-start.25) | collective-permute-done | bytes 180256 | tf_op jit(solution)/shard_map/ppermute | solution.py:88
  81.8 2.7 %middle.1 = (f32[512,1024]{1,0:T(8,128)S(1)}, bf16[512,1024]{1,0:T(8,128)(2,1)S(1)}, bf16[512,1024]{1,0:T(8,128)(2,1)S(1)}, bf16[256,1024]{1,0:T(8,128)(2,1)S(1)}) custom-call(s32[21]{0:T(128)S(1)} %dynamic-slice_bitcast_fusion.scal, bf16[130,1024]{1,0:T(8,128)(2,1)S(1)} %pack_tokens.1.refs_0_.block_ref, ...), custom_call_target="tpu_custom_call" | custom-call | flops 1073741824 | bytes 8929364 | tf_op jit(solution)/shard_map/middle/pallas_call | solution.py:160
  88.0 2.9 %hidden_units.1 = (f32[512,768]{1,0:T(8,128)S(1)}, f32[512,768]{1,0:T(8,128)S(1)}, bf16[512,768]{1,0:T(8,128)(2,1)S(1)}, bf16[1024,1536]{1,0:T(8,128)(2,1)S(1)}) custom-call(s32[21]{0:T(128)S(1)} %dynamic-slice_bitcast_fusion.scal, bf16[512,1024]{1,0:T(8,128)(2,1)S(1)} %get-tuple-element.269.h2_ref, ...), custom_call_target="tpu_custom_call" | custom-call | flops 1610612736 | bytes 11272276 | tf_op jit(solution)/shard_map/hidden_units/pallas_call | solution.py:160
  91.0 2.0 collective-permute-done.30.refs_5_
  96.3 2.4 %grad_down_parts.1 = (bf16[88,1024]{1,0:T(8,128)(2,1)S(1)}, bf16[88,1024]{1,0:T(8,128)(2,1)S(1)}, bf16[88,1024]{1,0:T(8,128)(2,1)S(1)}, bf16[88,1024]{1,0:T(8,12...) custom-call(s32[21]{0:T(128)S(1)} %dynamic-slice_bitcast_fusion.scal, ...), custom_call_target="tpu_custom_call" | custom-call | flops 805306368 | bytes 4325460 | tf_op jit(solution)/shard_map/grad_down_parts/pallas_call | solution.py:160
  101.6 4.8 %hidden_back.1 = (bf16[512,1536]{1,0:T(8,128)(2,1)S(1)}, f32[2,128,1024]{2,1,0:T(8,128)S(1)}, bf16[2,128,1024]{2,1,0:T(8,128)(2,1)S(1)}, bf16[768,1024]{1,0:T(8,128)(2,1)S(1)}) custom-call(s32[21]{0:T(128)S(1)} %dynamic-slice_bitcast_fusion.scal, bf16[512,1024]{1,0:T(8,128)(2,1)S(1)} %get-tuple-element.291.refs_0_, ...), custom_call_target="tpu_custom_call" | custom-call | flops 2415919104 | bytes 13500500 | tf_op jit(solution)/shard_map/hidden_back/pallas_call | solution.py:160
  109.5 4.0 %grad_in_parts.1 = (bf16[128,1536]{1,0:T(8,128)(2,1)S(1)}, bf16[128,1536]{1,0:T(8,128)(2,1)S(1)}, bf16[128,1536]{1,0:T(8,128)(2,1)S(1)}, bf16[128,1536]{1,0:T(8,...) custom-call(s32[21]{0:T(128)S(1)} %dynamic-slice_bitcast_fusion.scal, ...), custom_call_target="tpu_custom_call" | custom-call | flops 1610612736 | bytes 5767252 | tf_op jit(solution)/shard_map/grad_in_parts/pallas_call | solution.py:160
  113.9 3.1 %collective-permute-done.40.far_first = bf16[128,1024]{1,0:T(8,128)(2,1)S(1)} collective-permute-done((bf16[128,1024]{1,0:T(8,128)(2,1)S(1)}, bf16[128,1024]{1,0:T(8,128)(2,1)S(1)}, u32[]{:S(2)}, u32[]{:S(2)}) %collective-permute-start.40) | collective-permute-done | bytes 262176 | tf_op jit(solution)/shard_map/ppermute | solution.py:50
  121.9 2.1 %last_projection.1 = (f32[2,128,1024]{2,1,0:T(8,128)S(1)}, bf16[2,128,1024]{2,1,0:T(8,128)(2,1)S(1)}) custom-call(s32[21]{0:T(128)S(1)} %dynamic-slice_bitcast_fusion.scal, bf16[512,768]{1,0:T(8,128)(2,1)S(1)} %get-tuple-element.319.hid_ref, bf16[768,1024]{1,0:T(8,128)(2,1)S(1)} %get-tuple-element.320.down_ref), custom_call_target="tpu_custom_call" | custom-call | flops 805306368 | bytes 3932244 | tf_op jit(solution)/shard_map/last_projection/pallas_call | solution.py:160
  124.0 3.2 %collective-permute-done.41.right_got = bf16[88,1024]{1,0:T(8,128)(2,1)S(1)} collective-permute-done((bf16[88,1024]{1,0:T(8,128)(2,1)S(1)}, bf16[88,1024]{1,0:T(8,128)(2,1)S(1)}, u32[]{:S(2)}, u32[]{:S(2)}) %collective-permute-start.41) | collective-permute-done | bytes 180256 | tf_op jit(solution)/shard_map/ppermute | solution.py:88
  133.2 7.0 %attention_back.1 = (bf16[512,768]{1,0:T(8,128)(2,1)S(1)}, bf16[512,1024]{1,0:T(8,128)(2,1)S(1)}, f32[2,128,1024]{2,1,0:T(8,128)S(1)}, bf16[2,128,1024]{2,1,0:T(8,128)(2,1)S(1)}) custom-call(s32[21]{0:T(128)S(1)} %dynamic-slice_bitcast_fusion.scal, bf16[2,128,1024]{2,1,0:T(8,128)(2,1)S(1)} %get-tuple-element.335.ga_own, ...), custom_call_target="tpu_custom_call" | custom-call | flops 1879048192 | bytes 8650836 | tf_op jit(solution)/shard_map/attention_back/pallas_call | solution.py:160
  140.2 4.2 %collective-permute-done.49 = bf16[88,1024]{1,0:T(8,128)(2,1)S(1)} collective-permute-done((bf16[88,1024]{1,0:T(8,128)(2,1)S(1)}, bf16[88,1024]{1,0:T(8,128)(2,1)S(1)}, u32[]{:S(2)}, u32[]{:S(2)}) %collective-permute-start.49) | collective-permute-done | bytes 180256 | tf_op jit(solution)/shard_map/ppermute | solution.py:88
  146.9 2.1 %grad_first_parts.1 = (bf16[128,1024]{1,0:T(8,128)(2,1)S(1)}, bf16[128,1024]{1,0:T(8,128)(2,1)S(1)}, bf16[128,1024]{1,0:T(8,128)(2,1)S(1)}, bf16[128,1024]{1,0:T...) custom-call(s32[21]{0:T(128)S(1)} %dynamic-slice_bitcast_fusion.scal, ...), custom_call_target="tpu_custom_call" | custom-call | flops 1073741824 | bytes 6029396 | tf_op jit(solution)/shard_map/grad_first_parts/pallas_call | solution.py:160
  151.1 1.6 collective-permute-start.53
  152.7 4.1 %collective-permute-done.54.right_got = bf16[128,1536]{1,0:T(8,128)(2,1)S(1)} collective-permute-done((bf16[128,1536]{1,0:T(8,128)(2,1)S(1)}, bf16[128,1536]{1,0:T(8,128)(2,1)S(1)}, u32[]{:S(2)}, u32[]{:S(2)}) %collective-permute-start.54) | collective-permute-done | bytes 393248 | tf_op jit(solution)/shard_map/ppermute | solution.py:88
  163.7 4.0 %collective-permute-done.59.right_got = bf16[128,1024]{1,0:T(8,128)(2,1)S(1)} collective-permute-done((bf16[128,1024]{1,0:T(8,128)(2,1)S(1)}, bf16[128,1024]{1,0:T(8,128)(2,1)S(1)}, u32[]{:S(2)}, u32[]{:S(2)}) %collective-permute-start.59) | collective-permute-done | bytes 262176 | tf_op jit(solution)/shard_map/ppermute | solution.py:88
  170.0 6.2 %collective-permute-done.64.right_ref = bf16[128,1536]{1,0:T(8,128)(2,1)S(1)} collective-permute-done((bf16[128,1536]{1,0:T(8,128)(2,1)S(1)}, bf16[128,1536]{1,0:T(8,128)(2,1)S(1)}, u32[]{:S(2)}, u32[]{:S(2)}) %collective-permute-start.64) | collective-permute-done | bytes 393248 | tf_op jit(solution)/shard_map/ppermute | solution.py:88
  176.9 3.1 %collective-permute-done.62.right_got = bf16[128,1024]{1,0:T(8,128)(2,1)S(1)} collective-permute-done((bf16[128,1024]{1,0:T(8,128)(2,1)S(1)}, bf16[128,1024]{1,0:T(8,128)(2,1)S(1)}, u32[]{:S(2)}, u32[]{:S(2)}) %collective-permute-start.62) | collective-permute-done | bytes 262176 | tf_op jit(solution)/shard_map/ppermute | solution.py:88
  184.6 3.7 %collective-permute-done.67.right_ref = bf16[128,1024]{1,0:T(8,128)(2,1)S(1)} collective-permute-done((bf16[128,1024]{1,0:T(8,128)(2,1)S(1)}, bf16[128,1024]{1,0:T(8,128)(2,1)S(1)}, u32[]{:S(2)}, u32[]{:S(2)}) %collective-permute-start.67) | collective-permute-done | bytes 262176 | tf_op jit(solution)/shard_map/ppermute | solution.py:88
  195.3 1.8 finish_tokens.1
  198.1 2.4 %unpack_in.1 = f32[64,5632]{1,0:T(8,128)} custom-call(s32[21]{0:T(128)S(1)} %dynamic-slice_bitcast_fusion.scal, bf16[64,1536]{1,0:T(8,128)(2,1)S(1)} %get-tuple-element.408.own_ref, bf16[64,1536]{1,0:T(8,128)(2,1)S(1)} %collective-permute-done.66.near_ref, bf16[64,1536]{1,0:T(8,128)(2,1)S(1)} %collective-permute-done.69.far_ref, ...), custom_call_target="tpu_custom_call" | custom-call | bytes 2228308 | tf_op jit(solution)/shard_map/unpack_in/pallas_call | solution.py:160
  201.0 2.3 %collective-permute-done.72.diagonal_ref = bf16[64,1024]{1,0:T(8,128)(2,1)S(1)} collective-permute-done((bf16[64,1024]{1,0:T(8,128)(2,1)S(1)}, bf16[64,1024]{1,0:T(8,128)(2,1)S(1)}, u32[]{:S(2)}, u32[]{:S(2)}) %collective-permute-start.72) | collective-permute-done | bytes 131104 | tf_op jit(solution)/shard_map/ppermute | solution.py:50
  (185 shorter events, 86.9 us)
Async XLA Ops:
  5.4 9.5 %collective-permute-start.1 = (bf16[128,1024]{1,0:T(8,128)(2,1)S(1)}, bf16[128,1024]{1,0:T(8,128)(2,1)S(1)}, u32[]{:S(2)}, u32[]{:S(2)}) collective-permute-start(bf16[128,1024]{1,0:T(8,128)(2,1)S(1)} %constant_dynamic-update-slice_fusion.refs_4_.refs_0_), channel_id=1, source_target_pairs={{0,4},{4,8},{8,12},{12,14},{14,10},{10,6},{6,2},{2,0},{1,5},{5,9},... | collective-permute-start | bytes 786440 | tf_op jit(solution)/shard_map/ppermute | solution.py:88
  16.5 11.5 %collective-permute-start.6 = (bf16[130,1024]{1,0:T(8,128)(2,1)S(1)}, bf16[130,1024]{1,0:T(8,128)(2,1)S(1)}, u32[]{:S(2)}, u32[]{:S(2)}) collective-permute-start(bf16[130,1024]{1,0:T(8,128)(2,1)S(1)} %pack_tokens.1.refs_0_.block_ref), channel_id=1, source_target_pairs={{0,1},{1,0},{2,3},{3,2},{4,5},{5,4},{6,7},{7,6},{8,9},{9,8},{10,11... | collective-permute-start | bytes 798728 | tf_op jit(solution)/shard_map/ppermute | solution.py:54
  16.5 11.5 %collective-permute-start.5 = (bf16[130,1024]{1,0:T(8,128)(2,1)S(1)}, bf16[130,1024]{1,0:T(8,128)(2,1)S(1)}, u32[]{:S(2)}, u32[]{:S(2)}) collective-permute-start(bf16[130,1024]{1,0:T(8,128)(2,1)S(1)} %pack_tokens.1.refs_0_.block_ref), channel_id=1, source_target_pairs={{0,16},{16,0},{1,17},{17,1},{2,18},{18,2},{3,19},{19,3},{4,20},{20... | collective-permute-start | bytes 798728 | tf_op jit(solution)/shard_map/ppermute | solution.py:50
  30.6 22.8 %collective-permute-start.13 = (bf16[128,1536]{1,0:T(8,128)(2,1)S(1)}, bf16[128,1536]{1,0:T(8,128)(2,1)S(1)}, u32[]{:S(2)}, u32[]{:S(2)}) collective-permute-start(bf16[128,1536]{1,0:T(8,128)(2,1)S(1)} %constant_dynamic-update-slice_fusion.2.refs_0_), channel_id=1, source_target_pairs={{0,4},{4,8},{8,12},{12,14},{14,10},{10,6},{6,2},{2,0},{1,5},{5,9},... | collective-permute-start | bytes 1179656 | tf_op jit(solution)/shard_map/ppermute | solution.py:88
  32.2 21.3 %collective-permute-start.14 = (bf16[128,1536]{1,0:T(8,128)(2,1)S(1)}, bf16[128,1536]{1,0:T(8,128)(2,1)S(1)}, u32[]{:S(2)}, u32[]{:S(2)}) collective-permute-start(bf16[128,1536]{1,0:T(8,128)(2,1)S(1)} %constant_dynamic-update-slice_fusion.2.refs_0_), channel_id=1, source_target_pairs={{4,0},{8,4},{12,8},{14,12},{10,14},{6,10},{2,6},{0,2},{5,1},{9,5},... | collective-permute-start | bytes 1179656 | tf_op jit(solution)/shard_map/ppermute | solution.py:88
  38.8 14.6 %collective-permute-start.15 = (bf16[130,1024]{1,0:T(8,128)(2,1)S(1)}, bf16[130,1024]{1,0:T(8,128)(2,1)S(1)}, u32[]{:S(2)}, u32[]{:S(2)}) collective-permute-start(bf16[130,1024]{1,0:T(8,128)(2,1)S(1)} %collective-permute-done.5.refs_2_), channel_id=1, source_target_pairs={{0,1},{1,0},{2,3},{3,2},{4,5},{5,4},{6,7},{7,6},{8,9},{9,8},{10,11... | collective-permute-start | bytes 798728 | tf_op jit(solution)/shard_map/ppermute | solution.py:54
  39.4 14.0 %collective-permute-start.16 = (bf16[128,1024]{1,0:T(8,128)(2,1)S(1)}, bf16[128,1024]{1,0:T(8,128)(2,1)S(1)}, u32[]{:S(2)}, u32[]{:S(2)}) collective-permute-start(bf16[128,1024]{1,0:T(8,128)(2,1)S(1)} %bitcast.29), channel_id=1, source_target_pairs={{0,1},{1,0},{2,3},{3,2},{4,5},{5,4},{6,7},{7,6},{8,9},{9,8},{10,11... | collective-permute-start | bytes 786440 | tf_op jit(solution)/shard_map/ppermute | solution.py:54
  53.5 13.3 %collective-permute-start.17 = (bf16[128,1536]{1,0:T(8,128)(2,1)S(1)}, bf16[128,1536]{1,0:T(8,128)(2,1)S(1)}, u32[]{:S(2)}, u32[]{:S(2)}) collective-permute-start(bf16[128,1536]{1,0:T(8,128)(2,1)S(1)} %collective-permute-done.13.refs_6_), channel_id=1, source_target_pairs={{0,4},{4,8},{8,12},{12,14},{14,10},{10,6},{6,2},{2,0},{1,5},{5,9},... | collective-permute-start | bytes 1179656 | tf_op jit(solution)/shard_map/ppermute | solution.py:88
  55.0 11.7 %collective-permute-start.18 = (bf16[128,1536]{1,0:T(8,128)(2,1)S(1)}, bf16[128,1536]{1,0:T(8,128)(2,1)S(1)}, u32[]{:S(2)}, u32[]{:S(2)}) collective-permute-start(bf16[128,1536]{1,0:T(8,128)(2,1)S(1)} %collective-permute-done.14.refs_1_), channel_id=1, source_target_pairs={{4,0},{8,4},{12,8},{14,12},{10,14},{6,10},{2,6},{0,2},{5,1},{9,5},... | collective-permute-start | bytes 1179656 | tf_op jit(solution)/shard_map/ppermute | solution.py:88
  56.1 14.8 %collective-permute-start.22 = (bf16[1024,256]{1,0:T(8,128)(2,1)S(1)}, bf16[1024,256]{1,0:T(8,128)(2,1)S(1)}, u32[]{:S(2)}, u32[]{:S(2)}) collective-permute-start(bf16[1024,256]{1,0:T(8,128)(2,1)S(1)} %gather_out.1.refs_6_), channel_id=1, source_target_pairs={{0,16},{16,0},{1,17},{17,1},{2,18},{18,2},{3,19},{19,3},{4,20},{20... | collective-permute-start | bytes 1572872 | tf_op jit(solution)/shard_map/ppermute | solution.py:50
  56.7 9.8 %collective-permute-start.19 = (bf16[88,1024]{1,0:T(8,128)(2,1)S(1)}, bf16[88,1024]{1,0:T(8,128)(2,1)S(1)}, u32[]{:S(2)}, u32[]{:S(2)}) collective-permute-start(bf16[88,1024]{1,0:T(8,128)(2,1)S(1)} %get-tuple-element.292.refs_1_), channel_id=1, source_target_pairs={{0,4},{4,8},{8,12},{12,14},{14,10},{10,6},{6,2},{2,0},{1,5},{5,9},... | collective-permute-start | bytes 540680 | tf_op jit(solution)/shard_map/ppermute | solution.py:88
  66.8 11.4 %collective-permute-start.23 = (bf16[128,1536]{1,0:T(8,128)(2,1)S(1)}, bf16[128,1536]{1,0:T(8,128)(2,1)S(1)}, u32[]{:S(2)}, u32[]{:S(2)}) collective-permute-start(bf16[128,1536]{1,0:T(8,128)(2,1)S(1)} %collective-permute-done.17.refs_5_), channel_id=1, source_target_pairs={{0,4},{4,8},{8,12},{12,14},{14,10},{10,6},{6,2},{2,0},{1,5},{5,9},... | collective-permute-start | bytes 1179656 | tf_op jit(solution)/shard_map/ppermute | solution.py:88
  68.2 10.0 %collective-permute-start.24 = (bf16[128,1536]{1,0:T(8,128)(2,1)S(1)}, bf16[128,1536]{1,0:T(8,128)(2,1)S(1)}, u32[]{:S(2)}, u32[]{:S(2)}) collective-permute-start(bf16[128,1536]{1,0:T(8,128)(2,1)S(1)} %collective-permute-done.18.refs_2_), channel_id=1, source_target_pairs={{4,0},{8,4},{12,8},{14,12},{10,14},{6,10},{2,6},{0,2},{5,1},{9,5},... | collective-permute-start | bytes 1179656 | tf_op jit(solution)/shard_map/ppermute | solution.py:88
  68.8 9.4 %collective-permute-start.21 = (bf16[4,128,256]{2,1,0:T(8,128)(2,1)S(1)}, bf16[4,128,256]{2,1,0:T(8,128)(2,1)S(1)}, u32[]{:S(2)}, u32[]{:S(2)}) collective-permute-start(bf16[4,128,256]{2,1,0:T(8,128)(2,1)S(1)} %get-tuple-element.256.refs_4_), channel_id=1, source_target_pairs={{0,16},{16,0},{1,17},{17,1},{2,18},{18,2},{3,19},{19,3},{4,20},{20... | collective-permute-start | bytes 786440 | tf_op jit(solution)/shard_map/ppermute | solution.py:50
  117.1 10.4 %collective-permute-start.45 = (bf16[128,1024]{1,0:T(8,128)(2,1)S(1)}, bf16[128,1024]{1,0:T(8,128)(2,1)S(1)}, u32[]{:S(2)}, u32[]{:S(2)}) collective-permute-start(bf16[128,1024]{1,0:T(8,128)(2,1)S(1)} %slice_bitcast_fusion), channel_id=1, source_target_pairs={{0,16},{16,0},{1,17},{17,1},{2,18},{18,2},{3,19},{19,3},{4,20},{20... | collective-permute-start | bytes 786440 | tf_op jit(solution)/shard_map/ppermute | solution.py:50
  117.7 9.8 %collective-permute-start.43 = (bf16[64,1536]{1,0:T(8,128)(2,1)S(1)}, bf16[64,1536]{1,0:T(8,128)(2,1)S(1)}, u32[]{:S(2)}, u32[]{:S(2)}) collective-permute-start(bf16[64,1536]{1,0:T(8,128)(2,1)S(1)} %get-tuple-element.331), channel_id=1, source_target_pairs={{0,4},{4,8},{8,12},{12,14},{14,10},{10,6},{6,2},{2,0},{1,5},{5,9},... | collective-permute-start | bytes 589832 | tf_op jit(solution)/shard_map/ppermute | solution.py:88
  129.0 15.6 %collective-permute-start.47 = (bf16[128,1536]{1,0:T(8,128)(2,1)S(1)}, bf16[128,1536]{1,0:T(8,128)(2,1)S(1)}, u32[]{:S(2)}, u32[]{:S(2)}) collective-permute-start(bf16[128,1536]{1,0:T(8,128)(2,1)S(1)} %get-tuple-element.346), channel_id=1, source_target_pairs={{0,4},{4,8},{8,12},{12,14},{14,10},{10,6},{6,2},{2,0},{1,5},{5,9},... | collective-permute-start | bytes 1179656 | tf_op jit(solution)/shard_map/ppermute | solution.py:88
  129.5 15.1 %collective-permute-start.48 = (bf16[128,1536]{1,0:T(8,128)(2,1)S(1)}, bf16[128,1536]{1,0:T(8,128)(2,1)S(1)}, u32[]{:S(2)}, u32[]{:S(2)}) collective-permute-start(bf16[128,1536]{1,0:T(8,128)(2,1)S(1)} %get-tuple-element.347), channel_id=1, source_target_pairs={{4,0},{8,4},{12,8},{14,12},{10,14},{6,10},{2,6},{0,2},{5,1},{9,5},... | collective-permute-start | bytes 1179656 | tf_op jit(solution)/shard_map/ppermute | solution.py:88
  131.2 13.3 %collective-permute-start.49 = (bf16[88,1024]{1,0:T(8,128)(2,1)S(1)}, bf16[88,1024]{1,0:T(8,128)(2,1)S(1)}, u32[]{:S(2)}, u32[]{:S(2)}) collective-permute-start(bf16[88,1024]{1,0:T(8,128)(2,1)S(1)} %get-tuple-element.352), channel_id=1, source_target_pairs={{0,4},{4,8},{8,12},{12,14},{14,10},{10,6},{6,2},{2,0},{1,5},{5,9},... | collective-permute-start | bytes 540680 | tf_op jit(solution)/shard_map/ppermute | solution.py:88
  131.7 12.9 %collective-permute-start.50 = (bf16[88,1024]{1,0:T(8,128)(2,1)S(1)}, bf16[88,1024]{1,0:T(8,128)(2,1)S(1)}, u32[]{:S(2)}, u32[]{:S(2)}) collective-permute-start(bf16[88,1024]{1,0:T(8,128)(2,1)S(1)} %get-tuple-element.353), channel_id=1, source_target_pairs={{4,0},{8,4},{12,8},{14,12},{10,14},{6,10},{2,6},{0,2},{5,1},{9,5},... | collective-permute-start | bytes 540680 | tf_op jit(solution)/shard_map/ppermute | solution.py:88
  144.8 12.0 %collective-permute-start.54 = (bf16[128,1536]{1,0:T(8,128)(2,1)S(1)}, bf16[128,1536]{1,0:T(8,128)(2,1)S(1)}, u32[]{:S(2)}, u32[]{:S(2)}) collective-permute-start(bf16[128,1536]{1,0:T(8,128)(2,1)S(1)} %get-tuple-element.368), channel_id=1, source_target_pairs={{0,4},{4,8},{8,12},{12,14},{14,10},{10,6},{6,2},{2,0},{1,5},{5,9},... | collective-permute-start | bytes 1179656 | tf_op jit(solution)/shard_map/ppermute | solution.py:88
  145.3 13.0 %collective-permute-start.55 = (bf16[128,1536]{1,0:T(8,128)(2,1)S(1)}, bf16[128,1536]{1,0:T(8,128)(2,1)S(1)}, u32[]{:S(2)}, u32[]{:S(2)}) collective-permute-start(bf16[128,1536]{1,0:T(8,128)(2,1)S(1)} %get-tuple-element.369), channel_id=1, source_target_pairs={{4,0},{8,4},{12,8},{14,12},{10,14},{6,10},{2,6},{0,2},{5,1},{9,5},... | collective-permute-start | bytes 1179656 | tf_op jit(solution)/shard_map/ppermute | solution.py:88
  149.1 9.3 %collective-permute-start.56 = (bf16[128,1024]{1,0:T(8,128)(2,1)S(1)}, bf16[128,1024]{1,0:T(8,128)(2,1)S(1)}, u32[]{:S(2)}, u32[]{:S(2)}) collective-permute-start(bf16[128,1024]{1,0:T(8,128)(2,1)S(1)} %fusion.2), channel_id=1, source_target_pairs={{0,16},{16,0},{1,17},{17,1},{2,18},{18,2},{3,19},{19,3},{4,20},{20... | collective-permute-start | bytes 786440 | tf_op jit(solution)/shard_map/ppermute | solution.py:50
  158.5 9.3 %collective-permute-start.59 = (bf16[128,1024]{1,0:T(8,128)(2,1)S(1)}, bf16[128,1024]{1,0:T(8,128)(2,1)S(1)}, u32[]{:S(2)}, u32[]{:S(2)}) collective-permute-start(bf16[128,1024]{1,0:T(8,128)(2,1)S(1)} %get-tuple-element.379), channel_id=1, source_target_pairs={{0,4},{4,8},{8,12},{12,14},{14,10},{10,6},{6,2},{2,0},{1,5},{5,9},... | collective-permute-start | bytes 786440 | tf_op jit(solution)/shard_map/ppermute | solution.py:88
  160.6 23.3 %collective-permute-start.57 = (bf16[2,128,1024]{2,1,0:T(8,128)(2,1)S(1)}, bf16[2,128,1024]{2,1,0:T(8,128)(2,1)S(1)}, u32[]{:S(2)}, u32[]{:S(2)}) collective-permute-start(bf16[2,128,1024]{2,1,0:T(8,128)(2,1)S(1)} %get-tuple-element.373), channel_id=1, source_target_pairs={{0,1},{1,0},{2,3},{3,2},{4,5},{5,4},{6,7},{7,6},{8,9},{9,8},{10,11... | collective-permute-start | bytes 1572872 | tf_op jit(solution)/shard_map/ppermute | solution.py:54
  160.7 15.5 %collective-permute-start.64 = (bf16[128,1536]{1,0:T(8,128)(2,1)S(1)}, bf16[128,1536]{1,0:T(8,128)(2,1)S(1)}, u32[]{:S(2)}, u32[]{:S(2)}) collective-permute-start(bf16[128,1536]{1,0:T(8,128)(2,1)S(1)} %get-tuple-element.394), channel_id=1, source_target_pairs={{0,4},{4,8},{8,12},{12,14},{14,10},{10,6},{6,2},{2,0},{1,5},{5,9},... | collective-permute-start | bytes 1179656 | tf_op jit(solution)/shard_map/ppermute | solution.py:88
  162.3 13.9 %collective-permute-start.65 = (bf16[128,1536]{1,0:T(8,128)(2,1)S(1)}, bf16[128,1536]{1,0:T(8,128)(2,1)S(1)}, u32[]{:S(2)}, u32[]{:S(2)}) collective-permute-start(bf16[128,1536]{1,0:T(8,128)(2,1)S(1)} %get-tuple-element.395), channel_id=1, source_target_pairs={{4,0},{8,4},{12,8},{14,12},{10,14},{6,10},{2,6},{0,2},{5,1},{9,5},... | collective-permute-start | bytes 1179656 | tf_op jit(solution)/shard_map/ppermute | solution.py:88
  167.9 12.1 %collective-permute-start.62 = (bf16[128,1024]{1,0:T(8,128)(2,1)S(1)}, bf16[128,1024]{1,0:T(8,128)(2,1)S(1)}, u32[]{:S(2)}, u32[]{:S(2)}) collective-permute-start(bf16[128,1024]{1,0:T(8,128)(2,1)S(1)} %get-tuple-element.387), channel_id=1, source_target_pairs={{0,4},{4,8},{8,12},{12,14},{14,10},{10,6},{6,2},{2,0},{1,5},{5,9},... | collective-permute-start | bytes 786440 | tf_op jit(solution)/shard_map/ppermute | solution.py:88
  168.8 11.5 %collective-permute-start.63 = (bf16[128,1024]{1,0:T(8,128)(2,1)S(1)}, bf16[128,1024]{1,0:T(8,128)(2,1)S(1)}, u32[]{:S(2)}, u32[]{:S(2)}) collective-permute-start(bf16[128,1024]{1,0:T(8,128)(2,1)S(1)} %get-tuple-element.388), channel_id=1, source_target_pairs={{4,0},{8,4},{12,8},{14,12},{10,14},{6,10},{2,6},{0,2},{5,1},{9,5},... | collective-permute-start | bytes 786440 | tf_op jit(solution)/shard_map/ppermute | solution.py:88
  180.2 10.1 %collective-permute-start.69 = (bf16[64,1536]{1,0:T(8,128)(2,1)S(1)}, bf16[64,1536]{1,0:T(8,128)(2,1)S(1)}, u32[]{:S(2)}, u32[]{:S(2)}) collective-permute-start(bf16[64,1536]{1,0:T(8,128)(2,1)S(1)} %get-tuple-element.408.own_ref), channel_id=1, source_target_pairs={{0,16},{16,0},{1,17},{17,1},{2,18},{18,2},{3,19},{19,3},{4,20},{20... | collective-permute-start | bytes 589832 | tf_op jit(solution)/shard_map/ppermute | solution.py:50
  191.0 10.0 %collective-permute-start.71 = (bf16[64,1024]{1,0:T(8,128)(2,1)S(1)}, bf16[64,1024]{1,0:T(8,128)(2,1)S(1)}, u32[]{:S(2)}, u32[]{:S(2)}) collective-permute-start(bf16[64,1024]{1,0:T(8,128)(2,1)S(1)} %get-tuple-element.413.own_ref), channel_id=1, source_target_pairs={{0,16},{16,0},{1,17},{17,1},{2,18},{18,2},{3,19},{19,3},{4,20},{20... | collective-permute-start | bytes 393224 | tf_op jit(solution)/shard_map/ppermute | solution.py:50
  192.5 10.8 %collective-permute-start.72 = (bf16[64,1024]{1,0:T(8,128)(2,1)S(1)}, bf16[64,1024]{1,0:T(8,128)(2,1)S(1)}, u32[]{:S(2)}, u32[]{:S(2)}) collective-permute-start(bf16[64,1024]{1,0:T(8,128)(2,1)S(1)} %collective-permute-done.70.near_ref), channel_id=1, source_target_pairs={{0,16},{16,0},{1,17},{17,1},{2,18},{18,2},{3,19},{19,3},{4,20},{20... | collective-permute-start | bytes 393224 | tf_op jit(solution)/shard_map/ppermute | solution.py:50
  (50 other events, 355.0 us)

commit v4 on v3

--- a/solution.py
+++ b/solution.py
@@ -142,7 +142,7 @@
         place = ring.half - self.step
         terms = (self.parts[place], self.parts[ring.size - place])
         body = functools.partial(ring_add, self.cut if self.step == 1 else None)
-        self.state = tuple(call(body, [shape(t.shape, BF) for t in terms], [], 0, *terms, *self.got, smem=0))
+        self.state = tuple(call(body, [shape(t.shape, BF) for t in terms], [], 16000000000, *terms, *self.got, smem=0))
 
     def run(self):
         while self.step < self.ring.half - 1:
@@ -155,13 +155,14 @@
     return lax.optimization_barrier(values)
 
 
-def call(body, outs, scratch, flops, *args, smem=1):
+def call(body, outs, scratch, flops, *args, smem=1, still=0):
     nbytes = sum(a.size * a.dtype.itemsize for a in args) + sum(o.size * o.dtype.itemsize for o in outs)
+    spaces = [pltpu.SMEM] * smem + [pl.ANY] * still + [pltpu.VMEM] * (len(args) - smem - still)
     return pl.pallas_call(
         body,
         name=body.func.__name__,
         out_shape=outs,
-        in_specs=[pl.BlockSpec(memory_space=pltpu.SMEM)] * smem + [pl.BlockSpec(memory_space=pltpu.VMEM)] * (len(args) - smem),
+        in_specs=[pl.BlockSpec(memory_space=space) for space in spaces],
         out_specs=[pl.BlockSpec(memory_space=pltpu.VMEM)] * len(outs),
         scratch_shapes=scratch,
         compiler_params=pltpu.CompilerParams(vmem_limit_bytes=12 * MIB),
@@ -183,12 +184,16 @@
         own_ref[rows + m : rows + m + 1, :] = jnp.broadcast_to(prefix_ref[m : m + 1, :].astype(F32), (1, own_ref.shape[1])).astype(BF)
 
 
-def pack_first(size, width, scal, qkv_ref, out_ref, own_ref, sib_ref):
+def pack_first(size, width, scal, qkv_ref, out_ref, own_ref, sib_ref, sems):
     quarter = width // 4
+    copies = []
     for ref, member in ((own_ref, scal[2 * size + 1]), (sib_ref, scal[2 * size + 2])):
-        for j in range(3):
-            ref[:, j * quarter : (j + 1) * quarter] = qkv_ref[:, lanes(j * width + member * quarter, quarter)]
-        ref[:, 3 * quarter :] = out_ref[:, lanes(member * quarter, quarter)]
+        for j in range(4):
+            source = qkv_ref.at[:, lanes(j * width + member * quarter, quarter)] if j < 3 else out_ref.at[:, lanes(member * quarter, quarter)]
+            copies.append(pltpu.make_async_copy(source, ref.at[:, j * quarter : (j + 1) * quarter], sems.at[len(copies)]))
+            copies[-1].start()
+    for copy in copies:
+        copy.wait()
 
 
 def pack_in(size, units, piece, padded, scal, in_ref, down_ref, own_ref, sib_ref, rows_ref):
@@ -556,10 +561,19 @@
 
     tokens = tokens.reshape(rows, width)
     cot_own = cotangent.reshape(rows, width)
-    a_own, a_sib = call(functools.partial(pack_first, size, width), [shape((shard_rows, width), BF)] * 2, [], 0, scal, qkv_weight, out_weight)
+    a_own, a_sib = call(
+        functools.partial(pack_first, size, width),
+        [shape((shard_rows, width), BF)] * 2,
+        [pltpu.SemaphoreType.DMA((8,))],
+        0,
+        scal,
+        qkv_weight,
+        out_weight,
+        still=2,
+    )
     a = Gather(ring, jnp.concatenate([a_own, sibling(a_sib)], axis=0))
 
-    a.state, in_weight = sync(a.state, in_weight)
+    a.state, in_weight, tokens, cot_own = sync(a.state, in_weight, tokens, cot_own)
     a.advance()
     b_own, b_sib, down_rows = call(
         functools.partial(pack_in, size, units, piece, padded),
@@ -570,31 +584,32 @@
         in_weight,
         down_weight,
     )
-    b_own, b_sib, tokens = sync(b_own, b_sib, tokens)
+    c = Gather(ring, down_rows)
+    c.advance()
+    b_got = sibling(b_sib)
     (own,) = call(functools.partial(pack_tokens, rows), [shape((rows + micro, width), BF)], [], 0, prefix, tokens, smem=0)
-
-    a.state, own, b_own, b_sib = sync(a.state, own, b_own, b_sib)
+    near = sibling(own)
+    cot_near = sibling(cot_own)
+
+    a.state, own, b_own, b_got, near, cot_near = sync(a.state, own, b_own, b_got, near, cot_near)
     a.advance()
     far = across(own)
-    near = sibling(own)
-    b_got = sibling(b_sib)
     b = Gather(ring, jnp.concatenate([b_own, b_got], axis=0))
 
-    a.state, cot_own, far, near, b.state = sync(a.state, cot_own, far, near, b.state)
+    (a.state,) = sync(a.state)
     a.advance()
+    far, cot_own, b.state, c.state = sync(far, cot_own, b.state, c.state)
+    cot_far = across(cot_own)
     b.advance()
-    cot_far = across(cot_own)
 
     while a.step < ring.half - 1:
         (a.state,) = sync(a.state)
         a.advance()
-    a.state, far, cot_own, cot_far, down_rows = sync(a.state, far, cot_own, cot_far, down_rows)
+    a.state, far, cot_far = sync(a.state, far, cot_far)
     a_chunks = a.finish()
     diagonal = sibling(far)
-    cot_near = sibling(cot_own)
-    c = Gather(ring, down_rows)
-
-    a_chunks, b.state, c.state, diagonal, cot_near = sync(a_chunks, b.state, c.state, diagonal, cot_near)
+
+    a_chunks, b.state, c.state, diagonal = sync(a_chunks, b.state, c.state, diagonal)
     blocks = [own, near, far, diagonal]
     b.advance()
     c.advance()
@@ -627,7 +642,7 @@
     kept = [o_own.reshape(full_rows, quarter), o_far.reshape(full_rows, quarter), out_mine, out_far]
     near_all = sibling(jnp.concatenate(kept, axis=0))
     b_chunks = b.finish()
-    c.advance()
+    c_chunks = c.finish()
     x2, h2, o_all, out_rows = call(
         functools.partial(middle, size, rows, width),
         [
@@ -647,7 +662,7 @@
         near_all,
     )
 
-    h2, b_chunks, cot_far = sync(h2, b_chunks, cot_far)
+    h2, b_chunks, c_chunks, cot_far = sync(h2, b_chunks, c_chunks, cot_far)
     cot_diagonal = sibling(cot_far)
     up, gate, hid, in_mine = call(
         functools.partial(hidden_units, size, shard_rows, member_units, chunks),
@@ -663,8 +678,7 @@
         h2,
         *b_chunks,
     )
-    hid, c.state, cot_diagonal = sync(hid, c.state, cot_diagonal)
-    c_chunks = c.finish()
+    hid, cot_diagonal = sync(hid, cot_diagonal)
     *down_parts, gm = call(
         functools.partial(grad_down_parts, size, rows, padded),
         [shape((piece, width), BF)] * size + [shape((full_rows, width), BF)],
@@ -799,18 +813,18 @@
         return call(functools.partial(split_rows, size), [shape((shard_rows, columns), BF)] * 2, [], 0, scal, *summed)
 
     in_keep, in_give = halves(b.run())
-    a.got, in_keep, in_give = sync(a.got, in_keep, in_give)
+    in_near = sibling(in_give)
+    a.got, in_keep, in_near, y_far = sync(a.got, in_keep, in_near, y_far)
     a.add()
     a.send()
     in_far = across(in_keep)
-    in_near = sibling(in_give)
     in_diagonal = across(in_near)
     first_keep, first_give = halves(a.run())
     first_keep, first_give, in_far = sync(first_keep, first_give, in_far)
     first_far = across(first_keep)
     first_near = sibling(first_give)
     first_diagonal = across(first_near)
-    u1_far, y_far, down_other, in_near, first_near = sync(u1_far, y_far, down_other, in_near, first_near)
+    u1_far, y_far, down_other, in_keep, first_near = sync(u1_far, y_far, down_other, in_keep, first_near)
     (grad_tokens,) = call(
         functools.partial(finish_tokens, rows), [shape((rows, width), F32)], [], 0, scal, u1_keep, u1_got, u1_far, own, gx2
     )

time: 205 us -> 194 us (0.946)
  waiting for transfers between devices: 84.9 us -> 66.9 us
  starting transfers between devices: 64 us -> 71.7 us
    ppermute x24, waiting for transfers between devices: 55.7 us -> 36.8 us  [exchange(): lax.ppermute(pair[0], 'ring', self.right)]
    ppermute x24, starting transfers between devices: 27.9 us -> 39.5 us  [exchange(): lax.ppermute(pair[0], 'ring', self.right)]
    ppermute x24, starting transfers between devices: 22.6 us -> 13.1 us  [exchange(): lax.ppermute(pair[1], 'ring', self.left)]
    ppermute x13, starting transfers between devices: 12.2 us -> 16.9 us  [across(): return lax.ppermute(value, 'rep', SWAP)]
    ppermute x24, waiting for transfers between devices: 19.3 us -> 23.1 us  [exchange(): lax.ppermute(pair[1], 'ring', self.left)]
    unnamed x19 -> x23, local copies, waits for them, and re-layouts: 4.61 us -> 3.64 us
  transfers between devices with their start and end apart: 74 -> 74, of which waited for: 38 -> 33; matrix products, arithmetic and copies ran while one was open for 1% -> 1% of each run, Pallas kernels for 22% -> 22%
where the time goes in v4:
time: 194 us
  starting transfers between devices  71.7 us (37%)
  waiting for transfers between devices  66.9 us (34%)
  Pallas kernels  48.1 us (25%)
  local copies, waits for them, and re-layouts  4.6 us (2%)
    pallas_call x29, Pallas kernels, call(): pl.pallas_call(body, name=body.func.__name__, out_shape=outs, in_specs=[p...  48.1 us
    ppermute x24, starting transfers between devices, exchange(): lax.ppermute(pair[0], 'ring', self.right)  39.5 us
    ppermute x24, waiting for transfers between devices, exchange(): lax.ppermute(pair[0], 'ring', self.right)  36.8 us
    ppermute x24, waiting for transfers between devices, exchange(): lax.ppermute(pair[1], 'ring', self.left)  23.1 us
    ppermute x13, starting transfers between devices, across(): return lax.ppermute(value, 'rep', SWAP)  16.9 us
    ppermute x24, starting transfers between devices, exchange(): lax.ppermute(pair[1], 'ring', self.left)  13.1 us
    ppermute x13, waiting for transfers between devices, across(): return lax.ppermute(value, 'rep', SWAP)  5.7 us
  transfers between devices with their start and end apart: 74, of which 33 were waited for; matrix products, arithmetic and copies ran while one was open for 1% of the time, Pallas kernels for 22%

profile of v4, /device:TPU:0, one launch (start us, length us, event | category | flops | bytes accessed | tf_op | source)
XLA Modules:
  0.0 193.7 jit_solution(14128781336146602519)
XLA Ops:
  7.0 2.7 %collective-permute-start.1 = (bf16[128,1024]{1,0:T(8,128)(2,1)S(1)}, bf16[128,1024]{1,0:T(8,128)(2,1)S(1)}, u32[]{:S(2)}, u32[]{:S(2)}) collective-permute-start(bf16[128,1024]{1,0:T(8,128)(2,1)S(1)} %constant_dynamic-update-slice_fusion.refs_4_.refs_0_), channel_id=1, source_target_pairs={{0,4},{4,8},{8,12},{12,14},{14,10},{10,6},{6,2},{2,0},{1,5},{5,9},... | collective-permute-start | bytes 786440 | tf_op jit(solution)/shard_map/ppermute | solution.py:88
  12.2 2.0 %collective-permute-start.12 = (bf16[88,1024]{1,0:T(8,128)(2,1)S(1)}, bf16[88,1024]{1,0:T(8,128)(2,1)S(1)}, u32[]{:S(2)}, u32[]{:S(2)}) collective-permute-start(bf16[88,1024]{1,0:T(8,128)(2,1)S(1)} %get-tuple-element.305.refs_1_), channel_id=1, source_target_pairs={{4,0},{8,4},{12,8},{14,12},{10,14},{6,10},{2,6},{0,2},{5,1},{9,5},... | collective-permute-start | bytes 540680 | tf_op jit(solution)/shard_map/ppermute | solution.py:88
  14.2 2.3 %collective-permute-done.1.refs_10_.refs_6_ = bf16[128,1024]{1,0:T(8,128)(2,1)S(1)} collective-permute-done((bf16[128,1024]{1,0:T(8,128)(2,1)S(1)}, bf16[128,1024]{1,0:T(8,128)(2,1)S(1)}, u32[]{:S(2)}, u32[]{:S(2)}) %collective-permute-start.1) | collective-permute-done | bytes 262176 | tf_op jit(solution)/shard_map/ppermute | solution.py:88
  16.5 1.8 collective-permute-start.11
  22.5 5.9 %collective-permute-done.6.refs_9_.refs_5_ = bf16[128,1024]{1,0:T(8,128)(2,1)S(1)} collective-permute-done((bf16[128,1024]{1,0:T(8,128)(2,1)S(1)}, bf16[128,1024]{1,0:T(8,128)(2,1)S(1)}, u32[]{:S(2)}, u32[]{:S(2)}) %collective-permute-start.6) | collective-permute-done | bytes 262176 | tf_op jit(solution)/shard_map/ppermute | solution.py:88
  33.9 3.6 %collective-permute-done.8.refs_8_.refs_4_ = bf16[128,1024]{1,0:T(8,128)(2,1)S(1)} collective-permute-done((bf16[128,1024]{1,0:T(8,128)(2,1)S(1)}, bf16[128,1024]{1,0:T(8,128)(2,1)S(1)}, u32[]{:S(2)}, u32[]{:S(2)}) %collective-permute-start.8) | collective-permute-done | bytes 262176 | tf_op jit(solution)/shard_map/ppermute | solution.py:88
  41.3 6.4 %collective-permute-done.15.refs_12_.refs_8_ = bf16[64,1024]{1,0:T(8,128)(2,1)S(1)} collective-permute-done((bf16[64,1024]{1,0:T(8,128)(2,1)S(1)}, bf16[64,1024]{1,0:T(8,128)(2,1)S(1)}, u32[]{:S(2)}, u32[]{:S(2)}) %collective-permute-start.15) | collective-permute-done | bytes 131104 | tf_op jit(solution)/shard_map/ppermute | solution.py:88
  54.0 7.0 %attention.1 = (bf16[4,128,256]{2,1,0:T(8,128)(2,1)S(1)}, bf16[512,1024]{1,0:T(8,128)(2,1)S(1)}, bf16[512,768]{1,0:T(8,128)(2,1)S(1)}, f32[16,128,128]{2,1,0:T(8,128)S(1)}, bf16[1024,768]{1,0:T(8,128)(2,1)S(1)}) custom-call(s32[21]{0:T(128)S(1)} %dynamic-slice_bitcast_fusion.scal, bf16[130,1024]{1,0:T(8,128)(2,1)S(1)} %pack_tokens.1.refs_0_.block_ref, ...), custom_call_target="tpu_custom_call" | custom-call | flops 805306368 | bytes 8142932 | tf_op jit(solution)/shard_map/attention/pallas_call | solution.py:161
  67.3 5.9 %collective-permute-done.27.refs_5_ = bf16[88,1024]{1,0:T(8,128)(2,1)S(1)} collective-permute-done((bf16[88,1024]{1,0:T(8,128)(2,1)S(1)}, bf16[88,1024]{1,0:T(8,128)(2,1)S(1)}, u32[]{:S(2)}, u32[]{:S(2)}) %collective-permute-start.27) | collective-permute-done | bytes 180256 | tf_op jit(solution)/shard_map/ppermute | solution.py:88
  75.2 2.1 %collective-permute-start.30 = (bf16[64,1536]{1,0:T(8,128)(2,1)S(1)}, bf16[64,1536]{1,0:T(8,128)(2,1)S(1)}, u32[]{:S(2)}, u32[]{:S(2)}) collective-permute-start(bf16[64,1536]{1,0:T(8,128)(2,1)S(1)} %slice.66), channel_id=1, source_target_pairs={{0,4},{4,8},{8,12},{12,14},{14,10},{10,6},{6,2},{2,0},{1,5},{5,9},... | collective-permute-start | bytes 589832 | tf_op jit(solution)/shard_map/ppermute | solution.py:88
  77.4 2.2 %collective-permute-start.32 = (bf16[48,1024]{1,0:T(8,128)(2,1)S(1)}, bf16[48,1024]{1,0:T(8,128)(2,1)S(1)}, u32[]{:S(2)}, u32[]{:S(2)}) collective-permute-start(bf16[48,1024]{1,0:T(8,128)(2,1)S(1)} %slice.68), channel_id=1, source_target_pairs={{0,4},{4,8},{8,12},{12,14},{14,10},{10,6},{6,2},{2,0},{1,5},{5,9},... | collective-permute-start | bytes 294920 | tf_op jit(solution)/shard_map/ppermute | solution.py:88
  79.6 2.7 %middle.1 = (f32[512,1024]{1,0:T(8,128)S(1)}, bf16[512,1024]{1,0:T(8,128)(2,1)S(1)}, bf16[512,1024]{1,0:T(8,128)(2,1)S(1)}, bf16[256,1024]{1,0:T(8,128)(2,1)S(1)}) custom-call(s32[21]{0:T(128)S(1)} %dynamic-slice_bitcast_fusion.scal, bf16[130,1024]{1,0:T(8,128)(2,1)S(1)} %pack_tokens.1.refs_0_.block_ref, ...), custom_call_target="tpu_custom_call" | custom-call | flops 1073741824 | bytes 8929364 | tf_op jit(solution)/shard_map/middle/pallas_call | solution.py:161
  82.3 2.3 %collective-permute-done.33.refs_9_ = bf16[40,1024]{1,0:T(8,128)(2,1)S(1)} collective-permute-done((bf16[40,1024]{1,0:T(8,128)(2,1)S(1)}, bf16[40,1024]{1,0:T(8,128)(2,1)S(1)}, u32[]{:S(2)}, u32[]{:S(2)}) %collective-permute-start.33) | collective-permute-done | bytes 81952 | tf_op jit(solution)/shard_map/ppermute | solution.py:88
  84.7 2.9 %hidden_units.1 = (f32[512,768]{1,0:T(8,128)S(1)}, f32[512,768]{1,0:T(8,128)S(1)}, bf16[512,768]{1,0:T(8,128)(2,1)S(1)}, bf16[1024,1536]{1,0:T(8,128)(2,1)S(1)}) custom-call(s32[21]{0:T(128)S(1)} %dynamic-slice_bitcast_fusion.scal, bf16[512,1024]{1,0:T(8,128)(2,1)S(1)} %get-tuple-element.277.h2_ref, ...), custom_call_target="tpu_custom_call" | custom-call | flops 1610612736 | bytes 11272276 | tf_op jit(solution)/shard_map/hidden_units/pallas_call | solution.py:161
  87.6 2.4 %grad_down_parts.1 = (bf16[88,1024]{1,0:T(8,128)(2,1)S(1)}, bf16[88,1024]{1,0:T(8,128)(2,1)S(1)}, bf16[88,1024]{1,0:T(8,128)(2,1)S(1)}, bf16[88,1024]{1,0:T(8,12...) custom-call(s32[21]{0:T(128)S(1)} %dynamic-slice_bitcast_fusion.scal, ...), custom_call_target="tpu_custom_call" | custom-call | flops 805306368 | bytes 4325460 | tf_op jit(solution)/shard_map/grad_down_parts/pallas_call | solution.py:161
  92.3 4.8 %hidden_back.1 = (bf16[512,1536]{1,0:T(8,128)(2,1)S(1)}, f32[2,128,1024]{2,1,0:T(8,128)S(1)}, bf16[2,128,1024]{2,1,0:T(8,128)(2,1)S(1)}, bf16[768,1024]{1,0:T(8,128)(2,1)S(1)}) custom-call(s32[21]{0:T(128)S(1)} %dynamic-slice_bitcast_fusion.scal, bf16[512,1024]{1,0:T(8,128)(2,1)S(1)} %get-tuple-element.304.refs_0_, ...), custom_call_target="tpu_custom_call" | custom-call | flops 2415919104 | bytes 13500500 | tf_op jit(solution)/shard_map/hidden_back/pallas_call | solution.py:161
  97.5 1.8 collective-permute-start.38
  101.3 4.0 %grad_in_parts.1 = (bf16[128,1536]{1,0:T(8,128)(2,1)S(1)}, bf16[128,1536]{1,0:T(8,128)(2,1)S(1)}, bf16[128,1536]{1,0:T(8,128)(2,1)S(1)}, bf16[128,1536]{1,0:T(8,...) custom-call(s32[21]{0:T(128)S(1)} %dynamic-slice_bitcast_fusion.scal, ...), custom_call_target="tpu_custom_call" | custom-call | flops 1610612736 | bytes 5767252 | tf_op jit(solution)/shard_map/grad_in_parts/pallas_call | solution.py:161
  106.0 2.0 %collective-permute-done.40.far_first = bf16[128,1024]{1,0:T(8,128)(2,1)S(1)} collective-permute-done((bf16[128,1024]{1,0:T(8,128)(2,1)S(1)}, bf16[128,1024]{1,0:T(8,128)(2,1)S(1)}, u32[]{:S(2)}, u32[]{:S(2)}) %collective-permute-start.40) | collective-permute-done | bytes 262176 | tf_op jit(solution)/shard_map/ppermute | solution.py:50
  111.7 1.8 collective-permute-start.41
  113.8 2.1 %last_projection.1 = (f32[2,128,1024]{2,1,0:T(8,128)S(1)}, bf16[2,128,1024]{2,1,0:T(8,128)(2,1)S(1)}) custom-call(s32[21]{0:T(128)S(1)} %dynamic-slice_bitcast_fusion.scal, bf16[512,768]{1,0:T(8,128)(2,1)S(1)} %get-tuple-element.332.hid_ref, bf16[768,1024]{1,0:T(8,128)(2,1)S(1)} %get-tuple-element.333.down_ref), custom_call_target="tpu_custom_call" | custom-call | flops 805306368 | bytes 3932244 | tf_op jit(solution)/shard_map/last_projection/pallas_call | solution.py:161
  115.9 1.9 collective-permute-done.41.right_got
  119.4 1.8 collective-permute-start.47
  122.9 1.8 collective-permute-start.49
  125.0 7.0 %attention_back.1 = (bf16[512,768]{1,0:T(8,128)(2,1)S(1)}, bf16[512,1024]{1,0:T(8,128)(2,1)S(1)}, f32[2,128,1024]{2,1,0:T(8,128)S(1)}, bf16[2,128,1024]{2,1,0:T(8,128)(2,1)S(1)}) custom-call(s32[21]{0:T(128)S(1)} %dynamic-slice_bitcast_fusion.scal, bf16[2,128,1024]{2,1,0:T(8,128)(2,1)S(1)} %get-tuple-element.348.ga_own, ...), custom_call_target="tpu_custom_call" | custom-call | flops 1879048192 | bytes 8650836 | tf_op jit(solution)/shard_map/attention_back/pallas_call | solution.py:161
  136.5 2.1 %grad_first_parts.1 = (bf16[128,1024]{1,0:T(8,128)(2,1)S(1)}, bf16[128,1024]{1,0:T(8,128)(2,1)S(1)}, bf16[128,1024]{1,0:T(8,128)(2,1)S(1)}, bf16[128,1024]{1,0:T...) custom-call(s32[21]{0:T(128)S(1)} %dynamic-slice_bitcast_fusion.scal, ...), custom_call_target="tpu_custom_call" | custom-call | flops 1073741824 | bytes 6029396 | tf_op jit(solution)/shard_map/grad_first_parts/pallas_call | solution.py:161
  141.7 2.2 %collective-permute-done.54.right_got = bf16[128,1536]{1,0:T(8,128)(2,1)S(1)} collective-permute-done((bf16[128,1536]{1,0:T(8,128)(2,1)S(1)}, bf16[128,1536]{1,0:T(8,128)(2,1)S(1)}, u32[]{:S(2)}, u32[]{:S(2)}) %collective-permute-start.54) | collective-permute-done | bytes 393248 | tf_op jit(solution)/shard_map/ppermute | solution.py:88
  152.3 4.9 %collective-permute-done.58.right_got = bf16[128,1024]{1,0:T(8,128)(2,1)S(1)} collective-permute-done((bf16[128,1024]{1,0:T(8,128)(2,1)S(1)}, bf16[128,1024]{1,0:T(8,128)(2,1)S(1)}, u32[]{:S(2)}, u32[]{:S(2)}) %collective-permute-start.58) | collective-permute-done | bytes 262176 | tf_op jit(solution)/shard_map/ppermute | solution.py:88
  162.3 3.4 %collective-permute-done.63.right_ref = bf16[128,1536]{1,0:T(8,128)(2,1)S(1)} collective-permute-done((bf16[128,1536]{1,0:T(8,128)(2,1)S(1)}, bf16[128,1536]{1,0:T(8,128)(2,1)S(1)}, u32[]{:S(2)}, u32[]{:S(2)}) %collective-permute-start.63) | collective-permute-done | bytes 393248 | tf_op jit(solution)/shard_map/ppermute | solution.py:88
  174.1 4.0 %collective-permute-done.67.right_ref = bf16[128,1024]{1,0:T(8,128)(2,1)S(1)} collective-permute-done((bf16[128,1024]{1,0:T(8,128)(2,1)S(1)}, bf16[128,1024]{1,0:T(8,128)(2,1)S(1)}, u32[]{:S(2)}, u32[]{:S(2)}) %collective-permute-start.67) | collective-permute-done | bytes 262176 | tf_op jit(solution)/shard_map/ppermute | solution.py:88
  187.0 2.4 %unpack_in.1 = f32[64,5632]{1,0:T(8,128)} custom-call(s32[21]{0:T(128)S(1)} %dynamic-slice_bitcast_fusion.scal, bf16[64,1536]{1,0:T(8,128)(2,1)S(1)} %get-tuple-element.430.own_ref, bf16[64,1536]{1,0:T(8,128)(2,1)S(1)} %collective-permute-done.65.near_ref, bf16[64,1536]{1,0:T(8,128)(2,1)S(1)} %collective-permute-done.69.far_ref, ...), custom_call_target="tpu_custom_call" | custom-call | bytes 2228308 | tf_op jit(solution)/shard_map/unpack_in/pallas_call | solution.py:161
  189.8 2.4 %collective-permute-done.72.diagonal_ref = bf16[64,1024]{1,0:T(8,128)(2,1)S(1)} collective-permute-done((bf16[64,1024]{1,0:T(8,128)(2,1)S(1)}, bf16[64,1024]{1,0:T(8,128)(2,1)S(1)}, u32[]{:S(2)}, u32[]{:S(2)}) %collective-permute-start.72) | collective-permute-done | bytes 131104 | tf_op jit(solution)/shard_map/ppermute | solution.py:50
  (189 shorter events, 89.7 us)
Async XLA Ops:
  6.6 12.3 %collective-permute-start.4 = (bf16[130,1024]{1,0:T(8,128)(2,1)S(1)}, bf16[130,1024]{1,0:T(8,128)(2,1)S(1)}, u32[]{:S(2)}, u32[]{:S(2)}) collective-permute-start(bf16[130,1024]{1,0:T(8,128)(2,1)S(1)} %pack_tokens.1.refs_0_.block_ref), channel_id=1, source_target_pairs={{0,1},{1,0},{2,3},{3,2},{4,5},{5,4},{6,7},{7,6},{8,9},{9,8},{10,11... | collective-permute-start | bytes 798728 | tf_op jit(solution)/shard_map/ppermute | solution.py:54
  7.0 9.5 %collective-permute-start.1 = (bf16[128,1024]{1,0:T(8,128)(2,1)S(1)}, bf16[128,1024]{1,0:T(8,128)(2,1)S(1)}, u32[]{:S(2)}, u32[]{:S(2)}) collective-permute-start(bf16[128,1024]{1,0:T(8,128)(2,1)S(1)} %constant_dynamic-update-slice_fusion.refs_4_.refs_0_), channel_id=1, source_target_pairs={{0,4},{4,8},{8,12},{12,14},{14,10},{10,6},{6,2},{2,0},{1,5},{5,9},... | collective-permute-start | bytes 786440 | tf_op jit(solution)/shard_map/ppermute | solution.py:88
  12.2 18.1 %collective-permute-start.12 = (bf16[88,1024]{1,0:T(8,128)(2,1)S(1)}, bf16[88,1024]{1,0:T(8,128)(2,1)S(1)}, u32[]{:S(2)}, u32[]{:S(2)}) collective-permute-start(bf16[88,1024]{1,0:T(8,128)(2,1)S(1)} %get-tuple-element.305.refs_1_), channel_id=1, source_target_pairs={{4,0},{8,4},{12,8},{14,12},{10,14},{6,10},{2,6},{0,2},{5,1},{9,5},... | collective-permute-start | bytes 540680 | tf_op jit(solution)/shard_map/ppermute | solution.py:88
  16.5 13.9 %collective-permute-start.11 = (bf16[88,1024]{1,0:T(8,128)(2,1)S(1)}, bf16[88,1024]{1,0:T(8,128)(2,1)S(1)}, u32[]{:S(2)}, u32[]{:S(2)}) collective-permute-start(bf16[88,1024]{1,0:T(8,128)(2,1)S(1)} %get-tuple-element.305.refs_1_), channel_id=1, source_target_pairs={{0,4},{4,8},{8,12},{12,14},{14,10},{10,6},{6,2},{2,0},{1,5},{5,9},... | collective-permute-start | bytes 540680 | tf_op jit(solution)/shard_map/ppermute | solution.py:88
  18.9 9.4 %collective-permute-start.6 = (bf16[128,1024]{1,0:T(8,128)(2,1)S(1)}, bf16[128,1024]{1,0:T(8,128)(2,1)S(1)}, u32[]{:S(2)}, u32[]{:S(2)}) collective-permute-start(bf16[128,1024]{1,0:T(8,128)(2,1)S(1)} %collective-permute-done.1.refs_10_.refs_6_), channel_id=1, source_target_pairs={{0,4},{4,8},{8,12},{12,14},{14,10},{10,6},{6,2},{2,0},{1,5},{5,9},... | collective-permute-start | bytes 786440 | tf_op jit(solution)/shard_map/ppermute | solution.py:88
  20.9 9.5 %collective-permute-start.10 = (bf16[130,1024]{1,0:T(8,128)(2,1)S(1)}, bf16[130,1024]{1,0:T(8,128)(2,1)S(1)}, u32[]{:S(2)}, u32[]{:S(2)}) collective-permute-start(bf16[130,1024]{1,0:T(8,128)(2,1)S(1)} %pack_tokens.1.refs_0_.block_ref), channel_id=1, source_target_pairs={{0,16},{16,0},{1,17},{17,1},{2,18},{18,2},{3,19},{19,3},{4,20},{20... | collective-permute-start | bytes 798728 | tf_op jit(solution)/shard_map/ppermute | solution.py:50
  31.9 15.8 %collective-permute-start.16 = (bf16[128,1536]{1,0:T(8,128)(2,1)S(1)}, bf16[128,1536]{1,0:T(8,128)(2,1)S(1)}, u32[]{:S(2)}, u32[]{:S(2)}) collective-permute-start(bf16[128,1536]{1,0:T(8,128)(2,1)S(1)} %constant_dynamic-update-slice_fusion.2.refs_0_), channel_id=1, source_target_pairs={{0,4},{4,8},{8,12},{12,14},{14,10},{10,6},{6,2},{2,0},{1,5},{5,9},... | collective-permute-start | bytes 1179656 | tf_op jit(solution)/shard_map/ppermute | solution.py:88
  33.5 14.2 %collective-permute-start.17 = (bf16[128,1536]{1,0:T(8,128)(2,1)S(1)}, bf16[128,1536]{1,0:T(8,128)(2,1)S(1)}, u32[]{:S(2)}, u32[]{:S(2)}) collective-permute-start(bf16[128,1536]{1,0:T(8,128)(2,1)S(1)} %constant_dynamic-update-slice_fusion.2.refs_0_), channel_id=1, source_target_pairs={{4,0},{8,4},{12,8},{14,12},{10,14},{6,10},{2,6},{0,2},{5,1},{9,5},... | collective-permute-start | bytes 1179656 | tf_op jit(solution)/shard_map/ppermute | solution.py:88
  47.7 14.0 %collective-permute-start.19 = (bf16[128,1536]{1,0:T(8,128)(2,1)S(1)}, bf16[128,1536]{1,0:T(8,128)(2,1)S(1)}, u32[]{:S(2)}, u32[]{:S(2)}) collective-permute-start(bf16[128,1536]{1,0:T(8,128)(2,1)S(1)} %collective-permute-done.16.refs_6_), channel_id=1, source_target_pairs={{0,4},{4,8},{8,12},{12,14},{14,10},{10,6},{6,2},{2,0},{1,5},{5,9},... | collective-permute-start | bytes 1179656 | tf_op jit(solution)/shard_map/ppermute | solution.py:88
  49.3 12.4 %collective-permute-start.20 = (bf16[128,1536]{1,0:T(8,128)(2,1)S(1)}, bf16[128,1536]{1,0:T(8,128)(2,1)S(1)}, u32[]{:S(2)}, u32[]{:S(2)}) collective-permute-start(bf16[128,1536]{1,0:T(8,128)(2,1)S(1)} %collective-permute-done.17.refs_1_), channel_id=1, source_target_pairs={{4,0},{8,4},{12,8},{14,12},{10,14},{6,10},{2,6},{0,2},{5,1},{9,5},... | collective-permute-start | bytes 1179656 | tf_op jit(solution)/shard_map/ppermute | solution.py:88
  50.4 16.4 %collective-permute-start.24 = (bf16[1024,256]{1,0:T(8,128)(2,1)S(1)}, bf16[1024,256]{1,0:T(8,128)(2,1)S(1)}, u32[]{:S(2)}, u32[]{:S(2)}) collective-permute-start(bf16[1024,256]{1,0:T(8,128)(2,1)S(1)} %gather_out.1.refs_6_), channel_id=1, source_target_pairs={{0,16},{16,0},{1,17},{17,1},{2,18},{18,2},{3,19},{19,3},{4,20},{20... | collective-permute-start | bytes 1572872 | tf_op jit(solution)/shard_map/ppermute | solution.py:50
  61.7 12.8 %collective-permute-start.25 = (bf16[128,1536]{1,0:T(8,128)(2,1)S(1)}, bf16[128,1536]{1,0:T(8,128)(2,1)S(1)}, u32[]{:S(2)}, u32[]{:S(2)}) collective-permute-start(bf16[128,1536]{1,0:T(8,128)(2,1)S(1)} %collective-permute-done.19.refs_5_), channel_id=1, source_target_pairs={{0,4},{4,8},{8,12},{12,14},{14,10},{10,6},{6,2},{2,0},{1,5},{5,9},... | collective-permute-start | bytes 1179656 | tf_op jit(solution)/shard_map/ppermute | solution.py:88
  63.3 11.2 %collective-permute-start.26 = (bf16[128,1536]{1,0:T(8,128)(2,1)S(1)}, bf16[128,1536]{1,0:T(8,128)(2,1)S(1)}, u32[]{:S(2)}, u32[]{:S(2)}) collective-permute-start(bf16[128,1536]{1,0:T(8,128)(2,1)S(1)} %collective-permute-done.20.refs_2_), channel_id=1, source_target_pairs={{4,0},{8,4},{12,8},{14,12},{10,14},{6,10},{2,6},{0,2},{5,1},{9,5},... | collective-permute-start | bytes 1179656 | tf_op jit(solution)/shard_map/ppermute | solution.py:88
  63.8 10.7 %collective-permute-start.23 = (bf16[4,128,256]{2,1,0:T(8,128)(2,1)S(1)}, bf16[4,128,256]{2,1,0:T(8,128)(2,1)S(1)}, u32[]{:S(2)}, u32[]{:S(2)}) collective-permute-start(bf16[4,128,256]{2,1,0:T(8,128)(2,1)S(1)} %get-tuple-element.262.refs_4_), channel_id=1, source_target_pairs={{0,16},{16,0},{1,17},{17,1},{2,18},{18,2},{3,19},{19,3},{4,20},{20... | collective-permute-start | bytes 786440 | tf_op jit(solution)/shard_map/ppermute | solution.py:50
  74.7 9.9 %collective-permute-start.31 = (bf16[64,1536]{1,0:T(8,128)(2,1)S(1)}, bf16[64,1536]{1,0:T(8,128)(2,1)S(1)}, u32[]{:S(2)}, u32[]{:S(2)}) collective-permute-start(bf16[64,1536]{1,0:T(8,128)(2,1)S(1)} %slice.67), channel_id=1, source_target_pairs={{4,0},{8,4},{12,8},{14,12},{10,14},{6,10},{2,6},{0,2},{5,1},{9,5},... | collective-permute-start | bytes 589832 | tf_op jit(solution)/shard_map/ppermute | solution.py:88
  75.2 9.4 %collective-permute-start.30 = (bf16[64,1536]{1,0:T(8,128)(2,1)S(1)}, bf16[64,1536]{1,0:T(8,128)(2,1)S(1)}, u32[]{:S(2)}, u32[]{:S(2)}) collective-permute-start(bf16[64,1536]{1,0:T(8,128)(2,1)S(1)} %slice.66), channel_id=1, source_target_pairs={{0,4},{4,8},{8,12},{12,14},{14,10},{10,6},{6,2},{2,0},{1,5},{5,9},... | collective-permute-start | bytes 589832 | tf_op jit(solution)/shard_map/ppermute | solution.py:88
  108.0 11.3 %collective-permute-start.43 = (bf16[64,1536]{1,0:T(8,128)(2,1)S(1)}, bf16[64,1536]{1,0:T(8,128)(2,1)S(1)}, u32[]{:S(2)}, u32[]{:S(2)}) collective-permute-start(bf16[64,1536]{1,0:T(8,128)(2,1)S(1)} %get-tuple-element.344), channel_id=1, source_target_pairs={{0,4},{4,8},{8,12},{12,14},{14,10},{10,6},{6,2},{2,0},{1,5},{5,9},... | collective-permute-start | bytes 589832 | tf_op jit(solution)/shard_map/ppermute | solution.py:88
  109.8 9.5 %collective-permute-start.44 = (bf16[64,1536]{1,0:T(8,128)(2,1)S(1)}, bf16[64,1536]{1,0:T(8,128)(2,1)S(1)}, u32[]{:S(2)}, u32[]{:S(2)}) collective-permute-start(bf16[64,1536]{1,0:T(8,128)(2,1)S(1)} %get-tuple-element.345), channel_id=1, source_target_pairs={{4,0},{8,4},{12,8},{14,12},{10,14},{6,10},{2,6},{0,2},{5,1},{9,5},... | collective-permute-start | bytes 589832 | tf_op jit(solution)/shard_map/ppermute | solution.py:88
  119.4 14.8 %collective-permute-start.47 = (bf16[128,1536]{1,0:T(8,128)(2,1)S(1)}, bf16[128,1536]{1,0:T(8,128)(2,1)S(1)}, u32[]{:S(2)}, u32[]{:S(2)}) collective-permute-start(bf16[128,1536]{1,0:T(8,128)(2,1)S(1)} %get-tuple-element.359), channel_id=1, source_target_pairs={{0,4},{4,8},{8,12},{12,14},{14,10},{10,6},{6,2},{2,0},{1,5},{5,9},... | collective-permute-start | bytes 1179656 | tf_op jit(solution)/shard_map/ppermute | solution.py:88
  121.2 13.0 %collective-permute-start.48 = (bf16[128,1536]{1,0:T(8,128)(2,1)S(1)}, bf16[128,1536]{1,0:T(8,128)(2,1)S(1)}, u32[]{:S(2)}, u32[]{:S(2)}) collective-permute-start(bf16[128,1536]{1,0:T(8,128)(2,1)S(1)} %get-tuple-element.360), channel_id=1, source_target_pairs={{4,0},{8,4},{12,8},{14,12},{10,14},{6,10},{2,6},{0,2},{5,1},{9,5},... | collective-permute-start | bytes 1179656 | tf_op jit(solution)/shard_map/ppermute | solution.py:88
  122.9 9.8 %collective-permute-start.49 = (bf16[88,1024]{1,0:T(8,128)(2,1)S(1)}, bf16[88,1024]{1,0:T(8,128)(2,1)S(1)}, u32[]{:S(2)}, u32[]{:S(2)}) collective-permute-start(bf16[88,1024]{1,0:T(8,128)(2,1)S(1)} %get-tuple-element.365), channel_id=1, source_target_pairs={{0,4},{4,8},{8,12},{12,14},{14,10},{10,6},{6,2},{2,0},{1,5},{5,9},... | collective-permute-start | bytes 540680 | tf_op jit(solution)/shard_map/ppermute | solution.py:88
  124.7 9.5 %collective-permute-start.50 = (bf16[88,1024]{1,0:T(8,128)(2,1)S(1)}, bf16[88,1024]{1,0:T(8,128)(2,1)S(1)}, u32[]{:S(2)}, u32[]{:S(2)}) collective-permute-start(bf16[88,1024]{1,0:T(8,128)(2,1)S(1)} %get-tuple-element.366), channel_id=1, source_target_pairs={{4,0},{8,4},{12,8},{14,12},{10,14},{6,10},{2,6},{0,2},{5,1},{9,5},... | collective-permute-start | bytes 540680 | tf_op jit(solution)/shard_map/ppermute | solution.py:88
  134.4 9.6 %collective-permute-start.54 = (bf16[128,1536]{1,0:T(8,128)(2,1)S(1)}, bf16[128,1536]{1,0:T(8,128)(2,1)S(1)}, u32[]{:S(2)}, u32[]{:S(2)}) collective-permute-start(bf16[128,1536]{1,0:T(8,128)(2,1)S(1)} %get-tuple-element.381), channel_id=1, source_target_pairs={{0,4},{4,8},{8,12},{12,14},{14,10},{10,6},{6,2},{2,0},{1,5},{5,9},... | collective-permute-start | bytes 1179656 | tf_op jit(solution)/shard_map/ppermute | solution.py:88
  136.1 9.5 %collective-permute-start.55 = (bf16[128,1536]{1,0:T(8,128)(2,1)S(1)}, bf16[128,1536]{1,0:T(8,128)(2,1)S(1)}, u32[]{:S(2)}, u32[]{:S(2)}) collective-permute-start(bf16[128,1536]{1,0:T(8,128)(2,1)S(1)} %get-tuple-element.382), channel_id=1, source_target_pairs={{4,0},{8,4},{12,8},{14,12},{10,14},{6,10},{2,6},{0,2},{5,1},{9,5},... | collective-permute-start | bytes 1179656 | tf_op jit(solution)/shard_map/ppermute | solution.py:88
  148.0 9.3 %collective-permute-start.58 = (bf16[128,1024]{1,0:T(8,128)(2,1)S(1)}, bf16[128,1024]{1,0:T(8,128)(2,1)S(1)}, u32[]{:S(2)}, u32[]{:S(2)}) collective-permute-start(bf16[128,1024]{1,0:T(8,128)(2,1)S(1)} %get-tuple-element.394), channel_id=1, source_target_pairs={{0,4},{4,8},{8,12},{12,14},{14,10},{10,6},{6,2},{2,0},{1,5},{5,9},... | collective-permute-start | bytes 786440 | tf_op jit(solution)/shard_map/ppermute | solution.py:88
  150.2 15.5 %collective-permute-start.63 = (bf16[128,1536]{1,0:T(8,128)(2,1)S(1)}, bf16[128,1536]{1,0:T(8,128)(2,1)S(1)}, u32[]{:S(2)}, u32[]{:S(2)}) collective-permute-start(bf16[128,1536]{1,0:T(8,128)(2,1)S(1)} %get-tuple-element.406), channel_id=1, source_target_pairs={{0,4},{4,8},{8,12},{12,14},{14,10},{10,6},{6,2},{2,0},{1,5},{5,9},... | collective-permute-start | bytes 1179656 | tf_op jit(solution)/shard_map/ppermute | solution.py:88
  152.0 15.4 %collective-permute-start.64 = (bf16[128,1536]{1,0:T(8,128)(2,1)S(1)}, bf16[128,1536]{1,0:T(8,128)(2,1)S(1)}, u32[]{:S(2)}, u32[]{:S(2)}) collective-permute-start(bf16[128,1536]{1,0:T(8,128)(2,1)S(1)} %get-tuple-element.407), channel_id=1, source_target_pairs={{4,0},{8,4},{12,8},{14,12},{10,14},{6,10},{2,6},{0,2},{5,1},{9,5},... | collective-permute-start | bytes 1179656 | tf_op jit(solution)/shard_map/ppermute | solution.py:88
  159.1 10.5 %collective-permute-start.61 = (bf16[128,1024]{1,0:T(8,128)(2,1)S(1)}, bf16[128,1024]{1,0:T(8,128)(2,1)S(1)}, u32[]{:S(2)}, u32[]{:S(2)}) collective-permute-start(bf16[128,1024]{1,0:T(8,128)(2,1)S(1)} %get-tuple-element.399), channel_id=1, source_target_pairs={{0,4},{4,8},{8,12},{12,14},{14,10},{10,6},{6,2},{2,0},{1,5},{5,9},... | collective-permute-start | bytes 786440 | tf_op jit(solution)/shard_map/ppermute | solution.py:88
  159.7 11.3 %collective-permute-start.62 = (bf16[128,1024]{1,0:T(8,128)(2,1)S(1)}, bf16[128,1024]{1,0:T(8,128)(2,1)S(1)}, u32[]{:S(2)}, u32[]{:S(2)}) collective-permute-start(bf16[128,1024]{1,0:T(8,128)(2,1)S(1)} %get-tuple-element.400), channel_id=1, source_target_pairs={{4,0},{8,4},{12,8},{14,12},{10,14},{6,10},{2,6},{0,2},{5,1},{9,5},... | collective-permute-start | bytes 786440 | tf_op jit(solution)/shard_map/ppermute | solution.py:88
  161.2 9.8 %collective-permute-start.66 = (bf16[128,1024]{1,0:T(8,128)(2,1)S(1)}, bf16[128,1024]{1,0:T(8,128)(2,1)S(1)}, u32[]{:S(2)}, u32[]{:S(2)}) collective-permute-start(bf16[128,1024]{1,0:T(8,128)(2,1)S(1)} %fusion.3), channel_id=1, source_target_pairs={{0,16},{16,0},{1,17},{17,1},{2,18},{18,2},{3,19},{19,3},{4,20},{20... | collective-permute-start | bytes 786440 | tf_op jit(solution)/shard_map/ppermute | solution.py:50
  180.3 9.4 %collective-permute-start.71 = (bf16[64,1024]{1,0:T(8,128)(2,1)S(1)}, bf16[64,1024]{1,0:T(8,128)(2,1)S(1)}, u32[]{:S(2)}, u32[]{:S(2)}) collective-permute-start(bf16[64,1024]{1,0:T(8,128)(2,1)S(1)} %get-tuple-element.426.own_ref), channel_id=1, source_target_pairs={{0,16},{16,0},{1,17},{17,1},{2,18},{18,2},{3,19},{19,3},{4,20},{20... | collective-permute-start | bytes 393224 | tf_op jit(solution)/shard_map/ppermute | solution.py:50
  181.3 10.8 %collective-permute-start.72 = (bf16[64,1024]{1,0:T(8,128)(2,1)S(1)}, bf16[64,1024]{1,0:T(8,128)(2,1)S(1)}, u32[]{:S(2)}, u32[]{:S(2)}) collective-permute-start(bf16[64,1024]{1,0:T(8,128)(2,1)S(1)} %collective-permute-done.70.near_ref), channel_id=1, source_target_pairs={{0,16},{16,0},{1,17},{17,1},{2,18},{18,2},{3,19},{19,3},{4,20},{20... | collective-permute-start | bytes 393224 | tf_op jit(solution)/shard_map/ppermute | solution.py:50
  (52 other events, 447.5 us)

commit v5 on v4

--- a/solution.py
+++ b/solution.py
@@ -13,10 +13,12 @@
 HALF = HD // 2
 LANES = 128
 PACK = 16
+ROWS = 8
 BF = jnp.bfloat16
 F32 = jnp.float32
 SWAP = ((0, 1), (1, 0))
 MIB = 1 << 20
+WEIGHT = {'ring_add': 16000000000, 'unpack_in': 4000000000, 'pack_in': 0, 'hidden_back': 32000000000, 'grad_first_parts': 32000000000, 'middle_back': 8000000000, 'hidden_units': 16000000000}
 BLOCKS = ((0, 1, 2, 3), (1, 0, 3, 2), (2, 3, 0, 1), (3, 2, 1, 0))
 
 
@@ -166,7 +168,7 @@
         out_specs=[pl.BlockSpec(memory_space=pltpu.VMEM)] * len(outs),
         scratch_shapes=scratch,
         compiler_params=pltpu.CompilerParams(vmem_limit_bytes=12 * MIB),
-        cost_estimate=pl.CostEstimate(flops=flops, bytes_accessed=nbytes, transcendentals=0),
+        cost_estimate=pl.CostEstimate(flops=WEIGHT.get(body.func.__name__, flops), bytes_accessed=nbytes, transcendentals=0),
     )(*args)
 
 
@@ -176,6 +178,26 @@
 
 def lanes(start, size):
     return pl.ds(pl.multiple_of(start, LANES), size)
+
+
+def tiles_of(extent, tile=256):
+    return [(at, min(tile, extent - at)) for at in range(0, extent, tile)]
+
+
+def main_part(units):
+    return units // LANES * LANES
+
+
+def runs(size, stride, piece):
+    units = size * stride
+    main = main_part(units)
+    rest = units - main
+    for g in range(size):
+        first = g * stride
+        for low, high in ((first, min(first + piece, main)), (max(first, main), first + piece)):
+            if low < high:
+                columns = tuple(p * main + low if low < main else 2 * main + p * rest + low - main for p in range(2))
+                yield g, low - first, high - low, columns
 
 
 def pack_tokens(rows, prefix_ref, tokens_ref, own_ref):
@@ -205,16 +227,16 @@
             rows_ref[...] = down_ref[r * piece : (r + 1) * piece, :]
 
     for ref, member in ((own_ref, scal[2 * size + 1]), (sib_ref, scal[2 * size + 2])):
-        ref[...] = jnp.zeros_like(ref)
+        if padded > piece:
+            ref[...] = jnp.zeros_like(ref)
         for q in range(4):
 
             @pl.when(member == q)
             def _(ref=ref, q=q):
-                for part in range(2):
-                    for g in range(size):
-                        start = part * units + (g * 4 + q) * piece
-                        to = (part * size + g) * padded
-                        ref[:, to : to + piece] = in_ref[:, start : start + piece]
+                for g, offset, length, columns in runs(size, padded, piece):
+                    for part in range(2):
+                        start = part * units + (g * 4 + q) * piece + offset
+                        ref[:, columns[part] : columns[part] + length] = in_ref[:, start : start + length]
 
 
 def place_chunks(size, scal, chunk_refs, store):
@@ -338,16 +360,20 @@
         w_ref[pl.ds(row, shard_rows), :] = value
 
     place_rows(size, shard_rows, scal, chunks, put)
-    tile = 256
-
-    @pl.loop(0, members_units // tile)
-    def _(i):
-        at = pl.multiple_of(i * tile, tile)
-        up = dot(h2_ref[...], w_ref[:, pl.ds(at, tile)])
-        gate = dot(h2_ref[...], w_ref[:, pl.ds(members_units + at, tile)])
-        up_ref[:, pl.ds(at, tile)] = up
-        gate_ref[:, pl.ds(at, tile)] = gate
-        hid_ref[:, pl.ds(at, tile)] = (gate * jax.nn.sigmoid(gate) * up).astype(BF)
+    main = main_part(members_units)
+    rest = members_units - main
+
+    def put_units(columns, up, gate):
+        up_ref[:, columns] = up
+        gate_ref[:, columns] = gate
+        hid_ref[:, columns] = (gate * jax.nn.sigmoid(gate) * up).astype(BF)
+
+    for at, tile in tiles_of(main):
+        up = dot(h2_ref[...], w_ref[:, at : at + tile])
+        put_units(slice(at, at + tile), up, dot(h2_ref[...], w_ref[:, main + at : main + at + tile]))
+    if rest:
+        both = dot(h2_ref[...], w_ref[:, 2 * main :])
+        put_units(slice(main, members_units), both[:, :rest], both[:, rest:])
 
 
 def hidden_back(size, rows, padded, piece, n_chunks, scal, *refs):
@@ -356,23 +382,27 @@
     up_ref, gate_ref, w_in, ggu_ref, keep_ref, give_ref, down_ref = refs[1 + n_chunks :]
     units = up_ref.shape[1]
     width = gm_ref.shape[1]
-    down_ref[...] = jnp.zeros_like(down_ref)
+    if padded > piece:
+        down_ref[...] = jnp.zeros_like(down_ref)
 
     def store(chip, first, value):
-        down_ref[pl.ds(pl.multiple_of(chip * padded + first, PACK), value.shape[0]), :] = value
+        down_ref[pl.ds(pl.multiple_of(chip * padded + first, ROWS), value.shape[0]), :] = value
 
     place_chunks(size, scal, chunks, store)
     tile = 256
 
-    @pl.loop(0, units // tile)
-    def _(i):
-        at = pl.multiple_of(i * tile, tile)
-        grad = dot_rt(gm_ref[...], down_ref[pl.ds(at, tile), :])
-        up = up_ref[:, pl.ds(at, tile)]
-        gate = gate_ref[:, pl.ds(at, tile)]
+    main = main_part(units)
+    rest = units - main
+    pieces = [(at, size_, at, main + at) for at, size_ in tiles_of(main)]
+    if rest:
+        pieces.append((main, rest, 2 * main, 2 * main + rest))
+    for at, count, up_at, gate_at in pieces:
+        grad = dot_rt(gm_ref[...], down_ref[at : at + count, :])
+        up = up_ref[:, at : at + count]
+        gate = gate_ref[:, at : at + count]
         sig = jax.nn.sigmoid(gate)
-        ggu_ref[:, pl.ds(at, tile)] = (grad * (gate * sig)).astype(BF)
-        ggu_ref[:, pl.ds(units + at, tile)] = (grad * up * (sig * (1.0 + gate * (1.0 - sig)))).astype(BF)
+        ggu_ref[:, up_at : up_at + count] = (grad * (gate * sig)).astype(BF)
+        ggu_ref[:, gate_at : gate_at + count] = (grad * up * (sig * (1.0 + gate * (1.0 - sig)))).astype(BF)
 
     @pl.loop(0, width // tile)
     def _(i):
@@ -399,7 +429,7 @@
 
 def write_parts(size, stride, scal, total, refs):
     for k, ref in enumerate(refs):
-        ref[...] = total[pl.ds(pl.multiple_of(scal[k] * stride, PACK), ref.shape[0]), :].astype(BF)
+        ref[...] = total[pl.ds(pl.multiple_of(scal[k] * stride, ROWS), ref.shape[0]), :].astype(BF)
 
 
 def grad_down_parts(size, rows, padded, scal, hid_ref, *refs):
@@ -418,13 +448,8 @@
 
 def grad_in_parts(size, double, scal, h2_ref, ggu_ref, *refs):
     total = refs[-1]
-    tile = 256
-
-    @pl.loop(0, ggu_ref.shape[1] // tile)
-    def _(i):
-        columns = pl.ds(pl.multiple_of(i * tile, tile), tile)
-        total[:, columns] = dot_lt(h2_ref[...], ggu_ref[:, columns])
-
+    for at, tile in tiles_of(ggu_ref.shape[1]):
+        total[:, at : at + tile] = dot_lt(h2_ref[...], ggu_ref[:, at : at + tile])
     write_parts(size, double, scal, total, refs[:-1])
 
 
@@ -516,11 +541,10 @@
     for m, ref in enumerate((own_ref, near_ref, far_ref, diagonal_ref)):
         held[scal[2 * size + 1 + m]] = ref[...].astype(F32)
     for q in range(4):
-        for part in range(2):
-            for g in range(size):
-                start = part * units + (g * 4 + q) * piece
-                frm = (part * size + g) * padded
-                in_ref[:, start : start + piece] = held[q, :, frm : frm + piece]
+        for g, offset, length, columns in runs(size, padded, piece):
+            for part in range(2):
+                start = part * units + (g * 4 + q) * piece + offset
+                in_ref[:, start : start + length] = held[q, :, columns[part] : columns[part] + length]
 
 
 def local(tokens, prefix, qkv_weight, out_weight, in_weight, down_weight, cotangent):
@@ -536,9 +560,9 @@
     quarter = width // 4
     heads = quarter // HD
     piece = units // (4 * size)
-    padded = -(-piece // PACK) * PACK
-    while size * padded % 256:
-        padded += PACK
+    padded = -(-piece // ROWS) * ROWS
+    while 2 * size * padded % LANES:
+        padded += ROWS
     member_units = size * padded
     chunks = size + 1
     table = scalar_table(size)
@@ -801,8 +825,11 @@
     down_other = across(down_low)
     y_got = sibling(y_give)
 
+    (grad_tokens,) = call(
+        functools.partial(finish_tokens, rows), [shape((rows, width), F32)], [], 0, scal, u1_keep, u1_got, u1_far, own, gx2
+    )
     while a.step < ring.half - 2:
-        a.got, down_other = sync(a.got, down_other)
+        a.got, down_other, grad_tokens = sync(a.got, down_other, grad_tokens)
         a.add()
         a.send()
     y_low = (y_keep[1] + y_got[1].astype(F32)).astype(BF)
@@ -824,10 +851,7 @@
     first_far = across(first_keep)
     first_near = sibling(first_give)
     first_diagonal = across(first_near)
-    u1_far, y_far, down_other, in_keep, first_near = sync(u1_far, y_far, down_other, in_keep, first_near)
-    (grad_tokens,) = call(
-        functools.partial(finish_tokens, rows), [shape((rows, width), F32)], [], 0, scal, u1_keep, u1_got, u1_far, own, gx2
-    )
+    y_far, down_other, in_keep, first_near = sync(y_far, down_other, in_keep, first_near)
     result = (x2[:rows] + (y_keep[0] + y_got[0].astype(F32) + y_far.astype(F32))).astype(BF)
     (grad_down,) = call(functools.partial(unpack_down, size, piece), [shape((2 * piece, width), F32)], [], 0, scal, down_low, down_other)
     (grad_in,) = call(

time: 194 us -> 188 us (0.969)
  starting transfers between devices: 71.7 us -> 68.2 us
    ppermute x13, starting transfers between devices: 16.9 us -> 13.6 us  [across(): return lax.ppermute(value, 'rep', SWAP)]
  transfers between devices with their start and end apart: 74 -> 74, of which waited for: 33 -> 36; matrix products, arithmetic and copies ran while one was open for 1% -> 1% of each run, Pallas kernels for 22% -> 22%
where the time goes in v5:
time: 188 us
  starting transfers between devices  68.2 us (36%)
  waiting for transfers between devices  65.8 us (35%)
  Pallas kernels  47 us (25%)
  local copies, waits for them, and re-layouts  4.6 us (2%)
    pallas_call x29, Pallas kernels, call(): pl.pallas_call(body, name=body.func.__name__, out_shape=outs, in_specs=[p...  47 us
    ppermute x24, starting transfers between devices, exchange(): lax.ppermute(pair[0], 'ring', self.right)  39.9 us
    ppermute x24, waiting for transfers between devices, exchange(): lax.ppermute(pair[0], 'ring', self.right)  36.8 us
    ppermute x24, waiting for transfers between devices, exchange(): lax.ppermute(pair[1], 'ring', self.left)  22.5 us
    ppermute x13, starting transfers between devices, across(): return lax.ppermute(value, 'rep', SWAP)  13.6 us
    ppermute x24, starting transfers between devices, exchange(): lax.ppermute(pair[1], 'ring', self.left)  12.7 us
    ppermute x13, waiting for transfers between devices, across(): return lax.ppermute(value, 'rep', SWAP)  4.39 us
  transfers between devices with their start and end apart: 74, of which 36 were waited for; matrix products, arithmetic and copies ran while one was open for 1% of the time, Pallas kernels for 22%

profile of v5, /device:TPU:0, one launch (start us, length us, event | category | flops | bytes accessed | tf_op | source)
XLA Modules:
  0.0 188.0 jit_solution(14172265323943268426)
XLA Ops:
  7.0 2.7 %collective-permute-start.1 = (bf16[128,1024]{1,0:T(8,128)(2,1)S(1)}, bf16[128,1024]{1,0:T(8,128)(2,1)S(1)}, u32[]{:S(2)}, u32[]{:S(2)}) collective-permute-start(bf16[128,1024]{1,0:T(8,128)(2,1)S(1)} %constant_dynamic-update-slice_fusion.refs_4_.refs_0_), channel_id=1, source_target_pairs={{0,4},{4,8},{8,12},{12,14},{14,10},{10,6},{6,2},{2,0},{1,5},{5,9},... | collective-permute-start | bytes 786440 | tf_op jit(solution)/shard_map/ppermute | solution.py:90
  12.4 2.0 %collective-permute-start.12 = (bf16[88,1024]{1,0:T(8,128)(2,1)S(1)}, bf16[88,1024]{1,0:T(8,128)(2,1)S(1)}, u32[]{:S(2)}, u32[]{:S(2)}) collective-permute-start(bf16[88,1024]{1,0:T(8,128)(2,1)S(1)} %get-tuple-element.305.refs_1_), channel_id=1, source_target_pairs={{4,0},{8,4},{12,8},{14,12},{10,14},{6,10},{2,6},{0,2},{5,1},{9,5},... | collective-permute-start | bytes 540680 | tf_op jit(solution)/shard_map/ppermute | solution.py:90
  14.3 2.1 %collective-permute-done.1.refs_10_.refs_6_ = bf16[128,1024]{1,0:T(8,128)(2,1)S(1)} collective-permute-done((bf16[128,1024]{1,0:T(8,128)(2,1)S(1)}, bf16[128,1024]{1,0:T(8,128)(2,1)S(1)}, u32[]{:S(2)}, u32[]{:S(2)}) %collective-permute-start.1) | collective-permute-done | bytes 262176 | tf_op jit(solution)/shard_map/ppermute | solution.py:90
  16.5 1.8 collective-permute-start.11
  22.5 5.9 %collective-permute-done.6.refs_9_.refs_5_ = bf16[128,1024]{1,0:T(8,128)(2,1)S(1)} collective-permute-done((bf16[128,1024]{1,0:T(8,128)(2,1)S(1)}, bf16[128,1024]{1,0:T(8,128)(2,1)S(1)}, u32[]{:S(2)}, u32[]{:S(2)}) %collective-permute-start.6) | collective-permute-done | bytes 262176 | tf_op jit(solution)/shard_map/ppermute | solution.py:90
  34.0 3.6 %collective-permute-done.8.refs_8_.refs_4_ = bf16[128,1024]{1,0:T(8,128)(2,1)S(1)} collective-permute-done((bf16[128,1024]{1,0:T(8,128)(2,1)S(1)}, bf16[128,1024]{1,0:T(8,128)(2,1)S(1)}, u32[]{:S(2)}, u32[]{:S(2)}) %collective-permute-start.8) | collective-permute-done | bytes 262176 | tf_op jit(solution)/shard_map/ppermute | solution.py:90
  41.3 2.5 %collective-permute-done.16.refs_6_ = bf16[128,1408]{1,0:T(8,128)(2,1)S(1)} collective-permute-done((bf16[128,1408]{1,0:T(8,128)(2,1)S(1)}, bf16[128,1408]{1,0:T(8,128)(2,1)S(1)}, u32[]{:S(2)}, u32[]{:S(2)}) %collective-permute-start.16) | collective-permute-done | bytes 360480 | tf_op jit(solution)/shard_map/ppermute | solution.py:90
  43.8 1.8 collective-permute-done.17.refs_1_
  53.2 7.0 %attention.1 = (bf16[4,128,256]{2,1,0:T(8,128)(2,1)S(1)}, bf16[512,1024]{1,0:T(8,128)(2,1)S(1)}, bf16[512,768]{1,0:T(8,128)(2,1)S(1)}, f32[16,128,128]{2,1,0:T(8,128)S(1)}, bf16[1024,768]{1,0:T(8,128)(2,1)S(1)}) custom-call(s32[21]{0:T(128)S(1)} %dynamic-slice_bitcast_fusion.scal, bf16[130,1024]{1,0:T(8,128)(2,1)S(1)} %pack_tokens.1.refs_0_.block_ref, ...), custom_call_target="tpu_custom_call" | custom-call | flops 805306368 | bytes 8142932 | tf_op jit(solution)/shard_map/attention/pallas_call | solution.py:163
  66.5 5.9 %collective-permute-done.27.refs_5_ = bf16[88,1024]{1,0:T(8,128)(2,1)S(1)} collective-permute-done((bf16[88,1024]{1,0:T(8,128)(2,1)S(1)}, bf16[88,1024]{1,0:T(8,128)(2,1)S(1)}, u32[]{:S(2)}, u32[]{:S(2)}) %collective-permute-start.27) | collective-permute-done | bytes 180256 | tf_op jit(solution)/shard_map/ppermute | solution.py:90
  74.5 2.1 %collective-permute-start.30 = (bf16[64,1408]{1,0:T(8,128)(2,1)S(1)}, bf16[64,1408]{1,0:T(8,128)(2,1)S(1)}, u32[]{:S(2)}, u32[]{:S(2)}) collective-permute-start(bf16[64,1408]{1,0:T(8,128)(2,1)S(1)} %slice.66), channel_id=1, source_target_pairs={{0,4},{4,8},{8,12},{12,14},{14,10},{10,6},{6,2},{2,0},{1,5},{5,9},... | collective-permute-start | bytes 540680 | tf_op jit(solution)/shard_map/ppermute | solution.py:90
  76.6 2.2 %collective-permute-start.32 = (bf16[48,1024]{1,0:T(8,128)(2,1)S(1)}, bf16[48,1024]{1,0:T(8,128)(2,1)S(1)}, u32[]{:S(2)}, u32[]{:S(2)}) collective-permute-start(bf16[48,1024]{1,0:T(8,128)(2,1)S(1)} %slice.68), channel_id=1, source_target_pairs={{0,4},{4,8},{8,12},{12,14},{14,10},{10,6},{6,2},{2,0},{1,5},{5,9},... | collective-permute-start | bytes 294920 | tf_op jit(solution)/shard_map/ppermute | solution.py:90
  78.9 2.7 %middle.1 = (f32[512,1024]{1,0:T(8,128)S(1)}, bf16[512,1024]{1,0:T(8,128)(2,1)S(1)}, bf16[512,1024]{1,0:T(8,128)(2,1)S(1)}, bf16[256,1024]{1,0:T(8,128)(2,1)S(1)}) custom-call(s32[21]{0:T(128)S(1)} %dynamic-slice_bitcast_fusion.scal, bf16[130,1024]{1,0:T(8,128)(2,1)S(1)} %pack_tokens.1.refs_0_.block_ref, ...), custom_call_target="tpu_custom_call" | custom-call | flops 1073741824 | bytes 8929364 | tf_op jit(solution)/shard_map/middle/pallas_call | solution.py:163
  81.6 1.9 %collective-permute-done.33.refs_9_ = bf16[40,1024]{1,0:T(8,128)(2,1)S(1)} collective-permute-done((bf16[40,1024]{1,0:T(8,128)(2,1)S(1)}, bf16[40,1024]{1,0:T(8,128)(2,1)S(1)}, u32[]{:S(2)}, u32[]{:S(2)}) %collective-permute-start.33) | collective-permute-done | bytes 81952 | tf_op jit(solution)/shard_map/ppermute | solution.py:90
  83.6 3.0 %hidden_units.1 = (f32[512,704]{1,0:T(8,128)S(1)}, f32[512,704]{1,0:T(8,128)S(1)}, bf16[512,704]{1,0:T(8,128)(2,1)S(1)}, bf16[1024,1408]{1,0:T(8,128)(2,1)S(1)}) custom-call(s32[21]{0:T(128)S(1)} %dynamic-slice_bitcast_fusion.scal, bf16[512,1024]{1,0:T(8,128)(2,1)S(1)} %get-tuple-element.277.h2_ref, ...), custom_call_target="tpu_custom_call" | custom-call | flops 16000000000 | bytes 10420308 | tf_op jit(solution)/shard_map/hidden_units/pallas_call | solution.py:163
  86.6 2.4 %grad_down_parts.1 = (bf16[88,1024]{1,0:T(8,128)(2,1)S(1)}, bf16[88,1024]{1,0:T(8,128)(2,1)S(1)}, bf16[88,1024]{1,0:T(8,128)(2,1)S(1)}, bf16[88,1024]{1,0:T(8,12...) custom-call(s32[21]{0:T(128)S(1)} %dynamic-slice_bitcast_fusion.scal, ...), custom_call_target="tpu_custom_call" | custom-call | flops 805306368 | bytes 4259924 | tf_op jit(solution)/shard_map/grad_down_parts/pallas_call | solution.py:163
  91.2 4.8 %hidden_back.1 = (bf16[512,1408]{1,0:T(8,128)(2,1)S(1)}, f32[2,128,1024]{2,1,0:T(8,128)S(1)}, bf16[2,128,1024]{2,1,0:T(8,128)(2,1)S(1)}, bf16[704,1024]{1,0:T(8,128)(2,1)S(1)}) custom-call(s32[21]{0:T(128)S(1)} %dynamic-slice_bitcast_fusion.scal, bf16[512,1024]{1,0:T(8,128)(2,1)S(1)} %get-tuple-element.304.refs_0_, ...), custom_call_target="tpu_custom_call" | custom-call | flops 32000000000 | bytes 12714068 | tf_op jit(solution)/shard_map/hidden_back/pallas_call | solution.py:163
  96.3 1.8 collective-permute-start.38
  100.1 2.7 %grad_in_parts.1 = (bf16[128,1408]{1,0:T(8,128)(2,1)S(1)}, bf16[128,1408]{1,0:T(8,128)(2,1)S(1)}, bf16[128,1408]{1,0:T(8,128)(2,1)S(1)}, bf16[128,1408]{1,0:T(8,...) custom-call(s32[21]{0:T(128)S(1)} %dynamic-slice_bitcast_fusion.scal, ...), custom_call_target="tpu_custom_call" | custom-call | flops 1610612736 | bytes 5374036 | tf_op jit(solution)/shard_map/grad_in_parts/pallas_call | solution.py:163
  104.8 2.0 %collective-permute-done.40.far_first = bf16[128,1024]{1,0:T(8,128)(2,1)S(1)} collective-permute-done((bf16[128,1024]{1,0:T(8,128)(2,1)S(1)}, bf16[128,1024]{1,0:T(8,128)(2,1)S(1)}, u32[]{:S(2)}, u32[]{:S(2)}) %collective-permute-start.40) | collective-permute-done | bytes 262176 | tf_op jit(solution)/shard_map/ppermute | solution.py:52
  108.5 1.8 collective-permute-start.41
  110.6 1.8 collective-permute-start.43
  112.6 2.1 %last_projection.1 = (f32[2,128,1024]{2,1,0:T(8,128)S(1)}, bf16[2,128,1024]{2,1,0:T(8,128)(2,1)S(1)}) custom-call(s32[21]{0:T(128)S(1)} %dynamic-slice_bitcast_fusion.scal, bf16[512,704]{1,0:T(8,128)(2,1)S(1)} %get-tuple-element.332.hid_ref, bf16[704,1024]{1,0:T(8,128)(2,1)S(1)} %get-tuple-element.333.down_ref), custom_call_target="tpu_custom_call" | custom-call | flops 805306368 | bytes 3735636 | tf_op jit(solution)/shard_map/last_projection/pallas_call | solution.py:163
  124.9 7.0 %attention_back.1 = (bf16[512,768]{1,0:T(8,128)(2,1)S(1)}, bf16[512,1024]{1,0:T(8,128)(2,1)S(1)}, f32[2,128,1024]{2,1,0:T(8,128)S(1)}, bf16[2,128,1024]{2,1,0:T(8,128)(2,1)S(1)}) custom-call(s32[21]{0:T(128)S(1)} %dynamic-slice_bitcast_fusion.scal, bf16[2,128,1024]{2,1,0:T(8,128)(2,1)S(1)} %get-tuple-element.348.ga_own, ...), custom_call_target="tpu_custom_call" | custom-call | flops 1879048192 | bytes 8650836 | tf_op jit(solution)/shard_map/attention_back/pallas_call | solution.py:163
  134.8 2.1 %grad_first_parts.1 = (bf16[128,1024]{1,0:T(8,128)(2,1)S(1)}, bf16[128,1024]{1,0:T(8,128)(2,1)S(1)}, bf16[128,1024]{1,0:T(8,128)(2,1)S(1)}, bf16[128,1024]{1,0:T...) custom-call(s32[21]{0:T(128)S(1)} %dynamic-slice_bitcast_fusion.scal, ...), custom_call_target="tpu_custom_call" | custom-call | flops 32000000000 | bytes 6029396 | tf_op jit(solution)/shard_map/grad_first_parts/pallas_call | solution.py:163
  139.7 4.2 %collective-permute-done.54.right_got = bf16[128,1408]{1,0:T(8,128)(2,1)S(1)} collective-permute-done((bf16[128,1408]{1,0:T(8,128)(2,1)S(1)}, bf16[128,1408]{1,0:T(8,128)(2,1)S(1)}, u32[]{:S(2)}, u32[]{:S(2)}) %collective-permute-start.54) | collective-permute-done | bytes 360480 | tf_op jit(solution)/shard_map/ppermute | solution.py:90
  151.1 1.8 finish_tokens.1
  152.8 3.2 %collective-permute-done.58.right_got = bf16[128,1024]{1,0:T(8,128)(2,1)S(1)} collective-permute-done((bf16[128,1024]{1,0:T(8,128)(2,1)S(1)}, bf16[128,1024]{1,0:T(8,128)(2,1)S(1)}, u32[]{:S(2)}, u32[]{:S(2)}) %collective-permute-start.58) | collective-permute-done | bytes 262176 | tf_op jit(solution)/shard_map/ppermute | solution.py:90
  160.5 3.2 %collective-permute-done.63.right_ref = bf16[128,1408]{1,0:T(8,128)(2,1)S(1)} collective-permute-done((bf16[128,1408]{1,0:T(8,128)(2,1)S(1)}, bf16[128,1408]{1,0:T(8,128)(2,1)S(1)}, u32[]{:S(2)}, u32[]{:S(2)}) %collective-permute-start.63) | collective-permute-done | bytes 360480 | tf_op jit(solution)/shard_map/ppermute | solution.py:90
  172.8 3.3 %collective-permute-done.67.right_ref = bf16[128,1024]{1,0:T(8,128)(2,1)S(1)} collective-permute-done((bf16[128,1024]{1,0:T(8,128)(2,1)S(1)}, bf16[128,1024]{1,0:T(8,128)(2,1)S(1)}, u32[]{:S(2)}, u32[]{:S(2)}) %collective-permute-start.67) | collective-permute-done | bytes 262176 | tf_op jit(solution)/shard_map/ppermute | solution.py:90
  179.8 2.6 %unpack_in.1 = f32[64,5632]{1,0:T(8,128)} custom-call(s32[21]{0:T(128)S(1)} %dynamic-slice_bitcast_fusion.scal, bf16[64,1408]{1,0:T(8,128)(2,1)S(1)} %get-tuple-element.430.own_ref, bf16[64,1408]{1,0:T(8,128)(2,1)S(1)} %collective-permute-done.65.near_ref, bf16[64,1408]{1,0:T(8,128)(2,1)S(1)} %collective-permute-done.69.far_ref, ...), custom_call_target="tpu_custom_call" | custom-call | flops 4000000000 | bytes 2162772 | tf_op jit(solution)/shard_map/unpack_in/pallas_call | solution.py:163
  184.7 1.8 collective-permute-done.72.diagonal_ref
  (189 shorter events, 91.2 us)
Async XLA Ops:
  6.6 12.3 %collective-permute-start.4 = (bf16[130,1024]{1,0:T(8,128)(2,1)S(1)}, bf16[130,1024]{1,0:T(8,128)(2,1)S(1)}, u32[]{:S(2)}, u32[]{:S(2)}) collective-permute-start(bf16[130,1024]{1,0:T(8,128)(2,1)S(1)} %pack_tokens.1.refs_0_.block_ref), channel_id=1, source_target_pairs={{0,1},{1,0},{2,3},{3,2},{4,5},{5,4},{6,7},{7,6},{8,9},{9,8},{10,11... | collective-permute-start | bytes 798728 | tf_op jit(solution)/shard_map/ppermute | solution.py:56
  7.0 9.5 %collective-permute-start.1 = (bf16[128,1024]{1,0:T(8,128)(2,1)S(1)}, bf16[128,1024]{1,0:T(8,128)(2,1)S(1)}, u32[]{:S(2)}, u32[]{:S(2)}) collective-permute-start(bf16[128,1024]{1,0:T(8,128)(2,1)S(1)} %constant_dynamic-update-slice_fusion.refs_4_.refs_0_), channel_id=1, source_target_pairs={{0,4},{4,8},{8,12},{12,14},{14,10},{10,6},{6,2},{2,0},{1,5},{5,9},... | collective-permute-start | bytes 786440 | tf_op jit(solution)/shard_map/ppermute | solution.py:90
  9.7 9.2 %collective-permute-start.2 = (bf16[128,1024]{1,0:T(8,128)(2,1)S(1)}, bf16[128,1024]{1,0:T(8,128)(2,1)S(1)}, u32[]{:S(2)}, u32[]{:S(2)}) collective-permute-start(bf16[128,1024]{1,0:T(8,128)(2,1)S(1)} %constant_dynamic-update-slice_fusion.refs_4_.refs_0_), channel_id=1, source_target_pairs={{4,0},{8,4},{12,8},{14,12},{10,14},{6,10},{2,6},{0,2},{5,1},{9,5},... | collective-permute-start | bytes 786440 | tf_op jit(solution)/shard_map/ppermute | solution.py:90
  9.7 9.2 %collective-permute-start.5 = (bf16[128,1024]{1,0:T(8,128)(2,1)}, bf16[128,1024]{1,0:T(8,128)(2,1)S(1)}, u32[]{:S(2)}, u32[]{:S(2)}) collective-permute-start(bf16[128,1024]{1,0:T(8,128)(2,1)} %bitcast.29), channel_id=1, source_target_pairs={{0,1},{1,0},{2,3},{3,2},{4,5},{5,4},{6,7},{7,6},{8,9},{9,8},{10,11... | collective-permute-start | bytes 786440 | tf_op jit(solution)/shard_map/ppermute | solution.py:56
  12.4 18.0 %collective-permute-start.12 = (bf16[88,1024]{1,0:T(8,128)(2,1)S(1)}, bf16[88,1024]{1,0:T(8,128)(2,1)S(1)}, u32[]{:S(2)}, u32[]{:S(2)}) collective-permute-start(bf16[88,1024]{1,0:T(8,128)(2,1)S(1)} %get-tuple-element.305.refs_1_), channel_id=1, source_target_pairs={{4,0},{8,4},{12,8},{14,12},{10,14},{6,10},{2,6},{0,2},{5,1},{9,5},... | collective-permute-start | bytes 540680 | tf_op jit(solution)/shard_map/ppermute | solution.py:90
  16.5 13.9 %collective-permute-start.11 = (bf16[88,1024]{1,0:T(8,128)(2,1)S(1)}, bf16[88,1024]{1,0:T(8,128)(2,1)S(1)}, u32[]{:S(2)}, u32[]{:S(2)}) collective-permute-start(bf16[88,1024]{1,0:T(8,128)(2,1)S(1)} %get-tuple-element.305.refs_1_), channel_id=1, source_target_pairs={{0,4},{4,8},{8,12},{12,14},{14,10},{10,6},{6,2},{2,0},{1,5},{5,9},... | collective-permute-start | bytes 540680 | tf_op jit(solution)/shard_map/ppermute | solution.py:90
  18.9 9.4 %collective-permute-start.6 = (bf16[128,1024]{1,0:T(8,128)(2,1)S(1)}, bf16[128,1024]{1,0:T(8,128)(2,1)S(1)}, u32[]{:S(2)}, u32[]{:S(2)}) collective-permute-start(bf16[128,1024]{1,0:T(8,128)(2,1)S(1)} %collective-permute-done.1.refs_10_.refs_6_), channel_id=1, source_target_pairs={{0,4},{4,8},{8,12},{12,14},{14,10},{10,6},{6,2},{2,0},{1,5},{5,9},... | collective-permute-start | bytes 786440 | tf_op jit(solution)/shard_map/ppermute | solution.py:90
  20.9 9.5 %collective-permute-start.10 = (bf16[130,1024]{1,0:T(8,128)(2,1)S(1)}, bf16[130,1024]{1,0:T(8,128)(2,1)S(1)}, u32[]{:S(2)}, u32[]{:S(2)}) collective-permute-start(bf16[130,1024]{1,0:T(8,128)(2,1)S(1)} %pack_tokens.1.refs_0_.block_ref), channel_id=1, source_target_pairs={{0,16},{16,0},{1,17},{17,1},{2,18},{18,2},{3,19},{19,3},{4,20},{20... | collective-permute-start | bytes 798728 | tf_op jit(solution)/shard_map/ppermute | solution.py:52
  28.3 9.2 %collective-permute-start.8 = (bf16[128,1024]{1,0:T(8,128)(2,1)S(1)}, bf16[128,1024]{1,0:T(8,128)(2,1)S(1)}, u32[]{:S(2)}, u32[]{:S(2)}) collective-permute-start(bf16[128,1024]{1,0:T(8,128)(2,1)S(1)} %collective-permute-done.6.refs_9_.refs_5_), channel_id=1, source_target_pairs={{0,4},{4,8},{8,12},{12,14},{14,10},{10,6},{6,2},{2,0},{1,5},{5,9},... | collective-permute-start | bytes 786440 | tf_op jit(solution)/shard_map/ppermute | solution.py:90
  29.9 9.2 %collective-permute-start.9 = (bf16[128,1024]{1,0:T(8,128)(2,1)S(1)}, bf16[128,1024]{1,0:T(8,128)(2,1)S(1)}, u32[]{:S(2)}, u32[]{:S(2)}) collective-permute-start(bf16[128,1024]{1,0:T(8,128)(2,1)S(1)} %collective-permute-done.7.refs_6_.refs_2_), channel_id=1, source_target_pairs={{4,0},{8,4},{12,8},{14,12},{10,14},{6,10},{2,6},{0,2},{5,1},{9,5},... | collective-permute-start | bytes 786440 | tf_op jit(solution)/shard_map/ppermute | solution.py:90
  31.9 11.8 %collective-permute-start.16 = (bf16[128,1408]{1,0:T(8,128)(2,1)S(1)}, bf16[128,1408]{1,0:T(8,128)(2,1)S(1)}, u32[]{:S(2)}, u32[]{:S(2)}) collective-permute-start(bf16[128,1408]{1,0:T(8,128)(2,1)S(1)} %constant_dynamic-update-slice_fusion.2.refs_0_), channel_id=1, source_target_pairs={{0,4},{4,8},{8,12},{12,14},{14,10},{10,6},{6,2},{2,0},{1,5},{5,9},... | collective-permute-start | bytes 1081352 | tf_op jit(solution)/shard_map/ppermute | solution.py:90
  33.5 12.1 %collective-permute-start.17 = (bf16[128,1408]{1,0:T(8,128)(2,1)S(1)}, bf16[128,1408]{1,0:T(8,128)(2,1)S(1)}, u32[]{:S(2)}, u32[]{:S(2)}) collective-permute-start(bf16[128,1408]{1,0:T(8,128)(2,1)S(1)} %constant_dynamic-update-slice_fusion.2.refs_0_), channel_id=1, source_target_pairs={{4,0},{8,4},{12,8},{14,12},{10,14},{6,10},{2,6},{0,2},{5,1},{9,5},... | collective-permute-start | bytes 1081352 | tf_op jit(solution)/shard_map/ppermute | solution.py:90
  47.0 14.0 %collective-permute-start.19 = (bf16[128,1408]{1,0:T(8,128)(2,1)S(1)}, bf16[128,1408]{1,0:T(8,128)(2,1)S(1)}, u32[]{:S(2)}, u32[]{:S(2)}) collective-permute-start(bf16[128,1408]{1,0:T(8,128)(2,1)S(1)} %collective-permute-done.16.refs_6_), channel_id=1, source_target_pairs={{0,4},{4,8},{8,12},{12,14},{14,10},{10,6},{6,2},{2,0},{1,5},{5,9},... | collective-permute-start | bytes 1081352 | tf_op jit(solution)/shard_map/ppermute | solution.py:90
  48.6 12.4 %collective-permute-start.20 = (bf16[128,1408]{1,0:T(8,128)(2,1)S(1)}, bf16[128,1408]{1,0:T(8,128)(2,1)S(1)}, u32[]{:S(2)}, u32[]{:S(2)}) collective-permute-start(bf16[128,1408]{1,0:T(8,128)(2,1)S(1)} %collective-permute-done.17.refs_1_), channel_id=1, source_target_pairs={{4,0},{8,4},{12,8},{14,12},{10,14},{6,10},{2,6},{0,2},{5,1},{9,5},... | collective-permute-start | bytes 1081352 | tf_op jit(solution)/shard_map/ppermute | solution.py:90
  49.6 16.4 %collective-permute-start.24 = (bf16[1024,256]{1,0:T(8,128)(2,1)S(1)}, bf16[1024,256]{1,0:T(8,128)(2,1)S(1)}, u32[]{:S(2)}, u32[]{:S(2)}) collective-permute-start(bf16[1024,256]{1,0:T(8,128)(2,1)S(1)} %gather_out.1.refs_6_), channel_id=1, source_target_pairs={{0,16},{16,0},{1,17},{17,1},{2,18},{18,2},{3,19},{19,3},{4,20},{20... | collective-permute-start | bytes 1572872 | tf_op jit(solution)/shard_map/ppermute | solution.py:52
  61.0 12.8 %collective-permute-start.25 = (bf16[128,1408]{1,0:T(8,128)(2,1)S(1)}, bf16[128,1408]{1,0:T(8,128)(2,1)S(1)}, u32[]{:S(2)}, u32[]{:S(2)}) collective-permute-start(bf16[128,1408]{1,0:T(8,128)(2,1)S(1)} %collective-permute-done.19.refs_5_), channel_id=1, source_target_pairs={{0,4},{4,8},{8,12},{12,14},{14,10},{10,6},{6,2},{2,0},{1,5},{5,9},... | collective-permute-start | bytes 1081352 | tf_op jit(solution)/shard_map/ppermute | solution.py:90
  62.6 11.2 %collective-permute-start.26 = (bf16[128,1408]{1,0:T(8,128)(2,1)S(1)}, bf16[128,1408]{1,0:T(8,128)(2,1)S(1)}, u32[]{:S(2)}, u32[]{:S(2)}) collective-permute-start(bf16[128,1408]{1,0:T(8,128)(2,1)S(1)} %collective-permute-done.20.refs_2_), channel_id=1, source_target_pairs={{4,0},{8,4},{12,8},{14,12},{10,14},{6,10},{2,6},{0,2},{5,1},{9,5},... | collective-permute-start | bytes 1081352 | tf_op jit(solution)/shard_map/ppermute | solution.py:90
  63.0 10.7 %collective-permute-start.23 = (bf16[4,128,256]{2,1,0:T(8,128)(2,1)S(1)}, bf16[4,128,256]{2,1,0:T(8,128)(2,1)S(1)}, u32[]{:S(2)}, u32[]{:S(2)}) collective-permute-start(bf16[4,128,256]{2,1,0:T(8,128)(2,1)S(1)} %get-tuple-element.262.refs_4_), channel_id=1, source_target_pairs={{0,16},{16,0},{1,17},{17,1},{2,18},{18,2},{3,19},{19,3},{4,20},{20... | collective-permute-start | bytes 786440 | tf_op jit(solution)/shard_map/ppermute | solution.py:52
  74.0 9.5 %collective-permute-start.31 = (bf16[64,1408]{1,0:T(8,128)(2,1)S(1)}, bf16[64,1408]{1,0:T(8,128)(2,1)S(1)}, u32[]{:S(2)}, u32[]{:S(2)}) collective-permute-start(bf16[64,1408]{1,0:T(8,128)(2,1)S(1)} %slice.67), channel_id=1, source_target_pairs={{4,0},{8,4},{12,8},{14,12},{10,14},{6,10},{2,6},{0,2},{5,1},{9,5},... | collective-permute-start | bytes 540680 | tf_op jit(solution)/shard_map/ppermute | solution.py:90
  106.8 12.4 %collective-permute-start.45 = (bf16[128,1024]{1,0:T(8,128)(2,1)S(1)}, bf16[128,1024]{1,0:T(8,128)(2,1)S(1)}, u32[]{:S(2)}, u32[]{:S(2)}) collective-permute-start(bf16[128,1024]{1,0:T(8,128)(2,1)S(1)} %slice_bitcast_fusion), channel_id=1, source_target_pairs={{0,16},{16,0},{1,17},{17,1},{2,18},{18,2},{3,19},{19,3},{4,20},{20... | collective-permute-start | bytes 786440 | tf_op jit(solution)/shard_map/ppermute | solution.py:52
  119.3 13.2 %collective-permute-start.47 = (bf16[128,1408]{1,0:T(8,128)(2,1)S(1)}, bf16[128,1408]{1,0:T(8,128)(2,1)S(1)}, u32[]{:S(2)}, u32[]{:S(2)}) collective-permute-start(bf16[128,1408]{1,0:T(8,128)(2,1)S(1)} %get-tuple-element.359), channel_id=1, source_target_pairs={{0,4},{4,8},{8,12},{12,14},{14,10},{10,6},{6,2},{2,0},{1,5},{5,9},... | collective-permute-start | bytes 1081352 | tf_op jit(solution)/shard_map/ppermute | solution.py:90
  121.0 11.5 %collective-permute-start.48 = (bf16[128,1408]{1,0:T(8,128)(2,1)S(1)}, bf16[128,1408]{1,0:T(8,128)(2,1)S(1)}, u32[]{:S(2)}, u32[]{:S(2)}) collective-permute-start(bf16[128,1408]{1,0:T(8,128)(2,1)S(1)} %get-tuple-element.360), channel_id=1, source_target_pairs={{4,0},{8,4},{12,8},{14,12},{10,14},{6,10},{2,6},{0,2},{5,1},{9,5},... | collective-permute-start | bytes 1081352 | tf_op jit(solution)/shard_map/ppermute | solution.py:90
  122.8 9.1 %collective-permute-start.49 = (bf16[88,1024]{1,0:T(8,128)(2,1)S(1)}, bf16[88,1024]{1,0:T(8,128)(2,1)S(1)}, u32[]{:S(2)}, u32[]{:S(2)}) collective-permute-start(bf16[88,1024]{1,0:T(8,128)(2,1)S(1)} %get-tuple-element.365), channel_id=1, source_target_pairs={{0,4},{4,8},{8,12},{12,14},{14,10},{10,6},{6,2},{2,0},{1,5},{5,9},... | collective-permute-start | bytes 540680 | tf_op jit(solution)/shard_map/ppermute | solution.py:90
  132.7 11.1 %collective-permute-start.54 = (bf16[128,1408]{1,0:T(8,128)(2,1)S(1)}, bf16[128,1408]{1,0:T(8,128)(2,1)S(1)}, u32[]{:S(2)}, u32[]{:S(2)}) collective-permute-start(bf16[128,1408]{1,0:T(8,128)(2,1)S(1)} %get-tuple-element.381), channel_id=1, source_target_pairs={{0,4},{4,8},{8,12},{12,14},{14,10},{10,6},{6,2},{2,0},{1,5},{5,9},... | collective-permute-start | bytes 1081352 | tf_op jit(solution)/shard_map/ppermute | solution.py:90
  134.4 10.9 %collective-permute-start.55 = (bf16[128,1408]{1,0:T(8,128)(2,1)S(1)}, bf16[128,1408]{1,0:T(8,128)(2,1)S(1)}, u32[]{:S(2)}, u32[]{:S(2)}) collective-permute-start(bf16[128,1408]{1,0:T(8,128)(2,1)S(1)} %get-tuple-element.382), channel_id=1, source_target_pairs={{4,0},{8,4},{12,8},{14,12},{10,14},{6,10},{2,6},{0,2},{5,1},{9,5},... | collective-permute-start | bytes 1081352 | tf_op jit(solution)/shard_map/ppermute | solution.py:90
  137.1 9.6 %collective-permute-start.56 = (bf16[128,1024]{1,0:T(8,128)(2,1)S(1)}, bf16[128,1024]{1,0:T(8,128)(2,1)S(1)}, u32[]{:S(2)}, u32[]{:S(2)}) collective-permute-start(bf16[128,1024]{1,0:T(8,128)(2,1)S(1)} %fusion.2), channel_id=1, source_target_pairs={{0,16},{16,0},{1,17},{17,1},{2,18},{18,2},{3,19},{19,3},{4,20},{20... | collective-permute-start | bytes 786440 | tf_op jit(solution)/shard_map/ppermute | solution.py:52
  146.7 9.3 %collective-permute-start.58 = (bf16[128,1024]{1,0:T(8,128)(2,1)S(1)}, bf16[128,1024]{1,0:T(8,128)(2,1)S(1)}, u32[]{:S(2)}, u32[]{:S(2)}) collective-permute-start(bf16[128,1024]{1,0:T(8,128)(2,1)S(1)} %get-tuple-element.393), channel_id=1, source_target_pairs={{0,4},{4,8},{8,12},{12,14},{14,10},{10,6},{6,2},{2,0},{1,5},{5,9},... | collective-permute-start | bytes 786440 | tf_op jit(solution)/shard_map/ppermute | solution.py:90
  148.4 9.2 %collective-permute-start.59 = (bf16[128,1024]{1,0:T(8,128)(2,1)S(1)}, bf16[128,1024]{1,0:T(8,128)(2,1)S(1)}, u32[]{:S(2)}, u32[]{:S(2)}) collective-permute-start(bf16[128,1024]{1,0:T(8,128)(2,1)S(1)} %get-tuple-element.394), channel_id=1, source_target_pairs={{4,0},{8,4},{12,8},{14,12},{10,14},{6,10},{2,6},{0,2},{5,1},{9,5},... | collective-permute-start | bytes 786440 | tf_op jit(solution)/shard_map/ppermute | solution.py:90
  149.0 14.8 %collective-permute-start.63 = (bf16[128,1408]{1,0:T(8,128)(2,1)S(1)}, bf16[128,1408]{1,0:T(8,128)(2,1)S(1)}, u32[]{:S(2)}, u32[]{:S(2)}) collective-permute-start(bf16[128,1408]{1,0:T(8,128)(2,1)S(1)} %get-tuple-element.407), channel_id=1, source_target_pairs={{0,4},{4,8},{8,12},{12,14},{14,10},{10,6},{6,2},{2,0},{1,5},{5,9},... | collective-permute-start | bytes 1081352 | tf_op jit(solution)/shard_map/ppermute | solution.py:90
  150.7 14.7 %collective-permute-start.64 = (bf16[128,1408]{1,0:T(8,128)(2,1)S(1)}, bf16[128,1408]{1,0:T(8,128)(2,1)S(1)}, u32[]{:S(2)}, u32[]{:S(2)}) collective-permute-start(bf16[128,1408]{1,0:T(8,128)(2,1)S(1)} %get-tuple-element.408), channel_id=1, source_target_pairs={{4,0},{8,4},{12,8},{14,12},{10,14},{6,10},{2,6},{0,2},{5,1},{9,5},... | collective-permute-start | bytes 1081352 | tf_op jit(solution)/shard_map/ppermute | solution.py:90
  157.8 9.5 %collective-permute-start.61 = (bf16[128,1024]{1,0:T(8,128)(2,1)S(1)}, bf16[128,1024]{1,0:T(8,128)(2,1)S(1)}, u32[]{:S(2)}, u32[]{:S(2)}) collective-permute-start(bf16[128,1024]{1,0:T(8,128)(2,1)S(1)} %get-tuple-element.400), channel_id=1, source_target_pairs={{0,4},{4,8},{8,12},{12,14},{14,10},{10,6},{6,2},{2,0},{1,5},{5,9},... | collective-permute-start | bytes 786440 | tf_op jit(solution)/shard_map/ppermute | solution.py:90
  158.5 10.1 %collective-permute-start.62 = (bf16[128,1024]{1,0:T(8,128)(2,1)S(1)}, bf16[128,1024]{1,0:T(8,128)(2,1)S(1)}, u32[]{:S(2)}, u32[]{:S(2)}) collective-permute-start(bf16[128,1024]{1,0:T(8,128)(2,1)S(1)} %get-tuple-element.401), channel_id=1, source_target_pairs={{4,0},{8,4},{12,8},{14,12},{10,14},{6,10},{2,6},{0,2},{5,1},{9,5},... | collective-permute-start | bytes 786440 | tf_op jit(solution)/shard_map/ppermute | solution.py:90
  (52 other events, 449.3 us)

commit v6 on v5

--- a/solution.py
+++ b/solution.py
@@ -18,7 +18,7 @@
 F32 = jnp.float32
 SWAP = ((0, 1), (1, 0))
 MIB = 1 << 20
-WEIGHT = {'ring_add': 16000000000, 'unpack_in': 4000000000, 'pack_in': 0, 'hidden_back': 32000000000, 'grad_first_parts': 32000000000, 'middle_back': 8000000000, 'hidden_units': 16000000000}
+WEIGHT = {'ring_add': 16000000000, 'unpack_in': 4000000000, 'pack_in': 1000000000, 'hidden_back': 32000000000, 'grad_first_parts': 32000000000, 'middle_back': 4000000000, 'hidden_units': 16000000000, 'last_projection': 4000000000}
 BLOCKS = ((0, 1, 2, 3), (1, 0, 3, 2), (2, 3, 0, 1), (3, 2, 1, 0))
 
 
@@ -597,7 +597,7 @@
     )
     a = Gather(ring, jnp.concatenate([a_own, sibling(a_sib)], axis=0))
 
-    a.state, in_weight, tokens, cot_own = sync(a.state, in_weight, tokens, cot_own)
+    a.state, in_weight, tokens = sync(a.state, in_weight, tokens)
     a.advance()
     b_own, b_sib, down_rows = call(
         functools.partial(pack_in, size, units, piece, padded),
@@ -613,9 +613,8 @@
     b_got = sibling(b_sib)
     (own,) = call(functools.partial(pack_tokens, rows), [shape((rows + micro, width), BF)], [], 0, prefix, tokens, smem=0)
     near = sibling(own)
-    cot_near = sibling(cot_own)
-
-    a.state, own, b_own, b_got, near, cot_near = sync(a.state, own, b_own, b_got, near, cot_near)
+
+    a.state, own, b_own, b_got, near = sync(a.state, own, b_own, b_got, near)
     a.advance()
     far = across(own)
     b = Gather(ring, jnp.concatenate([b_own, b_got], axis=0))
@@ -686,7 +685,8 @@
         near_all,
     )
 
-    h2, b_chunks, c_chunks, cot_far = sync(h2, b_chunks, c_chunks, cot_far)
+    h2, b_chunks, c_chunks, cot_own, cot_far = sync(h2, b_chunks, c_chunks, cot_own, cot_far)
+    cot_near = sibling(cot_own)
     cot_diagonal = sibling(cot_far)
     up, gate, hid, in_mine = call(
         functools.partial(hidden_units, size, shard_rows, member_units, chunks),
@@ -702,7 +702,7 @@
         h2,
         *b_chunks,
     )
-    hid, cot_diagonal = sync(hid, cot_diagonal)
+    hid, cot_near, cot_diagonal = sync(hid, cot_near, cot_diagonal)
     *down_parts, gm = call(
         functools.partial(grad_down_parts, size, rows, padded),
         [shape((piece, width), BF)] * size + [shape((full_rows, width), BF)],
@@ -751,9 +751,10 @@
     )
 
     b = Scatter(ring, in_parts)
-    b.state, c.got, u2_first, u2_low, hid = sync(b.state, c.got, u2_first, u2_low, hid)
+    b.state, c.got = sync(b.state, c.got)
     b.send()
     c.add()
+    c.state, u2_first, u2_low, hid = sync(c.state, u2_first, u2_low, hid)
     c.send()
     u2_second = across(u2_low[1])
     y_keep, y_give = call(functools.partial(last_projection, rows), [pair_full, pair_low], [], 3 * project, scal, hid, down_mine)
@@ -794,7 +795,7 @@
         sine,
     )
 
-    gqkv, u1_give, b.got, c.got = sync(gqkv, u1_give, b.got, c.got)
+    gqkv, u1_give, b.got = sync(gqkv, u1_give, b.got)
     b.add()
     b.send()
     u1_got = sibling(u1_give)

time: 188 us -> 185 us (0.984)
  waiting for transfers between devices: 65.8 us -> 57.4 us
  starting transfers between devices: 68.2 us -> 72.4 us
    ppermute x24, waiting for transfers between devices: 36.8 us -> 31.2 us  [exchange(): lax.ppermute(pair[0], 'ring', self.right)]
    ppermute x13, starting transfers between devices: 13.6 us -> 19 us  [across(): return lax.ppermute(value, 'rep', SWAP)]
    ppermute x13, waiting for transfers between devices: 4.39 us -> 1.11 us  [across(): return lax.ppermute(value, 'rep', SWAP)]
    ppermute x24, waiting for transfers between devices: 22.5 us -> 24.8 us  [exchange(): lax.ppermute(pair[1], 'ring', self.left)]
  transfers between devices with their start and end apart: 74 -> 74, of which waited for: 36 -> 34; matrix products, arithmetic and copies ran while one was open for 1% -> 1% of each run, Pallas kernels for 22% -> 23%
where the time goes in v6:
time: 185 us
  starting transfers between devices  72.4 us (39%)
  waiting for transfers between devices  57.4 us (31%)
  Pallas kernels  47 us (25%)
  local copies, waits for them, and re-layouts  5.56 us (3%)
    pallas_call x29, Pallas kernels, call(): pl.pallas_call(body, name=body.func.__name__, out_shape=outs, in_specs=[p...  47 us
    ppermute x24, starting transfers between devices, exchange(): lax.ppermute(pair[0], 'ring', self.right)  39.3 us
    ppermute x24, waiting for transfers between devices, exchange(): lax.ppermute(pair[0], 'ring', self.right)  31.2 us
    ppermute x24, waiting for transfers between devices, exchange(): lax.ppermute(pair[1], 'ring', self.left)  24.8 us
    ppermute x13, starting transfers between devices, across(): return lax.ppermute(value, 'rep', SWAP)  19 us
    ppermute x24, starting transfers between devices, exchange(): lax.ppermute(pair[1], 'ring', self.left)  12.2 us
    unnamed x23, local copies, waits for them, and re-layouts  4.66 us
  transfers between devices with their start and end apart: 74, of which 34 were waited for; matrix products, arithmetic and copies ran while one was open for 1% of the time, Pallas kernels for 23%

profile of v6, /device:TPU:0, one launch (start us, length us, event | category | flops | bytes accessed | tf_op | source)
XLA Modules:
  0.0 184.7 jit_solution(15560932790552788412)
XLA Ops:
  5.5 3.0 %collective-permute-start.1 = (bf16[128,1024]{1,0:T(8,128)(2,1)S(1)}, bf16[128,1024]{1,0:T(8,128)(2,1)S(1)}, u32[]{:S(2)}, u32[]{:S(2)}) collective-permute-start(bf16[128,1024]{1,0:T(8,128)(2,1)S(1)} %constant_dynamic-update-slice_fusion.refs_4_.refs_0_), channel_id=1, source_target_pairs={{0,4},{4,8},{8,12},{12,14},{14,10},{10,6},{6,2},{2,0},{1,5},{5,9},... | collective-permute-start | bytes 786440 | tf_op jit(solution)/shard_map/ppermute | solution.py:90
  12.1 2.0 %collective-permute-start.11 = (bf16[88,1024]{1,0:T(8,128)(2,1)S(1)}, bf16[88,1024]{1,0:T(8,128)(2,1)S(1)}, u32[]{:S(2)}, u32[]{:S(2)}) collective-permute-start(bf16[88,1024]{1,0:T(8,128)(2,1)S(1)} %get-tuple-element.307.refs_1_), channel_id=1, source_target_pairs={{4,0},{8,4},{12,8},{14,12},{10,14},{6,10},{2,6},{0,2},{5,1},{9,5},... | collective-permute-start | bytes 540680 | tf_op jit(solution)/shard_map/ppermute | solution.py:90
  15.2 2.4 %collective-permute-done.2.refs_5_.refs_1_ = bf16[128,1024]{1,0:T(8,128)(2,1)S(1)} collective-permute-done((bf16[128,1024]{1,0:T(8,128)(2,1)S(1)}, bf16[128,1024]{1,0:T(8,128)(2,1)S(1)}, u32[]{:S(2)}, u32[]{:S(2)}) %collective-permute-start.2) | collective-permute-done | bytes 262176 | tf_op jit(solution)/shard_map/ppermute | solution.py:90
  21.2 4.7 %collective-permute-done.5.refs_9_.refs_5_ = bf16[128,1024]{1,0:T(8,128)(2,1)S(1)} collective-permute-done((bf16[128,1024]{1,0:T(8,128)(2,1)S(1)}, bf16[128,1024]{1,0:T(8,128)(2,1)S(1)}, u32[]{:S(2)}, u32[]{:S(2)}) %collective-permute-start.5) | collective-permute-done | bytes 262176 | tf_op jit(solution)/shard_map/ppermute | solution.py:90
  31.7 3.5 %collective-permute-done.7.refs_8_.refs_4_ = bf16[128,1024]{1,0:T(8,128)(2,1)S(1)} collective-permute-done((bf16[128,1024]{1,0:T(8,128)(2,1)S(1)}, bf16[128,1024]{1,0:T(8,128)(2,1)S(1)}, u32[]{:S(2)}, u32[]{:S(2)}) %collective-permute-start.7) | collective-permute-done | bytes 262176 | tf_op jit(solution)/shard_map/ppermute | solution.py:90
  39.0 2.3 %collective-permute-done.15.refs_6_ = bf16[128,1408]{1,0:T(8,128)(2,1)S(1)} collective-permute-done((bf16[128,1408]{1,0:T(8,128)(2,1)S(1)}, bf16[128,1408]{1,0:T(8,128)(2,1)S(1)}, u32[]{:S(2)}, u32[]{:S(2)}) %collective-permute-start.15) | collective-permute-done | bytes 360480 | tf_op jit(solution)/shard_map/ppermute | solution.py:90
  41.3 2.6 %collective-permute-done.16.refs_1_ = bf16[128,1408]{1,0:T(8,128)(2,1)S(1)} collective-permute-done((bf16[128,1408]{1,0:T(8,128)(2,1)S(1)}, bf16[128,1408]{1,0:T(8,128)(2,1)S(1)}, u32[]{:S(2)}, u32[]{:S(2)}) %collective-permute-start.16) | collective-permute-done | bytes 360480 | tf_op jit(solution)/shard_map/ppermute | solution.py:90
  51.6 7.0 %attention.1 = (bf16[4,128,256]{2,1,0:T(8,128)(2,1)S(1)}, bf16[512,1024]{1,0:T(8,128)(2,1)S(1)}, bf16[512,768]{1,0:T(8,128)(2,1)S(1)}, f32[16,128,128]{2,1,0:T(8,128)S(1)}, bf16[1024,768]{1,0:T(8,128)(2,1)S(1)}) custom-call(s32[21]{0:T(128)S(1)} %dynamic-slice_bitcast_fusion.scal, bf16[130,1024]{1,0:T(8,128)(2,1)S(1)} %pack_tokens.1.refs_0_.block_ref, ...), custom_call_target="tpu_custom_call" | custom-call | flops 805306368 | bytes 8142932 | tf_op jit(solution)/shard_map/attention/pallas_call | solution.py:163
  58.9 1.9 %collective-permute-start.24 = (bf16[128,1408]{1,0:T(8,128)(2,1)S(1)}, bf16[128,1408]{1,0:T(8,128)(2,1)S(1)}, u32[]{:S(2)}, u32[]{:S(2)}) collective-permute-start(bf16[128,1408]{1,0:T(8,128)(2,1)S(1)} %collective-permute-done.18.refs_5_), channel_id=1, source_target_pairs={{0,4},{4,8},{8,12},{12,14},{14,10},{10,6},{6,2},{2,0},{1,5},{5,9},... | collective-permute-start | bytes 1081352 | tf_op jit(solution)/shard_map/ppermute | solution.py:90
  62.4 1.9 %collective-permute-start.26 = (bf16[88,1024]{1,0:T(8,128)(2,1)S(1)}, bf16[88,1024]{1,0:T(8,128)(2,1)S(1)}, u32[]{:S(2)}, u32[]{:S(2)}) collective-permute-start(bf16[88,1024]{1,0:T(8,128)(2,1)S(1)} %collective-permute-done.20.refs_6_), channel_id=1, source_target_pairs={{0,4},{4,8},{8,12},{12,14},{14,10},{10,6},{6,2},{2,0},{1,5},{5,9},... | collective-permute-start | bytes 540680 | tf_op jit(solution)/shard_map/ppermute | solution.py:90
  64.5 5.5 %collective-permute-done.26.refs_5_ = bf16[88,1024]{1,0:T(8,128)(2,1)S(1)} collective-permute-done((bf16[88,1024]{1,0:T(8,128)(2,1)S(1)}, bf16[88,1024]{1,0:T(8,128)(2,1)S(1)}, u32[]{:S(2)}, u32[]{:S(2)}) %collective-permute-start.26) | collective-permute-done | bytes 180256 | tf_op jit(solution)/shard_map/ppermute | solution.py:90
  70.0 1.9 %collective-permute-done.27.refs_4_ = bf16[88,1024]{1,0:T(8,128)(2,1)S(1)} collective-permute-done((bf16[88,1024]{1,0:T(8,128)(2,1)S(1)}, bf16[88,1024]{1,0:T(8,128)(2,1)S(1)}, u32[]{:S(2)}, u32[]{:S(2)}) %collective-permute-start.27) | collective-permute-done | bytes 180256 | tf_op jit(solution)/shard_map/ppermute | solution.py:90
  72.5 1.7 collective-permute-start.29
  74.5 2.0 %collective-permute-start.31 = (bf16[48,1024]{1,0:T(8,128)(2,1)S(1)}, bf16[48,1024]{1,0:T(8,128)(2,1)S(1)}, u32[]{:S(2)}, u32[]{:S(2)}) collective-permute-start(bf16[48,1024]{1,0:T(8,128)(2,1)S(1)} %slice.68), channel_id=1, source_target_pairs={{0,4},{4,8},{8,12},{12,14},{14,10},{10,6},{6,2},{2,0},{1,5},{5,9},... | collective-permute-start | bytes 294920 | tf_op jit(solution)/shard_map/ppermute | solution.py:90
  76.5 2.7 %middle.1 = (f32[512,1024]{1,0:T(8,128)S(1)}, bf16[512,1024]{1,0:T(8,128)(2,1)S(1)}, bf16[512,1024]{1,0:T(8,128)(2,1)S(1)}, bf16[256,1024]{1,0:T(8,128)(2,1)S(1)}) custom-call(s32[21]{0:T(128)S(1)} %dynamic-slice_bitcast_fusion.scal, bf16[130,1024]{1,0:T(8,128)(2,1)S(1)} %pack_tokens.1.refs_0_.block_ref, ...), custom_call_target="tpu_custom_call" | custom-call | flops 1073741824 | bytes 8929364 | tf_op jit(solution)/shard_map/middle/pallas_call | solution.py:163
  81.8 3.0 %hidden_units.1 = (f32[512,704]{1,0:T(8,128)S(1)}, f32[512,704]{1,0:T(8,128)S(1)}, bf16[512,704]{1,0:T(8,128)(2,1)S(1)}, bf16[1024,1408]{1,0:T(8,128)(2,1)S(1)}) custom-call(s32[21]{0:T(128)S(1)} %dynamic-slice_bitcast_fusion.scal, bf16[512,1024]{1,0:T(8,128)(2,1)S(1)} %get-tuple-element.276.h2_ref, ...), custom_call_target="tpu_custom_call" | custom-call | flops 16000000000 | bytes 10420308 | tf_op jit(solution)/shard_map/hidden_units/pallas_call | solution.py:163
  84.8 2.4 %grad_down_parts.1 = (bf16[88,1024]{1,0:T(8,128)(2,1)S(1)}, bf16[88,1024]{1,0:T(8,128)(2,1)S(1)}, bf16[88,1024]{1,0:T(8,128)(2,1)S(1)}, bf16[88,1024]{1,0:T(8,12...) custom-call(s32[21]{0:T(128)S(1)} %dynamic-slice_bitcast_fusion.scal, ...), custom_call_target="tpu_custom_call" | custom-call | flops 805306368 | bytes 4259924 | tf_op jit(solution)/shard_map/grad_down_parts/pallas_call | solution.py:163
  89.3 4.8 %hidden_back.1 = (bf16[512,1408]{1,0:T(8,128)(2,1)S(1)}, f32[2,128,1024]{2,1,0:T(8,128)S(1)}, bf16[2,128,1024]{2,1,0:T(8,128)(2,1)S(1)}, bf16[704,1024]{1,0:T(8,128)(2,1)S(1)}) custom-call(s32[21]{0:T(128)S(1)} %dynamic-slice_bitcast_fusion.scal, bf16[512,1024]{1,0:T(8,128)(2,1)S(1)} %get-tuple-element.306.refs_0_, ...), custom_call_target="tpu_custom_call" | custom-call | flops 32000000000 | bytes 12714068 | tf_op jit(solution)/shard_map/hidden_back/pallas_call | solution.py:163
  94.2 1.8 collective-permute-start.38
  98.0 2.7 %grad_in_parts.1 = (bf16[128,1408]{1,0:T(8,128)(2,1)S(1)}, bf16[128,1408]{1,0:T(8,128)(2,1)S(1)}, bf16[128,1408]{1,0:T(8,128)(2,1)S(1)}, bf16[128,1408]{1,0:T(8,...) custom-call(s32[21]{0:T(128)S(1)} %dynamic-slice_bitcast_fusion.scal, ...), custom_call_target="tpu_custom_call" | custom-call | flops 1610612736 | bytes 5374036 | tf_op jit(solution)/shard_map/grad_in_parts/pallas_call | solution.py:163
  104.8 1.8 collective-permute-start.41
  108.5 2.1 %last_projection.1 = (f32[2,128,1024]{2,1,0:T(8,128)S(1)}, bf16[2,128,1024]{2,1,0:T(8,128)(2,1)S(1)}) custom-call(s32[21]{0:T(128)S(1)} %dynamic-slice_bitcast_fusion.scal, bf16[512,704]{1,0:T(8,128)(2,1)S(1)} %get-tuple-element.338.hid_ref, bf16[704,1024]{1,0:T(8,128)(2,1)S(1)} %get-tuple-element.339.down_ref), custom_call_target="tpu_custom_call" | custom-call | flops 4000000000 | bytes 3735636 | tf_op jit(solution)/shard_map/last_projection/pallas_call | solution.py:163
  121.0 7.0 %attention_back.1 = (bf16[512,768]{1,0:T(8,128)(2,1)S(1)}, bf16[512,1024]{1,0:T(8,128)(2,1)S(1)}, f32[2,128,1024]{2,1,0:T(8,128)S(1)}, bf16[2,128,1024]{2,1,0:T(8,128)(2,1)S(1)}) custom-call(s32[21]{0:T(128)S(1)} %dynamic-slice_bitcast_fusion.scal, bf16[2,128,1024]{2,1,0:T(8,128)(2,1)S(1)} %get-tuple-element.350.ga_own, ...), custom_call_target="tpu_custom_call" | custom-call | flops 1879048192 | bytes 8650836 | tf_op jit(solution)/shard_map/attention_back/pallas_call | solution.py:163
  129.7 1.8 collective-permute-start.54
  131.8 2.1 %grad_first_parts.1 = (bf16[128,1024]{1,0:T(8,128)(2,1)S(1)}, bf16[128,1024]{1,0:T(8,128)(2,1)S(1)}, bf16[128,1024]{1,0:T(8,128)(2,1)S(1)}, bf16[128,1024]{1,0:T...) custom-call(s32[21]{0:T(128)S(1)} %dynamic-slice_bitcast_fusion.scal, ...), custom_call_target="tpu_custom_call" | custom-call | flops 32000000000 | bytes 6029396 | tf_op jit(solution)/shard_map/grad_first_parts/pallas_call | solution.py:163
  137.5 2.9 %collective-permute-done.54.right_got = bf16[128,1408]{1,0:T(8,128)(2,1)S(1)} collective-permute-done((bf16[128,1408]{1,0:T(8,128)(2,1)S(1)}, bf16[128,1408]{1,0:T(8,128)(2,1)S(1)}, u32[]{:S(2)}, u32[]{:S(2)}) %collective-permute-start.54) | collective-permute-done | bytes 360480 | tf_op jit(solution)/shard_map/ppermute | solution.py:90
  140.5 1.9 %collective-permute-start.60 = (bf16[88,1024]{1,0:T(8,128)(2,1)S(1)}, bf16[88,1024]{1,0:T(8,128)(2,1)S(1)}, u32[]{:S(2)}, u32[]{:S(2)}) collective-permute-start(bf16[88,1024]{1,0:T(8,128)(2,1)S(1)} %add_convert_fusion.3.low_ref), channel_id=1, source_target_pairs={{0,16},{16,0},{1,17},{17,1},{2,18},{18,2},{3,19},{19,3},{4,20},{20... | collective-permute-start | bytes 540680 | tf_op jit(solution)/shard_map/ppermute | solution.py:52
  148.1 1.8 finish_tokens.1
  149.9 3.2 %collective-permute-done.58.right_got = bf16[128,1024]{1,0:T(8,128)(2,1)S(1)} collective-permute-done((bf16[128,1024]{1,0:T(8,128)(2,1)S(1)}, bf16[128,1024]{1,0:T(8,128)(2,1)S(1)}, u32[]{:S(2)}, u32[]{:S(2)}) %collective-permute-start.58) | collective-permute-done | bytes 262176 | tf_op jit(solution)/shard_map/ppermute | solution.py:90
  158.2 2.6 %collective-permute-done.63.right_ref = bf16[128,1408]{1,0:T(8,128)(2,1)S(1)} collective-permute-done((bf16[128,1408]{1,0:T(8,128)(2,1)S(1)}, bf16[128,1408]{1,0:T(8,128)(2,1)S(1)}, u32[]{:S(2)}, u32[]{:S(2)}) %collective-permute-start.63) | collective-permute-done | bytes 360480 | tf_op jit(solution)/shard_map/ppermute | solution.py:90
  169.8 3.0 %collective-permute-done.67.right_ref = bf16[128,1024]{1,0:T(8,128)(2,1)S(1)} collective-permute-done((bf16[128,1024]{1,0:T(8,128)(2,1)S(1)}, bf16[128,1024]{1,0:T(8,128)(2,1)S(1)}, u32[]{:S(2)}, u32[]{:S(2)}) %collective-permute-start.67) | collective-permute-done | bytes 262176 | tf_op jit(solution)/shard_map/ppermute | solution.py:90
  177.3 2.6 %unpack_in.1 = f32[64,5632]{1,0:T(8,128)} custom-call(s32[21]{0:T(128)S(1)} %dynamic-slice_bitcast_fusion.scal, bf16[64,1408]{1,0:T(8,128)(2,1)S(1)} %get-tuple-element.430.own_ref, bf16[64,1408]{1,0:T(8,128)(2,1)S(1)} %collective-permute-done.65.near_ref, bf16[64,1408]{1,0:T(8,128)(2,1)S(1)} %collective-permute-done.69.far_ref, ...), custom_call_target="tpu_custom_call" | custom-call | flops 4000000000 | bytes 2162772 | tf_op jit(solution)/shard_map/unpack_in/pallas_call | solution.py:163
  (189 shorter events, 91.1 us)
Async XLA Ops:
  5.5 9.7 %collective-permute-start.1 = (bf16[128,1024]{1,0:T(8,128)(2,1)S(1)}, bf16[128,1024]{1,0:T(8,128)(2,1)S(1)}, u32[]{:S(2)}, u32[]{:S(2)}) collective-permute-start(bf16[128,1024]{1,0:T(8,128)(2,1)S(1)} %constant_dynamic-update-slice_fusion.refs_4_.refs_0_), channel_id=1, source_target_pairs={{0,4},{4,8},{8,12},{12,14},{14,10},{10,6},{6,2},{2,0},{1,5},{5,9},... | collective-permute-start | bytes 786440 | tf_op jit(solution)/shard_map/ppermute | solution.py:90
  8.4 9.2 %collective-permute-start.2 = (bf16[128,1024]{1,0:T(8,128)(2,1)S(1)}, bf16[128,1024]{1,0:T(8,128)(2,1)S(1)}, u32[]{:S(2)}, u32[]{:S(2)}) collective-permute-start(bf16[128,1024]{1,0:T(8,128)(2,1)S(1)} %constant_dynamic-update-slice_fusion.refs_4_.refs_0_), channel_id=1, source_target_pairs={{4,0},{8,4},{12,8},{14,12},{10,14},{6,10},{2,6},{0,2},{5,1},{9,5},... | collective-permute-start | bytes 786440 | tf_op jit(solution)/shard_map/ppermute | solution.py:90
  12.1 15.9 %collective-permute-start.11 = (bf16[88,1024]{1,0:T(8,128)(2,1)S(1)}, bf16[88,1024]{1,0:T(8,128)(2,1)S(1)}, u32[]{:S(2)}, u32[]{:S(2)}) collective-permute-start(bf16[88,1024]{1,0:T(8,128)(2,1)S(1)} %get-tuple-element.307.refs_1_), channel_id=1, source_target_pairs={{4,0},{8,4},{12,8},{14,12},{10,14},{6,10},{2,6},{0,2},{5,1},{9,5},... | collective-permute-start | bytes 540680 | tf_op jit(solution)/shard_map/ppermute | solution.py:90
  14.1 14.0 %collective-permute-start.10 = (bf16[88,1024]{1,0:T(8,128)(2,1)S(1)}, bf16[88,1024]{1,0:T(8,128)(2,1)S(1)}, u32[]{:S(2)}, u32[]{:S(2)}) collective-permute-start(bf16[88,1024]{1,0:T(8,128)(2,1)S(1)} %get-tuple-element.307.refs_1_), channel_id=1, source_target_pairs={{0,4},{4,8},{8,12},{12,14},{14,10},{10,6},{6,2},{2,0},{1,5},{5,9},... | collective-permute-start | bytes 540680 | tf_op jit(solution)/shard_map/ppermute | solution.py:90
  26.0 9.2 %collective-permute-start.7 = (bf16[128,1024]{1,0:T(8,128)(2,1)S(1)}, bf16[128,1024]{1,0:T(8,128)(2,1)S(1)}, u32[]{:S(2)}, u32[]{:S(2)}) collective-permute-start(bf16[128,1024]{1,0:T(8,128)(2,1)S(1)} %collective-permute-done.5.refs_9_.refs_5_), channel_id=1, source_target_pairs={{0,4},{4,8},{8,12},{12,14},{14,10},{10,6},{6,2},{2,0},{1,5},{5,9},... | collective-permute-start | bytes 786440 | tf_op jit(solution)/shard_map/ppermute | solution.py:90
  27.6 9.2 %collective-permute-start.8 = (bf16[128,1024]{1,0:T(8,128)(2,1)S(1)}, bf16[128,1024]{1,0:T(8,128)(2,1)S(1)}, u32[]{:S(2)}, u32[]{:S(2)}) collective-permute-start(bf16[128,1024]{1,0:T(8,128)(2,1)S(1)} %collective-permute-done.6.refs_6_.refs_2_), channel_id=1, source_target_pairs={{4,0},{8,4},{12,8},{14,12},{10,14},{6,10},{2,6},{0,2},{5,1},{9,5},... | collective-permute-start | bytes 786440 | tf_op jit(solution)/shard_map/ppermute | solution.py:90
  28.1 8.8 %collective-permute-start.12 = (bf16[128,1024]{1,0:T(8,128)(2,1)S(1)}, bf16[128,1024]{1,0:T(8,128)(2,1)S(1)}, u32[]{:S(2)}, u32[]{:S(2)}) collective-permute-start(bf16[128,1024]{1,0:T(8,128)(2,1)S(1)} %bitcast.29), channel_id=1, source_target_pairs={{0,16},{16,0},{1,17},{17,1},{2,18},{18,2},{3,19},{19,3},{4,20},{20... | collective-permute-start | bytes 786440 | tf_op jit(solution)/shard_map/ppermute | solution.py:52
  29.7 11.6 %collective-permute-start.15 = (bf16[128,1408]{1,0:T(8,128)(2,1)S(1)}, bf16[128,1408]{1,0:T(8,128)(2,1)S(1)}, u32[]{:S(2)}, u32[]{:S(2)}) collective-permute-start(bf16[128,1408]{1,0:T(8,128)(2,1)S(1)} %constant_dynamic-update-slice_fusion.2.refs_0_), channel_id=1, source_target_pairs={{0,4},{4,8},{8,12},{12,14},{14,10},{10,6},{6,2},{2,0},{1,5},{5,9},... | collective-permute-start | bytes 1081352 | tf_op jit(solution)/shard_map/ppermute | solution.py:90
  31.2 12.7 %collective-permute-start.16 = (bf16[128,1408]{1,0:T(8,128)(2,1)S(1)}, bf16[128,1408]{1,0:T(8,128)(2,1)S(1)}, u32[]{:S(2)}, u32[]{:S(2)}) collective-permute-start(bf16[128,1408]{1,0:T(8,128)(2,1)S(1)} %constant_dynamic-update-slice_fusion.2.refs_0_), channel_id=1, source_target_pairs={{4,0},{8,4},{12,8},{14,12},{10,14},{6,10},{2,6},{0,2},{5,1},{9,5},... | collective-permute-start | bytes 1081352 | tf_op jit(solution)/shard_map/ppermute | solution.py:90
  36.9 8.5 %collective-permute-start.17 = (bf16[130,1024]{1,0:T(8,128)(2,1)S(1)}, bf16[130,1024]{1,0:T(8,128)(2,1)S(1)}, u32[]{:S(2)}, u32[]{:S(2)}) collective-permute-start(bf16[130,1024]{1,0:T(8,128)(2,1)S(1)} %collective-permute-done.9.refs_2_), channel_id=1, source_target_pairs={{0,1},{1,0},{2,3},{3,2},{4,5},{5,4},{6,7},{7,6},{8,9},{9,8},{10,11... | collective-permute-start | bytes 798728 | tf_op jit(solution)/shard_map/ppermute | solution.py:56
  45.4 13.6 %collective-permute-start.18 = (bf16[128,1408]{1,0:T(8,128)(2,1)S(1)}, bf16[128,1408]{1,0:T(8,128)(2,1)S(1)}, u32[]{:S(2)}, u32[]{:S(2)}) collective-permute-start(bf16[128,1408]{1,0:T(8,128)(2,1)S(1)} %collective-permute-done.15.refs_6_), channel_id=1, source_target_pairs={{0,4},{4,8},{8,12},{12,14},{14,10},{10,6},{6,2},{2,0},{1,5},{5,9},... | collective-permute-start | bytes 1081352 | tf_op jit(solution)/shard_map/ppermute | solution.py:90
  46.9 12.0 %collective-permute-start.19 = (bf16[128,1408]{1,0:T(8,128)(2,1)S(1)}, bf16[128,1408]{1,0:T(8,128)(2,1)S(1)}, u32[]{:S(2)}, u32[]{:S(2)}) collective-permute-start(bf16[128,1408]{1,0:T(8,128)(2,1)S(1)} %collective-permute-done.16.refs_1_), channel_id=1, source_target_pairs={{4,0},{8,4},{12,8},{14,12},{10,14},{6,10},{2,6},{0,2},{5,1},{9,5},... | collective-permute-start | bytes 1081352 | tf_op jit(solution)/shard_map/ppermute | solution.py:90
  48.0 16.3 %collective-permute-start.23 = (bf16[1024,256]{1,0:T(8,128)(2,1)S(1)}, bf16[1024,256]{1,0:T(8,128)(2,1)S(1)}, u32[]{:S(2)}, u32[]{:S(2)}) collective-permute-start(bf16[1024,256]{1,0:T(8,128)(2,1)S(1)} %gather_out.1.refs_6_), channel_id=1, source_target_pairs={{0,16},{16,0},{1,17},{17,1},{2,18},{18,2},{3,19},{19,3},{4,20},{20... | collective-permute-start | bytes 1572872 | tf_op jit(solution)/shard_map/ppermute | solution.py:52
  49.6 9.0 %collective-permute-start.20 = (bf16[88,1024]{1,0:T(8,128)(2,1)S(1)}, bf16[88,1024]{1,0:T(8,128)(2,1)S(1)}, u32[]{:S(2)}, u32[]{:S(2)}) collective-permute-start(bf16[88,1024]{1,0:T(8,128)(2,1)S(1)} %collective-permute-done.10.refs_7_), channel_id=1, source_target_pairs={{0,4},{4,8},{8,12},{12,14},{14,10},{10,6},{6,2},{2,0},{1,5},{5,9},... | collective-permute-start | bytes 540680 | tf_op jit(solution)/shard_map/ppermute | solution.py:90
  58.9 13.0 %collective-permute-start.24 = (bf16[128,1408]{1,0:T(8,128)(2,1)S(1)}, bf16[128,1408]{1,0:T(8,128)(2,1)S(1)}, u32[]{:S(2)}, u32[]{:S(2)}) collective-permute-start(bf16[128,1408]{1,0:T(8,128)(2,1)S(1)} %collective-permute-done.18.refs_5_), channel_id=1, source_target_pairs={{0,4},{4,8},{8,12},{12,14},{14,10},{10,6},{6,2},{2,0},{1,5},{5,9},... | collective-permute-start | bytes 1081352 | tf_op jit(solution)/shard_map/ppermute | solution.py:90
  60.8 11.1 %collective-permute-start.25 = (bf16[128,1408]{1,0:T(8,128)(2,1)S(1)}, bf16[128,1408]{1,0:T(8,128)(2,1)S(1)}, u32[]{:S(2)}, u32[]{:S(2)}) collective-permute-start(bf16[128,1408]{1,0:T(8,128)(2,1)S(1)} %collective-permute-done.19.refs_2_), channel_id=1, source_target_pairs={{4,0},{8,4},{12,8},{14,12},{10,14},{6,10},{2,6},{0,2},{5,1},{9,5},... | collective-permute-start | bytes 1081352 | tf_op jit(solution)/shard_map/ppermute | solution.py:90
  61.0 10.9 %collective-permute-start.22 = (bf16[4,128,256]{2,1,0:T(8,128)(2,1)S(1)}, bf16[4,128,256]{2,1,0:T(8,128)(2,1)S(1)}, u32[]{:S(2)}, u32[]{:S(2)}) collective-permute-start(bf16[4,128,256]{2,1,0:T(8,128)(2,1)S(1)} %get-tuple-element.261.refs_4_), channel_id=1, source_target_pairs={{0,16},{16,0},{1,17},{17,1},{2,18},{18,2},{3,19},{19,3},{4,20},{20... | collective-permute-start | bytes 786440 | tf_op jit(solution)/shard_map/ppermute | solution.py:52
  72.1 9.2 %collective-permute-start.30 = (bf16[64,1408]{1,0:T(8,128)(2,1)S(1)}, bf16[64,1408]{1,0:T(8,128)(2,1)S(1)}, u32[]{:S(2)}, u32[]{:S(2)}) collective-permute-start(bf16[64,1408]{1,0:T(8,128)(2,1)S(1)} %slice.67), channel_id=1, source_target_pairs={{4,0},{8,4},{12,8},{14,12},{10,14},{6,10},{2,6},{0,2},{5,1},{9,5},... | collective-permute-start | bytes 540680 | tf_op jit(solution)/shard_map/ppermute | solution.py:90
  72.5 8.8 %collective-permute-start.29 = (bf16[64,1408]{1,0:T(8,128)(2,1)S(1)}, bf16[64,1408]{1,0:T(8,128)(2,1)S(1)}, u32[]{:S(2)}, u32[]{:S(2)}) collective-permute-start(bf16[64,1408]{1,0:T(8,128)(2,1)S(1)} %slice.66), channel_id=1, source_target_pairs={{0,4},{4,8},{8,12},{12,14},{14,10},{10,6},{6,2},{2,0},{1,5},{5,9},... | collective-permute-start | bytes 540680 | tf_op jit(solution)/shard_map/ppermute | solution.py:90
  117.5 10.9 %collective-permute-start.47 = (bf16[128,1408]{1,0:T(8,128)(2,1)S(1)}, bf16[128,1408]{1,0:T(8,128)(2,1)S(1)}, u32[]{:S(2)}, u32[]{:S(2)}) collective-permute-start(bf16[128,1408]{1,0:T(8,128)(2,1)S(1)} %get-tuple-element.361), channel_id=1, source_target_pairs={{0,4},{4,8},{8,12},{12,14},{14,10},{10,6},{6,2},{2,0},{1,5},{5,9},... | collective-permute-start | bytes 1081352 | tf_op jit(solution)/shard_map/ppermute | solution.py:90
  119.0 10.5 %collective-permute-start.48 = (bf16[128,1408]{1,0:T(8,128)(2,1)S(1)}, bf16[128,1408]{1,0:T(8,128)(2,1)S(1)}, u32[]{:S(2)}, u32[]{:S(2)}) collective-permute-start(bf16[128,1408]{1,0:T(8,128)(2,1)S(1)} %get-tuple-element.362), channel_id=1, source_target_pairs={{4,0},{8,4},{12,8},{14,12},{10,14},{6,10},{2,6},{0,2},{5,1},{9,5},... | collective-permute-start | bytes 1081352 | tf_op jit(solution)/shard_map/ppermute | solution.py:90
  129.7 10.8 %collective-permute-start.54 = (bf16[128,1408]{1,0:T(8,128)(2,1)S(1)}, bf16[128,1408]{1,0:T(8,128)(2,1)S(1)}, u32[]{:S(2)}, u32[]{:S(2)}) collective-permute-start(bf16[128,1408]{1,0:T(8,128)(2,1)S(1)} %get-tuple-element.381), channel_id=1, source_target_pairs={{0,4},{4,8},{8,12},{12,14},{14,10},{10,6},{6,2},{2,0},{1,5},{5,9},... | collective-permute-start | bytes 1081352 | tf_op jit(solution)/shard_map/ppermute | solution.py:90
  131.4 10.9 %collective-permute-start.55 = (bf16[128,1408]{1,0:T(8,128)(2,1)S(1)}, bf16[128,1408]{1,0:T(8,128)(2,1)S(1)}, u32[]{:S(2)}, u32[]{:S(2)}) collective-permute-start(bf16[128,1408]{1,0:T(8,128)(2,1)S(1)} %get-tuple-element.382), channel_id=1, source_target_pairs={{4,0},{8,4},{12,8},{14,12},{10,14},{6,10},{2,6},{0,2},{5,1},{9,5},... | collective-permute-start | bytes 1081352 | tf_op jit(solution)/shard_map/ppermute | solution.py:90
  133.9 9.7 %collective-permute-start.56 = (bf16[128,1024]{1,0:T(8,128)(2,1)S(1)}, bf16[128,1024]{1,0:T(8,128)(2,1)S(1)}, u32[]{:S(2)}, u32[]{:S(2)}) collective-permute-start(bf16[128,1024]{1,0:T(8,128)(2,1)S(1)} %fusion.2), channel_id=1, source_target_pairs={{0,16},{16,0},{1,17},{17,1},{2,18},{18,2},{3,19},{19,3},{4,20},{20... | collective-permute-start | bytes 786440 | tf_op jit(solution)/shard_map/ppermute | solution.py:52
  140.5 9.4 %collective-permute-start.60 = (bf16[88,1024]{1,0:T(8,128)(2,1)S(1)}, bf16[88,1024]{1,0:T(8,128)(2,1)S(1)}, u32[]{:S(2)}, u32[]{:S(2)}) collective-permute-start(bf16[88,1024]{1,0:T(8,128)(2,1)S(1)} %add_convert_fusion.3.low_ref), channel_id=1, source_target_pairs={{0,16},{16,0},{1,17},{17,1},{2,18},{18,2},{3,19},{19,3},{4,20},{20... | collective-permute-start | bytes 540680 | tf_op jit(solution)/shard_map/ppermute | solution.py:52
  143.8 9.3 %collective-permute-start.58 = (bf16[128,1024]{1,0:T(8,128)(2,1)S(1)}, bf16[128,1024]{1,0:T(8,128)(2,1)S(1)}, u32[]{:S(2)}, u32[]{:S(2)}) collective-permute-start(bf16[128,1024]{1,0:T(8,128)(2,1)S(1)} %get-tuple-element.393), channel_id=1, source_target_pairs={{0,4},{4,8},{8,12},{12,14},{14,10},{10,6},{6,2},{2,0},{1,5},{5,9},... | collective-permute-start | bytes 786440 | tf_op jit(solution)/shard_map/ppermute | solution.py:90
  145.1 9.2 %collective-permute-start.59 = (bf16[128,1024]{1,0:T(8,128)(2,1)S(1)}, bf16[128,1024]{1,0:T(8,128)(2,1)S(1)}, u32[]{:S(2)}, u32[]{:S(2)}) collective-permute-start(bf16[128,1024]{1,0:T(8,128)(2,1)S(1)} %get-tuple-element.394), channel_id=1, source_target_pairs={{4,0},{8,4},{12,8},{14,12},{10,14},{6,10},{2,6},{0,2},{5,1},{9,5},... | collective-permute-start | bytes 786440 | tf_op jit(solution)/shard_map/ppermute | solution.py:90
  146.0 14.8 %collective-permute-start.63 = (bf16[128,1408]{1,0:T(8,128)(2,1)S(1)}, bf16[128,1408]{1,0:T(8,128)(2,1)S(1)}, u32[]{:S(2)}, u32[]{:S(2)}) collective-permute-start(bf16[128,1408]{1,0:T(8,128)(2,1)S(1)} %get-tuple-element.407), channel_id=1, source_target_pairs={{0,4},{4,8},{8,12},{12,14},{14,10},{10,6},{6,2},{2,0},{1,5},{5,9},... | collective-permute-start | bytes 1081352 | tf_op jit(solution)/shard_map/ppermute | solution.py:90
  147.4 14.7 %collective-permute-start.64 = (bf16[128,1408]{1,0:T(8,128)(2,1)S(1)}, bf16[128,1408]{1,0:T(8,128)(2,1)S(1)}, u32[]{:S(2)}, u32[]{:S(2)}) collective-permute-start(bf16[128,1408]{1,0:T(8,128)(2,1)S(1)} %get-tuple-element.408), channel_id=1, source_target_pairs={{4,0},{8,4},{12,8},{14,12},{10,14},{6,10},{2,6},{0,2},{5,1},{9,5},... | collective-permute-start | bytes 1081352 | tf_op jit(solution)/shard_map/ppermute | solution.py:90
  154.5 9.9 %collective-permute-start.61 = (bf16[128,1024]{1,0:T(8,128)(2,1)S(1)}, bf16[128,1024]{1,0:T(8,128)(2,1)S(1)}, u32[]{:S(2)}, u32[]{:S(2)}) collective-permute-start(bf16[128,1024]{1,0:T(8,128)(2,1)S(1)} %get-tuple-element.400), channel_id=1, source_target_pairs={{0,4},{4,8},{8,12},{12,14},{14,10},{10,6},{6,2},{2,0},{1,5},{5,9},... | collective-permute-start | bytes 786440 | tf_op jit(solution)/shard_map/ppermute | solution.py:90
  155.7 9.9 %collective-permute-start.62 = (bf16[128,1024]{1,0:T(8,128)(2,1)S(1)}, bf16[128,1024]{1,0:T(8,128)(2,1)S(1)}, u32[]{:S(2)}, u32[]{:S(2)}) collective-permute-start(bf16[128,1024]{1,0:T(8,128)(2,1)S(1)} %get-tuple-element.401), channel_id=1, source_target_pairs={{4,0},{8,4},{12,8},{14,12},{10,14},{6,10},{2,6},{0,2},{5,1},{9,5},... | collective-permute-start | bytes 786440 | tf_op jit(solution)/shard_map/ppermute | solution.py:90
  156.6 9.0 %collective-permute-start.66 = (bf16[128,1024]{1,0:T(8,128)(2,1)S(1)}, bf16[128,1024]{1,0:T(8,128)(2,1)S(1)}, u32[]{:S(2)}, u32[]{:S(2)}) collective-permute-start(bf16[128,1024]{1,0:T(8,128)(2,1)S(1)} %fusion.3), channel_id=1, source_target_pairs={{0,16},{16,0},{1,17},{17,1},{2,18},{18,2},{3,19},{19,3},{4,20},{20... | collective-permute-start | bytes 786440 | tf_op jit(solution)/shard_map/ppermute | solution.py:52
  (52 other events, 402.4 us)

commit v7 on v6

--- a/solution.py
+++ b/solution.py
@@ -389,7 +389,6 @@
         down_ref[pl.ds(pl.multiple_of(chip * padded + first, ROWS), value.shape[0]), :] = value
 
     place_chunks(size, scal, chunks, store)
-    tile = 256
 
     main = main_part(units)
     rest = units - main
@@ -404,11 +403,9 @@
         ggu_ref[:, up_at : up_at + count] = (grad * (gate * sig)).astype(BF)
         ggu_ref[:, gate_at : gate_at + count] = (grad * up * (sig * (1.0 + gate * (1.0 - sig)))).astype(BF)
 
-    @pl.loop(0, width // tile)
-    def _(i):
-        at = pl.multiple_of(i * tile, tile)
-        back = dot_rt(ggu_ref[...], w_in[pl.ds(at, tile), :])
-        share(back, rows, keep_ref, give_ref, pl.ds(at, tile))
+    for at, count in tiles_of(width):
+        back = dot_rt(ggu_ref[...], w_in[at : at + count, :])
+        share(back, rows, keep_ref, give_ref, slice(at, at + count))
 
 
 def share(partial, rows, keep_ref, give_ref, columns):
@@ -419,11 +416,8 @@
 
 
 def last_projection(rows, scal, hid_ref, down_ref, keep_ref, give_ref):
-    tile = 256
-
-    @pl.loop(0, down_ref.shape[1] // tile)
-    def _(i):
-        columns = pl.ds(pl.multiple_of(i * tile, tile), tile)
+    for at, count in tiles_of(down_ref.shape[1]):
+        columns = slice(at, at + count)
         share(dot(hid_ref[...], down_ref[:, columns]), rows, keep_ref, give_ref, columns)
 
 
@@ -436,11 +430,8 @@
     gm_ref, total = refs[-2:]
     for b in range(4):
         gm_ref[b * rows : (b + 1) * rows, :] = refs[b][...]
-    tile = 256
-
-    @pl.loop(0, gm_ref.shape[1] // tile)
-    def _(i):
-        columns = pl.ds(pl.multiple_of(i * tile, tile), tile)
+    for at, count in tiles_of(gm_ref.shape[1]):
+        columns = slice(at, at + count)
         total[:, columns] = dot_lt(hid_ref[...], gm_ref[:, columns])
 
     write_parts(size, padded, scal, total, refs[4:-2])

time: 185 us -> 184 us (level)
  Pallas kernels: 47 us -> 45 us
    pallas_call x29, Pallas kernels: 47 us -> 45 us  [call(): pl.pallas_call(body, name=body.func.__name__, out_shape=outs, in_specs=[p...]
  transfers between devices with their start and end apart: 74 -> 74, of which waited for: 34 -> 35; matrix products, arithmetic and copies ran while one was open for 1% -> 1% of each run, Pallas kernels for 23% -> 22%
where the time goes in v7:
time: 184 us; the launch traced here: 183 us
  starting transfers between devices  72.4 us (39%)
  waiting for transfers between devices  57.9 us (31%)
  Pallas kernels  45 us (24%)
  local copies, waits for them, and re-layouts  5.56 us (3%)
    pallas_call x29, Pallas kernels, call(): pl.pallas_call(body, name=body.func.__name__, out_shape=outs, in_specs=[p...  45 us
    ppermute x24, starting transfers between devices, exchange(): lax.ppermute(pair[0], 'ring', self.right)  39.3 us
    ppermute x24, waiting for transfers between devices, exchange(): lax.ppermute(pair[0], 'ring', self.right)  31.4 us
    ppermute x24, waiting for transfers between devices, exchange(): lax.ppermute(pair[1], 'ring', self.left)  25.2 us
    ppermute x13, starting transfers between devices, across(): return lax.ppermute(value, 'rep', SWAP)  19 us
    ppermute x24, starting transfers between devices, exchange(): lax.ppermute(pair[1], 'ring', self.left)  12.2 us
    unnamed x23, local copies, waits for them, and re-layouts  4.66 us
  transfers between devices with their start and end apart: 74, of which 35 were waited for; matrix products, arithmetic and copies ran while one was open for 1% of the time, Pallas kernels for 22%

profile of v7, /device:TPU:0, one launch (start us, length us, event | category | flops | bytes accessed | tf_op | source)
XLA Modules:
  0.0 183.3 jit_solution(8249571034525289258)
XLA Ops:
  5.5 3.0 %collective-permute-start.1 = (bf16[128,1024]{1,0:T(8,128)(2,1)S(1)}, bf16[128,1024]{1,0:T(8,128)(2,1)S(1)}, u32[]{:S(2)}, u32[]{:S(2)}) collective-permute-start(bf16[128,1024]{1,0:T(8,128)(2,1)S(1)} %constant_dynamic-update-slice_fusion.refs_4_.refs_0_), channel_id=1, source_target_pairs={{0,4},{4,8},{8,12},{12,14},{14,10},{10,6},{6,2},{2,0},{1,5},{5,9},... | collective-permute-start | bytes 786440 | tf_op jit(solution)/shard_map/ppermute | solution.py:90
  12.1 2.0 %collective-permute-start.11 = (bf16[88,1024]{1,0:T(8,128)(2,1)S(1)}, bf16[88,1024]{1,0:T(8,128)(2,1)S(1)}, u32[]{:S(2)}, u32[]{:S(2)}) collective-permute-start(bf16[88,1024]{1,0:T(8,128)(2,1)S(1)} %get-tuple-element.307.refs_1_), channel_id=1, source_target_pairs={{4,0},{8,4},{12,8},{14,12},{10,14},{6,10},{2,6},{0,2},{5,1},{9,5},... | collective-permute-start | bytes 540680 | tf_op jit(solution)/shard_map/ppermute | solution.py:90
  15.2 2.4 %collective-permute-done.2.refs_5_.refs_1_ = bf16[128,1024]{1,0:T(8,128)(2,1)S(1)} collective-permute-done((bf16[128,1024]{1,0:T(8,128)(2,1)S(1)}, bf16[128,1024]{1,0:T(8,128)(2,1)S(1)}, u32[]{:S(2)}, u32[]{:S(2)}) %collective-permute-start.2) | collective-permute-done | bytes 262176 | tf_op jit(solution)/shard_map/ppermute | solution.py:90
  21.2 4.7 %collective-permute-done.5.refs_9_.refs_5_ = bf16[128,1024]{1,0:T(8,128)(2,1)S(1)} collective-permute-done((bf16[128,1024]{1,0:T(8,128)(2,1)S(1)}, bf16[128,1024]{1,0:T(8,128)(2,1)S(1)}, u32[]{:S(2)}, u32[]{:S(2)}) %collective-permute-start.5) | collective-permute-done | bytes 262176 | tf_op jit(solution)/shard_map/ppermute | solution.py:90
  31.7 3.5 %collective-permute-done.7.refs_8_.refs_4_ = bf16[128,1024]{1,0:T(8,128)(2,1)S(1)} collective-permute-done((bf16[128,1024]{1,0:T(8,128)(2,1)S(1)}, bf16[128,1024]{1,0:T(8,128)(2,1)S(1)}, u32[]{:S(2)}, u32[]{:S(2)}) %collective-permute-start.7) | collective-permute-done | bytes 262176 | tf_op jit(solution)/shard_map/ppermute | solution.py:90
  39.0 2.3 %collective-permute-done.15.refs_6_ = bf16[128,1408]{1,0:T(8,128)(2,1)S(1)} collective-permute-done((bf16[128,1408]{1,0:T(8,128)(2,1)S(1)}, bf16[128,1408]{1,0:T(8,128)(2,1)S(1)}, u32[]{:S(2)}, u32[]{:S(2)}) %collective-permute-start.15) | collective-permute-done | bytes 360480 | tf_op jit(solution)/shard_map/ppermute | solution.py:90
  41.3 2.6 %collective-permute-done.16.refs_1_ = bf16[128,1408]{1,0:T(8,128)(2,1)S(1)} collective-permute-done((bf16[128,1408]{1,0:T(8,128)(2,1)S(1)}, bf16[128,1408]{1,0:T(8,128)(2,1)S(1)}, u32[]{:S(2)}, u32[]{:S(2)}) %collective-permute-start.16) | collective-permute-done | bytes 360480 | tf_op jit(solution)/shard_map/ppermute | solution.py:90
  51.6 7.0 %attention.1 = (bf16[4,128,256]{2,1,0:T(8,128)(2,1)S(1)}, bf16[512,1024]{1,0:T(8,128)(2,1)S(1)}, bf16[512,768]{1,0:T(8,128)(2,1)S(1)}, f32[16,128,128]{2,1,0:T(8,128)S(1)}, bf16[1024,768]{1,0:T(8,128)(2,1)S(1)}) custom-call(s32[21]{0:T(128)S(1)} %dynamic-slice_bitcast_fusion.scal, bf16[130,1024]{1,0:T(8,128)(2,1)S(1)} %pack_tokens.1.refs_0_.block_ref, ...), custom_call_target="tpu_custom_call" | custom-call | flops 805306368 | bytes 8142932 | tf_op jit(solution)/shard_map/attention/pallas_call | solution.py:163
  58.9 1.9 %collective-permute-start.24 = (bf16[128,1408]{1,0:T(8,128)(2,1)S(1)}, bf16[128,1408]{1,0:T(8,128)(2,1)S(1)}, u32[]{:S(2)}, u32[]{:S(2)}) collective-permute-start(bf16[128,1408]{1,0:T(8,128)(2,1)S(1)} %collective-permute-done.18.refs_5_), channel_id=1, source_target_pairs={{0,4},{4,8},{8,12},{12,14},{14,10},{10,6},{6,2},{2,0},{1,5},{5,9},... | collective-permute-start | bytes 1081352 | tf_op jit(solution)/shard_map/ppermute | solution.py:90
  62.4 1.9 %collective-permute-start.26 = (bf16[88,1024]{1,0:T(8,128)(2,1)S(1)}, bf16[88,1024]{1,0:T(8,128)(2,1)S(1)}, u32[]{:S(2)}, u32[]{:S(2)}) collective-permute-start(bf16[88,1024]{1,0:T(8,128)(2,1)S(1)} %collective-permute-done.20.refs_6_), channel_id=1, source_target_pairs={{0,4},{4,8},{8,12},{12,14},{14,10},{10,6},{6,2},{2,0},{1,5},{5,9},... | collective-permute-start | bytes 540680 | tf_op jit(solution)/shard_map/ppermute | solution.py:90
  64.5 5.5 %collective-permute-done.26.refs_5_ = bf16[88,1024]{1,0:T(8,128)(2,1)S(1)} collective-permute-done((bf16[88,1024]{1,0:T(8,128)(2,1)S(1)}, bf16[88,1024]{1,0:T(8,128)(2,1)S(1)}, u32[]{:S(2)}, u32[]{:S(2)}) %collective-permute-start.26) | collective-permute-done | bytes 180256 | tf_op jit(solution)/shard_map/ppermute | solution.py:90
  70.0 1.9 %collective-permute-done.27.refs_4_ = bf16[88,1024]{1,0:T(8,128)(2,1)S(1)} collective-permute-done((bf16[88,1024]{1,0:T(8,128)(2,1)S(1)}, bf16[88,1024]{1,0:T(8,128)(2,1)S(1)}, u32[]{:S(2)}, u32[]{:S(2)}) %collective-permute-start.27) | collective-permute-done | bytes 180256 | tf_op jit(solution)/shard_map/ppermute | solution.py:90
  72.5 1.7 collective-permute-start.29
  74.5 2.0 %collective-permute-start.31 = (bf16[48,1024]{1,0:T(8,128)(2,1)S(1)}, bf16[48,1024]{1,0:T(8,128)(2,1)S(1)}, u32[]{:S(2)}, u32[]{:S(2)}) collective-permute-start(bf16[48,1024]{1,0:T(8,128)(2,1)S(1)} %slice.68), channel_id=1, source_target_pairs={{0,4},{4,8},{8,12},{12,14},{14,10},{10,6},{6,2},{2,0},{1,5},{5,9},... | collective-permute-start | bytes 294920 | tf_op jit(solution)/shard_map/ppermute | solution.py:90
  76.5 2.7 %middle.1 = (f32[512,1024]{1,0:T(8,128)S(1)}, bf16[512,1024]{1,0:T(8,128)(2,1)S(1)}, bf16[512,1024]{1,0:T(8,128)(2,1)S(1)}, bf16[256,1024]{1,0:T(8,128)(2,1)S(1)}) custom-call(s32[21]{0:T(128)S(1)} %dynamic-slice_bitcast_fusion.scal, bf16[130,1024]{1,0:T(8,128)(2,1)S(1)} %pack_tokens.1.refs_0_.block_ref, ...), custom_call_target="tpu_custom_call" | custom-call | flops 1073741824 | bytes 8929364 | tf_op jit(solution)/shard_map/middle/pallas_call | solution.py:163
  79.2 1.7 collective-permute-done.32.refs_9_
  81.8 3.0 %hidden_units.1 = (f32[512,704]{1,0:T(8,128)S(1)}, f32[512,704]{1,0:T(8,128)S(1)}, bf16[512,704]{1,0:T(8,128)(2,1)S(1)}, bf16[1024,1408]{1,0:T(8,128)(2,1)S(1)}) custom-call(s32[21]{0:T(128)S(1)} %dynamic-slice_bitcast_fusion.scal, bf16[512,1024]{1,0:T(8,128)(2,1)S(1)} %get-tuple-element.276.h2_ref, ...), custom_call_target="tpu_custom_call" | custom-call | flops 16000000000 | bytes 10420308 | tf_op jit(solution)/shard_map/hidden_units/pallas_call | solution.py:163
  84.8 1.8 grad_down_parts.1
  88.7 3.9 %hidden_back.1 = (bf16[512,1408]{1,0:T(8,128)(2,1)S(1)}, f32[2,128,1024]{2,1,0:T(8,128)S(1)}, bf16[2,128,1024]{2,1,0:T(8,128)(2,1)S(1)}, bf16[704,1024]{1,0:T(8,128)(2,1)S(1)}) custom-call(s32[21]{0:T(128)S(1)} %dynamic-slice_bitcast_fusion.scal, bf16[512,1024]{1,0:T(8,128)(2,1)S(1)} %get-tuple-element.306.refs_0_, ...), custom_call_target="tpu_custom_call" | custom-call | flops 32000000000 | bytes 12714068 | tf_op jit(solution)/shard_map/hidden_back/pallas_call | solution.py:163
  92.8 1.8 collective-permute-start.38
  96.6 2.7 %grad_in_parts.1 = (bf16[128,1408]{1,0:T(8,128)(2,1)S(1)}, bf16[128,1408]{1,0:T(8,128)(2,1)S(1)}, bf16[128,1408]{1,0:T(8,128)(2,1)S(1)}, bf16[128,1408]{1,0:T(8,...) custom-call(s32[21]{0:T(128)S(1)} %dynamic-slice_bitcast_fusion.scal, ...), custom_call_target="tpu_custom_call" | custom-call | flops 1610612736 | bytes 5374036 | tf_op jit(solution)/shard_map/grad_in_parts/pallas_call | solution.py:163
  103.4 1.7 collective-permute-start.41
  119.6 7.0 %attention_back.1 = (bf16[512,768]{1,0:T(8,128)(2,1)S(1)}, bf16[512,1024]{1,0:T(8,128)(2,1)S(1)}, f32[2,128,1024]{2,1,0:T(8,128)S(1)}, bf16[2,128,1024]{2,1,0:T(8,128)(2,1)S(1)}) custom-call(s32[21]{0:T(128)S(1)} %dynamic-slice_bitcast_fusion.scal, bf16[2,128,1024]{2,1,0:T(8,128)(2,1)S(1)} %get-tuple-element.350.ga_own, ...), custom_call_target="tpu_custom_call" | custom-call | flops 1879048192 | bytes 8650836 | tf_op jit(solution)/shard_map/attention_back/pallas_call | solution.py:163
  128.2 1.7 collective-permute-start.54
  130.3 2.1 %grad_first_parts.1 = (bf16[128,1024]{1,0:T(8,128)(2,1)S(1)}, bf16[128,1024]{1,0:T(8,128)(2,1)S(1)}, bf16[128,1024]{1,0:T(8,128)(2,1)S(1)}, bf16[128,1024]{1,0:T...) custom-call(s32[21]{0:T(128)S(1)} %dynamic-slice_bitcast_fusion.scal, ...), custom_call_target="tpu_custom_call" | custom-call | flops 32000000000 | bytes 6029396 | tf_op jit(solution)/shard_map/grad_first_parts/pallas_call | solution.py:163
  136.1 3.0 %collective-permute-done.54.right_got = bf16[128,1408]{1,0:T(8,128)(2,1)S(1)} collective-permute-done((bf16[128,1408]{1,0:T(8,128)(2,1)S(1)}, bf16[128,1408]{1,0:T(8,128)(2,1)S(1)}, u32[]{:S(2)}, u32[]{:S(2)}) %collective-permute-start.54) | collective-permute-done | bytes 360480 | tf_op jit(solution)/shard_map/ppermute | solution.py:90
  139.0 1.8 collective-permute-start.60
  146.6 1.8 finish_tokens.1
  148.4 3.2 %collective-permute-done.58.right_got = bf16[128,1024]{1,0:T(8,128)(2,1)S(1)} collective-permute-done((bf16[128,1024]{1,0:T(8,128)(2,1)S(1)}, bf16[128,1024]{1,0:T(8,128)(2,1)S(1)}, u32[]{:S(2)}, u32[]{:S(2)}) %collective-permute-start.58) | collective-permute-done | bytes 262176 | tf_op jit(solution)/shard_map/ppermute | solution.py:90
  156.7 2.6 %collective-permute-done.63.right_ref = bf16[128,1408]{1,0:T(8,128)(2,1)S(1)} collective-permute-done((bf16[128,1408]{1,0:T(8,128)(2,1)S(1)}, bf16[128,1408]{1,0:T(8,128)(2,1)S(1)}, u32[]{:S(2)}, u32[]{:S(2)}) %collective-permute-start.63) | collective-permute-done | bytes 360480 | tf_op jit(solution)/shard_map/ppermute | solution.py:90
  168.3 3.0 %collective-permute-done.67.right_ref = bf16[128,1024]{1,0:T(8,128)(2,1)S(1)} collective-permute-done((bf16[128,1024]{1,0:T(8,128)(2,1)S(1)}, bf16[128,1024]{1,0:T(8,128)(2,1)S(1)}, u32[]{:S(2)}, u32[]{:S(2)}) %collective-permute-start.67) | collective-permute-done | bytes 262176 | tf_op jit(solution)/shard_map/ppermute | solution.py:90
  175.8 2.6 %unpack_in.1 = f32[64,5632]{1,0:T(8,128)} custom-call(s32[21]{0:T(128)S(1)} %dynamic-slice_bitcast_fusion.scal, bf16[64,1408]{1,0:T(8,128)(2,1)S(1)} %get-tuple-element.430.own_ref, bf16[64,1408]{1,0:T(8,128)(2,1)S(1)} %collective-permute-done.65.near_ref, bf16[64,1408]{1,0:T(8,128)(2,1)S(1)} %collective-permute-done.69.far_ref, ...), custom_call_target="tpu_custom_call" | custom-call | flops 4000000000 | bytes 2162772 | tf_op jit(solution)/shard_map/unpack_in/pallas_call | solution.py:163
  (189 shorter events, 91.5 us)
Async XLA Ops:
  5.5 9.7 %collective-permute-start.1 = (bf16[128,1024]{1,0:T(8,128)(2,1)S(1)}, bf16[128,1024]{1,0:T(8,128)(2,1)S(1)}, u32[]{:S(2)}, u32[]{:S(2)}) collective-permute-start(bf16[128,1024]{1,0:T(8,128)(2,1)S(1)} %constant_dynamic-update-slice_fusion.refs_4_.refs_0_), channel_id=1, source_target_pairs={{0,4},{4,8},{8,12},{12,14},{14,10},{10,6},{6,2},{2,0},{1,5},{5,9},... | collective-permute-start | bytes 786440 | tf_op jit(solution)/shard_map/ppermute | solution.py:90
  8.4 9.2 %collective-permute-start.2 = (bf16[128,1024]{1,0:T(8,128)(2,1)S(1)}, bf16[128,1024]{1,0:T(8,128)(2,1)S(1)}, u32[]{:S(2)}, u32[]{:S(2)}) collective-permute-start(bf16[128,1024]{1,0:T(8,128)(2,1)S(1)} %constant_dynamic-update-slice_fusion.refs_4_.refs_0_), channel_id=1, source_target_pairs={{4,0},{8,4},{12,8},{14,12},{10,14},{6,10},{2,6},{0,2},{5,1},{9,5},... | collective-permute-start | bytes 786440 | tf_op jit(solution)/shard_map/ppermute | solution.py:90
  12.1 15.9 %collective-permute-start.11 = (bf16[88,1024]{1,0:T(8,128)(2,1)S(1)}, bf16[88,1024]{1,0:T(8,128)(2,1)S(1)}, u32[]{:S(2)}, u32[]{:S(2)}) collective-permute-start(bf16[88,1024]{1,0:T(8,128)(2,1)S(1)} %get-tuple-element.307.refs_1_), channel_id=1, source_target_pairs={{4,0},{8,4},{12,8},{14,12},{10,14},{6,10},{2,6},{0,2},{5,1},{9,5},... | collective-permute-start | bytes 540680 | tf_op jit(solution)/shard_map/ppermute | solution.py:90
  14.1 14.0 %collective-permute-start.10 = (bf16[88,1024]{1,0:T(8,128)(2,1)S(1)}, bf16[88,1024]{1,0:T(8,128)(2,1)S(1)}, u32[]{:S(2)}, u32[]{:S(2)}) collective-permute-start(bf16[88,1024]{1,0:T(8,128)(2,1)S(1)} %get-tuple-element.307.refs_1_), channel_id=1, source_target_pairs={{0,4},{4,8},{8,12},{12,14},{14,10},{10,6},{6,2},{2,0},{1,5},{5,9},... | collective-permute-start | bytes 540680 | tf_op jit(solution)/shard_map/ppermute | solution.py:90
  26.0 9.2 %collective-permute-start.7 = (bf16[128,1024]{1,0:T(8,128)(2,1)S(1)}, bf16[128,1024]{1,0:T(8,128)(2,1)S(1)}, u32[]{:S(2)}, u32[]{:S(2)}) collective-permute-start(bf16[128,1024]{1,0:T(8,128)(2,1)S(1)} %collective-permute-done.5.refs_9_.refs_5_), channel_id=1, source_target_pairs={{0,4},{4,8},{8,12},{12,14},{14,10},{10,6},{6,2},{2,0},{1,5},{5,9},... | collective-permute-start | bytes 786440 | tf_op jit(solution)/shard_map/ppermute | solution.py:90
  27.6 9.2 %collective-permute-start.8 = (bf16[128,1024]{1,0:T(8,128)(2,1)S(1)}, bf16[128,1024]{1,0:T(8,128)(2,1)S(1)}, u32[]{:S(2)}, u32[]{:S(2)}) collective-permute-start(bf16[128,1024]{1,0:T(8,128)(2,1)S(1)} %collective-permute-done.6.refs_6_.refs_2_), channel_id=1, source_target_pairs={{4,0},{8,4},{12,8},{14,12},{10,14},{6,10},{2,6},{0,2},{5,1},{9,5},... | collective-permute-start | bytes 786440 | tf_op jit(solution)/shard_map/ppermute | solution.py:90
  28.1 8.8 %collective-permute-start.12 = (bf16[128,1024]{1,0:T(8,128)(2,1)S(1)}, bf16[128,1024]{1,0:T(8,128)(2,1)S(1)}, u32[]{:S(2)}, u32[]{:S(2)}) collective-permute-start(bf16[128,1024]{1,0:T(8,128)(2,1)S(1)} %bitcast.29), channel_id=1, source_target_pairs={{0,16},{16,0},{1,17},{17,1},{2,18},{18,2},{3,19},{19,3},{4,20},{20... | collective-permute-start | bytes 786440 | tf_op jit(solution)/shard_map/ppermute | solution.py:52
  29.7 11.6 %collective-permute-start.15 = (bf16[128,1408]{1,0:T(8,128)(2,1)S(1)}, bf16[128,1408]{1,0:T(8,128)(2,1)S(1)}, u32[]{:S(2)}, u32[]{:S(2)}) collective-permute-start(bf16[128,1408]{1,0:T(8,128)(2,1)S(1)} %constant_dynamic-update-slice_fusion.2.refs_0_), channel_id=1, source_target_pairs={{0,4},{4,8},{8,12},{12,14},{14,10},{10,6},{6,2},{2,0},{1,5},{5,9},... | collective-permute-start | bytes 1081352 | tf_op jit(solution)/shard_map/ppermute | solution.py:90
  31.2 12.7 %collective-permute-start.16 = (bf16[128,1408]{1,0:T(8,128)(2,1)S(1)}, bf16[128,1408]{1,0:T(8,128)(2,1)S(1)}, u32[]{:S(2)}, u32[]{:S(2)}) collective-permute-start(bf16[128,1408]{1,0:T(8,128)(2,1)S(1)} %constant_dynamic-update-slice_fusion.2.refs_0_), channel_id=1, source_target_pairs={{4,0},{8,4},{12,8},{14,12},{10,14},{6,10},{2,6},{0,2},{5,1},{9,5},... | collective-permute-start | bytes 1081352 | tf_op jit(solution)/shard_map/ppermute | solution.py:90
  36.9 8.5 %collective-permute-start.17 = (bf16[130,1024]{1,0:T(8,128)(2,1)S(1)}, bf16[130,1024]{1,0:T(8,128)(2,1)S(1)}, u32[]{:S(2)}, u32[]{:S(2)}) collective-permute-start(bf16[130,1024]{1,0:T(8,128)(2,1)S(1)} %collective-permute-done.9.refs_2_), channel_id=1, source_target_pairs={{0,1},{1,0},{2,3},{3,2},{4,5},{5,4},{6,7},{7,6},{8,9},{9,8},{10,11... | collective-permute-start | bytes 798728 | tf_op jit(solution)/shard_map/ppermute | solution.py:56
  45.4 13.6 %collective-permute-start.18 = (bf16[128,1408]{1,0:T(8,128)(2,1)S(1)}, bf16[128,1408]{1,0:T(8,128)(2,1)S(1)}, u32[]{:S(2)}, u32[]{:S(2)}) collective-permute-start(bf16[128,1408]{1,0:T(8,128)(2,1)S(1)} %collective-permute-done.15.refs_6_), channel_id=1, source_target_pairs={{0,4},{4,8},{8,12},{12,14},{14,10},{10,6},{6,2},{2,0},{1,5},{5,9},... | collective-permute-start | bytes 1081352 | tf_op jit(solution)/shard_map/ppermute | solution.py:90
  46.9 12.0 %collective-permute-start.19 = (bf16[128,1408]{1,0:T(8,128)(2,1)S(1)}, bf16[128,1408]{1,0:T(8,128)(2,1)S(1)}, u32[]{:S(2)}, u32[]{:S(2)}) collective-permute-start(bf16[128,1408]{1,0:T(8,128)(2,1)S(1)} %collective-permute-done.16.refs_1_), channel_id=1, source_target_pairs={{4,0},{8,4},{12,8},{14,12},{10,14},{6,10},{2,6},{0,2},{5,1},{9,5},... | collective-permute-start | bytes 1081352 | tf_op jit(solution)/shard_map/ppermute | solution.py:90
  48.0 16.3 %collective-permute-start.23 = (bf16[1024,256]{1,0:T(8,128)(2,1)S(1)}, bf16[1024,256]{1,0:T(8,128)(2,1)S(1)}, u32[]{:S(2)}, u32[]{:S(2)}) collective-permute-start(bf16[1024,256]{1,0:T(8,128)(2,1)S(1)} %gather_out.1.refs_6_), channel_id=1, source_target_pairs={{0,16},{16,0},{1,17},{17,1},{2,18},{18,2},{3,19},{19,3},{4,20},{20... | collective-permute-start | bytes 1572872 | tf_op jit(solution)/shard_map/ppermute | solution.py:52
  49.6 9.0 %collective-permute-start.20 = (bf16[88,1024]{1,0:T(8,128)(2,1)S(1)}, bf16[88,1024]{1,0:T(8,128)(2,1)S(1)}, u32[]{:S(2)}, u32[]{:S(2)}) collective-permute-start(bf16[88,1024]{1,0:T(8,128)(2,1)S(1)} %collective-permute-done.10.refs_7_), channel_id=1, source_target_pairs={{0,4},{4,8},{8,12},{12,14},{14,10},{10,6},{6,2},{2,0},{1,5},{5,9},... | collective-permute-start | bytes 540680 | tf_op jit(solution)/shard_map/ppermute | solution.py:90
  58.9 13.0 %collective-permute-start.24 = (bf16[128,1408]{1,0:T(8,128)(2,1)S(1)}, bf16[128,1408]{1,0:T(8,128)(2,1)S(1)}, u32[]{:S(2)}, u32[]{:S(2)}) collective-permute-start(bf16[128,1408]{1,0:T(8,128)(2,1)S(1)} %collective-permute-done.18.refs_5_), channel_id=1, source_target_pairs={{0,4},{4,8},{8,12},{12,14},{14,10},{10,6},{6,2},{2,0},{1,5},{5,9},... | collective-permute-start | bytes 1081352 | tf_op jit(solution)/shard_map/ppermute | solution.py:90
  60.8 11.1 %collective-permute-start.25 = (bf16[128,1408]{1,0:T(8,128)(2,1)S(1)}, bf16[128,1408]{1,0:T(8,128)(2,1)S(1)}, u32[]{:S(2)}, u32[]{:S(2)}) collective-permute-start(bf16[128,1408]{1,0:T(8,128)(2,1)S(1)} %collective-permute-done.19.refs_2_), channel_id=1, source_target_pairs={{4,0},{8,4},{12,8},{14,12},{10,14},{6,10},{2,6},{0,2},{5,1},{9,5},... | collective-permute-start | bytes 1081352 | tf_op jit(solution)/shard_map/ppermute | solution.py:90
  61.0 10.9 %collective-permute-start.22 = (bf16[4,128,256]{2,1,0:T(8,128)(2,1)S(1)}, bf16[4,128,256]{2,1,0:T(8,128)(2,1)S(1)}, u32[]{:S(2)}, u32[]{:S(2)}) collective-permute-start(bf16[4,128,256]{2,1,0:T(8,128)(2,1)S(1)} %get-tuple-element.261.refs_4_), channel_id=1, source_target_pairs={{0,16},{16,0},{1,17},{17,1},{2,18},{18,2},{3,19},{19,3},{4,20},{20... | collective-permute-start | bytes 786440 | tf_op jit(solution)/shard_map/ppermute | solution.py:52
  72.1 9.2 %collective-permute-start.30 = (bf16[64,1408]{1,0:T(8,128)(2,1)S(1)}, bf16[64,1408]{1,0:T(8,128)(2,1)S(1)}, u32[]{:S(2)}, u32[]{:S(2)}) collective-permute-start(bf16[64,1408]{1,0:T(8,128)(2,1)S(1)} %slice.67), channel_id=1, source_target_pairs={{4,0},{8,4},{12,8},{14,12},{10,14},{6,10},{2,6},{0,2},{5,1},{9,5},... | collective-permute-start | bytes 540680 | tf_op jit(solution)/shard_map/ppermute | solution.py:90
  72.5 8.8 %collective-permute-start.29 = (bf16[64,1408]{1,0:T(8,128)(2,1)S(1)}, bf16[64,1408]{1,0:T(8,128)(2,1)S(1)}, u32[]{:S(2)}, u32[]{:S(2)}) collective-permute-start(bf16[64,1408]{1,0:T(8,128)(2,1)S(1)} %slice.66), channel_id=1, source_target_pairs={{0,4},{4,8},{8,12},{12,14},{14,10},{10,6},{6,2},{2,0},{1,5},{5,9},... | collective-permute-start | bytes 540680 | tf_op jit(solution)/shard_map/ppermute | solution.py:90
  116.0 10.9 %collective-permute-start.47 = (bf16[128,1408]{1,0:T(8,128)(2,1)S(1)}, bf16[128,1408]{1,0:T(8,128)(2,1)S(1)}, u32[]{:S(2)}, u32[]{:S(2)}) collective-permute-start(bf16[128,1408]{1,0:T(8,128)(2,1)S(1)} %get-tuple-element.361), channel_id=1, source_target_pairs={{0,4},{4,8},{8,12},{12,14},{14,10},{10,6},{6,2},{2,0},{1,5},{5,9},... | collective-permute-start | bytes 1081352 | tf_op jit(solution)/shard_map/ppermute | solution.py:90
  117.5 10.5 %collective-permute-start.48 = (bf16[128,1408]{1,0:T(8,128)(2,1)S(1)}, bf16[128,1408]{1,0:T(8,128)(2,1)S(1)}, u32[]{:S(2)}, u32[]{:S(2)}) collective-permute-start(bf16[128,1408]{1,0:T(8,128)(2,1)S(1)} %get-tuple-element.362), channel_id=1, source_target_pairs={{4,0},{8,4},{12,8},{14,12},{10,14},{6,10},{2,6},{0,2},{5,1},{9,5},... | collective-permute-start | bytes 1081352 | tf_op jit(solution)/shard_map/ppermute | solution.py:90
  128.2 10.8 %collective-permute-start.54 = (bf16[128,1408]{1,0:T(8,128)(2,1)S(1)}, bf16[128,1408]{1,0:T(8,128)(2,1)S(1)}, u32[]{:S(2)}, u32[]{:S(2)}) collective-permute-start(bf16[128,1408]{1,0:T(8,128)(2,1)S(1)} %get-tuple-element.381), channel_id=1, source_target_pairs={{0,4},{4,8},{8,12},{12,14},{14,10},{10,6},{6,2},{2,0},{1,5},{5,9},... | collective-permute-start | bytes 1081352 | tf_op jit(solution)/shard_map/ppermute | solution.py:90
  130.0 10.9 %collective-permute-start.55 = (bf16[128,1408]{1,0:T(8,128)(2,1)S(1)}, bf16[128,1408]{1,0:T(8,128)(2,1)S(1)}, u32[]{:S(2)}, u32[]{:S(2)}) collective-permute-start(bf16[128,1408]{1,0:T(8,128)(2,1)S(1)} %get-tuple-element.382), channel_id=1, source_target_pairs={{4,0},{8,4},{12,8},{14,12},{10,14},{6,10},{2,6},{0,2},{5,1},{9,5},... | collective-permute-start | bytes 1081352 | tf_op jit(solution)/shard_map/ppermute | solution.py:90
  132.5 9.7 %collective-permute-start.56 = (bf16[128,1024]{1,0:T(8,128)(2,1)S(1)}, bf16[128,1024]{1,0:T(8,128)(2,1)S(1)}, u32[]{:S(2)}, u32[]{:S(2)}) collective-permute-start(bf16[128,1024]{1,0:T(8,128)(2,1)S(1)} %fusion.2), channel_id=1, source_target_pairs={{0,16},{16,0},{1,17},{17,1},{2,18},{18,2},{3,19},{19,3},{4,20},{20... | collective-permute-start | bytes 786440 | tf_op jit(solution)/shard_map/ppermute | solution.py:52
  139.0 9.3 %collective-permute-start.60 = (bf16[88,1024]{1,0:T(8,128)(2,1)S(1)}, bf16[88,1024]{1,0:T(8,128)(2,1)S(1)}, u32[]{:S(2)}, u32[]{:S(2)}) collective-permute-start(bf16[88,1024]{1,0:T(8,128)(2,1)S(1)} %add_convert_fusion.3.low_ref), channel_id=1, source_target_pairs={{0,16},{16,0},{1,17},{17,1},{2,18},{18,2},{3,19},{19,3},{4,20},{20... | collective-permute-start | bytes 540680 | tf_op jit(solution)/shard_map/ppermute | solution.py:52
  142.3 9.3 %collective-permute-start.58 = (bf16[128,1024]{1,0:T(8,128)(2,1)S(1)}, bf16[128,1024]{1,0:T(8,128)(2,1)S(1)}, u32[]{:S(2)}, u32[]{:S(2)}) collective-permute-start(bf16[128,1024]{1,0:T(8,128)(2,1)S(1)} %get-tuple-element.393), channel_id=1, source_target_pairs={{0,4},{4,8},{8,12},{12,14},{14,10},{10,6},{6,2},{2,0},{1,5},{5,9},... | collective-permute-start | bytes 786440 | tf_op jit(solution)/shard_map/ppermute | solution.py:90
  143.6 9.2 %collective-permute-start.59 = (bf16[128,1024]{1,0:T(8,128)(2,1)S(1)}, bf16[128,1024]{1,0:T(8,128)(2,1)S(1)}, u32[]{:S(2)}, u32[]{:S(2)}) collective-permute-start(bf16[128,1024]{1,0:T(8,128)(2,1)S(1)} %get-tuple-element.394), channel_id=1, source_target_pairs={{4,0},{8,4},{12,8},{14,12},{10,14},{6,10},{2,6},{0,2},{5,1},{9,5},... | collective-permute-start | bytes 786440 | tf_op jit(solution)/shard_map/ppermute | solution.py:90
  144.5 14.8 %collective-permute-start.63 = (bf16[128,1408]{1,0:T(8,128)(2,1)S(1)}, bf16[128,1408]{1,0:T(8,128)(2,1)S(1)}, u32[]{:S(2)}, u32[]{:S(2)}) collective-permute-start(bf16[128,1408]{1,0:T(8,128)(2,1)S(1)} %get-tuple-element.407), channel_id=1, source_target_pairs={{0,4},{4,8},{8,12},{12,14},{14,10},{10,6},{6,2},{2,0},{1,5},{5,9},... | collective-permute-start | bytes 1081352 | tf_op jit(solution)/shard_map/ppermute | solution.py:90
  145.9 14.7 %collective-permute-start.64 = (bf16[128,1408]{1,0:T(8,128)(2,1)S(1)}, bf16[128,1408]{1,0:T(8,128)(2,1)S(1)}, u32[]{:S(2)}, u32[]{:S(2)}) collective-permute-start(bf16[128,1408]{1,0:T(8,128)(2,1)S(1)} %get-tuple-element.408), channel_id=1, source_target_pairs={{4,0},{8,4},{12,8},{14,12},{10,14},{6,10},{2,6},{0,2},{5,1},{9,5},... | collective-permute-start | bytes 1081352 | tf_op jit(solution)/shard_map/ppermute | solution.py:90
  153.0 9.9 %collective-permute-start.61 = (bf16[128,1024]{1,0:T(8,128)(2,1)S(1)}, bf16[128,1024]{1,0:T(8,128)(2,1)S(1)}, u32[]{:S(2)}, u32[]{:S(2)}) collective-permute-start(bf16[128,1024]{1,0:T(8,128)(2,1)S(1)} %get-tuple-element.400), channel_id=1, source_target_pairs={{0,4},{4,8},{8,12},{12,14},{14,10},{10,6},{6,2},{2,0},{1,5},{5,9},... | collective-permute-start | bytes 786440 | tf_op jit(solution)/shard_map/ppermute | solution.py:90
  154.2 9.9 %collective-permute-start.62 = (bf16[128,1024]{1,0:T(8,128)(2,1)S(1)}, bf16[128,1024]{1,0:T(8,128)(2,1)S(1)}, u32[]{:S(2)}, u32[]{:S(2)}) collective-permute-start(bf16[128,1024]{1,0:T(8,128)(2,1)S(1)} %get-tuple-element.401), channel_id=1, source_target_pairs={{4,0},{8,4},{12,8},{14,12},{10,14},{6,10},{2,6},{0,2},{5,1},{9,5},... | collective-permute-start | bytes 786440 | tf_op jit(solution)/shard_map/ppermute | solution.py:90
  155.2 8.9 %collective-permute-start.66 = (bf16[128,1024]{1,0:T(8,128)(2,1)S(1)}, bf16[128,1024]{1,0:T(8,128)(2,1)S(1)}, u32[]{:S(2)}, u32[]{:S(2)}) collective-permute-start(bf16[128,1024]{1,0:T(8,128)(2,1)S(1)} %fusion.3), channel_id=1, source_target_pairs={{0,16},{16,0},{1,17},{17,1},{2,18},{18,2},{3,19},{19,3},{4,20},{20... | collective-permute-start | bytes 786440 | tf_op jit(solution)/shard_map/ppermute | solution.py:52
  (52 other events, 400.3 us)

commit v8 on v7

--- a/solution.py
+++ b/solution.py
@@ -202,8 +202,8 @@
 
 def pack_tokens(rows, prefix_ref, tokens_ref, own_ref):
     own_ref[:rows, :] = tokens_ref[...]
-    for m in range(own_ref.shape[0] - rows):
-        own_ref[rows + m : rows + m + 1, :] = jnp.broadcast_to(prefix_ref[m : m + 1, :].astype(F32), (1, own_ref.shape[1])).astype(BF)
+    for m in range(prefix_ref.shape[1]):
+        own_ref[rows + m : rows + m + 1, :] = jnp.broadcast_to(prefix_ref[:, m : m + 1].astype(F32), (1, own_ref.shape[1])).astype(BF)
 
 
 def pack_first(size, width, scal, qkv_ref, out_ref, own_ref, sib_ref, sems):
@@ -602,7 +602,7 @@
     c = Gather(ring, down_rows)
     c.advance()
     b_got = sibling(b_sib)
-    (own,) = call(functools.partial(pack_tokens, rows), [shape((rows + micro, width), BF)], [], 0, prefix, tokens, smem=0)
+    (own,) = call(functools.partial(pack_tokens, rows), [shape((rows + micro, width), BF)], [], 0, prefix.reshape(1, micro), tokens, smem=0)
     near = sibling(own)
 
     a.state, own, b_own, b_got, near = sync(a.state, own, b_own, b_got, near)

time: 184 us -> 184 us (level)
    ppermute x24, waiting for transfers between devices: 25.2 us -> 23.1 us  [exchange(): lax.ppermute(pair[1], 'ring', self.left)]
    ppermute x24, waiting for transfers between devices: 31.4 us -> 33.4 us  [exchange(): lax.ppermute(pair[0], 'ring', self.right)]
    unnamed x23 -> x24, local copies, waits for them, and re-layouts: 4.66 us -> 4.57 us
  transfers between devices with their start and end apart: 74 -> 74, of which waited for: 35 -> 36; matrix products, arithmetic and copies ran while one was open for 1% -> 1% of each run, Pallas kernels for 22% -> 22%
where the time goes in v8:
time: 184 us
  starting transfers between devices  72.2 us (39%)
  waiting for transfers between devices  58.8 us (32%)
  Pallas kernels  45.1 us (25%)
  local copies, waits for them, and re-layouts  5.46 us (3%)
    pallas_call x29, Pallas kernels, call(): pl.pallas_call(body, name=body.func.__name__, out_shape=outs, in_specs=[p...  45.1 us
    ppermute x24, starting transfers between devices, exchange(): lax.ppermute(pair[0], 'ring', self.right)  37.9 us
    ppermute x24, waiting for transfers between devices, exchange(): lax.ppermute(pair[0], 'ring', self.right)  33.4 us
    ppermute x24, waiting for transfers between devices, exchange(): lax.ppermute(pair[1], 'ring', self.left)  23.1 us
    ppermute x13, starting transfers between devices, across(): return lax.ppermute(value, 'rep', SWAP)  18.9 us
    ppermute x24, starting transfers between devices, exchange(): lax.ppermute(pair[1], 'ring', self.left)  13.5 us
    unnamed x24, local copies, waits for them, and re-layouts  4.57 us
  transfers between devices with their start and end apart: 74, of which 36 were waited for; matrix products, arithmetic and copies ran while one was open for 1% of the time, Pallas kernels for 22%

profile of v8, /device:TPU:0, one launch (start us, length us, event | category | flops | bytes accessed | tf_op | source)
XLA Modules:
  0.0 184.0 jit_solution(16013337069391722035)
XLA Ops:
  5.5 3.0 %collective-permute-start.1 = (bf16[128,1024]{1,0:T(8,128)(2,1)S(1)}, bf16[128,1024]{1,0:T(8,128)(2,1)S(1)}, u32[]{:S(2)}, u32[]{:S(2)}) collective-permute-start(bf16[128,1024]{1,0:T(8,128)(2,1)S(1)} %constant_dynamic-update-slice_fusion.refs_4_.refs_0_), channel_id=1, source_target_pairs={{0,4},{4,8},{8,12},{12,14},{14,10},{10,6},{6,2},{2,0},{1,5},{5,9},... | collective-permute-start | bytes 786440 | tf_op jit(solution)/shard_map/ppermute | solution.py:90
  12.8 2.0 %collective-permute-start.11 = (bf16[88,1024]{1,0:T(8,128)(2,1)S(1)}, bf16[88,1024]{1,0:T(8,128)(2,1)S(1)}, u32[]{:S(2)}, u32[]{:S(2)}) collective-permute-start(bf16[88,1024]{1,0:T(8,128)(2,1)S(1)} %get-tuple-element.307.refs_1_), channel_id=1, source_target_pairs={{4,0},{8,4},{12,8},{14,12},{10,14},{6,10},{2,6},{0,2},{5,1},{9,5},... | collective-permute-start | bytes 540680 | tf_op jit(solution)/shard_map/ppermute | solution.py:90
  20.7 5.9 %collective-permute-done.5.refs_9_.refs_5_ = bf16[128,1024]{1,0:T(8,128)(2,1)S(1)} collective-permute-done((bf16[128,1024]{1,0:T(8,128)(2,1)S(1)}, bf16[128,1024]{1,0:T(8,128)(2,1)S(1)}, u32[]{:S(2)}, u32[]{:S(2)}) %collective-permute-start.5) | collective-permute-done | bytes 262176 | tf_op jit(solution)/shard_map/ppermute | solution.py:90
  26.6 1.7 collective-permute-start.7
  28.7 1.7 collective-permute-start.12
  32.4 3.5 %collective-permute-done.7.refs_8_.refs_4_ = bf16[128,1024]{1,0:T(8,128)(2,1)S(1)} collective-permute-done((bf16[128,1024]{1,0:T(8,128)(2,1)S(1)}, bf16[128,1024]{1,0:T(8,128)(2,1)S(1)}, u32[]{:S(2)}, u32[]{:S(2)}) %collective-permute-start.7) | collective-permute-done | bytes 262176 | tf_op jit(solution)/shard_map/ppermute | solution.py:90
  35.8 1.7 collective-permute-done.8.refs_7_.refs_3_
  38.0 1.7 collective-permute-start.13
  39.7 2.9 %collective-permute-done.15.refs_6_ = bf16[128,1408]{1,0:T(8,128)(2,1)S(1)} collective-permute-done((bf16[128,1408]{1,0:T(8,128)(2,1)S(1)}, bf16[128,1408]{1,0:T(8,128)(2,1)S(1)}, u32[]{:S(2)}, u32[]{:S(2)}) %collective-permute-start.15) | collective-permute-done | bytes 360480 | tf_op jit(solution)/shard_map/ppermute | solution.py:90
  42.5 2.4 %collective-permute-done.16.refs_1_ = bf16[128,1408]{1,0:T(8,128)(2,1)S(1)} collective-permute-done((bf16[128,1408]{1,0:T(8,128)(2,1)S(1)}, bf16[128,1408]{1,0:T(8,128)(2,1)S(1)}, u32[]{:S(2)}, u32[]{:S(2)}) %collective-permute-start.16) | collective-permute-done | bytes 360480 | tf_op jit(solution)/shard_map/ppermute | solution.py:90
  52.5 7.0 %attention.1 = (bf16[4,128,256]{2,1,0:T(8,128)(2,1)S(1)}, bf16[512,1024]{1,0:T(8,128)(2,1)S(1)}, bf16[512,768]{1,0:T(8,128)(2,1)S(1)}, f32[16,128,128]{2,1,0:T(8,128)S(1)}, bf16[1024,768]{1,0:T(8,128)(2,1)S(1)}) custom-call(s32[21]{0:T(128)S(1)} %dynamic-slice_bitcast_fusion.scal, bf16[130,1024]{1,0:T(8,128)(2,1)S(1)} %pack_tokens.1.refs_0_.block_ref, ...), custom_call_target="tpu_custom_call" | custom-call | flops 805306368 | bytes 8142932 | tf_op jit(solution)/shard_map/attention/pallas_call | solution.py:163
  65.7 5.8 %collective-permute-done.26.refs_5_ = bf16[88,1024]{1,0:T(8,128)(2,1)S(1)} collective-permute-done((bf16[88,1024]{1,0:T(8,128)(2,1)S(1)}, bf16[88,1024]{1,0:T(8,128)(2,1)S(1)}, u32[]{:S(2)}, u32[]{:S(2)}) %collective-permute-start.26) | collective-permute-done | bytes 180256 | tf_op jit(solution)/shard_map/ppermute | solution.py:90
  75.6 1.8 collective-permute-start.31
  77.4 2.7 %middle.1 = (f32[512,1024]{1,0:T(8,128)S(1)}, bf16[512,1024]{1,0:T(8,128)(2,1)S(1)}, bf16[512,1024]{1,0:T(8,128)(2,1)S(1)}, bf16[256,1024]{1,0:T(8,128)(2,1)S(1)}) custom-call(s32[21]{0:T(128)S(1)} %dynamic-slice_bitcast_fusion.scal, bf16[130,1024]{1,0:T(8,128)(2,1)S(1)} %pack_tokens.1.refs_0_.block_ref, ...), custom_call_target="tpu_custom_call" | custom-call | flops 1073741824 | bytes 8929364 | tf_op jit(solution)/shard_map/middle/pallas_call | solution.py:163
  80.1 1.7 collective-permute-done.32.refs_9_
  82.8 3.0 %hidden_units.1 = (f32[512,704]{1,0:T(8,128)S(1)}, f32[512,704]{1,0:T(8,128)S(1)}, bf16[512,704]{1,0:T(8,128)(2,1)S(1)}, bf16[1024,1408]{1,0:T(8,128)(2,1)S(1)}) custom-call(s32[21]{0:T(128)S(1)} %dynamic-slice_bitcast_fusion.scal, bf16[512,1024]{1,0:T(8,128)(2,1)S(1)} %get-tuple-element.276.h2_ref, ...), custom_call_target="tpu_custom_call" | custom-call | flops 16000000000 | bytes 10420308 | tf_op jit(solution)/shard_map/hidden_units/pallas_call | solution.py:163
  85.8 1.8 grad_down_parts.1
  89.8 3.9 %hidden_back.1 = (bf16[512,1408]{1,0:T(8,128)(2,1)S(1)}, f32[2,128,1024]{2,1,0:T(8,128)S(1)}, bf16[2,128,1024]{2,1,0:T(8,128)(2,1)S(1)}, bf16[704,1024]{1,0:T(8,128)(2,1)S(1)}) custom-call(s32[21]{0:T(128)S(1)} %dynamic-slice_bitcast_fusion.scal, bf16[512,1024]{1,0:T(8,128)(2,1)S(1)} %get-tuple-element.306.refs_0_, ...), custom_call_target="tpu_custom_call" | custom-call | flops 32000000000 | bytes 12714068 | tf_op jit(solution)/shard_map/hidden_back/pallas_call | solution.py:163
  93.8 1.6 collective-permute-start.38
  97.6 2.7 %grad_in_parts.1 = (bf16[128,1408]{1,0:T(8,128)(2,1)S(1)}, bf16[128,1408]{1,0:T(8,128)(2,1)S(1)}, bf16[128,1408]{1,0:T(8,128)(2,1)S(1)}, bf16[128,1408]{1,0:T(8,...) custom-call(s32[21]{0:T(128)S(1)} %dynamic-slice_bitcast_fusion.scal, ...), custom_call_target="tpu_custom_call" | custom-call | flops 1610612736 | bytes 5374036 | tf_op jit(solution)/shard_map/grad_in_parts/pallas_call | solution.py:163
  113.2 1.6 collective-permute-start.50
  116.8 1.6 collective-permute-start.47
  120.4 7.0 %attention_back.1 = (bf16[512,768]{1,0:T(8,128)(2,1)S(1)}, bf16[512,1024]{1,0:T(8,128)(2,1)S(1)}, f32[2,128,1024]{2,1,0:T(8,128)S(1)}, bf16[2,128,1024]{2,1,0:T(8,128)(2,1)S(1)}) custom-call(s32[21]{0:T(128)S(1)} %dynamic-slice_bitcast_fusion.scal, bf16[2,128,1024]{2,1,0:T(8,128)(2,1)S(1)} %get-tuple-element.350.ga_own, ...), custom_call_target="tpu_custom_call" | custom-call | flops 1879048192 | bytes 8650836 | tf_op jit(solution)/shard_map/attention_back/pallas_call | solution.py:163
  129.1 1.6 collective-permute-start.54
  131.2 2.1 %grad_first_parts.1 = (bf16[128,1024]{1,0:T(8,128)(2,1)S(1)}, bf16[128,1024]{1,0:T(8,128)(2,1)S(1)}, bf16[128,1024]{1,0:T(8,128)(2,1)S(1)}, bf16[128,1024]{1,0:T...) custom-call(s32[21]{0:T(128)S(1)} %dynamic-slice_bitcast_fusion.scal, ...), custom_call_target="tpu_custom_call" | custom-call | flops 32000000000 | bytes 6029396 | tf_op jit(solution)/shard_map/grad_first_parts/pallas_call | solution.py:163
  137.0 2.9 %collective-permute-done.54.right_got = bf16[128,1408]{1,0:T(8,128)(2,1)S(1)} collective-permute-done((bf16[128,1408]{1,0:T(8,128)(2,1)S(1)}, bf16[128,1408]{1,0:T(8,128)(2,1)S(1)}, u32[]{:S(2)}, u32[]{:S(2)}) %collective-permute-start.54) | collective-permute-done | bytes 360480 | tf_op jit(solution)/shard_map/ppermute | solution.py:90
  139.9 1.8 %collective-permute-start.60 = (bf16[88,1024]{1,0:T(8,128)(2,1)S(1)}, bf16[88,1024]{1,0:T(8,128)(2,1)S(1)}, u32[]{:S(2)}, u32[]{:S(2)}) collective-permute-start(bf16[88,1024]{1,0:T(8,128)(2,1)S(1)} %add_convert_fusion.3.low_ref), channel_id=1, source_target_pairs={{0,16},{16,0},{1,17},{17,1},{2,18},{18,2},{3,19},{19,3},{4,20},{20... | collective-permute-start | bytes 540680 | tf_op jit(solution)/shard_map/ppermute | solution.py:52
  147.4 1.8 finish_tokens.1
  149.2 3.2 %collective-permute-done.58.right_got = bf16[128,1024]{1,0:T(8,128)(2,1)S(1)} collective-permute-done((bf16[128,1024]{1,0:T(8,128)(2,1)S(1)}, bf16[128,1024]{1,0:T(8,128)(2,1)S(1)}, u32[]{:S(2)}, u32[]{:S(2)}) %collective-permute-start.58) | collective-permute-done | bytes 262176 | tf_op jit(solution)/shard_map/ppermute | solution.py:90
  157.5 2.6 %collective-permute-done.63.right_ref = bf16[128,1408]{1,0:T(8,128)(2,1)S(1)} collective-permute-done((bf16[128,1408]{1,0:T(8,128)(2,1)S(1)}, bf16[128,1408]{1,0:T(8,128)(2,1)S(1)}, u32[]{:S(2)}, u32[]{:S(2)}) %collective-permute-start.63) | collective-permute-done | bytes 360480 | tf_op jit(solution)/shard_map/ppermute | solution.py:90
  169.1 3.0 %collective-permute-done.67.right_ref = bf16[128,1024]{1,0:T(8,128)(2,1)S(1)} collective-permute-done((bf16[128,1024]{1,0:T(8,128)(2,1)S(1)}, bf16[128,1024]{1,0:T(8,128)(2,1)S(1)}, u32[]{:S(2)}, u32[]{:S(2)}) %collective-permute-start.67) | collective-permute-done | bytes 262176 | tf_op jit(solution)/shard_map/ppermute | solution.py:90
  176.5 2.6 %unpack_in.1 = f32[64,5632]{1,0:T(8,128)} custom-call(s32[21]{0:T(128)S(1)} %dynamic-slice_bitcast_fusion.scal, bf16[64,1408]{1,0:T(8,128)(2,1)S(1)} %get-tuple-element.430.own_ref, bf16[64,1408]{1,0:T(8,128)(2,1)S(1)} %collective-permute-done.65.near_ref, bf16[64,1408]{1,0:T(8,128)(2,1)S(1)} %collective-permute-done.69.far_ref, ...), custom_call_target="tpu_custom_call" | custom-call | flops 4000000000 | bytes 2162772 | tf_op jit(solution)/shard_map/unpack_in/pallas_call | solution.py:163
  (190 shorter events, 92.7 us)
Async XLA Ops:
  5.5 10.4 %collective-permute-start.1 = (bf16[128,1024]{1,0:T(8,128)(2,1)S(1)}, bf16[128,1024]{1,0:T(8,128)(2,1)S(1)}, u32[]{:S(2)}, u32[]{:S(2)}) collective-permute-start(bf16[128,1024]{1,0:T(8,128)(2,1)S(1)} %constant_dynamic-update-slice_fusion.refs_4_.refs_0_), channel_id=1, source_target_pairs={{0,4},{4,8},{8,12},{12,14},{14,10},{10,6},{6,2},{2,0},{1,5},{5,9},... | collective-permute-start | bytes 786440 | tf_op jit(solution)/shard_map/ppermute | solution.py:90
  8.4 8.8 %collective-permute-start.2 = (bf16[128,1024]{1,0:T(8,128)(2,1)S(1)}, bf16[128,1024]{1,0:T(8,128)(2,1)S(1)}, u32[]{:S(2)}, u32[]{:S(2)}) collective-permute-start(bf16[128,1024]{1,0:T(8,128)(2,1)S(1)} %constant_dynamic-update-slice_fusion.refs_4_.refs_0_), channel_id=1, source_target_pairs={{4,0},{8,4},{12,8},{14,12},{10,14},{6,10},{2,6},{0,2},{5,1},{9,5},... | collective-permute-start | bytes 786440 | tf_op jit(solution)/shard_map/ppermute | solution.py:90
  12.8 15.9 %collective-permute-start.11 = (bf16[88,1024]{1,0:T(8,128)(2,1)S(1)}, bf16[88,1024]{1,0:T(8,128)(2,1)S(1)}, u32[]{:S(2)}, u32[]{:S(2)}) collective-permute-start(bf16[88,1024]{1,0:T(8,128)(2,1)S(1)} %get-tuple-element.307.refs_1_), channel_id=1, source_target_pairs={{4,0},{8,4},{12,8},{14,12},{10,14},{6,10},{2,6},{0,2},{5,1},{9,5},... | collective-permute-start | bytes 540680 | tf_op jit(solution)/shard_map/ppermute | solution.py:90
  14.7 13.9 %collective-permute-start.10 = (bf16[88,1024]{1,0:T(8,128)(2,1)S(1)}, bf16[88,1024]{1,0:T(8,128)(2,1)S(1)}, u32[]{:S(2)}, u32[]{:S(2)}) collective-permute-start(bf16[88,1024]{1,0:T(8,128)(2,1)S(1)} %get-tuple-element.307.refs_1_), channel_id=1, source_target_pairs={{0,4},{4,8},{8,12},{12,14},{14,10},{10,6},{6,2},{2,0},{1,5},{5,9},... | collective-permute-start | bytes 540680 | tf_op jit(solution)/shard_map/ppermute | solution.py:90
  17.3 9.3 %collective-permute-start.5 = (bf16[128,1024]{1,0:T(8,128)(2,1)S(1)}, bf16[128,1024]{1,0:T(8,128)(2,1)S(1)}, u32[]{:S(2)}, u32[]{:S(2)}) collective-permute-start(bf16[128,1024]{1,0:T(8,128)(2,1)S(1)} %collective-permute-done.1.refs_10_.refs_6_), channel_id=1, source_target_pairs={{0,4},{4,8},{8,12},{12,14},{14,10},{10,6},{6,2},{2,0},{1,5},{5,9},... | collective-permute-start | bytes 786440 | tf_op jit(solution)/shard_map/ppermute | solution.py:90
  19.3 9.3 %collective-permute-start.9 = (bf16[130,1024]{1,0:T(8,128)(2,1)S(1)}, bf16[130,1024]{1,0:T(8,128)(2,1)S(1)}, u32[]{:S(2)}, u32[]{:S(2)}) collective-permute-start(bf16[130,1024]{1,0:T(8,128)(2,1)S(1)} %pack_tokens.1.refs_0_.block_ref), channel_id=1, source_target_pairs={{0,16},{16,0},{1,17},{17,1},{2,18},{18,2},{3,19},{19,3},{4,20},{20... | collective-permute-start | bytes 798728 | tf_op jit(solution)/shard_map/ppermute | solution.py:52
  26.6 9.2 %collective-permute-start.7 = (bf16[128,1024]{1,0:T(8,128)(2,1)S(1)}, bf16[128,1024]{1,0:T(8,128)(2,1)S(1)}, u32[]{:S(2)}, u32[]{:S(2)}) collective-permute-start(bf16[128,1024]{1,0:T(8,128)(2,1)S(1)} %collective-permute-done.5.refs_9_.refs_5_), channel_id=1, source_target_pairs={{0,4},{4,8},{8,12},{12,14},{14,10},{10,6},{6,2},{2,0},{1,5},{5,9},... | collective-permute-start | bytes 786440 | tf_op jit(solution)/shard_map/ppermute | solution.py:90
  28.3 9.2 %collective-permute-start.8 = (bf16[128,1024]{1,0:T(8,128)(2,1)S(1)}, bf16[128,1024]{1,0:T(8,128)(2,1)S(1)}, u32[]{:S(2)}, u32[]{:S(2)}) collective-permute-start(bf16[128,1024]{1,0:T(8,128)(2,1)S(1)} %collective-permute-done.6.refs_6_.refs_2_), channel_id=1, source_target_pairs={{4,0},{8,4},{12,8},{14,12},{10,14},{6,10},{2,6},{0,2},{5,1},{9,5},... | collective-permute-start | bytes 786440 | tf_op jit(solution)/shard_map/ppermute | solution.py:90
  28.7 8.9 %collective-permute-start.12 = (bf16[128,1024]{1,0:T(8,128)(2,1)S(1)}, bf16[128,1024]{1,0:T(8,128)(2,1)S(1)}, u32[]{:S(2)}, u32[]{:S(2)}) collective-permute-start(bf16[128,1024]{1,0:T(8,128)(2,1)S(1)} %bitcast.31), channel_id=1, source_target_pairs={{0,16},{16,0},{1,17},{17,1},{2,18},{18,2},{3,19},{19,3},{4,20},{20... | collective-permute-start | bytes 786440 | tf_op jit(solution)/shard_map/ppermute | solution.py:52
  30.3 12.2 %collective-permute-start.15 = (bf16[128,1408]{1,0:T(8,128)(2,1)S(1)}, bf16[128,1408]{1,0:T(8,128)(2,1)S(1)}, u32[]{:S(2)}, u32[]{:S(2)}) collective-permute-start(bf16[128,1408]{1,0:T(8,128)(2,1)S(1)} %constant_dynamic-update-slice_fusion.2.refs_0_), channel_id=1, source_target_pairs={{0,4},{4,8},{8,12},{12,14},{14,10},{10,6},{6,2},{2,0},{1,5},{5,9},... | collective-permute-start | bytes 1081352 | tf_op jit(solution)/shard_map/ppermute | solution.py:90
  31.9 13.0 %collective-permute-start.16 = (bf16[128,1408]{1,0:T(8,128)(2,1)S(1)}, bf16[128,1408]{1,0:T(8,128)(2,1)S(1)}, u32[]{:S(2)}, u32[]{:S(2)}) collective-permute-start(bf16[128,1408]{1,0:T(8,128)(2,1)S(1)} %constant_dynamic-update-slice_fusion.2.refs_0_), channel_id=1, source_target_pairs={{4,0},{8,4},{12,8},{14,12},{10,14},{6,10},{2,6},{0,2},{5,1},{9,5},... | collective-permute-start | bytes 1081352 | tf_op jit(solution)/shard_map/ppermute | solution.py:90
  46.3 13.8 %collective-permute-start.18 = (bf16[128,1408]{1,0:T(8,128)(2,1)S(1)}, bf16[128,1408]{1,0:T(8,128)(2,1)S(1)}, u32[]{:S(2)}, u32[]{:S(2)}) collective-permute-start(bf16[128,1408]{1,0:T(8,128)(2,1)S(1)} %collective-permute-done.15.refs_6_), channel_id=1, source_target_pairs={{0,4},{4,8},{8,12},{12,14},{14,10},{10,6},{6,2},{2,0},{1,5},{5,9},... | collective-permute-start | bytes 1081352 | tf_op jit(solution)/shard_map/ppermute | solution.py:90
  47.9 12.3 %collective-permute-start.19 = (bf16[128,1408]{1,0:T(8,128)(2,1)S(1)}, bf16[128,1408]{1,0:T(8,128)(2,1)S(1)}, u32[]{:S(2)}, u32[]{:S(2)}) collective-permute-start(bf16[128,1408]{1,0:T(8,128)(2,1)S(1)} %collective-permute-done.16.refs_1_), channel_id=1, source_target_pairs={{4,0},{8,4},{12,8},{14,12},{10,14},{6,10},{2,6},{0,2},{5,1},{9,5},... | collective-permute-start | bytes 1081352 | tf_op jit(solution)/shard_map/ppermute | solution.py:90
  49.0 16.3 %collective-permute-start.23 = (bf16[1024,256]{1,0:T(8,128)(2,1)S(1)}, bf16[1024,256]{1,0:T(8,128)(2,1)S(1)}, u32[]{:S(2)}, u32[]{:S(2)}) collective-permute-start(bf16[1024,256]{1,0:T(8,128)(2,1)S(1)} %gather_out.1.refs_6_), channel_id=1, source_target_pairs={{0,16},{16,0},{1,17},{17,1},{2,18},{18,2},{3,19},{19,3},{4,20},{20... | collective-permute-start | bytes 1572872 | tf_op jit(solution)/shard_map/ppermute | solution.py:52
  50.5 9.1 %collective-permute-start.20 = (bf16[88,1024]{1,0:T(8,128)(2,1)S(1)}, bf16[88,1024]{1,0:T(8,128)(2,1)S(1)}, u32[]{:S(2)}, u32[]{:S(2)}) collective-permute-start(bf16[88,1024]{1,0:T(8,128)(2,1)S(1)} %collective-permute-done.10.refs_7_), channel_id=1, source_target_pairs={{0,4},{4,8},{8,12},{12,14},{14,10},{10,6},{6,2},{2,0},{1,5},{5,9},... | collective-permute-start | bytes 540680 | tf_op jit(solution)/shard_map/ppermute | solution.py:90
  60.1 12.6 %collective-permute-start.24 = (bf16[128,1408]{1,0:T(8,128)(2,1)S(1)}, bf16[128,1408]{1,0:T(8,128)(2,1)S(1)}, u32[]{:S(2)}, u32[]{:S(2)}) collective-permute-start(bf16[128,1408]{1,0:T(8,128)(2,1)S(1)} %collective-permute-done.18.refs_5_), channel_id=1, source_target_pairs={{0,4},{4,8},{8,12},{12,14},{14,10},{10,6},{6,2},{2,0},{1,5},{5,9},... | collective-permute-start | bytes 1081352 | tf_op jit(solution)/shard_map/ppermute | solution.py:90
  61.7 11.1 %collective-permute-start.25 = (bf16[128,1408]{1,0:T(8,128)(2,1)S(1)}, bf16[128,1408]{1,0:T(8,128)(2,1)S(1)}, u32[]{:S(2)}, u32[]{:S(2)}) collective-permute-start(bf16[128,1408]{1,0:T(8,128)(2,1)S(1)} %collective-permute-done.19.refs_2_), channel_id=1, source_target_pairs={{4,0},{8,4},{12,8},{14,12},{10,14},{6,10},{2,6},{0,2},{5,1},{9,5},... | collective-permute-start | bytes 1081352 | tf_op jit(solution)/shard_map/ppermute | solution.py:90
  62.2 10.6 %collective-permute-start.22 = (bf16[4,128,256]{2,1,0:T(8,128)(2,1)S(1)}, bf16[4,128,256]{2,1,0:T(8,128)(2,1)S(1)}, u32[]{:S(2)}, u32[]{:S(2)}) collective-permute-start(bf16[4,128,256]{2,1,0:T(8,128)(2,1)S(1)} %get-tuple-element.261.refs_4_), channel_id=1, source_target_pairs={{0,16},{16,0},{1,17},{17,1},{2,18},{18,2},{3,19},{19,3},{4,20},{20... | collective-permute-start | bytes 786440 | tf_op jit(solution)/shard_map/ppermute | solution.py:52
  73.0 9.3 %collective-permute-start.30 = (bf16[64,1408]{1,0:T(8,128)(2,1)S(1)}, bf16[64,1408]{1,0:T(8,128)(2,1)S(1)}, u32[]{:S(2)}, u32[]{:S(2)}) collective-permute-start(bf16[64,1408]{1,0:T(8,128)(2,1)S(1)} %slice.67), channel_id=1, source_target_pairs={{4,0},{8,4},{12,8},{14,12},{10,14},{6,10},{2,6},{0,2},{5,1},{9,5},... | collective-permute-start | bytes 540680 | tf_op jit(solution)/shard_map/ppermute | solution.py:90
  116.8 10.9 %collective-permute-start.47 = (bf16[128,1408]{1,0:T(8,128)(2,1)S(1)}, bf16[128,1408]{1,0:T(8,128)(2,1)S(1)}, u32[]{:S(2)}, u32[]{:S(2)}) collective-permute-start(bf16[128,1408]{1,0:T(8,128)(2,1)S(1)} %get-tuple-element.361), channel_id=1, source_target_pairs={{0,4},{4,8},{8,12},{12,14},{14,10},{10,6},{6,2},{2,0},{1,5},{5,9},... | collective-permute-start | bytes 1081352 | tf_op jit(solution)/shard_map/ppermute | solution.py:90
  118.4 10.5 %collective-permute-start.48 = (bf16[128,1408]{1,0:T(8,128)(2,1)S(1)}, bf16[128,1408]{1,0:T(8,128)(2,1)S(1)}, u32[]{:S(2)}, u32[]{:S(2)}) collective-permute-start(bf16[128,1408]{1,0:T(8,128)(2,1)S(1)} %get-tuple-element.362), channel_id=1, source_target_pairs={{4,0},{8,4},{12,8},{14,12},{10,14},{6,10},{2,6},{0,2},{5,1},{9,5},... | collective-permute-start | bytes 1081352 | tf_op jit(solution)/shard_map/ppermute | solution.py:90
  129.1 10.8 %collective-permute-start.54 = (bf16[128,1408]{1,0:T(8,128)(2,1)S(1)}, bf16[128,1408]{1,0:T(8,128)(2,1)S(1)}, u32[]{:S(2)}, u32[]{:S(2)}) collective-permute-start(bf16[128,1408]{1,0:T(8,128)(2,1)S(1)} %get-tuple-element.381), channel_id=1, source_target_pairs={{0,4},{4,8},{8,12},{12,14},{14,10},{10,6},{6,2},{2,0},{1,5},{5,9},... | collective-permute-start | bytes 1081352 | tf_op jit(solution)/shard_map/ppermute | solution.py:90
  130.7 11.1 %collective-permute-start.55 = (bf16[128,1408]{1,0:T(8,128)(2,1)S(1)}, bf16[128,1408]{1,0:T(8,128)(2,1)S(1)}, u32[]{:S(2)}, u32[]{:S(2)}) collective-permute-start(bf16[128,1408]{1,0:T(8,128)(2,1)S(1)} %get-tuple-element.382), channel_id=1, source_target_pairs={{4,0},{8,4},{12,8},{14,12},{10,14},{6,10},{2,6},{0,2},{5,1},{9,5},... | collective-permute-start | bytes 1081352 | tf_op jit(solution)/shard_map/ppermute | solution.py:90
  133.4 9.5 %collective-permute-start.56 = (bf16[128,1024]{1,0:T(8,128)(2,1)S(1)}, bf16[128,1024]{1,0:T(8,128)(2,1)S(1)}, u32[]{:S(2)}, u32[]{:S(2)}) collective-permute-start(bf16[128,1024]{1,0:T(8,128)(2,1)S(1)} %fusion.2), channel_id=1, source_target_pairs={{0,16},{16,0},{1,17},{17,1},{2,18},{18,2},{3,19},{19,3},{4,20},{20... | collective-permute-start | bytes 786440 | tf_op jit(solution)/shard_map/ppermute | solution.py:52
  139.9 9.2 %collective-permute-start.60 = (bf16[88,1024]{1,0:T(8,128)(2,1)S(1)}, bf16[88,1024]{1,0:T(8,128)(2,1)S(1)}, u32[]{:S(2)}, u32[]{:S(2)}) collective-permute-start(bf16[88,1024]{1,0:T(8,128)(2,1)S(1)} %add_convert_fusion.3.low_ref), channel_id=1, source_target_pairs={{0,16},{16,0},{1,17},{17,1},{2,18},{18,2},{3,19},{19,3},{4,20},{20... | collective-permute-start | bytes 540680 | tf_op jit(solution)/shard_map/ppermute | solution.py:52
  143.0 9.3 %collective-permute-start.58 = (bf16[128,1024]{1,0:T(8,128)(2,1)S(1)}, bf16[128,1024]{1,0:T(8,128)(2,1)S(1)}, u32[]{:S(2)}, u32[]{:S(2)}) collective-permute-start(bf16[128,1024]{1,0:T(8,128)(2,1)S(1)} %get-tuple-element.393), channel_id=1, source_target_pairs={{0,4},{4,8},{8,12},{12,14},{14,10},{10,6},{6,2},{2,0},{1,5},{5,9},... | collective-permute-start | bytes 786440 | tf_op jit(solution)/shard_map/ppermute | solution.py:90
  144.4 9.2 %collective-permute-start.59 = (bf16[128,1024]{1,0:T(8,128)(2,1)S(1)}, bf16[128,1024]{1,0:T(8,128)(2,1)S(1)}, u32[]{:S(2)}, u32[]{:S(2)}) collective-permute-start(bf16[128,1024]{1,0:T(8,128)(2,1)S(1)} %get-tuple-element.394), channel_id=1, source_target_pairs={{4,0},{8,4},{12,8},{14,12},{10,14},{6,10},{2,6},{0,2},{5,1},{9,5},... | collective-permute-start | bytes 786440 | tf_op jit(solution)/shard_map/ppermute | solution.py:90
  145.3 14.7 %collective-permute-start.63 = (bf16[128,1408]{1,0:T(8,128)(2,1)S(1)}, bf16[128,1408]{1,0:T(8,128)(2,1)S(1)}, u32[]{:S(2)}, u32[]{:S(2)}) collective-permute-start(bf16[128,1408]{1,0:T(8,128)(2,1)S(1)} %get-tuple-element.407), channel_id=1, source_target_pairs={{0,4},{4,8},{8,12},{12,14},{14,10},{10,6},{6,2},{2,0},{1,5},{5,9},... | collective-permute-start | bytes 1081352 | tf_op jit(solution)/shard_map/ppermute | solution.py:90
  146.7 14.7 %collective-permute-start.64 = (bf16[128,1408]{1,0:T(8,128)(2,1)S(1)}, bf16[128,1408]{1,0:T(8,128)(2,1)S(1)}, u32[]{:S(2)}, u32[]{:S(2)}) collective-permute-start(bf16[128,1408]{1,0:T(8,128)(2,1)S(1)} %get-tuple-element.408), channel_id=1, source_target_pairs={{4,0},{8,4},{12,8},{14,12},{10,14},{6,10},{2,6},{0,2},{5,1},{9,5},... | collective-permute-start | bytes 1081352 | tf_op jit(solution)/shard_map/ppermute | solution.py:90
  153.8 9.9 %collective-permute-start.61 = (bf16[128,1024]{1,0:T(8,128)(2,1)S(1)}, bf16[128,1024]{1,0:T(8,128)(2,1)S(1)}, u32[]{:S(2)}, u32[]{:S(2)}) collective-permute-start(bf16[128,1024]{1,0:T(8,128)(2,1)S(1)} %get-tuple-element.400), channel_id=1, source_target_pairs={{0,4},{4,8},{8,12},{12,14},{14,10},{10,6},{6,2},{2,0},{1,5},{5,9},... | collective-permute-start | bytes 786440 | tf_op jit(solution)/shard_map/ppermute | solution.py:90
  155.0 9.9 %collective-permute-start.62 = (bf16[128,1024]{1,0:T(8,128)(2,1)S(1)}, bf16[128,1024]{1,0:T(8,128)(2,1)S(1)}, u32[]{:S(2)}, u32[]{:S(2)}) collective-permute-start(bf16[128,1024]{1,0:T(8,128)(2,1)S(1)} %get-tuple-element.401), channel_id=1, source_target_pairs={{4,0},{8,4},{12,8},{14,12},{10,14},{6,10},{2,6},{0,2},{5,1},{9,5},... | collective-permute-start | bytes 786440 | tf_op jit(solution)/shard_map/ppermute | solution.py:90
  155.9 9.0 %collective-permute-start.66 = (bf16[128,1024]{1,0:T(8,128)(2,1)S(1)}, bf16[128,1024]{1,0:T(8,128)(2,1)S(1)}, u32[]{:S(2)}, u32[]{:S(2)}) collective-permute-start(bf16[128,1024]{1,0:T(8,128)(2,1)S(1)} %fusion.3), channel_id=1, source_target_pairs={{0,16},{16,0},{1,17},{17,1},{2,18},{18,2},{3,19},{19,3},{4,20},{20... | collective-permute-start | bytes 786440 | tf_op jit(solution)/shard_map/ppermute | solution.py:52
  (53 other events, 404.7 us)
